TPU v7x, 32 devices: a whole 2x2x4 slice. The times are simulated.
32 devices in a mesh: ctx: 16 (over z, y, x), fsdp: 2 (over core).
Axes of the slice: x: 2, y: 2, z: 4, core: 2. Of those that a mesh axis runs over, the one named last changes fastest.
Arguments:
- inputs: bfloat16 [2, 2, 2048, 960], P(None, 'fsdp', 'ctx'), may hold values from -6 to 6
- gain_attn: bfloat16 [960], P('fsdp'), may hold values from 0.099609375 to 1.8984375
- w_query: bfloat16 [960, 960], P('fsdp'), may hold values from -0.1875 to 0.1875
- w_keyval: bfloat16 [960, 640], P('fsdp'), may hold values from -0.1875 to 0.1875
- w_out: bfloat16 [960, 960], P('fsdp'), may hold values from -0.75 to 0.75
- gain_mlp: bfloat16 [960], P('fsdp'), may hold values from 0.099609375 to 1.8984375
- w_gate: bfloat16 [960, 2560], P('fsdp'), may hold values from -0.1875 to 0.1875
- w_up: bfloat16 [960, 2560], P('fsdp'), may hold values from -0.1875 to 0.1875
- w_down: bfloat16 [2560, 960], P('fsdp'), may hold values from -0.125 to 0.125
- cotangent: bfloat16 [2, 2, 2048, 960], P(None, 'fsdp', 'ctx'), may hold values from -6 to 6
- seq_blocks: int32 [2, 2, 2], replicated, may hold values from 8 to 8, as said below
- block_slots: int32 [2, 2, 16], replicated, may hold values from 0 to 15, each once within a row
Outputs:
- layer_out: bfloat16 [2, 2, 2048, 960], P(None, 'fsdp', 'ctx')
- input_grad: float32 [2, 2, 2048, 960], P(None, 'fsdp', 'ctx')
- gain_attn_grad: float32 [960], P('fsdp')
- query_grad: float32 [960, 960], P('fsdp')
- keyval_grad: float32 [960, 640], P('fsdp')
- out_grad: float32 [960, 960], P('fsdp')
- gain_mlp_grad: float32 [960], P('fsdp')
- gate_grad: float32 [960, 2560], P('fsdp')
- up_grad: float32 [960, 2560], P('fsdp')
- down_grad: float32 [2560, 960], P('fsdp')
Inputs may be any that keep to these rules, and one draw needn't show every extreme that they name: `seq_blocks`: each row holds the lengths in blocks of 128 tokens of the 2 sequences of one group, in natural order; they sum to 16. `block_slots`: each row is a permutation of the slots of one group.
All inputs are finite; a program needn't handle non-finite values.
Results may differ from a plain program's by a relative error of at most 0.015.
Values may be sent and summed in bfloat16 or wider, within the bound.
No kernel may reach another device: no remote copies, remote signals or barrier semaphores. Data moves between devices by JAX's collectives and lax.ppermute only.
A program may use at most 320 MiB of HBM per device.

v0:
```python
import jax
import jax.numpy as jnp
from jax import lax
from jax.sharding import PartitionSpec as P

HEADS = 15
KVH = 5
HD = 64
WINDOW = 2048
BLK = 128


EPS = 1e-05
NEG = -1e30


def matmul(left, right):
    return jnp.dot(left, right, preferred_element_type=jnp.float32)


def matmul_left_t(left, right):
    return lax.dot_general(
        left, right, (((0,), (0,)), ((), ())), preferred_element_type=jnp.float32
    )


def matmul_right_t(left, right):
    return lax.dot_general(
        left, right, (((1,), (1,)), ((), ())), preferred_element_type=jnp.float32
    )


def rms_inverse(values):
    return lax.rsqrt(jnp.mean(values * values, axis=-1, keepdims=True) + EPS)


def rms_back(values, inverse, normalized_gradient, gain):
    scaled = normalized_gradient * gain
    gain_part = jnp.sum(normalized_gradient * values * inverse, axis=0)
    cubed = inverse * inverse * inverse
    input_part = inverse * scaled - values * cubed * jnp.mean(
        scaled * values, axis=-1, keepdims=True
    )
    return (input_part, gain_part)


def group_layout(sequence_lengths_row, slots_row, block_count):
    blocks = jnp.arange(block_count, dtype=jnp.int32)
    block_ends = jnp.cumsum(sequence_lengths_row)
    seq_natural = jnp.sum((block_ends[None, :] <= blocks[:, None]).astype(jnp.int32), axis=1)
    slot_match = (slots_row[None, :] == blocks[:, None]).astype(jnp.int32)
    natural = jnp.sum(slot_match * blocks[None, :], axis=1)
    seq_slot = jnp.sum(slot_match * seq_natural[None, :], axis=1)
    offsets = jnp.arange(BLK, dtype=jnp.int32)
    positions = (natural[:, None] * BLK + offsets[None, :]).reshape(-1)
    sequence = jnp.broadcast_to(seq_slot[:, None], (block_count, BLK)).reshape(-1)
    return (positions, sequence)


def visible(query_pos, query_seq, key_pos, key_seq):
    same_seq = query_seq[:, None] == key_seq[None, :]
    causal = key_pos[None, :] <= query_pos[:, None]
    inside = query_pos[:, None] - key_pos[None, :] < WINDOW
    return same_seq & causal & inside


def scores_for(query_heads, key_rows, logit_scale_factor):
    return (
        jnp.einsum("tgrd,kgd->grtk", query_heads, key_rows, preferred_element_type=jnp.float32)
        * logit_scale_factor
    )


def attention_forward(
    query_heads,
    key_tiles,
    value_tiles,
    pos_tiles,
    seq_tiles,
    query_pos,
    query_seq,
    logit_scale_factor,
):
    tokens, kv_heads, group_size, head_dim = query_heads.shape

    def max_step(carried, tile_data):
        key_rows, key_pos, key_seq = tile_data
        allowed = visible(query_pos, query_seq, key_pos, key_seq)
        running_max, running_sum = carried
        scores = jnp.where(allowed, scores_for(query_heads, key_rows, logit_scale_factor), NEG)
        new_max = jnp.maximum(running_max, jnp.max(scores, axis=-1))
        shifted = jnp.where(allowed, jnp.exp(scores - new_max[..., None]), 0.0)
        carried = (
            new_max,
            running_sum * jnp.exp(running_max - new_max) + jnp.sum(shifted, axis=-1),
        )
        return (carried, None)

    start_max = jnp.full((kv_heads, group_size, tokens), NEG, jnp.float32)
    start_sum = jnp.zeros((kv_heads, group_size, tokens), jnp.float32)
    (row_max, row_sum), unused = lax.scan(
        max_step, (start_max, start_sum), (key_tiles, pos_tiles, seq_tiles)
    )
    log_total = row_max + jnp.log(row_sum)

    def value_step(carried, tile_data):
        key_rows, value_rows, key_pos, key_seq = tile_data
        allowed = visible(query_pos, query_seq, key_pos, key_seq)
        probs_low = jnp.where(
            allowed,
            jnp.exp(scores_for(query_heads, key_rows, logit_scale_factor) - log_total[..., None]),
            0.0,
        ).astype(jnp.bfloat16)
        carried = carried + jnp.einsum(
            "grtk,kgd->tgrd", probs_low, value_rows, preferred_element_type=jnp.float32
        )
        return (carried, None)

    start_out = jnp.zeros((tokens, kv_heads, group_size, head_dim), jnp.float32)
    attended, unused = lax.scan(
        value_step, start_out, (key_tiles, value_tiles, pos_tiles, seq_tiles)
    )
    return (log_total, attended)


def attention_backward(
    query_heads,
    key_tiles,
    value_tiles,
    pos_tiles,
    seq_tiles,
    query_pos,
    query_seq,
    logit_scale_factor,
    log_total,
    head_gradients,
    softmax_correction,
):
    tokens, kv_heads, group_size, head_dim = query_heads.shape
    tile_rows = key_tiles.shape[1]

    def grad_step(carried, tile_data):
        key_rows, value_rows, key_pos, key_seq = tile_data
        allowed = visible(query_pos, query_seq, key_pos, key_seq)
        grad_query = carried
        probs = jnp.where(
            allowed,
            jnp.exp(scores_for(query_heads, key_rows, logit_scale_factor) - log_total[..., None]),
            0.0,
        )
        grad_probs = jnp.einsum(
            "tgrd,kgd->grtk", head_gradients, value_rows, preferred_element_type=jnp.float32
        )
        grad_scores = (probs * (grad_probs - softmax_correction[..., None])).astype(jnp.bfloat16)
        grad_query = grad_query + jnp.einsum(
            "grtk,kgd->tgrd", grad_scores, key_rows, preferred_element_type=jnp.float32
        )
        grad_keys = (
            jnp.einsum(
                "grtk,tgrd->kgd", grad_scores, query_heads, preferred_element_type=jnp.float32
            )
            * logit_scale_factor
        )
        grad_values = jnp.einsum(
            "grtk,tgrd->kgd",
            probs.astype(jnp.bfloat16),
            head_gradients,
            preferred_element_type=jnp.float32,
        )
        tile_grad = jnp.concatenate(
            [grad_keys.reshape(tile_rows, -1), grad_values.reshape(tile_rows, -1)], axis=1
        )
        carried, tile_grad = (grad_query, tile_grad)
        return (carried, tile_grad)

    start_grad = jnp.zeros((tokens, kv_heads, group_size, head_dim), jnp.float32)
    grad_query, tile_grads = lax.scan(
        grad_step, start_grad, (key_tiles, value_tiles, pos_tiles, seq_tiles)
    )
    return (grad_query * logit_scale_factor, tile_grads.reshape(-1, tile_grads.shape[-1]))


def reduce_grads(grads):
    halves = (
        lax.psum_scatter(
            grads[0].astype(jnp.bfloat16), "fsdp", scatter_dimension=0, tiled=True
        ).astype(jnp.float32),
        lax.psum_scatter(
            grads[1].astype(jnp.bfloat16), "fsdp", scatter_dimension=0, tiled=True
        ).astype(jnp.float32),
        lax.psum_scatter(
            grads[2].astype(jnp.bfloat16), "fsdp", scatter_dimension=0, tiled=True
        ).astype(jnp.float32),
        lax.psum_scatter(
            grads[3].astype(jnp.bfloat16), "fsdp", scatter_dimension=0, tiled=True
        ).astype(jnp.float32),
        lax.psum_scatter(
            grads[4].astype(jnp.bfloat16), "fsdp", scatter_dimension=0, tiled=True
        ).astype(jnp.float32),
        lax.psum_scatter(
            grads[5].astype(jnp.bfloat16), "fsdp", scatter_dimension=0, tiled=True
        ).astype(jnp.float32),
        lax.psum_scatter(
            grads[6].astype(jnp.bfloat16), "fsdp", scatter_dimension=0, tiled=True
        ).astype(jnp.float32),
        lax.psum_scatter(
            grads[7].astype(jnp.bfloat16), "fsdp", scatter_dimension=0, tiled=True
        ).astype(jnp.float32),
    )
    return lax.psum(
        (halves[0], halves[1], halves[2], halves[3], halves[4], halves[5], halves[6], halves[7]),
        "ctx",
    )


def add_tuples(first, second):
    if first is None:
        return second
    return tuple((left_part + right_part for left_part, right_part in zip(first, second)))


def per_device(
    inputs,
    gain_attn,
    w_query,
    w_keyval,
    w_out,
    gain_mlp,
    w_gate,
    w_up,
    w_down,
    cotangent,
    seq_blocks,
    block_slots,
):
    micro_count = inputs.shape[0]
    tokens = inputs.shape[2]
    whole = tokens * lax.axis_size("ctx")
    block_count = whole // BLK
    tile_rows = 4 * BLK
    tile_count = whole // tile_rows
    kv_width = KVH * HD
    group_size = HEADS // KVH
    logit_scale_factor = HD ** (-0.5)
    shard_index = lax.axis_index("fsdp")
    first_row = lax.axis_index("ctx") * tokens
    outputs = []
    input_grads = []
    local_sums = None
    for micro_index in range(micro_count):
        gathered = (
            lax.all_gather(gain_attn, "fsdp", axis=0, tiled=True),
            lax.all_gather(w_query, "fsdp", axis=0, tiled=True),
            lax.all_gather(w_keyval, "fsdp", axis=0, tiled=True),
            lax.all_gather(w_out, "fsdp", axis=0, tiled=True),
            lax.all_gather(gain_mlp, "fsdp", axis=0, tiled=True),
            lax.all_gather(w_gate, "fsdp", axis=0, tiled=True),
            lax.all_gather(w_up, "fsdp", axis=0, tiled=True),
            lax.all_gather(w_down, "fsdp", axis=0, tiled=True),
        )
        (
            attn_gain_low,
            query_full,
            keyval_full,
            out_full,
            mlp_gain_low,
            gate_full,
            up_full,
            down_full,
        ) = gathered
        attn_gain = attn_gain_low.astype(jnp.float32)
        mlp_gain = mlp_gain_low.astype(jnp.float32)
        sequence_lengths_row = lax.dynamic_index_in_dim(
            seq_blocks[micro_index], shard_index, 0, keepdims=False
        )
        slots_row = lax.dynamic_index_in_dim(
            block_slots[micro_index], shard_index, 0, keepdims=False
        )
        key_pos, key_seq = group_layout(sequence_lengths_row, slots_row, block_count)
        query_pos = lax.dynamic_slice_in_dim(key_pos, first_row, tokens)
        query_seq = lax.dynamic_slice_in_dim(key_seq, first_row, tokens)
        in_rows = inputs[micro_index, 0].astype(jnp.float32)
        inverse_attn = rms_inverse(in_rows)
        normed = (in_rows * inverse_attn * attn_gain).astype(jnp.bfloat16)
        queries = matmul(normed, query_full).astype(jnp.bfloat16)
        keyvals = matmul(normed, keyval_full).astype(jnp.bfloat16)
        all_keyvals = lax.all_gather(keyvals, "ctx", axis=0, tiled=True)
        key_tiles = all_keyvals[:, :kv_width].reshape(tile_count, tile_rows, KVH, HD)
        value_tiles = all_keyvals[:, kv_width:].reshape(tile_count, tile_rows, KVH, HD)
        pos_tiles = key_pos.reshape(tile_count, tile_rows)
        seq_tiles = key_seq.reshape(tile_count, tile_rows)
        query_heads = queries.reshape(tokens, KVH, group_size, HD)
        log_total, attended_complete = attention_forward(
            query_heads,
            key_tiles,
            value_tiles,
            pos_tiles,
            seq_tiles,
            query_pos,
            query_seq,
            logit_scale_factor,
        )
        attended = attended_complete.reshape(tokens, -1).astype(jnp.bfloat16)
        mixed = in_rows + matmul(attended, out_full)
        inverse_mlp = rms_inverse(mixed)
        normed_mlp = (mixed * inverse_mlp * mlp_gain).astype(jnp.bfloat16)
        gate_pre = matmul(normed_mlp, gate_full)
        up_pre = matmul(normed_mlp, up_full)
        sigmoid_gate = jax.nn.sigmoid(gate_pre)
        hidden = (gate_pre * sigmoid_gate * up_pre).astype(jnp.bfloat16)
        outputs.append((mixed + matmul(hidden, down_full)).astype(jnp.bfloat16))
        grad_out = cotangent[micro_index, 0]
        grad_hidden = matmul_right_t(grad_out, down_full)
        down_grad = matmul_left_t(hidden, grad_out)
        grad_gate = (
            grad_hidden * up_pre * sigmoid_gate * (1.0 + gate_pre * (1.0 - sigmoid_gate))
        ).astype(jnp.bfloat16)
        grad_up = (grad_hidden * gate_pre * sigmoid_gate).astype(jnp.bfloat16)
        gate_grad = matmul_left_t(normed_mlp, grad_gate)
        up_grad = matmul_left_t(normed_mlp, grad_up)
        grad_normed_mlp = matmul_right_t(grad_gate, gate_full) + matmul_right_t(grad_up, up_full)
        mlp_part, mlp_gain_grad = rms_back(mixed, inverse_mlp, grad_normed_mlp, mlp_gain)
        grad_mixed = grad_out.astype(jnp.float32) + mlp_part
        grad_mixed_low = grad_mixed.astype(jnp.bfloat16)
        out_grad = matmul_left_t(attended, grad_mixed_low)
        grad_attended = matmul_right_t(grad_mixed_low, out_full).astype(jnp.bfloat16)
        head_gradients = grad_attended.reshape(tokens, KVH, group_size, HD)
        softmax_correction = jnp.einsum(
            "lmsq,lmsq->msl", head_gradients.astype(jnp.float32), attended_complete
        )
        grad_query_full, key_grads = attention_backward(
            query_heads,
            key_tiles,
            value_tiles,
            pos_tiles,
            seq_tiles,
            query_pos,
            query_seq,
            logit_scale_factor,
            log_total,
            head_gradients,
            softmax_correction,
        )
        summed_keyvals = lax.psum_scatter(key_grads, "ctx", scatter_dimension=0, tiled=True)
        grad_keyvals = summed_keyvals.astype(jnp.bfloat16)
        grad_queries = grad_query_full.reshape(tokens, -1).astype(jnp.bfloat16)
        query_grad = matmul_left_t(normed, grad_queries)
        keyval_grad = matmul_left_t(normed, grad_keyvals)
        normalized_gradient = matmul_right_t(grad_queries, query_full) + matmul_right_t(
            grad_keyvals, keyval_full
        )
        attn_part, attn_gain_grad = rms_back(in_rows, inverse_attn, normalized_gradient, attn_gain)
        input_grads.append(grad_mixed + attn_part)
        step_grads = (
            attn_gain_grad,
            query_grad,
            keyval_grad,
            out_grad,
            mlp_gain_grad,
            gate_grad,
            up_grad,
            down_grad,
        )
        local_sums = add_tuples(local_sums, step_grads)
    final_grads = reduce_grads(local_sums)
    layer_out = jnp.stack(outputs)[:, None]
    input_grad = jnp.stack(input_grads)[:, None]
    return (
        layer_out,
        input_grad,
        final_grads[0],
        final_grads[1],
        final_grads[2],
        final_grads[3],
        final_grads[4],
        final_grads[5],
        final_grads[6],
        final_grads[7],
    )


def solution(mesh):
    return jax.shard_map(
        per_device,
        mesh=mesh,
        in_specs=(
            P(None, "fsdp", "ctx", None),
            P("fsdp"),
            P("fsdp", None),
            P("fsdp", None),
            P("fsdp", None),
            P("fsdp"),
            P("fsdp", None),
            P("fsdp", None),
            P("fsdp", None),
            P(None, "fsdp", "ctx", None),
            P(),
            P(),
        ),
        out_specs=(
            P(None, "fsdp", "ctx", None),
            P(None, "fsdp", "ctx", None),
            P("fsdp"),
            P("fsdp", None),
            P("fsdp", None),
            P("fsdp", None),
            P("fsdp"),
            P("fsdp", None),
            P("fsdp", None),
            P("fsdp", None),
        ),
        check_vma=False,
    )
```

profile of v0, /device:TPU:0, one launch (start us, length us, event | category | flops | bytes accessed | tf_op | source)
XLA Modules:
  0.0 1464.1 jit_solution(11352369221350321904)
XLA Ops:
  16.9 4.7 all-gather.9.cloned.1.call-done
  40.0 63.2 %all-gather.11.cloned.1.call-done = bf16[2048,640]{1,0:T(8,128)(2,1)} async-done(((bf16[128,640]{1,0:T(8,128)(2,1)}), bf16[2048,640]{1,0:T(8,128)(2,1)}) %all-gather.11.cloned.1.call-update) | async-done | bytes 2621456 | tf_op jit(solution)/shard_map/all_gather | solution.py:287
  111.4 8.0 while.74
  119.5 49.9 %all-gather.23.cloned.1.call-done = bf16[2048,640]{1,0:T(8,128)(2,1)} async-done(((bf16[128,640]{1,0:T(8,128)(2,1)}), bf16[2048,640]{1,0:T(8,128)(2,1)}) %all-gather.23.cloned.1.call-update) | async-done | bytes 2621456 | tf_op jit(solution)/shard_map/all_gather | solution.py:287
  174.8 4.2 reshape.310
  180.5 8.0 while.76
  191.2 4.2 reshape.306
  198.1 13.3 while.77
  216.1 4.1 reshape.300
  222.9 13.6 while.75
  243.4 4.4 fusion.184
  247.8 4.3 fusion.183
  252.1 5.6 multiply_convert_fusion.2
  259.2 4.9 multiply_reduce_fusion.1
  276.2 36.6 %while.78 = (s32[]{:T(128)}, f32[128,5,3,64]{0,3,2,1:T(8,128)S(1)}, f32[4,512,640]{2,1,0:T(8,128)}, bf16[4,512,5,64]{1,3,2,0:T(8,128)(2,1)}, s32[128]{0:T(128)S(...) while((s32[]{:T(128)}, f32[128,5,3,64]{0,3,2,1:T(8,128)S(1)}, ...), condition=%wide.region_26.27_spmd.clone, body=%wide.region_25.26_spmd.clone.sunk | while | flops 640106496 | bytes 33984232 | solution.py:177
  320.3 40.5 %while.79 = (s32[]{:T(128)}, f32[128,5,3,64]{0,3,2,1:T(8,128)S(1)}, f32[4,512,640]{2,1,0:T(8,128)}, bf16[4,512,5,64]{1,3,2,0:T(8,128)(2,1)}, s32[128]{0:T(128)S(...) while((s32[]{:T(128)}, f32[128,5,3,64]{0,3,2,1:T(8,128)S(1)}, ...), condition=%wide.region_31.32_spmd.clone, body=%wide.region_30.31_spmd.clone.sunk | while | flops 640106496 | bytes 30052020 | solution.py:177
  397.2 31.1 %reduce-scatter.9.cloned.1.call-done = f32[128,640]{1,0:T(8,128)} async-done(((f32[2048,640]{1,0:T(8,128)}), f32[128,640]{1,0:T(8,128)}) %reduce-scatter.9.cloned.1.call-update) | async-done | bytes 327696 | tf_op jit(solution)/shard_map/reduce_scatter | solution.py:344
  431.4 115.6 %reduce-scatter.11.cloned.1.call-done = f32[128,640]{1,0:T(8,128)} async-done(((f32[2048,640]{1,0:T(8,128)}), f32[128,640]{1,0:T(8,128)}) %reduce-scatter.11.cloned.1.call-update) | async-done | bytes 327696 | tf_op jit(solution)/shard_map/reduce_scatter | solution.py:344
  552.7 7.6 reduce-scatter.17.cloned.1.call-done
  560.3 13.4 reduce-scatter.13.cloned.1.call-done
  573.7 16.9 %reduce-scatter.21.cloned.1.call-done = bf16[480,2560]{1,0:T(8,128)(2,1)} async-done(((bf16[960,2560]{1,0:T(8,128)(2,1)}), bf16[480,2560]{1,0:T(8,128)(2,1)}) %reduce-scatter.21.cloned.1.call-update) | async-done | bytes 2457616 | tf_op jit(solution)/shard_map/reduce_scatter | solution.py:203
  590.6 16.8 %reduce-scatter.19.cloned.1.call-done = bf16[480,2560]{1,0:T(8,128)(2,1)} async-done(((bf16[960,2560]{1,0:T(8,128)(2,1)}), bf16[480,2560]{1,0:T(8,128)(2,1)}) %reduce-scatter.19.cloned.1.call-update) | async-done | bytes 2457616 | tf_op jit(solution)/shard_map/reduce_scatter | solution.py:200
  607.5 16.8 %reduce-scatter.23.cloned.1.call-done = bf16[1280,960]{0,1:T(8,128)(2,1)} async-done(((bf16[2560,960]{0,1:T(8,128)(2,1)}), bf16[1280,960]{0,1:T(8,128)(2,1)}) %reduce-scatter.23.cloned.1.call-update) | async-done | bytes 2457616 | tf_op jit(solution)/shard_map/reduce_scatter | solution.py:206
  637.0 820.3 %all-reduce.8 = (f32[480]{0:T(512)}, f32[480,960]{1,0:T(8,128)}, f32[480,640]{1,0:T(8,128)}, f32[480,960]{1,0:T(8,128)}, f32[480]{0:T(512)}, /*index=5*/f32[480,...) all-reduce(f32[480]{0:T(512)S(1)} %dynamic-slice_convert_fusion.1, ...), channel_id=1, replica_groups=mesh['ctx'=16,'fsdp'=2] {'ctx'}, use_global_device_ids=true, to_apply=%region_37.38 | all-reduce | flops 4916160 | bytes 29498880 | tf_op jit(solution)/shard_map/psum | solution.py:210
  (467 shorter events, 257.9 us)
Async XLA Ops:
  7.2 14.4 all-gather.9.cloned.1.call-start
  7.9 26.8 %all-gather.13.cloned.1.call-start = ((), (), s32[]{:S(2)}) async-start(), calls=%async_computation.10 | async-start | bytes 2949120 | tf_op jit(solution)/shard_map/all_gather | solution.py:253
  8.7 94.5 %all-gather.11.cloned.1.call-start = ((), (), s32[]{:S(2)}) async-start(), calls=%async_computation.9 | async-start | bytes 2785280 | tf_op jit(solution)/shard_map/all_gather | solution.py:287
  15.1 22.3 %copy-start.53 = (f32[960]{0:T(1024)}, f32[960]{0:T(1024)S(1)}, u32[]{:S(2)}) copy-start(f32[960]{0:T(1024)S(1)} %convert_element_type.212) | copy-start | bytes 11524
  24.3 145.1 %all-gather.23.cloned.1.call-start = ((), (), s32[]{:S(2)}) async-start(), calls=%async_computation.15 | async-start | bytes 2785280 | tf_op jit(solution)/shard_map/all_gather | solution.py:287
  26.9 211.8 %all-gather.15.cloned.1.call-start = ((), (), s32[]{:S(2)}) async-start(), calls=%async_computation.11 | async-start | bytes 2949120 | tf_op jit(solution)/shard_map/all_gather | solution.py:255
  27.5 215.9 %all-gather.19.cloned.1.call-start = ((), (), s32[]{:S(2)}) async-start(), calls=%async_computation.13 | async-start | bytes 7372800 | tf_op jit(solution)/shard_map/all_gather | solution.py:258
  28.1 219.7 %all-gather.17.cloned.1.call-start = ((), (), s32[]{:S(2)}) async-start(), calls=%async_computation.12 | async-start | bytes 7372800 | tf_op jit(solution)/shard_map/all_gather | solution.py:257
  28.8 223.3 %all-gather.21.cloned.1.call-start = ((), (), s32[]{:S(2)}) async-start(), calls=%async_computation.14 | async-start | bytes 7372800 | tf_op jit(solution)/shard_map/all_gather | solution.py:259
  29.6 398.8 %reduce-scatter.9.cloned.1.call-start = ((), (), s32[]{:S(2)}) async-start(), calls=%async_computation.16 | async-start | bytes 5570560 | tf_op jit(solution)/shard_map/reduce_scatter | solution.py:344
  241.4 30.0 %copy-start.15 = (f32[128,960]{0,1:T(8,128)}, f32[128,960]{0,1:T(8,128)S(1)}, u32[]{:S(2)}) copy-start(f32[128,960]{0,1:T(8,128)S(1)} %get-tuple-element.1068) | copy-start | bytes 1474564
  313.5 233.4 %reduce-scatter.11.cloned.1.call-start = ((), (), s32[]{:S(2)}) async-start(), calls=%async_computation.17 | async-start | bytes 5570560 | tf_op jit(solution)/shard_map/reduce_scatter | solution.py:344
  360.8 199.4 %reduce-scatter.17.cloned.1.call-start = ((), (), s32[]{:S(2)}) async-start(), calls=%async_computation.20 | async-start | bytes 2949120 | tf_op jit(solution)/shard_map/reduce_scatter | solution.py:194
  364.6 209.1 %reduce-scatter.13.cloned.1.call-start = ((), (), s32[]{:S(2)}) async-start(), calls=%async_computation.18 | async-start | bytes 2949120 | tf_op jit(solution)/shard_map/reduce_scatter | solution.py:188
  368.5 222.1 %reduce-scatter.21.cloned.1.call-start = ((), (), s32[]{:S(2)}) async-start(), calls=%async_computation.22 | async-start | bytes 7372800 | tf_op jit(solution)/shard_map/reduce_scatter | solution.py:203
  373.8 233.7 %reduce-scatter.19.cloned.1.call-start = ((), (), s32[]{:S(2)}) async-start(), calls=%async_computation.21 | async-start | bytes 7372800 | tf_op jit(solution)/shard_map/reduce_scatter | solution.py:200
  380.0 244.3 %reduce-scatter.23.cloned.1.call-start = ((), (), s32[]{:S(2)}) async-start(), calls=%async_computation.23 | async-start | bytes 7372800 | tf_op jit(solution)/shard_map/reduce_scatter | solution.py:206
  386.4 250.6 %reduce-scatter.15.cloned.1.call-start = ((), (), s32[]{:S(2)}) async-start(), calls=%async_computation.19 | async-start | bytes 1843200 | tf_op jit(solution)/shard_map/reduce_scatter | solution.py:191
  431.4 119.8 %copy-start.59 = (f32[960]{0:T(1024)S(1)}, f32[960]{0:T(1024)}, u32[]{:S(2)}) copy-start(f32[960]{0:T(1024)} %get-tuple-element.864) | copy-start | bytes 11524
  552.6 73.7 %copy-start.9 = (bf16[960,640]{1,0:T(8,128)(2,1)S(1)}, bf16[960,640]{1,0:T(8,128)(2,1)}, u32[]{:S(2)}) copy-start(bf16[960,640]{1,0:T(8,128)(2,1)} %all-gather.9.cloned.1.call-done) | copy-start | bytes 3686404
  552.6 78.7 %copy-start.22 = (f32[128,960]{0,1:T(8,128)S(1)}, f32[128,960]{0,1:T(8,128)}, u32[]{:S(2)}) copy-start(f32[128,960]{0,1:T(8,128)} %copy-done.20) | copy-start | bytes 1474564
  552.6 78.7 %copy-start.25 = (f32[128,960]{0,1:T(8,128)S(1)}, f32[128,960]{0,1:T(8,128)}, u32[]{:S(2)}) copy-start(f32[128,960]{0,1:T(8,128)} %get-tuple-element.1047) | copy-start | bytes 1474564
  552.6 78.7 %copy-start.62 = (f32[128]{0:T(128)S(1)}, f32[128]{0:T(128)}, u32[]{:S(2)}) copy-start(f32[128]{0:T(128)} %get-tuple-element.1059) | copy-start | bytes 1540
  552.6 78.7 %copy-start.63 = (f32[128]{0:T(128)S(1)}, f32[128]{0:T(128)}, u32[]{:S(2)}) copy-start(f32[128]{0:T(128)} %get-tuple-element.1073) | copy-start | bytes 1540
  (66 other events, 206.8 us)
Sparse Core Ops, SparseCore 0:
  9.6 11.9 all-gather.8
  23.1 11.5 all-gather.12
  38.0 65.1 all-gather.10
  106.3 62.9 all-gather.22
  170.7 9.3 all-gather.14
  181.5 15.8 all-gather.18
  199.0 15.8 all-gather.16
  216.4 15.8 all-gather.20
  313.7 114.6 reduce-scatter.8
  430.5 116.4 reduce-scatter.10
  549.8 10.4 reduce-scatter.16
  563.0 10.6 reduce-scatter.12
  576.6 13.9 reduce-scatter.20
  593.4 14.0 reduce-scatter.18
  610.2 14.0 reduce-scatter.22
  627.0 9.9 reduce-scatter.14
where the time goes:
time: 1470 us; the launch traced here: 1460 us
  blocking collectives  825 us (56%)
  waiting for transfers between devices  346 us (24%)
  matrix products  178 us (12%)
  local copies, waits for them, and re-layouts  68.8 us (5%)
  other arithmetic  26.3 us (2%)
  between operations  16.5 us (1%)
    psum x1, blocking collectives, reduce_grads(): lax.psum((halves[0], halves[1], halves[2], halves[3], halves[4], halves[5...  820 us
    reduce_scatter x2, waiting for transfers between devices, per_device(): lax.psum_scatter(key_grads, 'ctx', scatter_dimension=0, tiled=True)  147 us
    all_gather x2, waiting for transfers between devices, per_device(): all_keyvals = lax.all_gather(keyvals, 'ctx', axis=0, tiled=True)  113 us
    dot_general x12, matrix products, matmul(): return jnp.dot(left, right, preferred_element_type=jnp.float32)  32.3 us
  transfers between devices with their start and end apart: 16, of which 12 were waited for; matrix products, arithmetic and copies ran while one was open for 14% of the time, Pallas kernels for 0%

commit v1 on v0

v1 whole, which is shorter than its diff:
```python
import functools

import jax
import jax.numpy as jnp
from jax import lax
from jax.experimental import pallas as pl
from jax.experimental.pallas import tpu as pltpu
from jax.sharding import PartitionSpec as P

HEADS = 15
KVH = 5
HD = 64
REP = HEADS // KVH
WINDOW = 2048
BLK = 128
HALF = BLK // 2
KVW = 2 * KVH * HD
EPS = 1e-05
NEG = -1e30
SCALE = HD ** (-0.5)
LANES = 128
GCOLS = REP * BLK

bf16 = jnp.bfloat16
f32 = jnp.float32


def dot(left, right, left_dim, right_dim):
    return lax.dot_general(
        left, right, (((left_dim,), (right_dim,)), ((), ())), preferred_element_type=f32
    )


def flip_ctx(value, bit):
    size = lax.axis_size("ctx")
    return lax.ppermute(value, "ctx", [(i, i ^ (1 << bit)) for i in range(size)])


def swap_fsdp(value):
    return lax.ppermute(value, "fsdp", [(0, 1), (1, 0)])


def bit_orders(size):
    count = size.bit_length() - 1
    high = list(range(count - 1, 1, -1))
    return (high + [1, 0], high + [0, 1])


def gather_blocks(piece, order):
    held = piece[None]
    for bit in order:
        held = jnp.concatenate([held, flip_ctx(held, bit)], axis=0)
    return held


def scatter_blocks(held, order):
    for bit in reversed(order):
        half = held.shape[0] // 2
        arrived = flip_ctx(held[half:], bit)
        held = (held[:half].astype(f32) + arrived.astype(f32)).astype(bf16)
    return held[0]


def place_of(relative, order):
    place = jnp.zeros_like(relative)
    for position, bit in enumerate(order):
        place = place | (((relative >> bit) & 1) << position)
    return place


def sum_stages(size, first_swapped):
    count = size.bit_length() - 1
    low = [1, 0] if first_swapped else [0, 1]
    return low + list(range(2, count))


def reduce_chunk(grad, stages):
    me = lax.axis_index("ctx")
    for bit, dim in stages:
        half = grad.shape[dim] // 2
        own = (me >> bit) & 1
        sent = lax.dynamic_slice_in_dim(grad, (1 - own) * half, half, dim).astype(bf16)
        kept = lax.dynamic_slice_in_dim(grad, own * half, half, dim)
        grad = (kept.astype(f32) + flip_ctx(sent, bit).astype(f32)).astype(bf16)
    return grad


def gather_chunk(chunk, stages, last_type):
    me = lax.axis_index("ctx")
    for number, (bit, dim) in enumerate(reversed(stages)):
        low = ((me >> bit) & 1) == 0
        arrived = flip_ctx(chunk, bit)
        if number == len(stages) - 1:
            chunk, arrived = chunk.astype(last_type), arrived.astype(last_type)
        chunk = jnp.concatenate(
            [jnp.where(low, chunk, arrived), jnp.where(low, arrived, chunk)], axis=dim
        )
    return chunk


def sum_vector(vector):
    count = lax.axis_size("ctx").bit_length() - 1
    for bit in range(count):
        vector = vector + flip_ctx(vector, bit)
    return vector


def key_tile(first_ref, second_ref, first, second, unit):
    lanes = pl.ds((unit // 2) * LANES, LANES)
    return jnp.concatenate([first_ref[first, :, lanes], second_ref[second, :, lanes]], axis=0)


def heads_t(rows_t, group, unit):
    parts = [
        rows_t[(group * REP + r) * HD : (group * REP + r + 1) * HD, :] for r in range(REP)
    ]
    block = jnp.concatenate(parts, axis=1)
    zero = jnp.zeros_like(block)
    return jnp.concatenate([zero, block] if unit % 2 else [block, zero], axis=0)


def half_rows(tile_t, unit):
    return tile_t[(unit % 2) * HD : (unit % 2 + 1) * HD, :]


def block_mask(kind):
    key = lax.broadcasted_iota(jnp.int32, (BLK, GCOLS), 0)
    query = lax.broadcasted_iota(jnp.int32, (BLK, GCOLS), 1) % BLK
    return key <= query if kind == "first" else key > query


def forward_kernel(far, table, first_ref, second_ref, query_ref, out_ref, lse_ref):
    count = table[0, 0]
    queries = query_ref[...]
    for group in range(KVH):
        q_pad = heads_t(queries, group, group)
        value_unit = KVH + group

        def step(index, carried, mask):
            high, total, acc = carried
            first, second = table[1, index], table[2, index]
            keys = key_tile(first_ref, second_ref, first, second, group)
            values = key_tile(first_ref, second_ref, first, second, value_unit)
            scores = dot(keys, q_pad, 1, 0) * SCALE
            if mask is not None:
                scores = jnp.where(mask, scores, NEG)
            new_high = jnp.maximum(high, jnp.max(scores, axis=0, keepdims=True))
            weights = jnp.exp(scores - new_high)
            fade = jnp.exp(high - new_high)
            total = total * fade + jnp.sum(weights, axis=0, keepdims=True)
            values_t = half_rows(values.T, value_unit)
            acc = acc * fade + dot(values_t, weights.astype(bf16), 1, 0)
            return (new_high, total, acc)

        start = (
            jnp.full((1, GCOLS), NEG, f32),
            jnp.zeros((1, GCOLS), f32),
            jnp.zeros((HD, GCOLS), f32),
        )
        carried = step(0, start, block_mask("first"))
        near = jnp.minimum(count, WINDOW // BLK) if far else count
        carried = lax.fori_loop(1, near, lambda i, c: step(i, c, None), carried)
        if far:
            carried = lax.fori_loop(
                near, count, lambda i, c: step(i, c, block_mask("last")), carried
            )
        high, total, acc = carried
        acc = acc / total
        lse = high + jnp.log(total)
        for r in range(REP):
            head = group * REP + r
            columns = slice(r * BLK, (r + 1) * BLK)
            out_ref[head * HD : (head + 1) * HD, :] = acc[:, columns]
        lse_ref[:, group * GCOLS : (group + 1) * GCOLS] = lse


def backward_kernel(
    far,
    table,
    first_ref,
    second_ref,
    query_ref,
    grad_ref,
    out_ref,
    lse_ref,
    dq_ref,
    dfirst_ref,
    dsecond_ref,
    right_ref,
    delta_ref,
    left_ref,
    acc_ref,
):
    count = table[0, 0]
    queries = query_ref[...]
    grads = grad_ref[...]
    product = grads.astype(f32) * out_ref[...]
    for head in range(HEADS):
        delta_ref[:, head * BLK : (head + 1) * BLK] = jnp.sum(
            product[head * HD : (head + 1) * HD, :], axis=0, keepdims=True
        )
    for unit in range(2 * KVH):
        group = unit % KVH
        source = queries if unit < KVH else grads
        padded = heads_t(source, group, unit)
        right_ref[unit * GCOLS : (unit + 1) * GCOLS, :] = padded.astype(f32).T.astype(bf16)
    dfirst_ref[...] = jnp.zeros_like(dfirst_ref)
    dsecond_ref[...] = jnp.zeros_like(dsecond_ref)
    acc_ref[...] = jnp.zeros_like(acc_ref)

    def step(index, mask):
        first, second = table[1, index], table[2, index]
        for group in range(KVH):
            value_unit = KVH + group
            columns = slice(group * GCOLS, (group + 1) * GCOLS)
            q_pad = heads_t(queries, group, group)
            g_pad = heads_t(grads, group, value_unit)
            keys = key_tile(first_ref, second_ref, first, second, group)
            values = key_tile(first_ref, second_ref, first, second, value_unit)
            scores = dot(keys, q_pad, 1, 0) * SCALE
            probs = jnp.exp(scores - lse_ref[:, columns])
            if mask is not None:
                probs = jnp.where(mask, probs, 0.0)
            grad_probs = dot(values, g_pad, 1, 0)
            grad_scores = (probs * (grad_probs - delta_ref[:, columns])).astype(bf16)
            left_ref[:, columns] = grad_scores
            left_ref[:, (KVH * GCOLS) + group * GCOLS : (KVH * GCOLS) + (group + 1) * GCOLS] = (
                probs.astype(bf16)
            )
            keys_t = half_rows(keys.T, group)
            acc_ref[:, columns] += dot(keys_t, grad_scores, 1, 0)
        for tile in range(KVH):
            rows = slice(2 * tile * GCOLS, 2 * (tile + 1) * GCOLS)
            lanes = slice(tile * LANES, (tile + 1) * LANES)
            block = dot(left_ref[:, rows], right_ref[rows, :], 1, 0)
            lane = lax.broadcasted_iota(jnp.int32, (1, LANES), 1) + tile * LANES
            block = block * jnp.where(lane < KVH * HD, SCALE, 1.0)
            dfirst_ref[first, :, lanes] = block[:HALF].astype(bf16)
            dsecond_ref[second, :, lanes] = block[HALF:].astype(bf16)

    step(0, block_mask("first"))
    near = jnp.minimum(count, WINDOW // BLK) if far else count

    @pl.loop(1, near)
    def _(index):
        step(index, None)

    if far:

        @pl.loop(near, count)
        def _(index):
            step(index, block_mask("last"))

    for head in range(HEADS):
        columns = slice(head * BLK, (head + 1) * BLK)
        dq_ref[head * HD : (head + 1) * HD, :] = (acc_ref[:, columns] * SCALE).astype(bf16)


VMEM_SPEC = pl.BlockSpec(memory_space=pltpu.VMEM)
SMEM_SPEC = pl.BlockSpec(memory_space=pltpu.SMEM)


def attention_forward(table, first, second, queries_t):
    steps = first.shape[0]
    far = steps > WINDOW // BLK
    return pl.pallas_call(
        functools.partial(forward_kernel, far),
        out_shape=(
            jax.ShapeDtypeStruct((HEADS * HD, BLK), f32),
            jax.ShapeDtypeStruct((1, HEADS * BLK), f32),
        ),
        in_specs=[SMEM_SPEC] + [VMEM_SPEC] * 3,
        out_specs=(VMEM_SPEC,) * 2,
        compiler_params=pltpu.CompilerParams(vmem_limit_bytes=40 << 20),
        cost_estimate=pl.CostEstimate(
            flops=4 * HEADS * HD * BLK * BLK * 8,
            bytes_accessed=first.size * 4,
            transcendentals=HEADS * BLK * BLK * 8,
        ),
        name="attention_forward",
    )(table, first, second, queries_t)


def attention_backward(table, first, second, queries_t, grads_t, out_t, lse):
    steps = first.shape[0]
    far = steps > WINDOW // BLK
    return pl.pallas_call(
        functools.partial(backward_kernel, far),
        out_shape=(
            jax.ShapeDtypeStruct((HEADS * HD, BLK), bf16),
            jax.ShapeDtypeStruct(first.shape, bf16),
            jax.ShapeDtypeStruct(second.shape, bf16),
        ),
        in_specs=[SMEM_SPEC] + [VMEM_SPEC] * 6,
        out_specs=(VMEM_SPEC,) * 3,
        scratch_shapes=[
            pltpu.VMEM((2 * KVH * GCOLS, LANES), bf16),
            pltpu.VMEM((1, HEADS * BLK), f32),
            pltpu.VMEM((BLK, 2 * KVH * GCOLS), bf16),
            pltpu.VMEM((HD, HEADS * BLK), f32),
        ],
        compiler_params=pltpu.CompilerParams(vmem_limit_bytes=48 << 20),
        cost_estimate=pl.CostEstimate(
            flops=10 * HEADS * HD * BLK * BLK * 8,
            bytes_accessed=first.size * 8,
            transcendentals=HEADS * BLK * BLK * 8,
        ),
        name="attention_backward",
    )(table, first, second, queries_t, grads_t, out_t, lse)


def block_table(lengths, slots, orders):
    me = lax.axis_index("ctx")
    count = slots.shape[0]
    naturals = jnp.arange(count, dtype=jnp.int32)
    own = jnp.sum(jnp.where(slots == me, naturals, 0))
    end = jnp.int32(0)
    start = jnp.int32(0)
    for i in range(lengths.shape[0]):
        end = end + lengths[i]
        start = jnp.where(end <= own, end, start)
    lowest = jnp.maximum(start, own - WINDOW // BLK)
    wanted = jnp.maximum(own - naturals, 0)
    match = wanted[:, None] == naturals[None, :]
    slot_back = jnp.sum(jnp.where(match, slots[None, :], 0), axis=1)
    relative = slot_back ^ me
    head = jnp.broadcast_to(own - lowest + 1, (count,))
    return jnp.stack([head, place_of(relative, orders[0]), place_of(relative, orders[1])])


def rms_back(values, inverse, normalized_gradient, gain):
    scaled = normalized_gradient * gain
    gain_part = jnp.sum(normalized_gradient * values * inverse, axis=0)
    cubed = inverse * inverse * inverse
    input_part = inverse * scaled - values * cubed * jnp.mean(
        scaled * values, axis=-1, keepdims=True
    )
    return (input_part, gain_part)


def rms_inverse(values):
    return lax.rsqrt(jnp.mean(values * values, axis=-1, keepdims=True) + EPS)


def per_device(
    inputs,
    gain_attn,
    w_query,
    w_keyval,
    w_out,
    gain_mlp,
    w_gate,
    w_up,
    w_down,
    cotangent,
    seq_blocks,
    block_slots,
):
    micro = inputs.shape[0]
    size = lax.axis_size("ctx")
    shard = lax.axis_index("fsdp")
    orders = bit_orders(size)
    is_low = shard == 0

    def joined(part):
        other = swap_fsdp(part)
        return jnp.concatenate(
            [jnp.where(is_low, part, other), jnp.where(is_low, other, part)], axis=0
        )

    def whole(part):
        return lax.all_gather(part, "fsdp", axis=0, tiled=True)

    def halves(value, dim):
        half = value.shape[dim] // 2
        mine = lax.dynamic_slice_in_dim(value, shard * half, half, dim)
        theirs = lax.dynamic_slice_in_dim(value, (1 - shard) * half, half, dim)
        return mine, theirs

    attn_gain = joined(gain_attn).astype(f32)
    keyval_full = joined(w_keyval)
    query_full = joined(w_query)
    mlp_gain = joined(gain_mlp).astype(f32)
    out_full = whole(w_out)
    gate_full = whole(w_gate)
    up_full = whole(w_up)
    down_full = whole(w_down)

    rows = micro * BLK
    in_rows = inputs[:, 0].reshape(rows, -1).astype(f32)
    grad_out = cotangent[:, 0].reshape(rows, -1)
    inverse_attn = rms_inverse(in_rows)
    normed = (in_rows * inverse_attn * attn_gain).astype(bf16)
    keyvals = dot(normed, keyval_full, 1, 0).astype(bf16)

    tables, firsts, seconds = [], [], []
    for m in range(micro):
        lengths = lax.dynamic_index_in_dim(seq_blocks[m], shard, 0, keepdims=False)
        slots = lax.dynamic_index_in_dim(block_slots[m], shard, 0, keepdims=False)
        tables.append(block_table(lengths, slots, orders))
        firsts.append(gather_blocks(keyvals[m * BLK : m * BLK + HALF], orders[0]))
        seconds.append(gather_blocks(keyvals[m * BLK + HALF : (m + 1) * BLK], orders[1]))

    queries_t = dot(query_full, normed, 0, 1).astype(bf16)
    normed_mine, normed_theirs = halves(normed, 1)
    normed_other = swap_fsdp(normed_theirs)
    grad_out_other = swap_fsdp(grad_out)

    queries, outs, lses = [], [], []
    for m in range(micro):
        queries.append(queries_t[:, m * BLK : (m + 1) * BLK])
        out_t, lse = attention_forward(tables[m], firsts[m], seconds[m], queries[m])
        outs.append(out_t)
        lses.append(lse)
    attended_t = jnp.concatenate(outs, axis=1).astype(bf16)

    mixed = in_rows + dot(attended_t, out_full, 0, 0)
    inverse_mlp = rms_inverse(mixed)
    normed_mlp = (mixed * inverse_mlp * mlp_gain).astype(bf16)
    gate_pre = dot(normed_mlp, gate_full, 1, 0)
    up_pre = dot(normed_mlp, up_full, 1, 0)
    sigmoid_gate = jax.nn.sigmoid(gate_pre)
    hidden = (gate_pre * sigmoid_gate * up_pre).astype(bf16)
    layer_out = (mixed + dot(hidden, down_full, 1, 0)).astype(bf16)

    hidden_mine, hidden_theirs = halves(hidden, 1)
    hidden_other = swap_fsdp(hidden_theirs)
    down_grad = (
        dot(hidden_mine, grad_out, 0, 0) + dot(hidden_other, grad_out_other, 0, 0)
    ).astype(bf16)

    grad_hidden = dot(grad_out, down_full, 1, 1)
    grad_gate = (
        grad_hidden * up_pre * sigmoid_gate * (1.0 + gate_pre * (1.0 - sigmoid_gate))
    ).astype(bf16)
    grad_up = (grad_hidden * gate_pre * sigmoid_gate).astype(bf16)
    mlp_mine, mlp_theirs = halves(normed_mlp, 1)
    mlp_other = swap_fsdp(mlp_theirs)
    gate_grad = (
        dot(mlp_mine, grad_gate, 0, 0) + dot(mlp_other, swap_fsdp(grad_gate), 0, 0)
    ).astype(bf16)
    up_grad = (
        dot(mlp_mine, grad_up, 0, 0) + dot(mlp_other, swap_fsdp(grad_up), 0, 0)
    ).astype(bf16)
    grad_normed_mlp = dot(grad_gate, gate_full, 1, 1) + dot(grad_up, up_full, 1, 1)
    mlp_part, mlp_gain_grad = rms_back(mixed, inverse_mlp, grad_normed_mlp, mlp_gain)
    grad_mixed = grad_out.astype(f32) + mlp_part
    grad_mixed_low = grad_mixed.astype(bf16)

    grad_attended_t = dot(out_full, grad_mixed_low, 1, 1).astype(bf16)
    query_grads, keyval_grads = [], []
    for m in range(micro):
        dq_t, dfirst, dsecond = attention_backward(
            tables[m],
            firsts[m],
            seconds[m],
            queries[m],
            grad_attended_t[:, m * BLK : (m + 1) * BLK],
            outs[m],
            lses[m],
        )
        query_grads.append(dq_t)
        keyval_grads.append(scatter_blocks(dfirst, orders[0]))
        keyval_grads.append(scatter_blocks(dsecond, orders[1]))
    grad_queries_t = jnp.concatenate(query_grads, axis=1)
    grad_keyvals = jnp.concatenate(keyval_grads, axis=0)

    attended_mine, attended_theirs = halves(attended_t, 0)
    attended_other = swap_fsdp(attended_theirs)
    out_grad = dot(attended_mine, grad_mixed_low, 1, 0) + dot(
        attended_other, swap_fsdp(grad_mixed_low), 1, 0
    )
    query_grad = dot(normed_mine, grad_queries_t, 0, 1) + dot(
        normed_other, swap_fsdp(grad_queries_t), 0, 1
    )
    keyval_grad = dot(normed_mine, grad_keyvals, 0, 0) + dot(
        normed_other, swap_fsdp(grad_keyvals), 0, 0
    )
    attn_grad = jnp.concatenate([query_grad, out_grad, keyval_grad], axis=1).astype(bf16)

    normalized_gradient = dot(grad_queries_t, query_full, 0, 1) + dot(
        grad_keyvals, keyval_full, 1, 1
    )
    attn_part, attn_gain_grad = rms_back(in_rows, inverse_attn, normalized_gradient, attn_gain)
    input_grad = grad_mixed + attn_part

    def wide(first_swapped):
        bits = sum_stages(size, first_swapped)
        return [(bit, 0 if number < 2 else 1) for number, bit in enumerate(bits)]

    def tall(first_swapped):
        return [(bit, 0) for bit in sum_stages(size, first_swapped)]

    def summed(grad, stages):
        return gather_chunk(reduce_chunk(grad, stages), stages, f32)

    cut = down_grad.shape[0] // 2
    down_sum = jnp.concatenate(
        [summed(down_grad[:cut], tall(False)), summed(down_grad[cut:], tall(True))], axis=0
    )
    gate_sum = summed(gate_grad, wide(False))
    up_sum = summed(up_grad, wide(True))
    cut = attn_grad.shape[1] // 2
    attn_sum = jnp.concatenate(
        [summed(attn_grad[:, :cut], wide(False)), summed(attn_grad[:, cut:], wide(True))], axis=1
    )

    def summed_gain(vector):
        mine, theirs = halves(vector, 0)
        return sum_vector(mine + swap_fsdp(theirs))

    mlp_gain_sum = summed_gain(mlp_gain_grad)
    attn_gain_sum = summed_gain(attn_gain_grad)
    width = query_grad.shape[1]
    shape = (micro, 1, BLK, in_rows.shape[1])
    return (
        layer_out.reshape(shape),
        input_grad.reshape(shape),
        attn_gain_sum,
        attn_sum[:, :width],
        attn_sum[:, 2 * width :],
        attn_sum[:, width : 2 * width],
        mlp_gain_sum,
        gate_sum,
        up_sum,
        down_sum,
    )


def solution(mesh):
    tokens = P(None, "fsdp", "ctx", None)
    vector = P("fsdp")
    matrix = P("fsdp", None)
    return jax.shard_map(
        per_device,
        mesh=mesh,
        in_specs=(
            tokens,
            vector,
            matrix,
            matrix,
            matrix,
            vector,
            matrix,
            matrix,
            matrix,
            tokens,
            P(),
            P(),
        ),
        out_specs=(
            tokens,
            tokens,
            vector,
            matrix,
            matrix,
            matrix,
            vector,
            matrix,
            matrix,
            matrix,
        ),
        check_vma=False,
    )
```

time: 1470 us -> 626 us (0.43)
  blocking collectives: 825 us -> 0 us
  starting transfers between devices: 1.11 us -> 115 us
  matrix products: 178 us -> 68.9 us
  waiting for transfers between devices: 346 us -> 259 us
  Pallas kernels: 0 us -> 29.9 us
  other arithmetic: 26.3 us -> 55.8 us
    psum x1 -> x0, blocking collectives: 820 us -> none  [reduce_grads(): lax.psum((halves[0], halves[1], halves[2], halves[3], halves[4], halves[5...]
    ppermute x0 -> x104, waiting for transfers between devices: none -> 257 us  [the longest x88 257 us: flip_ctx(): return lax.ppermute(value, 'ctx', [(i, i ^ 1 << bit) for i in range(size)])]
    reduce_scatter x8 -> x0, waiting for transfers between devices: 222 us -> none  [the longest x2 147 us: per_device(): lax.psum_scatter(key_grads, 'ctx', scatter_dimension=0, tiled=True)]
    all_gather x8 -> x4, waiting for transfers between devices: 121 us -> 0.01 us  [whole(): return lax.all_gather(part, 'fsdp', axis=0, tiled=True)]
    ppermute x0 -> x104, starting transfers between devices: none -> 115 us  [the longest x88 109 us: flip_ctx(): return lax.ppermute(value, 'ctx', [(i, i ^ 1 << bit) for i in range(size)])]
    dot_general x92 -> x24, matrix products: 178 us -> 68.9 us  [dot(): lax.dot_general(left, right, (((left_dim,), (right_dim,)), ((), ())), pre...]
    pallas_call x0 -> x4, Pallas kernels: none -> 29.9 us  [the longest x2 19.6 us: attention_backward(): pl.pallas_call(functools.partial(backward_kernel, far), out_shape=(jax.Sh...]
    concatenate x0 -> x37, other arithmetic: none -> 17.5 us  [the longest x21 12.1 us: gather_chunk(): jnp.concatenate([jnp.where(low, chunk, arrived), jnp.where(low, arrived,...]
  transfers between devices with their start and end apart: 16 -> 108, of which waited for: 12 -> 54; matrix products, arithmetic and copies ran while one was open for 14% -> 28% of each run, Pallas kernels for 0% -> 5%
where the time goes in v1:
time: 626 us; the launch traced here: 614 us
  waiting for transfers between devices  259 us (41%)
  starting transfers between devices  115 us (18%)
  matrix products  68.9 us (11%)
  local copies, waits for them, and re-layouts  59.2 us (9%)
  other arithmetic  55.8 us (9%)
  Pallas kernels  29.9 us (5%)
  between operations  26.9 us (4%)
    ppermute x88, waiting for transfers between devices, flip_ctx(): return lax.ppermute(value, 'ctx', [(i, i ^ 1 << bit) for i in range(size)])  257 us
    ppermute x88, starting transfers between devices, flip_ctx(): return lax.ppermute(value, 'ctx', [(i, i ^ 1 << bit) for i in range(size)])  109 us
    dot_general x24, matrix products, dot(): lax.dot_general(left, right, (((left_dim,), (right_dim,)), ((), ())), pre...  68.9 us
    pallas_call x2, Pallas kernels, attention_backward(): pl.pallas_call(functools.partial(backward_kernel, far), out_shape=(jax.Sh...  19.6 us
    unnamed x216, local copies, waits for them, and re-layouts  14.3 us
    dynamic_slice x24, local copies, waits for them, and re-layouts, reduce_chunk(): lax.dynamic_slice_in_dim(grad, (1 - own) * half, half, dim).astype(bf16)  12.8 us
  transfers between devices with their start and end apart: 108, of which 54 were waited for; matrix products, arithmetic and copies ran while one was open for 28% of the time, Pallas kernels for 5%

profile of v1, /device:TPU:0, one launch (start us, length us, event | category | flops | bytes accessed | tf_op | source)
XLA Modules:
  0.0 614.2 jit_solution(9305483823470881279)
XLA Ops:
  81.8 11.0 %collective-permute-done.14 = bf16[8,64,640]{2,1,0:T(8,128)(2,1)S(1)} collective-permute-done((bf16[8,64,640]{2,1,0:T(8,128)(2,1)S(1)}, bf16[8,64,640]{2,1,0:T(8,128)(2,1)S(1)}, u32[]{:S(2)}, u32[]{:S(2)}) %collective-permute-start.14) | collective-permute-done | bytes 655392 | tf_op jit(solution)/shard_map/ppermute | solution.py:36
  97.2 7.7 %collective-permute-done.5 = bf16[8,64,640]{2,1,0:T(8,128)(2,1)S(1)} collective-permute-done((bf16[8,64,640]{2,1,0:T(8,128)(2,1)S(1)}, bf16[8,64,640]{2,1,0:T(8,128)(2,1)S(1)}, u32[]{:S(2)}, u32[]{:S(2)}) %collective-permute-start.5) | collective-permute-done | bytes 655392 | tf_op jit(solution)/shard_map/ppermute | solution.py:36
  105.2 6.1 attention_forward.2
  127.6 8.5 %multiply_convert_fusion = (bf16[256,2560]{1,0:T(8,128)(2,1)}, bf16[256,2560]{1,0:T(8,128)(2,1)}, bf16[256,2560]{1,0:T(8,128)(2,1)}) fusion(f32[256,2560]{1,0:T(8,128)} %fusion.50, f32[256,2560]{1,0:T(8,128)} %fusion.61, bf16[256,960]{0,1:T(8,128)(2,1)S(1)} %multiply_convert_fusion.3, bf16[960,2560]{1,0:T(8,128)(2,1)} %all-gather.7.cloned.1.call-done), kind=kOutput, calls=%fused_computation.9 | convolution fusion | flops 1268776960 | bytes 14581760 | tf_op jit(solution)/shard_map/dot_general | solution.py:29
  155.1 6.2 %attention_backward.2 = (bf16[960,128]{1,0:T(8,128)(2,1)S(1)}, bf16[16,64,640]{2,1,0:T(8,128)(2,1)S(1)}, bf16[16,64,640]{2,1,0:T(8,128)(2,1)S(1)}) custom-call(s32[3,16]{1,0:T(4,128)S(1)} %pad_add_fusion.table, bf16[16,64,640]{2,1,0:T(8,128)(2,1)S(1)} %copy-done.10, bf16[16,64,640]{2,1,0:T(8,128)(2,1)} %copy-done.8, bf16[960,128]{1,0:T(8,128)(2,1)S(1)} %copy-done.7, ...), custom_call_target="tpu_custom_call" | custom-call | flops 1258291200 | bytes 5242880 | tf_op jit(solution)/shard_map/attention_backward/pallas_call | solution.py:287
  162.6 13.4 %attention_backward.3 = (bf16[960,128]{1,0:T(8,128)(2,1)S(1)}, bf16[16,64,640]{2,1,0:T(8,128)(2,1)S(1)}, bf16[16,64,640]{2,1,0:T(8,128)(2,1)S(1)}) custom-call(s32[3,16]{1,0:T(4,128)S(1)} %pad_add_fusion.1.table, bf16[16,64,640]{2,1,0:T(8,128)(2,1)S(1)} %copy-done.13, bf16[16,64,640]{2,1,0:T(8,128)(2,1)} %copy-done.11, ...), custom_call_target="tpu_custom_call" | custom-call | flops 1258291200 | bytes 5242880 | tf_op jit(solution)/shard_map/attention_backward/pallas_call | solution.py:287
  178.4 21.5 %collective-permute-start.63 = (f32[480]{0:T(512)S(1)}, f32[480]{0:T(512)S(1)}, u32[]{:S(2)}, u32[]{:S(2)}) collective-permute-start(f32[480]{0:T(512)S(1)} %dynamic-slice_add_fusion), channel_id=1, source_target_pairs={{0,2},{2,0},{4,6},{6,4},{8,10},{10,8},{12,14},{14,12},{16,18},{18,... | collective-permute-start | bytes 5768 | tf_op jit(solution)/shard_map/ppermute | solution.py:36
  232.0 7.9 %collective-permute-done.32 = bf16[8,64,640]{2,1,0:T(8,128)(2,1)S(1)} collective-permute-done((bf16[8,64,640]{2,1,0:T(8,128)(2,1)S(1)}, bf16[8,64,640]{2,1,0:T(8,128)(2,1)S(1)}, u32[]{:S(2)}, u32[]{:S(2)}) %collective-permute-start.32) | collective-permute-done | bytes 655392 | tf_op jit(solution)/shard_map/ppermute | solution.py:36
  244.8 8.2 %collective-permute-done.24 = bf16[8,64,640]{2,1,0:T(8,128)(2,1)S(1)} collective-permute-done((bf16[8,64,640]{2,1,0:T(8,128)(2,1)S(1)}, bf16[8,64,640]{2,1,0:T(8,128)(2,1)S(1)}, u32[]{:S(2)}, u32[]{:S(2)}) %collective-permute-start.24) | collective-permute-done | bytes 655392 | tf_op jit(solution)/shard_map/ppermute | solution.py:36
  319.0 9.1 %collective-permute-done.38 = f32[480]{0:T(512)S(1)} collective-permute-done((f32[480]{0:T(512)S(1)}, f32[480]{0:T(512)S(1)}, u32[]{:S(2)}, u32[]{:S(2)}) %collective-permute-start.38) | collective-permute-done | bytes 1952 | tf_op jit(solution)/shard_map/ppermute | solution.py:36
  360.9 5.9 collective-permute-done.90
  374.3 9.8 %collective-permute-done.91 = bf16[40,960]{0,1:T(8,128)(2,1)S(1)} collective-permute-done((bf16[40,960]{0,1:T(8,128)(2,1)S(1)}, bf16[40,960]{0,1:T(8,128)(2,1)S(1)}, u32[]{:S(2)}, u32[]{:S(2)}) %collective-permute-start.91) | collective-permute-done | bytes 76832 | tf_op jit(solution)/shard_map/ppermute | solution.py:36
  384.2 11.3 %collective-permute-done.99 = bf16[40,960]{0,1:T(8,128)(2,1)S(1)} collective-permute-done((bf16[40,960]{0,1:T(8,128)(2,1)S(1)}, bf16[40,960]{0,1:T(8,128)(2,1)S(1)}, u32[]{:S(2)}, u32[]{:S(2)}) %collective-permute-start.99) | collective-permute-done | bytes 76832 | tf_op jit(solution)/shard_map/ppermute | solution.py:36
  395.6 13.8 %collective-permute-done.92 = bf16[40,960]{0,1:T(8,128)(2,1)S(1)} collective-permute-done((bf16[40,960]{0,1:T(8,128)(2,1)S(1)}, bf16[40,960]{0,1:T(8,128)(2,1)S(1)}, u32[]{:S(2)}, u32[]{:S(2)}) %collective-permute-start.92) | collective-permute-done | bytes 76832 | tf_op jit(solution)/shard_map/ppermute | solution.py:36
  409.7 12.4 %collective-permute-done.100 = bf16[40,960]{0,1:T(8,128)(2,1)S(1)} collective-permute-done((bf16[40,960]{0,1:T(8,128)(2,1)S(1)}, bf16[40,960]{0,1:T(8,128)(2,1)S(1)}, u32[]{:S(2)}, u32[]{:S(2)}) %collective-permute-start.100) | collective-permute-done | bytes 76832 | tf_op jit(solution)/shard_map/ppermute | solution.py:36
  422.3 7.7 %collective-permute-done.93 = bf16[80,960]{0,1:T(8,128)(2,1)S(1)} collective-permute-done((bf16[80,960]{0,1:T(8,128)(2,1)S(1)}, bf16[80,960]{0,1:T(8,128)(2,1)S(1)}, u32[]{:S(2)}, u32[]{:S(2)}) %collective-permute-start.93) | collective-permute-done | bytes 153632 | tf_op jit(solution)/shard_map/ppermute | solution.py:36
  430.7 6.3 %collective-permute-done.101 = bf16[80,960]{0,1:T(8,128)(2,1)S(1)} collective-permute-done((bf16[80,960]{0,1:T(8,128)(2,1)S(1)}, bf16[80,960]{0,1:T(8,128)(2,1)S(1)}, u32[]{:S(2)}, u32[]{:S(2)}) %collective-permute-start.101) | collective-permute-done | bytes 153632 | tf_op jit(solution)/shard_map/ppermute | solution.py:36
  481.1 7.1 %collective-permute-done.48 = bf16[120,320]{1,0:T(8,128)(2,1)S(1)} collective-permute-done((bf16[120,320]{1,0:T(8,128)(2,1)S(1)}, bf16[120,320]{1,0:T(8,128)(2,1)S(1)}, u32[]{:S(2)}, u32[]{:S(2)}) %collective-permute-start.48) | collective-permute-done | bytes 76832 | tf_op jit(solution)/shard_map/ppermute | solution.py:36
  488.4 6.0 collective-permute-done.58
  494.5 6.1 collective-permute-done.49
  522.8 6.3 %concatenate.218 = f32[1280,960]{0,1:T(8,128)} concatenate(f32[320,960]{0,1:T(8,128)S(1)} %get-tuple-element.84, f32[320,960]{0,1:T(8,128)S(1)} %get-tuple-element.83, f32[320,960]{0,1:T(8,128)} %get-tuple-element.82, f32[320,960]{0,1:T(8,128)} %get-tuple-element.81), dimensions={0} | concatenate | bytes 9830400 | tf_op jit(solution)/shard_map/concatenate | solution.py:498
  541.8 6.9 %collective-permute-done.80 = bf16[120,1280]{1,0:T(8,128)(2,1)S(1)} collective-permute-done((bf16[120,1280]{1,0:T(8,128)(2,1)S(1)}, bf16[120,1280]{1,0:T(8,128)(2,1)S(1)}, u32[]{:S(2)}, u32[]{:S(2)}) %collective-permute-start.80) | collective-permute-done | bytes 307232 | tf_op jit(solution)/shard_map/ppermute | solution.py:36
  572.2 11.5 %collective-permute-done.75 = bf16[120,2560]{1,0:T(8,128)(2,1)S(1)} collective-permute-done((bf16[120,2560]{1,0:T(8,128)(2,1)S(1)}, bf16[120,2560]{1,0:T(8,128)(2,1)S(1)}, u32[]{:S(2)}, u32[]{:S(2)}) %collective-permute-start.75) | collective-permute-done | bytes 614432 | tf_op jit(solution)/shard_map/ppermute | solution.py:36
  587.9 12.9 %collective-permute-done.76 = bf16[240,2560]{1,0:T(8,128)(2,1)S(1)} collective-permute-done((bf16[240,2560]{1,0:T(8,128)(2,1)S(1)}, bf16[240,2560]{1,0:T(8,128)(2,1)S(1)}, u32[]{:S(2)}, u32[]{:S(2)}) %collective-permute-start.76) | collective-permute-done | bytes 1228832 | tf_op jit(solution)/shard_map/ppermute | solution.py:36
  (651 shorter events, 363.7 us)
Async XLA Ops:
  7.2 105.8 %all-gather.5.cloned.1.call-start = ((), (), s32[]{:S(2)}) async-start(), calls=%async_computation | async-start | bytes 2949120 | tf_op jit(solution)/shard_map/all_gather | solution.py:372
  7.9 108.8 %all-gather.11.cloned.1.call-start = ((), (), s32[]{:S(2)}) async-start(), calls=%async_computation.3 | async-start | bytes 7372800 | tf_op jit(solution)/shard_map/all_gather | solution.py:372
  8.7 113.5 %all-gather.9.cloned.1.call-start = ((), (), s32[]{:S(2)}) async-start(), calls=%async_computation.2 | async-start | bytes 7372800 | tf_op jit(solution)/shard_map/all_gather | solution.py:372
  9.4 118.2 %all-gather.7.cloned.1.call-start = ((), (), s32[]{:S(2)}) async-start(), calls=%async_computation.1 | async-start | bytes 7372800 | tf_op jit(solution)/shard_map/all_gather | solution.py:372
  10.5 55.9 %collective-permute-start.10 = (bf16[480,960]{1,0:T(8,128)(2,1)}, bf16[480,960]{1,0:T(8,128)(2,1)}, u32[]{:S(2)}, u32[]{:S(2)}) collective-permute-start(bf16[480,960]{1,0:T(8,128)(2,1)} %param.14), channel_id=1, source_target_pairs={{0,1},{1,0},{2,3},{3,2},{4,5},{5,4},{6,7},{7,6},{8,9},{9,8},{10,11... | collective-permute-start | bytes 2764808 | tf_op jit(solution)/shard_map/ppermute | solution.py:40
  12.1 245.7 %collective-permute-start.87 = (bf16[256,960]{0,1:T(8,128)(2,1)}, bf16[256,960]{0,1:T(8,128)(2,1)}, u32[]{:S(2)}, u32[]{:S(2)}) collective-permute-start(bf16[256,960]{0,1:T(8,128)(2,1)} %bitcast.127), channel_id=1, source_target_pairs={{0,1},{1,0},{2,3},{3,2},{4,5},{5,4},{6,7},{7,6},{8,9},{9,8},{10,11... | collective-permute-start | bytes 1474568 | tf_op jit(solution)/shard_map/ppermute | solution.py:40
  74.7 30.2 %collective-permute-start.5 = (bf16[8,64,640]{2,1,0:T(8,128)(2,1)S(1)}, bf16[8,64,640]{2,1,0:T(8,128)(2,1)S(1)}, u32[]{:S(2)}, u32[]{:S(2)}) collective-permute-start(bf16[8,64,640]{2,1,0:T(8,128)(2,1)S(1)} %pad_maximum_fusion.16), channel_id=1, source_target_pairs={{0,2},{2,0},{4,6},{6,4},{8,10},{10,8},{12,14},{14,12},{16,18},{18,... | collective-permute-start | bytes 1966088 | tf_op jit(solution)/shard_map/ppermute | solution.py:36
  113.0 108.7 %collective-permute-start.43 = (bf16[480,256]{1,0:T(8,128)(2,1)}, bf16[480,256]{1,0:T(8,128)(2,1)}, u32[]{:S(2)}, u32[]{:S(2)}) collective-permute-start(bf16[480,256]{1,0:T(8,128)(2,1)} %fusion.22), channel_id=1, source_target_pairs={{0,1},{1,0},{2,3},{3,2},{4,5},{5,4},{6,7},{7,6},{8,9},{9,8},{10,11... | collective-permute-start | bytes 737288 | tf_op jit(solution)/shard_map/ppermute | solution.py:40
  152.2 70.0 %collective-permute-start.44 = (bf16[256,960]{0,1:T(8,128)(2,1)}, bf16[256,960]{0,1:T(8,128)(2,1)}, u32[]{:S(2)}, u32[]{:S(2)}) collective-permute-start(bf16[256,960]{0,1:T(8,128)(2,1)} %fusion.51), channel_id=1, source_target_pairs={{0,1},{1,0},{2,3},{3,2},{4,5},{5,4},{6,7},{7,6},{8,9},{9,8},{10,11... | collective-permute-start | bytes 1474568 | tf_op jit(solution)/shard_map/ppermute | solution.py:40
  176.8 49.4 %collective-permute-start.42 = (bf16[960,256]{1,0:T(8,128)(2,1)}, bf16[960,256]{1,0:T(8,128)(2,1)}, u32[]{:S(2)}, u32[]{:S(2)}) collective-permute-start(bf16[960,256]{1,0:T(8,128)(2,1)} %constant_dynamic-update-slice_fusion.20), channel_id=1, source_target_pairs={{0,1},{1,0},{2,3},{3,2},{4,5},{5,4},{6,7},{7,6},{8,9},{9,8},{10,11... | collective-permute-start | bytes 1474568 | tf_op jit(solution)/shard_map/ppermute | solution.py:40
  221.7 122.4 %collective-permute-start.67 = (bf16[256,480]{0,1:T(8,128)(2,1)}, bf16[256,480]{0,1:T(8,128)(2,1)S(1)}, u32[]{:S(2)}, u32[]{:S(2)}) collective-permute-start(bf16[256,480]{0,1:T(8,128)(2,1)} %constant_dynamic-slice_fusion.17), channel_id=1, source_target_pairs={{0,1},{1,0},{2,3},{3,2},{4,5},{5,4},{6,7},{7,6},{8,9},{9,8},{10,11... | collective-permute-start | bytes 737288 | tf_op jit(solution)/shard_map/ppermute | solution.py:40
  226.3 26.7 %collective-permute-start.24 = (bf16[8,64,640]{2,1,0:T(8,128)(2,1)S(1)}, bf16[8,64,640]{2,1,0:T(8,128)(2,1)S(1)}, u32[]{:S(2)}, u32[]{:S(2)}) collective-permute-start(bf16[8,64,640]{2,1,0:T(8,128)(2,1)S(1)} %slice.196), channel_id=1, source_target_pairs={{0,4},{2,6},{4,0},{6,2},{8,12},{10,14},{12,8},{14,10},{16,20},{18,... | collective-permute-start | bytes 1966088 | tf_op jit(solution)/shard_map/ppermute | solution.py:36
  253.0 92.0 %collective-permute-start.68 = (bf16[256,2560]{1,0:T(8,128)(2,1)}, bf16[256,2560]{1,0:T(8,128)(2,1)}, u32[]{:S(2)}, u32[]{:S(2)}) collective-permute-start(bf16[256,2560]{1,0:T(8,128)(2,1)} %get-tuple-element.69), channel_id=1, source_target_pairs={{0,1},{1,0},{2,3},{3,2},{4,5},{5,4},{6,7},{7,6},{8,9},{9,8},{10,11... | collective-permute-start | bytes 3932168 | tf_op jit(solution)/shard_map/ppermute | solution.py:40
  268.5 68.3 %collective-permute-start.88 = (bf16[320,960]{1,0:T(8,128)(2,1)}, bf16[320,960]{1,0:T(8,128)(2,1)}, u32[]{:S(2)}, u32[]{:S(2)}) collective-permute-start(bf16[320,960]{1,0:T(8,128)(2,1)} %copy.40), channel_id=1, source_target_pairs={{0,2},{2,0},{4,6},{6,4},{8,10},{10,8},{12,14},{14,12},{16,18},{18,... | collective-permute-start | bytes 1843208 | tf_op jit(solution)/shard_map/ppermute | solution.py:36
  310.3 29.9 %collective-permute-start.96 = (bf16[320,960]{1,0:T(8,128)(2,1)}, bf16[320,960]{1,0:T(8,128)(2,1)}, u32[]{:S(2)}, u32[]{:S(2)}) collective-permute-start(bf16[320,960]{1,0:T(8,128)(2,1)} %copy.44), channel_id=1, source_target_pairs={{0,4},{2,6},{4,0},{6,2},{8,12},{10,14},{12,8},{14,10},{16,20},{18,... | collective-permute-start | bytes 1843208 | tf_op jit(solution)/shard_map/ppermute | solution.py:36
  349.8 114.9 %collective-permute-start.69 = (bf16[240,2560]{1,0:T(8,128)(2,1)}, bf16[240,2560]{1,0:T(8,128)(2,1)}, u32[]{:S(2)}, u32[]{:S(2)}) collective-permute-start(bf16[240,2560]{1,0:T(8,128)(2,1)} %constant_dynamic-slice_fusion.16), channel_id=1, source_target_pairs={{0,2},{2,0},{4,6},{6,4},{8,10},{10,8},{12,14},{14,12},{16,18},{18,... | collective-permute-start | bytes 3686408 | tf_op jit(solution)/shard_map/ppermute | solution.py:36
  354.4 114.4 %collective-permute-start.78 = (bf16[240,2560]{1,0:T(8,128)(2,1)}, bf16[240,2560]{1,0:T(8,128)(2,1)}, u32[]{:S(2)}, u32[]{:S(2)}) collective-permute-start(bf16[240,2560]{1,0:T(8,128)(2,1)} %constant_dynamic-slice_fusion.12), channel_id=1, source_target_pairs={{0,4},{2,6},{4,0},{6,2},{8,12},{10,14},{12,8},{14,10},{16,20},{18,... | collective-permute-start | bytes 3686408 | tf_op jit(solution)/shard_map/ppermute | solution.py:36
  356.6 82.4 %collective-permute-start.54 = (bf16[240,1280]{1,0:T(8,128)(2,1)S(1)}, bf16[240,1280]{1,0:T(8,128)(2,1)S(1)}, u32[]{:S(2)}, u32[]{:S(2)}) collective-permute-start(bf16[240,1280]{1,0:T(8,128)(2,1)S(1)} %get-tuple-element.101), channel_id=1, source_target_pairs={{0,4},{2,6},{4,0},{6,2},{8,12},{10,14},{12,8},{14,10},{16,20},{18,... | collective-permute-start | bytes 1843208 | tf_op jit(solution)/shard_map/ppermute | solution.py:36
  358.1 81.9 %collective-permute-start.45 = (bf16[240,1280]{1,0:T(8,128)(2,1)S(1)}, bf16[240,1280]{1,0:T(8,128)(2,1)S(1)}, u32[]{:S(2)}, u32[]{:S(2)}) collective-permute-start(bf16[240,1280]{1,0:T(8,128)(2,1)S(1)} %get-tuple-element.102), channel_id=1, source_target_pairs={{0,2},{2,0},{4,6},{6,4},{8,10},{10,8},{12,14},{14,12},{16,18},{18,... | collective-permute-start | bytes 1843208 | tf_op jit(solution)/shard_map/ppermute | solution.py:36
  453.5 59.9 %collective-permute-start.95 = (bf16[320,960]{1,0:T(8,128)(2,1)}, bf16[320,960]{1,0:T(8,128)(2,1)}, u32[]{:S(2)}, u32[]{:S(2)}) collective-permute-start(bf16[320,960]{1,0:T(8,128)(2,1)} %copy.42), channel_id=1, source_target_pairs={{0,2},{2,0},{4,6},{6,4},{8,10},{10,8},{12,14},{14,12},{16,18},{18,... | collective-permute-start | bytes 1843208 | tf_op jit(solution)/shard_map/ppermute | solution.py:36
  460.2 56.6 %collective-permute-start.103 = (bf16[320,960]{1,0:T(8,128)(2,1)}, bf16[320,960]{1,0:T(8,128)(2,1)}, u32[]{:S(2)}, u32[]{:S(2)}) collective-permute-start(bf16[320,960]{1,0:T(8,128)(2,1)} %copy.46), channel_id=1, source_target_pairs={{0,4},{2,6},{4,0},{6,2},{8,12},{10,14},{12,8},{14,10},{16,20},{18,... | collective-permute-start | bytes 1843208 | tf_op jit(solution)/shard_map/ppermute | solution.py:36
  468.7 60.3 %collective-permute-start.70 = (bf16[120,2560]{1,0:T(8,128)(2,1)}, bf16[120,2560]{1,0:T(8,128)(2,1)}, u32[]{:S(2)}, u32[]{:S(2)}) collective-permute-start(bf16[120,2560]{1,0:T(8,128)(2,1)} %constant_dynamic-slice_fusion.15), channel_id=1, source_target_pairs={{0,4},{2,6},{4,0},{6,2},{8,12},{10,14},{12,8},{14,10},{16,20},{18,... | collective-permute-start | bytes 1843208 | tf_op jit(solution)/shard_map/ppermute | solution.py:36
  472.1 58.9 %collective-permute-start.79 = (bf16[120,2560]{1,0:T(8,128)(2,1)}, bf16[120,2560]{1,0:T(8,128)(2,1)}, u32[]{:S(2)}, u32[]{:S(2)}) collective-permute-start(bf16[120,2560]{1,0:T(8,128)(2,1)} %constant_dynamic-slice_fusion.11), channel_id=1, source_target_pairs={{0,2},{2,0},{4,6},{6,4},{8,10},{10,8},{12,14},{14,12},{16,18},{18,... | collective-permute-start | bytes 1843208 | tf_op jit(solution)/shard_map/ppermute | solution.py:36
  535.2 28.4 %collective-permute-start.61 = (bf16[240,1280]{1,0:T(8,128)(2,1)S(1)}, bf16[240,1280]{1,0:T(8,128)(2,1)S(1)}, u32[]{:S(2)}, u32[]{:S(2)}) collective-permute-start(bf16[240,1280]{1,0:T(8,128)(2,1)S(1)} %pad_maximum_fusion.22), channel_id=1, source_target_pairs={{0,4},{2,6},{4,0},{6,2},{8,12},{10,14},{12,8},{14,10},{16,20},{18,... | collective-permute-start | bytes 1843208 | tf_op jit(solution)/shard_map/ppermute | solution.py:36
  (183 other events, 1983.7 us)
Sparse Core Ops, SparseCore 0:
  9.6 13.0 all-gather.4
  24.2 15.8 all-gather.10
  41.7 15.8 all-gather.8
  59.0 15.8 all-gather.6

commit v2 on v1

v2 whole, which is shorter than its diff:
```python
import functools

import jax
import jax.numpy as jnp
from jax import lax
from jax.experimental import pallas as pl
from jax.experimental.pallas import tpu as pltpu
from jax.sharding import PartitionSpec as P

HEADS = 15
KVH = 5
HD = 64
REP = HEADS // KVH
WINDOW = 2048
BLK = 128
HALF = BLK // 2
KVW = 2 * KVH * HD
EPS = 1e-05
NEG = -1e30
SCALE = HD ** (-0.5)
LANES = 128
GCOLS = REP * BLK

bf16 = jnp.bfloat16
f32 = jnp.float32


def dot(left, right, left_dim, right_dim):
    return lax.dot_general(
        left, right, (((left_dim,), (right_dim,)), ((), ())), preferred_element_type=f32
    )


def flip_ctx(value, bit):
    size = lax.axis_size("ctx")
    return lax.ppermute(value, "ctx", [(i, i ^ (1 << bit)) for i in range(size)])


def swap_fsdp(value):
    return lax.ppermute(value, "fsdp", [(0, 1), (1, 0)])


def tie(values):
    return lax.optimization_barrier(tuple(values))


def own_bit(bit):
    return (lax.axis_index("ctx") >> bit) & 1


def high_bits():
    return list(range(2, lax.axis_size("ctx").bit_length() - 1))


def add_low(kept, arrived):
    return (kept.astype(f32) + arrived.astype(f32)).astype(bf16)


def by_bit(bit, mine, arrived):
    low = own_bit(bit) == 0
    return jnp.where(low, mine, arrived), jnp.where(low, arrived, mine)


def in_order(bit, mine, arrived, dim):
    return jnp.concatenate(by_bit(bit, mine, arrived), axis=dim)


class GatherBlocks:
    def __init__(self, block):
        self.held = block[None]
        self.stages = high_bits()[::-1] + [None, None]
        self.halves = None

    def operands(self):
        if self.stages[0] is not None:
            return [(self.held, self.stages[0])]
        if self.halves is None:
            self.halves = [self.held[:, :HALF], self.held[:, HALF:]]
            self.bits = (1, 0)
        return list(zip(self.halves, self.bits))

    def absorb(self, arrived):
        if self.stages.pop(0) is not None:
            self.held = jnp.concatenate([self.held, arrived[0]], axis=0)
        else:
            self.halves = [
                jnp.concatenate([h, a], axis=0) for h, a in zip(self.halves, arrived)
            ]
            self.bits = (0, 1)


class ScatterBlocks:
    def __init__(self, firsts, seconds):
        self.halves = [firsts, seconds]
        self.bits = (0, 1)
        self.stages = [None, None] + high_bits()
        self.held = None

    def operands(self):
        if self.stages[0] is None:
            count = self.halves[0][0].shape[0] // 2
            sent = [jnp.stack([b[count:] for b in half]) for half in self.halves]
            return list(zip(sent, self.bits))
        if self.held is None:
            self.held = [jnp.concatenate([a, b], axis=1) for a, b in zip(*self.halves)]
        count = self.held[0].shape[0] // 2
        return [(jnp.stack([b[count:] for b in self.held]), self.stages[0])]

    def absorb(self, arrived):
        def add(blocks, sums):
            count = blocks[0].shape[0] // 2
            return [add_low(b[:count], sums[m]) for m, b in enumerate(blocks)]

        if self.stages.pop(0) is None:
            self.halves = [add(half, a) for half, a in zip(self.halves, arrived)]
            self.bits = (1, 0)
        else:
            self.held = add(self.held, arrived[0])


class Reduce:
    def __init__(self, first, second):
        self.ready = [first, second]
        self.stages = [(0, 1), (1, 0)] + high_bits()

    def cut(self, value, bit, dim):
        half = value.shape[dim] // 2
        own = own_bit(bit)
        sent = lax.dynamic_slice_in_dim(value, (1 - own) * half, half, dim)
        return lax.dynamic_slice_in_dim(value, own * half, half, dim), sent

    def operands(self):
        stage = self.stages[0]
        if isinstance(stage, tuple):
            if self.ready is None:
                self.ready = [self.cut(v, b, 0)[::-1] for v, b in zip(self.pair, stage)]
            self.kept = [r[1] for r in self.ready]
            sent = [(r[0], b) for r, b in zip(self.ready, stage)]
            self.ready = None
            return sent
        if self.pair is not None:
            kept, sent = by_bit(stage, *self.pair)
            self.pair = None
        else:
            kept, sent = self.cut(self.held, stage, 1)
        self.kept = [kept]
        return [(sent, stage)]

    def absorb(self, arrived):
        sums = [add_low(k, a) for k, a in zip(self.kept, arrived)]
        if isinstance(self.stages.pop(0), tuple):
            self.pair = sums
        else:
            self.held = sums[0]


class Spread:
    def __init__(self, chunk):
        self.held = chunk
        self.stages = high_bits()[::-1] + [(1, 0), (0, 1)]
        self.pair = None

    def operands(self):
        stage = self.stages[0]
        if isinstance(stage, tuple):
            return list(zip(self.pair, stage))
        return [(self.held, stage)]

    def absorb(self, arrived):
        stage = self.stages.pop(0)
        if isinstance(stage, tuple):
            kind = bf16 if self.stages else f32
            self.pair = [
                in_order(b, v.astype(kind), a.astype(kind), 0)
                for v, a, b in zip(self.pair, arrived, stage)
            ]
        elif stage == 2:
            self.pair = list(by_bit(stage, self.held, arrived[0]))
        else:
            self.held = in_order(stage, self.held, arrived[0], 1)


class Solo:
    def __init__(self, value):
        self.value = value
        high = [(bit, None) for bit in high_bits()]
        self.stages = [(0, True), (1, True)] + high + [(1, False), (0, False)]

    def operands(self):
        bit, cuts = self.stages[0]
        if not cuts:
            return [(self.value, bit)]
        half = self.value.shape[0] // 2
        own = own_bit(bit)
        sent = lax.dynamic_slice_in_dim(self.value, (1 - own) * half, half, 0)
        self.value = lax.dynamic_slice_in_dim(self.value, own * half, half, 0)
        return [(sent, bit)]

    def absorb(self, arrived):
        bit, cuts = self.stages.pop(0)
        if cuts is not False:
            self.value = add_low(self.value, arrived[0])
        else:
            kind = bf16 if self.stages else f32
            self.value = in_order(bit, self.value.astype(kind), arrived[0].astype(kind), 0)


class Rounds:
    def __init__(self):
        self.flying = {}

    def begin(self, *jobs):
        for job in jobs:
            self.flying[job] = [flip_ctx(v, b) for v, b in job.operands()]

    def end(self, jobs, values=()):
        values = list(values)
        arrived = [a for job in jobs for a in self.flying[job]]
        tied = tie(values + arrived)
        rest = list(tied[len(values) :])
        for job in jobs:
            count = len(self.flying.pop(job))
            job.absorb(rest[:count])
            rest = rest[count:]
        return tied[: len(values)]


def key_tile(first_ref, second_ref, places, unit):
    lanes = pl.ds((unit // 2) * LANES, LANES)
    parts = []
    for first, second in places:
        parts += [first_ref[first, :, lanes], second_ref[second, :, lanes]]
    return jnp.concatenate(parts, axis=0)


def heads_t(rows_t, group, unit):
    parts = [
        rows_t[(group * REP + r) * HD : (group * REP + r + 1) * HD, :] for r in range(REP)
    ]
    block = jnp.concatenate(parts, axis=1)
    zero = jnp.zeros_like(block)
    return jnp.concatenate([zero, block] if unit % 2 else [block, zero], axis=0)


def half_rows(tile_t, unit):
    return tile_t[(unit % 2) * HD : (unit % 2 + 1) * HD, :]


def seen_blocks(bits, which, ids, lengths, slots):
    me, shard = ids[0], ids[1]

    def look(j, own):
        return jnp.where(slots[which, shard, j] == me, j, own)

    own = lax.fori_loop(0, slots.shape[2], look, jnp.int32(0))
    end = jnp.int32(0)
    start = jnp.int32(0)
    for i in range(lengths.shape[2]):
        end = end + lengths[which, shard, i]
        start = jnp.where(end <= own, end, start)
    lowest = jnp.maximum(start, own - WINDOW // BLK)

    def places(index):
        relative = slots[which, shard, jnp.maximum(own - index, 0)] ^ me
        high = jnp.int32(0)
        for position, bit in enumerate(range(bits - 1, 1, -1)):
            high = high | (((relative >> bit) & 1) << position)
        one = (relative & 1) << (bits - 1)
        two = ((relative >> 1) & 1) << (bits - 2)
        swapped = ((relative & 1) << (bits - 2)) | (((relative >> 1) & 1) << (bits - 1))
        return high | one | two, high | swapped

    return own - lowest + 1, places


def pair_mask(far, count, index):
    key = lax.broadcasted_iota(jnp.int32, (BLK, GCOLS), 0)
    query = lax.broadcasted_iota(jnp.int32, (BLK, GCOLS), 1) & (BLK - 1)
    ahead = key - query
    masks = []
    for i in (index, index + 1):
        most = jnp.where(i < count, i * BLK, -2 * BLK)
        mask = ahead <= most
        if far:
            mask = mask & (ahead > i * BLK - WINDOW)
        masks.append(mask)
    return jnp.concatenate(masks, axis=0)


def forward_kernel(
    far, bits, which, ids, lengths, slots, first_ref, second_ref, query_ref, out_ref, lse_ref, pad_ref
):
    count, places = seen_blocks(bits, which, ids, lengths, slots)
    queries = query_ref[...]
    for group in range(KVH):
        pad_ref[:, group * GCOLS : (group + 1) * GCOLS] = heads_t(queries, group, group)

    for group in range(KVH):
        columns = slice(group * GCOLS, (group + 1) * GCOLS)
        value_unit = KVH + group

        def step(pair, carried):
            high, total, acc = carried
            index = 2 * pair
            held = (places(index), places(index + 1))
            keys = key_tile(first_ref, second_ref, held, group)
            values = key_tile(first_ref, second_ref, held, value_unit)
            scores = dot(keys, pad_ref[:, columns], 1, 0) * SCALE
            scores = jnp.where(pair_mask(far, count, index), scores, NEG)
            new_high = jnp.maximum(high, jnp.max(scores, axis=0, keepdims=True))
            weights = jnp.exp(scores - new_high)
            fade = jnp.exp(high - new_high)
            total = total * fade + jnp.sum(weights, axis=0, keepdims=True)
            values_t = half_rows(values.T, value_unit)
            acc = acc * fade + dot(values_t, weights.astype(bf16), 1, 0)
            return (new_high, total, acc)

        start = (
            jnp.full((1, GCOLS), NEG, f32),
            jnp.zeros((1, GCOLS), f32),
            jnp.zeros((HD, GCOLS), f32),
        )
        high, total, acc = lax.fori_loop(0, (count + 1) // 2, step, start)
        acc = acc / total
        for r in range(REP):
            head = group * REP + r
            out_ref[head * HD : (head + 1) * HD, :] = acc[:, r * BLK : (r + 1) * BLK]
        lse_ref[:, columns] = high + jnp.log(total)


def backward_kernel(
    far,
    bits,
    which,
    ids,
    lengths,
    slots,
    first_ref,
    second_ref,
    query_ref,
    grad_ref,
    out_ref,
    lse_ref,
    dq_ref,
    dfirst_ref,
    dsecond_ref,
    pad_ref,
    right_ref,
    delta_ref,
    left_ref,
    acc_ref,
):
    count, places = seen_blocks(bits, which, ids, lengths, slots)
    queries = query_ref[...]
    grads = grad_ref[...]
    product = grads.astype(f32) * out_ref[...]
    for head in range(HEADS):
        delta_ref[:, head * BLK : (head + 1) * BLK] = jnp.sum(
            product[head * HD : (head + 1) * HD, :], axis=0, keepdims=True
        )
    for unit in range(2 * KVH):
        padded = heads_t(queries if unit < KVH else grads, unit % KVH, unit)
        rows = slice(unit * GCOLS, (unit + 1) * GCOLS)
        pad_ref[:, rows] = padded
        right_ref[rows, :] = padded.T
    dfirst_ref[...] = jnp.zeros_like(dfirst_ref)
    dsecond_ref[...] = jnp.zeros_like(dsecond_ref)
    acc_ref[...] = jnp.zeros_like(acc_ref)

    @pl.loop(0, (count + 1) // 2)
    def _(pair):
        index = 2 * pair
        held = (places(index), places(index + 1))
        mask = pair_mask(far, count, index)
        for group in range(KVH):
            value_unit = KVH + group
            columns = slice(group * GCOLS, (group + 1) * GCOLS)
            value_columns = slice(value_unit * GCOLS, (value_unit + 1) * GCOLS)
            keys = key_tile(first_ref, second_ref, held, group)
            values = key_tile(first_ref, second_ref, held, value_unit)
            scores = dot(keys, pad_ref[:, columns], 1, 0) * SCALE
            probs = jnp.where(mask, jnp.exp(scores - lse_ref[:, columns]), 0.0)
            grad_probs = dot(values, pad_ref[:, value_columns], 1, 0)
            grad_scores = (probs * (grad_probs - delta_ref[:, columns])).astype(bf16)
            left_ref[:, columns] = grad_scores
            left_ref[:, value_columns] = probs.astype(bf16)
            keys_t = half_rows(keys.T, group)
            acc_ref[:, columns] += dot(keys_t, grad_scores, 1, 0)
        for tile in range(KVH):
            rows = slice(2 * tile * GCOLS, 2 * (tile + 1) * GCOLS)
            lanes = slice(tile * LANES, (tile + 1) * LANES)
            block = dot(left_ref[:, rows], right_ref[rows, :], 1, 0)
            lane = lax.broadcasted_iota(jnp.int32, (1, LANES), 1) + tile * LANES
            block = (block * jnp.where(lane < KVH * HD, SCALE, 1.0)).astype(bf16)
            first, second = held[0]
            dfirst_ref[first, :, lanes] = block[:HALF]
            dsecond_ref[second, :, lanes] = block[HALF:BLK]

            @pl.when(index + 1 < count)
            def _():
                first, second = held[1]
                dfirst_ref[first, :, lanes] = block[BLK : BLK + HALF]
                dsecond_ref[second, :, lanes] = block[BLK + HALF :]

    for head in range(HEADS):
        columns = slice(head * BLK, (head + 1) * BLK)
        dq_ref[head * HD : (head + 1) * HD, :] = (acc_ref[:, columns] * SCALE).astype(bf16)


VMEM_SPEC = pl.BlockSpec(memory_space=pltpu.VMEM)
SMEM_SPEC = pl.BlockSpec(memory_space=pltpu.SMEM)


def attention_forward(which, tables, first, second, queries_t):
    steps = first.shape[0]
    return pl.pallas_call(
        functools.partial(
            forward_kernel, steps > WINDOW // BLK, steps.bit_length() - 1, which
        ),
        out_shape=(
            jax.ShapeDtypeStruct((HEADS * HD, BLK), f32),
            jax.ShapeDtypeStruct((1, HEADS * BLK), f32),
        ),
        in_specs=[SMEM_SPEC] * 3 + [VMEM_SPEC] * 3,
        out_specs=(VMEM_SPEC,) * 2,
        scratch_shapes=[pltpu.VMEM((LANES, HEADS * BLK), bf16)],
        compiler_params=pltpu.CompilerParams(vmem_limit_bytes=40 << 20),
        cost_estimate=pl.CostEstimate(
            flops=4 * HEADS * HD * BLK * BLK * 8,
            bytes_accessed=first.size * 4,
            transcendentals=HEADS * BLK * BLK * 8,
        ),
        name="attention_forward",
    )(*tables, first, second, queries_t)


def attention_backward(which, tables, first, second, queries_t, grads_t, out_t, lse):
    steps = first.shape[0]
    return pl.pallas_call(
        functools.partial(
            backward_kernel, steps > WINDOW // BLK, steps.bit_length() - 1, which
        ),
        out_shape=(
            jax.ShapeDtypeStruct((HEADS * HD, BLK), bf16),
            jax.ShapeDtypeStruct(first.shape, bf16),
            jax.ShapeDtypeStruct(second.shape, bf16),
        ),
        in_specs=[SMEM_SPEC] * 3 + [VMEM_SPEC] * 6,
        out_specs=(VMEM_SPEC,) * 3,
        scratch_shapes=[
            pltpu.VMEM((LANES, 2 * KVH * GCOLS), bf16),
            pltpu.VMEM((2 * KVH * GCOLS, LANES), bf16),
            pltpu.VMEM((1, HEADS * BLK), f32),
            pltpu.VMEM((2 * BLK, 2 * KVH * GCOLS), bf16),
            pltpu.VMEM((HD, HEADS * BLK), f32),
        ],
        compiler_params=pltpu.CompilerParams(vmem_limit_bytes=48 << 20),
        cost_estimate=pl.CostEstimate(
            flops=10 * HEADS * HD * BLK * BLK * 8,
            bytes_accessed=first.size * 8,
            transcendentals=HEADS * BLK * BLK * 8,
        ),
        name="attention_backward",
    )(*tables, first, second, queries_t, grads_t, out_t, lse)


def block_kernel(
    x_ref,
    cot_ref,
    att_ref,
    out_w_ref,
    gain_ref,
    gate_w_ref,
    up_w_ref,
    down_w_ref,
    hidden_ref,
    grads_ref,
    normed_ref,
    layer_ref,
    grad_mixed_ref,
    grad_low_ref,
    grad_att_ref,
    gain_grad_ref,
    mixed,
    normed,
    cot,
    grad_normed,
    layer,
):
    step = pl.program_id(0)

    @pl.when(step == 0)
    def _():
        cot[...] = cot_ref[...].T
        values = x_ref[...].astype(f32).T + dot(att_ref[...], out_w_ref[...], 0, 0)
        mixed[...] = values
        inverse = lax.rsqrt(jnp.mean(values * values, axis=-1, keepdims=True) + EPS)
        low = (values * inverse * gain_ref[...]).astype(bf16)
        normed[...] = low
        normed_ref[...] = low.T
        layer[...] = values
        grad_normed[...] = jnp.zeros_like(grad_normed)

    grad_hidden = dot(cot[...], down_w_ref[...], 1, 0)
    gate = dot(normed[...], gate_w_ref[...], 1, 0)
    up = dot(normed[...], up_w_ref[...], 1, 0)
    sigmoid = jax.nn.sigmoid(gate)
    silu = gate * sigmoid
    hidden = (silu * up).astype(bf16)
    grad_gate = (grad_hidden * up * sigmoid * (1.0 + gate * (1.0 - sigmoid))).astype(bf16)
    grad_up = (grad_hidden * silu).astype(bf16)
    hidden_ref[...] = hidden
    grads_ref[0] = grad_gate
    grads_ref[1] = grad_up
    layer[...] += dot(hidden, down_w_ref[...], 1, 1)
    grad_normed[...] += dot(grad_gate, gate_w_ref[...], 1, 1) + dot(
        grad_up, up_w_ref[...], 1, 1
    )

    @pl.when(step == pl.num_programs(0) - 1)
    def _():
        values = mixed[...]
        layer_ref[...] = layer[...].astype(bf16).T
        inverse = lax.rsqrt(jnp.mean(values * values, axis=-1, keepdims=True) + EPS)
        grads = grad_normed[...]
        gain_grad_ref[...] = jnp.sum(grads * values * inverse, axis=0, keepdims=True)
        scaled = grads * gain_ref[...]
        cubed = inverse * inverse * inverse
        back = inverse * scaled - values * cubed * jnp.mean(
            scaled * values, axis=-1, keepdims=True
        )
        grad_mixed = cot[...].astype(f32) + back
        low = grad_mixed.astype(bf16)
        grad_mixed_ref[...] = grad_mixed.T
        grad_low_ref[...] = low
        grad_att_ref[...] = dot(out_w_ref[...], low, 1, 1).astype(bf16)


def feed_forward(x_t, cot_t, attended_t, out_w, gain, gate_w, up_w, down_w_t):
    width, rows = x_t.shape
    inner = gate_w.shape[1]
    tile = 256

    def fixed(shape):
        return pl.BlockSpec(shape, lambda i: (0,) * len(shape))

    weight = pl.BlockSpec((width, tile), lambda i: (0, i))
    wide = (width, rows)
    return pl.pallas_call(
        block_kernel,
        grid=(inner // tile,),
        in_specs=[fixed(wide)] * 3
        + [fixed(out_w.shape), fixed((1, width)), weight, weight, weight],
        out_specs=(
            pl.BlockSpec((rows, tile), lambda i: (0, i)),
            pl.BlockSpec((2, rows, tile), lambda i: (0, 0, i)),
            fixed(wide),
            fixed(wide),
            fixed(wide),
            fixed((rows, width)),
            fixed(wide),
            fixed((1, width)),
        ),
        out_shape=(
            jax.ShapeDtypeStruct((rows, inner), bf16),
            jax.ShapeDtypeStruct((2, rows, inner), bf16),
            jax.ShapeDtypeStruct(wide, bf16),
            jax.ShapeDtypeStruct(wide, bf16),
            jax.ShapeDtypeStruct(wide, f32),
            jax.ShapeDtypeStruct((rows, width), bf16),
            jax.ShapeDtypeStruct(wide, bf16),
            jax.ShapeDtypeStruct((1, width), f32),
        ),
        scratch_shapes=[
            pltpu.VMEM((rows, width), f32),
            pltpu.VMEM((rows, width), bf16),
            pltpu.VMEM((rows, width), bf16),
            pltpu.VMEM((rows, width), f32),
            pltpu.VMEM((rows, width), f32),
        ],
        compiler_params=pltpu.CompilerParams(vmem_limit_bytes=40 << 20),
        cost_estimate=pl.CostEstimate(
            flops=12 * rows * width * inner,
            bytes_accessed=8 * width * inner,
            transcendentals=rows * inner,
        ),
        name="feed_forward",
    )(x_t, cot_t, attended_t, out_w, gain, gate_w, up_w, down_w_t)


def pair_grad_kernel(sides, ids, *refs):
    count = len(sides)
    ins, outs = refs[: 4 * count], refs[4 * count :]
    for number, (bit, base_row, by_shard, right_t) in enumerate(sides):
        left, left_other, right, right_other = ins[4 * number : 4 * number + 4]
        sent, kept = outs[2 * number : 2 * number + 2]
        rows = sent.shape[0]
        own = (ids[0] >> bit) & 1
        dim = 1 if right_t else 0
        mine = base_row + (ids[1] * (2 * rows) if by_shard else 0)
        pair = ((sent, 1 - own), (kept, own))
        for out, place in pair:
            near = left[pl.ds(pl.multiple_of(mine + place * rows, 8), rows), :]
            base = base_row if not by_shard else 0
            far = left_other[pl.ds(pl.multiple_of(base + place * rows, 8), rows), :]
            value = dot(near, right[...].reshape(right.shape[-2:]), 1, dim) + dot(
                far, right_other[...].reshape(right_other.shape[-2:]), 1, dim
            )
            out[...] = value.astype(bf16)


def pair_grad(name, ids, sides, operands, right_specs, tiles, rows, columns):
    tile = columns // tiles
    specs = []
    for (left, left_other, right, right_other), (spec, spec_other) in zip(operands, right_specs):
        specs += [
            pl.BlockSpec(left.shape, lambda i, ids: (0, 0)),
            pl.BlockSpec(left_other.shape, lambda i, ids: (0, 0)),
            spec,
            spec_other,
        ]
    out = pl.BlockSpec((rows, tile), lambda i, ids: (0, i))
    return pl.pallas_call(
        functools.partial(pair_grad_kernel, sides),
        grid_spec=pltpu.PrefetchScalarGridSpec(
            num_scalar_prefetch=1,
            grid=(tiles,),
            in_specs=specs,
            out_specs=[out] * (2 * len(sides)),
        ),
        out_shape=[jax.ShapeDtypeStruct((rows, columns), bf16)] * (2 * len(sides)),
        compiler_params=pltpu.CompilerParams(vmem_limit_bytes=40 << 20),
        cost_estimate=pl.CostEstimate(
            flops=4 * len(sides) * rows * columns * 512,
            bytes_accessed=8 * rows * columns,
            transcendentals=0,
        ),
        name=name,
    )(ids, *[o for group in operands for o in group])


def per_device(
    inputs,
    gain_attn,
    w_query,
    w_keyval,
    w_out,
    gain_mlp,
    w_gate,
    w_up,
    w_down,
    cotangent,
    seq_blocks,
    block_slots,
):
    micro = inputs.shape[0]
    shard = lax.axis_index("fsdp")
    is_low = shard == 0
    rounds = Rounds()

    def joined(part, other):
        return jnp.concatenate(
            [jnp.where(is_low, part, other), jnp.where(is_low, other, part)], axis=0
        )

    def whole(part):
        return lax.all_gather(part, "fsdp", axis=0, tiled=True)

    def theirs(value, dim):
        half = value.shape[dim] // 2
        return lax.dynamic_slice_in_dim(value, (1 - shard) * half, half, dim)

    def tokens_last(value):
        return jnp.concatenate([value[m, 0].T for m in range(micro)], axis=1)

    out_full = whole(w_out)
    gate_full = whole(w_gate)
    up_full = whole(w_up)
    down_full_t = whole(w_down).T

    attn_gain = joined(gain_attn, swap_fsdp(gain_attn)).astype(f32)[:, None]
    keyval_full = joined(w_keyval, swap_fsdp(w_keyval))
    x_t = tokens_last(inputs)
    in_t = x_t.astype(f32)
    inverse_attn = lax.rsqrt(jnp.mean(in_t * in_t, axis=0, keepdims=True) + EPS)
    normed_t = (in_t * inverse_attn * attn_gain).astype(bf16)
    keyvals = dot(normed_t, keyval_full, 0, 0).astype(bf16)
    gathers = [GatherBlocks(keyvals[m * BLK : (m + 1) * BLK]) for m in range(micro)]

    rounds.begin(gathers[0])
    (w_query, gain_mlp, cotangent, normed_t) = rounds.end(
        gathers[:1], (w_query, gain_mlp, cotangent, normed_t)
    )
    rounds.begin(*gathers[:2])
    query_other, gain_other = swap_fsdp(w_query), swap_fsdp(gain_mlp)
    cot_t = tokens_last(cotangent)
    (query_other, gain_other, cot_t) = rounds.end(
        gathers[:2], (query_other, gain_other, cot_t)
    )
    for step in range(len(gathers[0].stages)):
        rounds.begin(*[g for g in gathers if len(g.stages) > 2 or g is gathers[0]])
        if step == 0:
            query_full = joined(w_query, query_other)
            mlp_gain = joined(gain_mlp, gain_other).astype(f32)[None]
            queries_t = dot(query_full, normed_t, 0, 0).astype(bf16)
            normed_theirs = theirs(normed_t, 0)
            (queries_t, mlp_gain, normed_theirs) = rounds.end(
                list(rounds.flying), (queries_t, mlp_gain, normed_theirs)
            )
        elif step == 1:
            normed_other = swap_fsdp(normed_theirs)
            cot_other = swap_fsdp(cot_t)
            (normed_other, cot_other) = rounds.end(
                list(rounds.flying), (normed_other, cot_other)
            )
        else:
            rounds.end(list(rounds.flying))
    queries = [queries_t[:, m * BLK : (m + 1) * BLK] for m in range(micro)]
    ids = jnp.stack([lax.axis_index("ctx"), shard]).astype(jnp.int32)
    tables = (ids, seq_blocks, block_slots)

    rounds.begin(gathers[1])
    first = attention_forward(0, tables, *gathers[0].halves, queries[0])
    first = rounds.end([gathers[1]], first)
    rounds.begin(gathers[1])
    rounds.end([gathers[1]])
    second = attention_forward(1, tables, *gathers[1].halves, queries[1])
    outs, lses = zip(first, second)
    attended_t = jnp.concatenate(outs, axis=1).astype(bf16)

    attended_other = swap_fsdp(theirs(attended_t, 0))
    (
        hidden,
        grad_inner,
        normed_mlp_t,
        layer_out_t,
        grad_mixed_t,
        grad_mixed_low,
        grad_attended_t,
        mlp_gain_grad,
    ) = feed_forward(
        x_t, cot_t, attended_t, out_full, mlp_gain, gate_full, up_full, down_full_t
    )
    hidden_other = swap_fsdp(theirs(hidden, 1))
    inner_other = swap_fsdp(grad_inner)
    mlp_other = swap_fsdp(theirs(normed_mlp_t, 0))

    part = hidden_other.shape[1]
    width = cot_t.shape[0]
    rows = width // 4
    tokens = hidden.shape[0]
    tiles = 2
    near = pl.BlockSpec((tokens, part // tiles), lambda i, ids: (0, ids[1] * tiles + i))
    far = pl.BlockSpec((tokens, part // tiles), lambda i, ids: (0, i))
    down_parts = pair_grad(
        "down_grad",
        ids,
        ((0, 0, False, False), (1, 2 * rows, False, False)),
        ((cot_t, cot_other, hidden, hidden_other),) * 2,
        ((near, far),) * 2,
        tiles,
        rows,
        part,
    )
    down_job = Reduce(down_parts[:2], down_parts[2:])

    rounds.begin(down_job)
    inner = hidden.shape[1]
    tiles = 5
    specs = [
        pl.BlockSpec((1, tokens, inner // tiles), lambda i, ids, n=n: (n, 0, i)) for n in range(2)
    ]
    inner_parts = pair_grad(
        "inner_grad",
        ids,
        ((0, 0, True, False), (1, 0, True, False)),
        ((normed_mlp_t, mlp_other, grad_inner, inner_other),) * 2,
        [(spec, spec) for spec in specs],
        tiles,
        rows,
        inner,
    )
    inner_parts = rounds.end([down_job], inner_parts)
    mlp_job = Reduce(inner_parts[:2], inner_parts[2:])

    def attention_back(m):
        return attention_backward(
            m,
            tables,
            *gathers[m].halves,
            queries[m],
            grad_attended_t[:, m * BLK : (m + 1) * BLK],
            outs[m],
            lses[m],
        )

    rounds.begin(mlp_job, down_job)
    back_first = attention_back(0)
    back_first = rounds.end([down_job], back_first)
    rounds.begin(down_job)
    mixed_other = swap_fsdp(grad_mixed_low)
    (mixed_other,) = rounds.end([down_job], (mixed_other,))
    while down_job.stages:
        rounds.begin(down_job)
        rounds.end([down_job])
    down_spread = Spread(down_job.held)
    rounds.begin(down_spread)
    back_second = attention_back(1)
    back_second = rounds.end([down_spread, mlp_job], back_second)
    key_job = ScatterBlocks(*zip(back_first[1:], back_second[1:]))
    grad_queries_t = jnp.concatenate([back_first[0], back_second[0]], axis=1)

    rounds.begin(mlp_job, down_spread)
    queries_other = swap_fsdp(grad_queries_t)
    (queries_other,) = rounds.end([mlp_job, down_spread], (queries_other,))
    rounds.begin(key_job, mlp_job)
    half = rows * 2
    flat = pl.BlockSpec((width, tokens), lambda i, ids: (0, 0))
    tall = pl.BlockSpec((tokens, width), lambda i, ids: (0, 0))
    query_parts = pair_grad(
        "query_grad",
        ids,
        ((0, 0, True, True), (1, 0, True, False)),
        (
            (normed_t, normed_other, grad_queries_t, queries_other),
            (attended_t, attended_other, grad_mixed_low, mixed_other),
        ),
        ((flat, flat), (tall, tall)),
        1,
        rows,
        width,
    )
    query_parts = rounds.end([mlp_job], query_parts)
    query_job = Reduce(query_parts[:2], query_parts[2:])
    while mlp_job.stages:
        rounds.begin(mlp_job)
        rounds.end([mlp_job] if len(mlp_job.stages) > 1 else [mlp_job, key_job])
    mlp_spread = Spread(mlp_job.held)
    rounds.begin(key_job, mlp_spread)
    grad_normed_t = dot(query_full, grad_queries_t, 1, 0)
    (grad_normed_t,) = rounds.end([key_job, mlp_spread], (grad_normed_t,))
    while len(mlp_spread.stages) > 3:
        rounds.begin(mlp_spread)
        rounds.end([mlp_spread])
    while len(down_spread.stages) > 2:
        rounds.begin(down_spread)
        rounds.end([down_spread])
    rounds.begin(key_job, query_job)
    rounds.end([key_job, query_job])
    rounds.begin(key_job, query_job, down_spread)
    rounds.end([key_job, query_job, down_spread])
    while key_job.stages:
        rounds.begin(key_job)
        rounds.end([key_job])
    grad_keyvals = jnp.concatenate([b[0] for b in key_job.held], axis=0)

    rounds.begin(mlp_spread, query_job, down_spread)
    keyvals_other = swap_fsdp(grad_keyvals)
    grad_normed_t = grad_normed_t + dot(keyval_full, grad_keyvals, 1, 1)
    attn_gain_grad = jnp.sum(grad_normed_t * in_t * inverse_attn, axis=1)
    scaled = grad_normed_t * attn_gain
    cubed = inverse_attn * inverse_attn * inverse_attn
    input_grad_t = (
        grad_mixed_t
        + inverse_attn * scaled
        - in_t * cubed * jnp.mean(scaled * in_t, axis=0, keepdims=True)
    )
    gains = jnp.stack([attn_gain_grad, mlp_gain_grad[0]], axis=1)
    gains_theirs = theirs(gains, 0)
    normed_mine = lax.dynamic_slice_in_dim(normed_t, shard * half, half, 0)
    keyval_grad = dot(normed_mine, grad_keyvals, 1, 0) + dot(normed_other, keyvals_other, 1, 0)
    gains_mine = lax.dynamic_slice_in_dim(gains, shard * half, half, 0) + swap_fsdp(gains_theirs)
    pad = jnp.zeros((half, LANES - 2), bf16)
    last = jnp.concatenate([keyval_grad.astype(bf16), gains_mine.astype(bf16), pad], axis=1)
    (last, input_grad_t) = rounds.end(
        [mlp_spread, query_job, down_spread], (last, input_grad_t)
    )
    last_job = Solo(last)
    rounds.begin(last_job, mlp_spread, query_job)
    down_sum = jnp.concatenate(down_spread.pair, axis=0)
    (down_sum,) = rounds.end([last_job, mlp_spread, query_job], (down_sum,))
    while query_job.stages:
        rounds.begin(query_job)
        rounds.end([query_job])
    query_spread = Spread(query_job.held)
    rounds.begin(mlp_spread, query_spread, last_job)
    while last_job.stages:
        ahead = len(last_job.stages)
        rounds.end([j for j in rounds.flying if j is not mlp_spread or ahead == 2])
        more = [last_job]
        if len(query_spread.stages) > 2 or ahead <= 3:
            more.append(query_spread)
        rounds.begin(*[j for j in more if j.stages])
    rounds.end(list(rounds.flying))
    while query_spread.stages:
        rounds.begin(query_spread)
        rounds.end([query_spread])

    def by_token(value_t):
        parts = [value_t[:, m * BLK : (m + 1) * BLK].T[None] for m in range(micro)]
        return jnp.stack(parts)

    columns = keyval_grad.shape[1]
    return (
        by_token(layer_out_t),
        by_token(input_grad_t),
        last_job.value[:, columns],
        query_spread.pair[0],
        last_job.value[:, :columns],
        query_spread.pair[1],
        last_job.value[:, columns + 1],
        mlp_spread.pair[0],
        mlp_spread.pair[1],
        down_sum.T,
    )


def solution(mesh):
    tokens = P(None, "fsdp", "ctx", None)
    vector = P("fsdp")
    matrix = P("fsdp", None)
    return jax.shard_map(
        per_device,
        mesh=mesh,
        in_specs=(
            tokens,
            vector,
            matrix,
            matrix,
            matrix,
            vector,
            matrix,
            matrix,
            matrix,
            tokens,
            P(),
            P(),
        ),
        out_specs=(
            tokens,
            tokens,
            vector,
            matrix,
            matrix,
            matrix,
            vector,
            matrix,
            matrix,
            matrix,
        ),
        check_vma=False,
    )
```

time: 626 us -> 459 us (0.73)
  matrix products: 68.9 us -> 5.36 us
  waiting for transfers between devices: 259 us -> 211 us
  local copies, waits for them, and re-layouts: 59.2 us -> 25.9 us
  starting transfers between devices: 115 us -> 97.1 us
  Pallas kernels: 29.9 us -> 46.4 us
  between operations: 26.9 us -> 16.2 us
  other arithmetic: 55.8 us -> 49.5 us
    dot_general x24 -> x6, matrix products: 68.9 us -> 5.36 us  [dot(): lax.dot_general(left, right, (((left_dim,), (right_dim,)), ((), ())), pre...]
    ppermute x88 -> x60, waiting for transfers between devices: 257 us -> 203 us  [flip_ctx(): return lax.ppermute(value, 'ctx', [(i, i ^ 1 << bit) for i in range(size)])]
    ppermute x88 -> x60, starting transfers between devices: 109 us -> 91.9 us  [flip_ctx(): return lax.ppermute(value, 'ctx', [(i, i ^ 1 << bit) for i in range(size)])]
    pallas_call x4 -> x8, Pallas kernels: 29.9 us -> 46.4 us  [the longest x1 17.6 us: feed_forward(): pl.pallas_call(block_kernel, grid=(inner // tile,), in_specs=[fixed(wide)...]
    dynamic_slice x30 -> x14, local copies, waits for them, and re-layouts: 15.5 us -> 2.53 us  [the longest x3 1.28 us: theirs(): return lax.dynamic_slice_in_dim(value, (1 - shard) * half, half, dim)]
    concatenate x8 -> x4, local copies, waits for them, and re-layouts: 11.9 us -> 0.15 us  [the longest x1 0.08 us: per_device(): jnp.concatenate([keyval_grad.astype(bf16), gains_mine.astype(bf16), pad],...]
    ppermute x4 -> x0, local copies, waits for them, and re-layouts: 7.39 us -> none  [flip_ctx(): return lax.ppermute(value, 'ctx', [(i, i ^ 1 << bit) for i in range(size)])]
    unnamed x216 -> x247, local copies, waits for them, and re-layouts: 14.3 us -> 21.7 us
  transfers between devices with their start and end apart: 108 -> 78, of which waited for: 54 -> 45; matrix products, arithmetic and copies ran while one was open for 28% -> 11% of each run, Pallas kernels for 5% -> 6%
where the time goes in v2:
time: 459 us; the launch traced here: 452 us
  waiting for transfers between devices  211 us (46%)
  starting transfers between devices  97.1 us (21%)
  other arithmetic  49.5 us (11%)
  Pallas kernels  46.4 us (10%)
  local copies, waits for them, and re-layouts  25.9 us (6%)
  between operations  16.2 us (4%)
  matrix products  5.36 us (1%)
    ppermute x60, waiting for transfers between devices, flip_ctx(): return lax.ppermute(value, 'ctx', [(i, i ^ 1 << bit) for i in range(size)])  203 us
    ppermute x60, starting transfers between devices, flip_ctx(): return lax.ppermute(value, 'ctx', [(i, i ^ 1 << bit) for i in range(size)])  91.9 us
    unnamed x247, local copies, waits for them, and re-layouts  21.7 us
    pallas_call x1, Pallas kernels, feed_forward(): pl.pallas_call(block_kernel, grid=(inner // tile,), in_specs=[fixed(wide)...  17.6 us
    pallas_call x3, Pallas kernels, pair_grad(): pl.pallas_call(functools.partial(pair_grad_kernel, sides), grid_spec=pltp...  12.4 us
    concatenate x15, other arithmetic, in_order(): return jnp.concatenate(by_bit(bit, mine, arrived), axis=dim)  12.1 us
    convert_element_type x21, other arithmetic, add_low(): return (kept.astype(f32) + arrived.astype(f32)).astype(bf16)  12 us
    pallas_call x2, Pallas kernels, attention_backward(): pl.pallas_call(functools.partial(backward_kernel, steps > WINDOW // BLK,...  10 us
  transfers between devices with their start and end apart: 78, of which 45 were waited for; matrix products, arithmetic and copies ran while one was open for 11% of the time, Pallas kernels for 6%

profile of v2, /device:TPU:0, one launch (start us, length us, event | category | flops | bytes accessed | tf_op | source)
XLA Modules:
  0.0 451.6 jit_solution(13189026016675126022)
XLA Ops:
  17.1 8.2 %collective-permute-done.2 = bf16[1,128,640]{2,1,0:T(8,128)(2,1)S(1)} collective-permute-done((bf16[1,128,640]{2,1,0:T(8,128)(2,1)S(1)}, bf16[1,128,640]{2,1,0:T(8,128)(2,1)S(1)}, u32[]{:S(2)}, u32[]{:S(2)}) %collective-permute-start.2) | collective-permute-done | bytes 163872 | tf_op jit(solution)/shard_map/ppermute | solution.py:36
  30.0 6.5 %collective-permute-done.6 = bf16[1,128,640]{2,1,0:T(8,128)(2,1)S(1)} collective-permute-done((bf16[1,128,640]{2,1,0:T(8,128)(2,1)S(1)}, bf16[1,128,640]{2,1,0:T(8,128)(2,1)S(1)}, u32[]{:S(2)}, u32[]{:S(2)}) %collective-permute-start.6) | collective-permute-done | bytes 163872 | tf_op jit(solution)/shard_map/ppermute | solution.py:36
  56.4 13.2 %collective-permute-done.13 = bf16[8,64,640]{2,1,0:T(8,128)(2,1)S(1)} collective-permute-done((bf16[8,64,640]{2,1,0:T(8,128)(2,1)S(1)}, bf16[8,64,640]{2,1,0:T(8,128)(2,1)S(1)}, u32[]{:S(2)}, u32[]{:S(2)}) %collective-permute-start.13) | collective-permute-done | bytes 655392 | tf_op jit(solution)/shard_map/ppermute | solution.py:36
  79.0 11.7 %collective-permute-done.17 = bf16[8,64,640]{2,1,0:T(8,128)(2,1)S(1)} collective-permute-done((bf16[8,64,640]{2,1,0:T(8,128)(2,1)S(1)}, bf16[8,64,640]{2,1,0:T(8,128)(2,1)S(1)}, u32[]{:S(2)}, u32[]{:S(2)}) %collective-permute-start.17) | collective-permute-done | bytes 655392 | tf_op jit(solution)/shard_map/ppermute | solution.py:36
  101.8 17.6 %feed_forward.1 = (bf16[256,2560]{1,0:T(8,128)(2,1)S(1)}, bf16[2,256,2560]{2,1,0:T(8,128)(2,1)S(1)}, bf16[960,256]{1,0:T(8,128)(2,1)S(1)}, bf16[960,256]{1,0:T(8...) custom-call(bf16[960,256]{1,0:T(8,128)(2,1)S(1)} %copy-done.46, ...), custom_call_target="tpu_custom_call" | custom-call | flops 7549747200 | bytes 19660800 | tf_op jit(solution)/shard_map/feed_forward/pallas_call | solution.py:549
  143.3 6.0 %inner_grad.1 = (bf16[240,2560]{1,0:T(8,128)(2,1)S(1)}, bf16[240,2560]{1,0:T(8,128)(2,1)S(1)}, bf16[240,2560]{1,0:T(8,128)(2,1)S(1)}, bf16[240,2560]{1,0:T(8,128)(2,1)S(1)}) custom-call(s32[2]{0:T(128)S(1)} %pad_add_fusion.ids, bf16[960,256]{1,0:T(8,128)(2,1)S(1)} %copy-done.6, bf16[480,256]{1,0:T(8,128)(2,1)S(1)} %collective-permute-done.19.refs_1_.refs_5_, ...), custom_call_target="tpu_custom_call" | custom-call | flops 2516582400 | bytes 4915200 | tf_op jit(solution)/shard_map/inner_grad/pallas_call | solution.py:623
  150.3 5.0 %collective-permute-done.21 = bf16[240,1280]{1,0:T(8,128)(2,1)} collective-permute-done((bf16[240,1280]{1,0:T(8,128)(2,1)}, bf16[240,1280]{1,0:T(8,128)(2,1)}, u32[]{:S(2)}, u32[]{:S(2)}) %collective-permute-start.21) | collective-permute-done | bytes 614432 | tf_op jit(solution)/shard_map/ppermute | solution.py:36
  168.8 9.6 %collective-permute-start.26 = (bf16[120,1280]{1,0:T(8,128)(2,1)}, bf16[120,1280]{1,0:T(8,128)(2,1)}, u32[]{:S(2)}, u32[]{:S(2)}) collective-permute-start(bf16[120,1280]{1,0:T(8,128)(2,1)} %broadcast_select_fusion.19), channel_id=1, source_target_pairs={{0,8},{2,10},{4,12},{6,14},{8,0},{10,2},{12,4},{14,6},{16,24},{18,... | collective-permute-start | bytes 921608 | tf_op jit(solution)/shard_map/ppermute | solution.py:36
  185.1 5.3 %collective-permute-start.27 = (bf16[120,640]{1,0:T(8,128)(2,1)S(1)}, bf16[120,640]{1,0:T(8,128)(2,1)S(1)}, u32[]{:S(2)}, u32[]{:S(2)}) collective-permute-start(bf16[120,640]{1,0:T(8,128)(2,1)S(1)} %constant_dynamic-slice_fusion.8), channel_id=1, source_target_pairs={{0,16},{2,18},{4,20},{6,22},{8,24},{10,26},{12,28},{14,30},{16,0},... | collective-permute-start | bytes 460808 | tf_op jit(solution)/shard_map/ppermute | solution.py:36
  191.5 5.1 %attention_backward.3 = (bf16[960,128]{1,0:T(8,128)(2,1)S(1)}, bf16[16,64,640]{2,1,0:T(8,128)(2,1)S(1)}, bf16[16,64,640]{2,1,0:T(8,128)(2,1)S(1)}) custom-call(s32[2]{0:T(128)S(1)} %pad_add_fusion.ids, s32[2,2,2]{2,1,0:T(2,128)S(1)} %copy-done.58, s32[2,2,16]{2,1,0:T(2,128)S(1)} %copy-done.59, bf16[16,64,640]{2,1,0:T(8,128)(2,1)S(1)} %copy-done.15, ...), custom_call_target="tpu_custom_call" | custom-call | flops 1258291200 | bytes 5242880 | tf_op jit(solution)/shard_map/attention_backward/pallas_call | solution.py:439
  196.7 8.5 %collective-permute-start.28 = (bf16[120,640]{1,0:T(8,128)(2,1)S(1)}, bf16[120,640]{1,0:T(8,128)(2,1)S(1)}, u32[]{:S(2)}, u32[]{:S(2)}) collective-permute-start(bf16[120,640]{1,0:T(8,128)(2,1)S(1)} %add_convert_fusion.20), channel_id=1, source_target_pairs={{0,16},{2,18},{4,20},{6,22},{8,24},{10,26},{12,28},{14,30},{16,0},... | collective-permute-start | bytes 460808 | tf_op jit(solution)/shard_map/ppermute | solution.py:36
  205.3 7.6 %collective-permute-done.28 = bf16[120,640]{1,0:T(8,128)(2,1)S(1)} collective-permute-done((bf16[120,640]{1,0:T(8,128)(2,1)S(1)}, bf16[120,640]{1,0:T(8,128)(2,1)S(1)}, u32[]{:S(2)}, u32[]{:S(2)}) %collective-permute-start.28) | collective-permute-done | bytes 153632 | tf_op jit(solution)/shard_map/ppermute | solution.py:36
  216.8 5.3 %collective-permute-done.34 = bf16[120,1280]{1,0:T(8,128)(2,1)S(1)} collective-permute-done((bf16[120,1280]{1,0:T(8,128)(2,1)S(1)}, bf16[120,1280]{1,0:T(8,128)(2,1)S(1)}, u32[]{:S(2)}, u32[]{:S(2)}) %collective-permute-start.34) | collective-permute-done | bytes 307232 | tf_op jit(solution)/shard_map/ppermute | solution.py:36
  222.1 8.8 %collective-permute-done.33 = bf16[120,2560]{1,0:T(8,128)(2,1)S(1)} collective-permute-done((bf16[120,2560]{1,0:T(8,128)(2,1)S(1)}, bf16[120,2560]{1,0:T(8,128)(2,1)S(1)}, u32[]{:S(2)}, u32[]{:S(2)}) %collective-permute-start.33) | collective-permute-done | bytes 614432 | tf_op jit(solution)/shard_map/ppermute | solution.py:36
  241.1 5.0 %collective-permute-done.36 = bf16[120,2560]{1,0:T(8,128)(2,1)S(1)} collective-permute-done((bf16[120,2560]{1,0:T(8,128)(2,1)S(1)}, bf16[120,2560]{1,0:T(8,128)(2,1)S(1)}, u32[]{:S(2)}, u32[]{:S(2)}) %collective-permute-start.36) | collective-permute-done | bytes 614432 | tf_op jit(solution)/shard_map/ppermute | solution.py:36
  249.8 13.7 %collective-permute-done.39 = bf16[2,8,64,640]{3,2,1,0:T(8,128)(2,1)} collective-permute-done((bf16[2,8,64,640]{3,2,1,0:T(8,128)(2,1)}, bf16[2,8,64,640]{3,2,1,0:T(8,128)(2,1)}, u32[]{:S(2)}, u32[]{:S(2)}) %collective-permute-start.39) | collective-permute-done | bytes 1310752 | tf_op jit(solution)/shard_map/ppermute | solution.py:36
  276.4 9.5 %collective-permute-done.42 = bf16[120,1280]{1,0:T(8,128)(2,1)S(1)} collective-permute-done((bf16[120,1280]{1,0:T(8,128)(2,1)S(1)}, bf16[120,1280]{1,0:T(8,128)(2,1)S(1)}, u32[]{:S(2)}, u32[]{:S(2)}) %collective-permute-start.42) | collective-permute-done | bytes 307232 | tf_op jit(solution)/shard_map/ppermute | solution.py:36
  291.7 14.2 %collective-permute-done.44 = bf16[240,960]{1,0:T(8,128)(2,1)S(1)} collective-permute-done((bf16[240,960]{1,0:T(8,128)(2,1)S(1)}, bf16[240,960]{1,0:T(8,128)(2,1)S(1)}, u32[]{:S(2)}, u32[]{:S(2)}) %collective-permute-start.44) | collective-permute-done | bytes 460832 | tf_op jit(solution)/shard_map/ppermute | solution.py:36
  315.9 9.3 %collective-permute-done.46 = bf16[2,1,128,640]{3,2,1,0:T(8,128)(2,1)S(1)} collective-permute-done((bf16[2,1,128,640]{3,2,1,0:T(8,128)(2,1)S(1)}, bf16[2,1,128,640]{3,2,1,0:T(8,128)(2,1)S(1)}, u32[]{:S(2)}, u32[]{:S(2)}) %collective-permute-start.46) | collective-permute-done | bytes 327712 | tf_op jit(solution)/shard_map/ppermute | solution.py:36
  340.0 8.3 %collective-permute-done.55 = bf16[240,1280]{1,0:T(8,128)(2,1)} collective-permute-done((bf16[240,1280]{1,0:T(8,128)(2,1)}, bf16[240,1280]{1,0:T(8,128)(2,1)}, u32[]{:S(2)}, u32[]{:S(2)}) %collective-permute-start.55) | collective-permute-done | bytes 614432 | tf_op jit(solution)/shard_map/ppermute | solution.py:36
  368.4 10.7 %collective-permute-done.59 = bf16[120,2560]{1,0:T(8,128)(2,1)S(1)} collective-permute-done((bf16[120,2560]{1,0:T(8,128)(2,1)S(1)}, bf16[120,2560]{1,0:T(8,128)(2,1)S(1)}, u32[]{:S(2)}, u32[]{:S(2)}) %collective-permute-start.59) | collective-permute-done | bytes 614432 | tf_op jit(solution)/shard_map/ppermute | solution.py:36
  404.7 7.5 %collective-permute-done.70 = bf16[120,960]{1,0:T(8,128)(2,1)S(1)} collective-permute-done((bf16[120,960]{1,0:T(8,128)(2,1)S(1)}, bf16[120,960]{1,0:T(8,128)(2,1)S(1)}, u32[]{:S(2)}, u32[]{:S(2)}) %collective-permute-start.70) | collective-permute-done | bytes 230432 | tf_op jit(solution)/shard_map/ppermute | solution.py:36
  412.2 8.5 %collective-permute-done.69 = bf16[120,960]{1,0:T(8,128)(2,1)S(1)} collective-permute-done((bf16[120,960]{1,0:T(8,128)(2,1)S(1)}, bf16[120,960]{1,0:T(8,128)(2,1)S(1)}, u32[]{:S(2)}, u32[]{:S(2)}) %collective-permute-start.69) | collective-permute-done | bytes 230432 | tf_op jit(solution)/shard_map/ppermute | solution.py:36
  433.9 5.3 %collective-permute-done.72 = bf16[240,960]{1,0:T(8,128)(2,1)S(1)} collective-permute-done((bf16[240,960]{1,0:T(8,128)(2,1)S(1)}, bf16[240,960]{1,0:T(8,128)(2,1)S(1)}, u32[]{:S(2)}, u32[]{:S(2)}) %collective-permute-start.72) | collective-permute-done | bytes 460832 | tf_op jit(solution)/shard_map/ppermute | solution.py:36
  (540 shorter events, 225.0 us)
Async XLA Ops:
  7.2 91.0 %all-gather.5.cloned.1.call-start = ((), (), s32[]{:S(2)}) async-start(), calls=%async_computation | async-start | bytes 2949120 | tf_op jit(solution)/shard_map/all_gather | solution.py:667
  7.9 90.3 %all-gather.7.cloned.1.call-start = ((), (), s32[]{:S(2)}) async-start(), calls=%async_computation.1 | async-start | bytes 7372800 | tf_op jit(solution)/shard_map/all_gather | solution.py:667
  8.7 89.5 %all-gather.9.cloned.1.call-start = ((), (), s32[]{:S(2)}) async-start(), calls=%async_computation.2 | async-start | bytes 7372800 | tf_op jit(solution)/shard_map/all_gather | solution.py:667
  9.4 88.8 %all-gather.11.cloned.1.call-start = ((), (), s32[]{:S(2)}) async-start(), calls=%async_computation.3 | async-start | bytes 7372800 | tf_op jit(solution)/shard_map/all_gather | solution.py:667
  51.8 17.7 %collective-permute-start.13 = (bf16[8,64,640]{2,1,0:T(8,128)(2,1)S(1)}, bf16[8,64,640]{2,1,0:T(8,128)(2,1)S(1)}, u32[]{:S(2)}, u32[]{:S(2)}) collective-permute-start(bf16[8,64,640]{2,1,0:T(8,128)(2,1)S(1)} %pad_maximum_fusion.22), channel_id=1, source_target_pairs={{0,4},{2,6},{4,0},{6,2},{8,12},{10,14},{12,8},{14,10},{16,20},{18,... | collective-permute-start | bytes 1966088 | tf_op jit(solution)/shard_map/ppermute | solution.py:36
  54.2 21.2 %collective-permute-start.15 = (bf16[4,64,640]{2,1,0:T(8,128)(2,1)S(1)}, bf16[4,64,640]{2,1,0:T(8,128)(2,1)S(1)}, u32[]{:S(2)}, u32[]{:S(2)}) collective-permute-start(bf16[4,64,640]{2,1,0:T(8,128)(2,1)S(1)} %get-tuple-element.294), channel_id=1, source_target_pairs={{0,2},{2,0},{4,6},{6,4},{8,10},{10,8},{12,14},{14,12},{16,18},{18,... | collective-permute-start | bytes 983048 | tf_op jit(solution)/shard_map/ppermute | solution.py:36
  55.8 19.7 %collective-permute-start.14 = (bf16[4,64,640]{2,1,0:T(8,128)(2,1)S(1)}, bf16[4,64,640]{2,1,0:T(8,128)(2,1)S(1)}, u32[]{:S(2)}, u32[]{:S(2)}) collective-permute-start(bf16[4,64,640]{2,1,0:T(8,128)(2,1)S(1)} %get-tuple-element.295), channel_id=1, source_target_pairs={{0,4},{2,6},{4,0},{6,2},{8,12},{10,14},{12,8},{14,10},{16,20},{18,... | collective-permute-start | bytes 983048 | tf_op jit(solution)/shard_map/ppermute | solution.py:36
  140.7 41.0 %collective-permute-start.25 = (bf16[256,960]{1,0:T(8,128)(2,1)}, bf16[256,960]{1,0:T(8,128)(2,1)}, u32[]{:S(2)}, u32[]{:S(2)}) collective-permute-start(bf16[256,960]{1,0:T(8,128)(2,1)} %copy-done.32), channel_id=1, source_target_pairs={{0,1},{1,0},{2,3},{3,2},{4,5},{5,4},{6,7},{7,6},{8,9},{9,8},{10,11... | collective-permute-start | bytes 1474568 | tf_op jit(solution)/shard_map/ppermute | solution.py:40
  178.4 34.5 %collective-permute-start.29 = (bf16[240,2560]{1,0:T(8,128)(2,1)}, bf16[240,2560]{1,0:T(8,128)(2,1)S(1)}, u32[]{:S(2)}, u32[]{:S(2)}) collective-permute-start(bf16[240,2560]{1,0:T(8,128)(2,1)} %copy-done.53), channel_id=1, source_target_pairs={{0,2},{2,0},{4,6},{6,4},{8,10},{10,8},{12,14},{14,12},{16,18},{18,... | collective-permute-start | bytes 3686408 | tf_op jit(solution)/shard_map/ppermute | solution.py:36
  178.4 34.5 %collective-permute-start.30 = (bf16[240,2560]{1,0:T(8,128)(2,1)}, bf16[240,2560]{1,0:T(8,128)(2,1)S(1)}, u32[]{:S(2)}, u32[]{:S(2)}) collective-permute-start(bf16[240,2560]{1,0:T(8,128)(2,1)} %copy-done.52), channel_id=1, source_target_pairs={{0,4},{2,6},{4,0},{6,2},{8,12},{10,14},{12,8},{14,10},{16,20},{18,... | collective-permute-start | bytes 3686408 | tf_op jit(solution)/shard_map/ppermute | solution.py:36
  191.4 46.8 %collective-permute-start.35 = (bf16[480,256]{1,0:T(8,128)(2,1)S(1)}, bf16[480,256]{1,0:T(8,128)(2,1)S(1)}, u32[]{:S(2)}, u32[]{:S(2)}) collective-permute-start(bf16[480,256]{1,0:T(8,128)(2,1)S(1)} %fusion.28), channel_id=1, source_target_pairs={{0,1},{1,0},{2,3},{3,2},{4,5},{5,4},{6,7},{7,6},{8,9},{9,8},{10,11... | collective-permute-start | bytes 737288 | tf_op jit(solution)/shard_map/ppermute | solution.py:40
  234.1 29.3 %collective-permute-start.39 = (bf16[2,8,64,640]{3,2,1,0:T(8,128)(2,1)}, bf16[2,8,64,640]{3,2,1,0:T(8,128)(2,1)}, u32[]{:S(2)}, u32[]{:S(2)}) collective-permute-start(bf16[2,8,64,640]{3,2,1,0:T(8,128)(2,1)} %pad_maximum_fusion.11), channel_id=1, source_target_pairs={{0,4},{2,6},{4,0},{6,2},{8,12},{10,14},{12,8},{14,10},{16,20},{18,... | collective-permute-start | bytes 3932168 | tf_op jit(solution)/shard_map/ppermute | solution.py:36
  236.5 29.1 %collective-permute-start.38 = (bf16[2,8,64,640]{3,2,1,0:T(8,128)(2,1)}, bf16[2,8,64,640]{3,2,1,0:T(8,128)(2,1)}, u32[]{:S(2)}, u32[]{:S(2)}) collective-permute-start(bf16[2,8,64,640]{3,2,1,0:T(8,128)(2,1)} %pad_maximum_fusion.10), channel_id=1, source_target_pairs={{0,2},{2,0},{4,6},{6,4},{8,10},{10,8},{12,14},{14,12},{16,18},{18,... | collective-permute-start | bytes 3932168 | tf_op jit(solution)/shard_map/ppermute | solution.py:36
  247.5 18.1 %collective-permute-start.37 = (bf16[120,1280]{1,0:T(8,128)(2,1)}, bf16[120,1280]{1,0:T(8,128)(2,1)}, u32[]{:S(2)}, u32[]{:S(2)}) collective-permute-start(bf16[120,1280]{1,0:T(8,128)(2,1)} %constant_dynamic-slice_fusion.5), channel_id=1, source_target_pairs={{0,16},{2,18},{4,20},{6,22},{8,24},{10,26},{12,28},{14,30},{16,0},... | collective-permute-start | bytes 921608 | tf_op jit(solution)/shard_map/ppermute | solution.py:36
  286.5 20.4 %collective-permute-start.43 = (bf16[2,2,128,640]{3,2,1,0:T(8,128)(2,1)S(1)}, bf16[2,2,128,640]{3,2,1,0:T(8,128)(2,1)S(1)}, u32[]{:S(2)}, u32[]{:S(2)}) collective-permute-start(bf16[2,2,128,640]{3,2,1,0:T(8,128)(2,1)S(1)} %pad_maximum_fusion.28), channel_id=1, source_target_pairs={{0,8},{2,10},{4,12},{6,14},{8,0},{10,2},{12,4},{14,6},{16,24},{18,... | collective-permute-start | bytes 1966088 | tf_op jit(solution)/shard_map/ppermute | solution.py:36
  287.5 25.8 %collective-permute-start.50 = (bf16[120,1280]{1,0:T(8,128)(2,1)S(1)}, bf16[120,1280]{1,0:T(8,128)(2,1)S(1)}, u32[]{:S(2)}, u32[]{:S(2)}) collective-permute-start(bf16[120,1280]{1,0:T(8,128)(2,1)S(1)} %get-tuple-element.304), channel_id=1, source_target_pairs={{0,2},{2,0},{4,6},{6,4},{8,10},{10,8},{12,14},{14,12},{16,18},{18,... | collective-permute-start | bytes 921608 | tf_op jit(solution)/shard_map/ppermute | solution.py:36
  288.5 25.9 %collective-permute-start.49 = (bf16[120,1280]{1,0:T(8,128)(2,1)S(1)}, bf16[120,1280]{1,0:T(8,128)(2,1)S(1)}, u32[]{:S(2)}, u32[]{:S(2)}) collective-permute-start(bf16[120,1280]{1,0:T(8,128)(2,1)S(1)} %get-tuple-element.305), channel_id=1, source_target_pairs={{0,4},{2,6},{4,0},{6,2},{8,12},{10,14},{12,8},{14,10},{16,20},{18,... | collective-permute-start | bytes 921608 | tf_op jit(solution)/shard_map/ppermute | solution.py:36
  313.3 26.6 %collective-permute-start.53 = (bf16[120,2560]{1,0:T(8,128)(2,1)}, bf16[120,2560]{1,0:T(8,128)(2,1)}, u32[]{:S(2)}, u32[]{:S(2)}) collective-permute-start(bf16[120,2560]{1,0:T(8,128)(2,1)} %pad_maximum_fusion.29), channel_id=1, source_target_pairs={{0,8},{2,10},{4,12},{6,14},{8,0},{10,2},{12,4},{14,6},{16,24},{18,... | collective-permute-start | bytes 1843208 | tf_op jit(solution)/shard_map/ppermute | solution.py:36
  359.3 19.8 %collective-permute-start.59 = (bf16[120,2560]{1,0:T(8,128)(2,1)S(1)}, bf16[120,2560]{1,0:T(8,128)(2,1)S(1)}, u32[]{:S(2)}, u32[]{:S(2)}) collective-permute-start(bf16[120,2560]{1,0:T(8,128)(2,1)S(1)} %get-tuple-element.272), channel_id=1, source_target_pairs={{0,2},{2,0},{4,6},{6,4},{8,10},{10,8},{12,14},{14,12},{16,18},{18,... | collective-permute-start | bytes 1843208 | tf_op jit(solution)/shard_map/ppermute | solution.py:36
  360.5 18.6 %collective-permute-start.58 = (bf16[120,2560]{1,0:T(8,128)(2,1)S(1)}, bf16[120,2560]{1,0:T(8,128)(2,1)S(1)}, u32[]{:S(2)}, u32[]{:S(2)}) collective-permute-start(bf16[120,2560]{1,0:T(8,128)(2,1)S(1)} %get-tuple-element.273), channel_id=1, source_target_pairs={{0,4},{2,6},{4,0},{6,2},{8,12},{10,14},{12,8},{14,10},{16,20},{18,... | collective-permute-start | bytes 1843208 | tf_op jit(solution)/shard_map/ppermute | solution.py:36
  380.6 42.2 %collective-permute-start.66 = (bf16[240,2560]{1,0:T(8,128)(2,1)S(1)}, bf16[240,2560]{1,0:T(8,128)(2,1)S(1)}, u32[]{:S(2)}, u32[]{:S(2)}) collective-permute-start(bf16[240,2560]{1,0:T(8,128)(2,1)S(1)} %pad_maximum_fusion.15), channel_id=1, source_target_pairs={{0,2},{2,0},{4,6},{6,4},{8,10},{10,8},{12,14},{14,12},{16,18},{18,... | collective-permute-start | bytes 3686408 | tf_op jit(solution)/shard_map/ppermute | solution.py:36
  388.5 34.3 %collective-permute-start.67 = (bf16[240,2560]{1,0:T(8,128)(2,1)S(1)}, bf16[240,2560]{1,0:T(8,128)(2,1)S(1)}, u32[]{:S(2)}, u32[]{:S(2)}) collective-permute-start(bf16[240,2560]{1,0:T(8,128)(2,1)S(1)} %pad_maximum_fusion.16), channel_id=1, source_target_pairs={{0,4},{2,6},{4,0},{6,2},{8,12},{10,14},{12,8},{14,10},{16,20},{18,... | collective-permute-start | bytes 3686408 | tf_op jit(solution)/shard_map/ppermute | solution.py:36
  400.2 20.5 %collective-permute-start.69 = (bf16[120,960]{1,0:T(8,128)(2,1)S(1)}, bf16[120,960]{1,0:T(8,128)(2,1)S(1)}, u32[]{:S(2)}, u32[]{:S(2)}) collective-permute-start(bf16[120,960]{1,0:T(8,128)(2,1)S(1)} %get-tuple-element.311), channel_id=1, source_target_pairs={{0,4},{2,6},{4,0},{6,2},{8,12},{10,14},{12,8},{14,10},{16,20},{18,... | collective-permute-start | bytes 691208 | tf_op jit(solution)/shard_map/ppermute | solution.py:36
  402.9 20.0 %collective-permute-start.68 = (bf16[120,768]{1,0:T(8,128)(2,1)S(1)}, bf16[120,768]{1,0:T(8,128)(2,1)S(1)}, u32[]{:S(2)}, u32[]{:S(2)}) collective-permute-start(bf16[120,768]{1,0:T(8,128)(2,1)S(1)} %add_convert_fusion.17), channel_id=1, source_target_pairs={{0,4},{2,6},{4,0},{6,2},{8,12},{10,14},{12,8},{14,10},{16,20},{18,... | collective-permute-start | bytes 552968 | tf_op jit(solution)/shard_map/ppermute | solution.py:36
  (176 other events, 1676.0 us)
Sparse Core Ops, SparseCore 0:
  9.6 13.0 all-gather.4
  24.2 15.8 all-gather.6
  41.7 16.2 all-gather.8
  59.4 15.5 all-gather.10

commit v3 on v2

--- a/solution.py
+++ b/solution.py
@@ -73,11 +73,11 @@
 
     def operands(self):
         if self.stages[0] is not None:
-            return [(self.held, self.stages[0])]
+            return [self.held], [self.stages[0]]
         if self.halves is None:
             self.halves = [self.held[:, :HALF], self.held[:, HALF:]]
             self.bits = (1, 0)
-        return list(zip(self.halves, self.bits))
+        return self.halves, self.bits
 
     def absorb(self, arrived):
         if self.stages.pop(0) is not None:
@@ -90,26 +90,24 @@
 
 
 class ScatterBlocks:
-    def __init__(self, firsts, seconds):
-        self.halves = [firsts, seconds]
+    def __init__(self, first, second):
+        self.halves = [first, second]
         self.bits = (0, 1)
         self.stages = [None, None] + high_bits()
         self.held = None
 
     def operands(self):
         if self.stages[0] is None:
-            count = self.halves[0][0].shape[0] // 2
-            sent = [jnp.stack([b[count:] for b in half]) for half in self.halves]
-            return list(zip(sent, self.bits))
+            count = self.halves[0].shape[0] // 2
+            return [half[count:] for half in self.halves], self.bits
         if self.held is None:
-            self.held = [jnp.concatenate([a, b], axis=1) for a, b in zip(*self.halves)]
-        count = self.held[0].shape[0] // 2
-        return [(jnp.stack([b[count:] for b in self.held]), self.stages[0])]
+            self.held = jnp.concatenate(self.halves, axis=1)
+        count = self.held.shape[0] // 2
+        return [self.held[count:]], [self.stages[0]]
 
     def absorb(self, arrived):
         def add(blocks, sums):
-            count = blocks[0].shape[0] // 2
-            return [add_low(b[:count], sums[m]) for m, b in enumerate(blocks)]
+            return add_low(blocks[: blocks.shape[0] // 2], sums)
 
         if self.stages.pop(0) is None:
             self.halves = [add(half, a) for half, a in zip(self.halves, arrived)]
@@ -118,33 +116,36 @@
             self.held = add(self.held, arrived[0])
 
 
+def cut(value, bit, dim):
+    half = value.shape[dim] // 2
+    own = own_bit(bit)
+    sent = lax.dynamic_slice_in_dim(value, (1 - own) * half, half, dim)
+    return lax.dynamic_slice_in_dim(value, own * half, half, dim), sent
+
+
 class Reduce:
-    def __init__(self, first, second):
-        self.ready = [first, second]
+    def __init__(self, parts, dims):
+        self.first = [parts[0], parts[2]]
+        self.kept = [parts[1], parts[3]]
+        self.dims = dims
         self.stages = [(0, 1), (1, 0)] + high_bits()
-
-    def cut(self, value, bit, dim):
-        half = value.shape[dim] // 2
-        own = own_bit(bit)
-        sent = lax.dynamic_slice_in_dim(value, (1 - own) * half, half, dim)
-        return lax.dynamic_slice_in_dim(value, own * half, half, dim), sent
 
     def operands(self):
         stage = self.stages[0]
-        if isinstance(stage, tuple):
-            if self.ready is None:
-                self.ready = [self.cut(v, b, 0)[::-1] for v, b in zip(self.pair, stage)]
-            self.kept = [r[1] for r in self.ready]
-            sent = [(r[0], b) for r, b in zip(self.ready, stage)]
-            self.ready = None
-            return sent
-        if self.pair is not None:
-            kept, sent = by_bit(stage, *self.pair)
-            self.pair = None
+        if self.first is not None:
+            sent, self.first = self.first, None
+        elif isinstance(stage, tuple):
+            parts = [cut(v, b, self.dims[0]) for v, b in zip(self.pair, stage)]
+            self.kept = [p[0] for p in parts]
+            sent = [p[1] for p in parts]
         else:
-            kept, sent = self.cut(self.held, stage, 1)
-        self.kept = [kept]
-        return [(sent, stage)]
+            if self.pair is not None:
+                kept, out = by_bit(stage, *self.pair)
+                self.pair = None
+            else:
+                kept, out = cut(self.held, stage, self.dims[1])
+            self.kept, sent, stage = [kept], [out], [stage]
+        return sent, stage
 
     def absorb(self, arrived):
         sums = [add_low(k, a) for k, a in zip(self.kept, arrived)]
@@ -155,29 +156,30 @@
 
 
 class Spread:
-    def __init__(self, chunk):
-        self.held = chunk
+    def __init__(self, job):
+        self.held = job.held
+        self.dims = job.dims
         self.stages = high_bits()[::-1] + [(1, 0), (0, 1)]
         self.pair = None
 
     def operands(self):
         stage = self.stages[0]
         if isinstance(stage, tuple):
-            return list(zip(self.pair, stage))
-        return [(self.held, stage)]
+            return self.pair, stage
+        return [self.held], [stage]
 
     def absorb(self, arrived):
         stage = self.stages.pop(0)
         if isinstance(stage, tuple):
-            kind = bf16 if self.stages else f32
+            kind, dim = (bf16, self.dims[0]) if self.stages else (f32, 0)
             self.pair = [
-                in_order(b, v.astype(kind), a.astype(kind), 0)
+                in_order(b, v.astype(kind), a.astype(kind), dim)
                 for v, a, b in zip(self.pair, arrived, stage)
             ]
         elif stage == 2:
             self.pair = list(by_bit(stage, self.held, arrived[0]))
         else:
-            self.held = in_order(stage, self.held, arrived[0], 1)
+            self.held = in_order(stage, self.held, arrived[0], self.dims[1])
 
 
 class Solo:
@@ -189,12 +191,9 @@
     def operands(self):
         bit, cuts = self.stages[0]
         if not cuts:
-            return [(self.value, bit)]
-        half = self.value.shape[0] // 2
-        own = own_bit(bit)
-        sent = lax.dynamic_slice_in_dim(self.value, (1 - own) * half, half, 0)
-        self.value = lax.dynamic_slice_in_dim(self.value, own * half, half, 0)
-        return [(sent, bit)]
+            return [self.value], [bit]
+        self.value, sent = cut(self.value, bit, 0)
+        return [sent], [bit]
 
     def absorb(self, arrived):
         bit, cuts = self.stages.pop(0)
@@ -208,21 +207,40 @@
 class Rounds:
     def __init__(self):
         self.flying = {}
+        self.ready = {}
+        self.fresh = []
 
     def begin(self, *jobs):
         for job in jobs:
-            self.flying[job] = [flip_ctx(v, b) for v, b in job.operands()]
-
-    def end(self, jobs, values=()):
-        values = list(values)
-        arrived = [a for job in jobs for a in self.flying[job]]
-        tied = tie(values + arrived)
-        rest = list(tied[len(values) :])
+            arrays, bits = self.ready.pop(job, None) or job.operands()
+            self.flying[job] = [flip_ctx(v, b) for v, b in zip(arrays, bits)]
+
+    def prepare(self, *jobs):
+        for job in jobs:
+            self.ready[job] = job.operands()
+            self.fresh.append(job)
+
+    def end(self, jobs, *values):
+        ahead = [job for job in self.fresh if job in self.ready]
+        self.fresh = []
+        arrays = [a for job in jobs for a in self.flying[job]]
+        sent = [a for job in ahead for a in self.ready[job][0]]
+        rest = list(tie([*values, *arrays, *sent]))
+        values, rest = rest[: len(values)], rest[len(values) :]
         for job in jobs:
             count = len(self.flying.pop(job))
             job.absorb(rest[:count])
             rest = rest[count:]
-        return tied[: len(values)]
+        for job in ahead:
+            count = len(self.ready[job][0])
+            self.ready[job] = (rest[:count], self.ready[job][1])
+            rest = rest[count:]
+        return values
+
+    def run(self, job, left):
+        while len(job.stages) > left:
+            self.begin(job)
+            self.end([job])
 
 
 def key_tile(first_ref, second_ref, places, unit):
@@ -407,6 +425,10 @@
         dq_ref[head * HD : (head + 1) * HD, :] = (acc_ref[:, columns] * SCALE).astype(bf16)
 
 
+def in_hbm(values):
+    return [pltpu.with_memory_space_constraint(v, pltpu.HBM) for v in values]
+
+
 VMEM_SPEC = pl.BlockSpec(memory_space=pltpu.VMEM)
 SMEM_SPEC = pl.BlockSpec(memory_space=pltpu.SMEM)
 
@@ -424,7 +446,7 @@
         in_specs=[SMEM_SPEC] * 3 + [VMEM_SPEC] * 3,
         out_specs=(VMEM_SPEC,) * 2,
         scratch_shapes=[pltpu.VMEM((LANES, HEADS * BLK), bf16)],
-        compiler_params=pltpu.CompilerParams(vmem_limit_bytes=40 << 20),
+        compiler_params=pltpu.CompilerParams(vmem_limit_bytes=8 << 20),
         cost_estimate=pl.CostEstimate(
             flops=4 * HEADS * HD * BLK * BLK * 8,
             bytes_accessed=first.size * 4,
@@ -454,11 +476,11 @@
             pltpu.VMEM((2 * BLK, 2 * KVH * GCOLS), bf16),
             pltpu.VMEM((HD, HEADS * BLK), f32),
         ],
-        compiler_params=pltpu.CompilerParams(vmem_limit_bytes=48 << 20),
+        compiler_params=pltpu.CompilerParams(vmem_limit_bytes=16 << 20),
         cost_estimate=pl.CostEstimate(
-            flops=10 * HEADS * HD * BLK * BLK * 8,
-            bytes_accessed=first.size * 8,
-            transcendentals=HEADS * BLK * BLK * 8,
+            flops=10 * HEADS * HD * BLK * BLK,
+            bytes_accessed=first.size,
+            transcendentals=HEADS * BLK * BLK,
         ),
         name="attention_backward",
     )(*tables, first, second, queries_t, grads_t, out_t, lse)
@@ -562,14 +584,14 @@
             fixed((1, width)),
         ),
         out_shape=(
-            jax.ShapeDtypeStruct((rows, inner), bf16),
-            jax.ShapeDtypeStruct((2, rows, inner), bf16),
-            jax.ShapeDtypeStruct(wide, bf16),
-            jax.ShapeDtypeStruct(wide, bf16),
-            jax.ShapeDtypeStruct(wide, f32),
-            jax.ShapeDtypeStruct((rows, width), bf16),
-            jax.ShapeDtypeStruct(wide, bf16),
-            jax.ShapeDtypeStruct((1, width), f32),
+            pltpu.HBM((rows, inner), bf16),
+            pltpu.HBM((2, rows, inner), bf16),
+            pltpu.HBM(wide, bf16),
+            pltpu.HBM(wide, bf16),
+            pltpu.HBM(wide, f32),
+            pltpu.HBM((rows, width), bf16),
+            pltpu.HBM(wide, bf16),
+            pltpu.HBM((1, width), f32),
         ),
         scratch_shapes=[
             pltpu.VMEM((rows, width), f32),
@@ -578,65 +600,73 @@
             pltpu.VMEM((rows, width), f32),
             pltpu.VMEM((rows, width), f32),
         ],
-        compiler_params=pltpu.CompilerParams(vmem_limit_bytes=40 << 20),
+        compiler_params=pltpu.CompilerParams(vmem_limit_bytes=24 << 20),
         cost_estimate=pl.CostEstimate(
             flops=12 * rows * width * inner,
             bytes_accessed=8 * width * inner,
             transcendentals=rows * inner,
         ),
         name="feed_forward",
-    )(x_t, cot_t, attended_t, out_w, gain, gate_w, up_w, down_w_t)
-
-
-def pair_grad_kernel(sides, ids, *refs):
-    count = len(sides)
-    ins, outs = refs[: 4 * count], refs[4 * count :]
-    for number, (bit, base_row, by_shard, right_t) in enumerate(sides):
-        left, left_other, right, right_other = ins[4 * number : 4 * number + 4]
+    )(*in_hbm([x_t, cot_t, attended_t, out_w, gain, gate_w, up_w, down_w_t]))
+
+
+def weight_grad_kernel(products, sides, ids, *refs):
+    values = []
+    for number, (by_shard, right_t) in enumerate(products):
+        left, left_other, right, right_other = refs[4 * number : 4 * number + 4]
+        rows = left_other.shape[0]
+        start = pl.multiple_of(ids[1] * rows if by_shard else 0, 8)
+        dim = 1 if right_t else 0
+        values.append(
+            dot(left[pl.ds(start, rows), :], right[...].reshape(right.shape[-2:]), 1, dim)
+            + dot(left_other[...], right_other[...].reshape(right_other.shape[-2:]), 1, dim)
+        )
+    outs = refs[4 * len(products) :]
+    for number, (product, first, rows, bit) in enumerate(sides):
         sent, kept = outs[2 * number : 2 * number + 2]
-        rows = sent.shape[0]
+        half = rows // 2
+        low = values[product][first : first + half].astype(bf16)
+        high = values[product][first + half : first + rows].astype(bf16)
         own = (ids[0] >> bit) & 1
-        dim = 1 if right_t else 0
-        mine = base_row + (ids[1] * (2 * rows) if by_shard else 0)
-        pair = ((sent, 1 - own), (kept, own))
-        for out, place in pair:
-            near = left[pl.ds(pl.multiple_of(mine + place * rows, 8), rows), :]
-            base = base_row if not by_shard else 0
-            far = left_other[pl.ds(pl.multiple_of(base + place * rows, 8), rows), :]
-            value = dot(near, right[...].reshape(right.shape[-2:]), 1, dim) + dot(
-                far, right_other[...].reshape(right_other.shape[-2:]), 1, dim
-            )
-            out[...] = value.astype(bf16)
-
-
-def pair_grad(name, ids, sides, operands, right_specs, tiles, rows, columns):
+
+        @pl.when(own == 0)
+        def _():
+            kept[...] = low
+            sent[...] = high
+
+        @pl.when(own != 0)
+        def _():
+            kept[...] = high
+            sent[...] = low
+
+
+def weight_grad(name, ids, products, operands, right_specs, sides, tiles, columns):
     tile = columns // tiles
     specs = []
-    for (left, left_other, right, right_other), (spec, spec_other) in zip(operands, right_specs):
+    for (left, left_other, _, _), rights in zip(operands, right_specs):
         specs += [
             pl.BlockSpec(left.shape, lambda i, ids: (0, 0)),
             pl.BlockSpec(left_other.shape, lambda i, ids: (0, 0)),
-            spec,
-            spec_other,
+            *rights,
         ]
-    out = pl.BlockSpec((rows, tile), lambda i, ids: (0, i))
+    shapes = [(side[2] // 2, columns) for side in sides for _ in range(2)]
     return pl.pallas_call(
-        functools.partial(pair_grad_kernel, sides),
+        functools.partial(weight_grad_kernel, products, sides),
         grid_spec=pltpu.PrefetchScalarGridSpec(
             num_scalar_prefetch=1,
             grid=(tiles,),
             in_specs=specs,
-            out_specs=[out] * (2 * len(sides)),
-        ),
-        out_shape=[jax.ShapeDtypeStruct((rows, columns), bf16)] * (2 * len(sides)),
-        compiler_params=pltpu.CompilerParams(vmem_limit_bytes=40 << 20),
+            out_specs=[pl.BlockSpec((rows, tile), lambda i, ids: (0, i)) for rows, _ in shapes],
+        ),
+        out_shape=[pltpu.HBM(shape, bf16) for shape in shapes],
+        compiler_params=pltpu.CompilerParams(vmem_limit_bytes=16 << 20),
         cost_estimate=pl.CostEstimate(
-            flops=4 * len(sides) * rows * columns * 512,
-            bytes_accessed=8 * rows * columns,
+            flops=2 * sum(rows * width for rows, width in shapes) * 512,
+            bytes_accessed=2 * sum(rows * width for rows, width in shapes),
             transcendentals=0,
         ),
         name=name,
-    )(ids, *[o for group in operands for o in group])
+    )(ids, *in_hbm([o for group in operands for o in group]))
 
 
 def per_device(
@@ -689,14 +719,12 @@
 
     rounds.begin(gathers[0])
     (w_query, gain_mlp, cotangent, normed_t) = rounds.end(
-        gathers[:1], (w_query, gain_mlp, cotangent, normed_t)
-    )
-    rounds.begin(*gathers[:2])
+        gathers[:1], w_query, gain_mlp, cotangent, normed_t
+    )
+    rounds.begin(*gathers)
     query_other, gain_other = swap_fsdp(w_query), swap_fsdp(gain_mlp)
     cot_t = tokens_last(cotangent)
-    (query_other, gain_other, cot_t) = rounds.end(
-        gathers[:2], (query_other, gain_other, cot_t)
-    )
+    (query_other, gain_other, cot_t) = rounds.end(gathers, query_other, gain_other, cot_t)
     for step in range(len(gathers[0].stages)):
         rounds.begin(*[g for g in gathers if len(g.stages) > 2 or g is gathers[0]])
         if step == 0:
@@ -705,14 +733,12 @@
             queries_t = dot(query_full, normed_t, 0, 0).astype(bf16)
             normed_theirs = theirs(normed_t, 0)
             (queries_t, mlp_gain, normed_theirs) = rounds.end(
-                list(rounds.flying), (queries_t, mlp_gain, normed_theirs)
+                list(rounds.flying), queries_t, mlp_gain, normed_theirs
             )
         elif step == 1:
             normed_other = swap_fsdp(normed_theirs)
             cot_other = swap_fsdp(cot_t)
-            (normed_other, cot_other) = rounds.end(
-                list(rounds.flying), (normed_other, cot_other)
-            )
+            (normed_other, cot_other) = rounds.end(list(rounds.flying), normed_other, cot_other)
         else:
             rounds.end(list(rounds.flying))
     queries = [queries_t[:, m * BLK : (m + 1) * BLK] for m in range(micro)]
@@ -720,10 +746,10 @@
     tables = (ids, seq_blocks, block_slots)
 
     rounds.begin(gathers[1])
+    rounds.end(gathers[1:])
+    rounds.begin(gathers[1])
     first = attention_forward(0, tables, *gathers[0].halves, queries[0])
-    first = rounds.end([gathers[1]], first)
-    rounds.begin(gathers[1])
-    rounds.end([gathers[1]])
+    first = rounds.end(gathers[1:], *first)
     second = attention_forward(1, tables, *gathers[1].halves, queries[1])
     outs, lses = zip(first, second)
     attended_t = jnp.concatenate(outs, axis=1).astype(bf16)
@@ -742,46 +768,44 @@
         x_t, cot_t, attended_t, out_full, mlp_gain, gate_full, up_full, down_full_t
     )
     hidden_other = swap_fsdp(theirs(hidden, 1))
+    mlp_other = swap_fsdp(theirs(normed_mlp_t, 0))
     inner_other = swap_fsdp(grad_inner)
-    mlp_other = swap_fsdp(theirs(normed_mlp_t, 0))
 
     part = hidden_other.shape[1]
     width = cot_t.shape[0]
-    rows = width // 4
-    tokens = hidden.shape[0]
-    tiles = 2
-    near = pl.BlockSpec((tokens, part // tiles), lambda i, ids: (0, ids[1] * tiles + i))
-    far = pl.BlockSpec((tokens, part // tiles), lambda i, ids: (0, i))
-    down_parts = pair_grad(
-        "down_grad",
-        ids,
-        ((0, 0, False, False), (1, 2 * rows, False, False)),
-        ((cot_t, cot_other, hidden, hidden_other),) * 2,
-        ((near, far),) * 2,
-        tiles,
-        rows,
-        part,
-    )
-    down_job = Reduce(down_parts[:2], down_parts[2:])
-
-    rounds.begin(down_job)
-    inner = hidden.shape[1]
-    tiles = 5
-    specs = [
-        pl.BlockSpec((1, tokens, inner // tiles), lambda i, ids, n=n: (n, 0, i)) for n in range(2)
-    ]
-    inner_parts = pair_grad(
-        "inner_grad",
-        ids,
-        ((0, 0, True, False), (1, 0, True, False)),
-        ((normed_mlp_t, mlp_other, grad_inner, inner_other),) * 2,
-        [(spec, spec) for spec in specs],
-        tiles,
-        rows,
-        inner,
-    )
-    inner_parts = rounds.end([down_job], inner_parts)
-    mlp_job = Reduce(inner_parts[:2], inner_parts[2:])
+    half = width // 2
+    tokens, inner = hidden.shape
+    near = pl.BlockSpec((tokens, part // 2), lambda i, ids: (0, ids[1] * 2 + i))
+    far = pl.BlockSpec((tokens, part // 2), lambda i, ids: (0, i))
+    down_job = Reduce(
+        weight_grad(
+            "down_grad",
+            ids,
+            ((False, False),),
+            ((cot_t, cot_other, hidden, hidden_other),),
+            ((near, far),),
+            ((0, 0, half, 0), (0, half, half, 1)),
+            2,
+            part,
+        ),
+        (1, 0),
+    )
+
+    def inner_job(n):
+        spec = pl.BlockSpec((1, tokens, inner // 5), lambda i, ids: (n, 0, i))
+        return Reduce(
+            weight_grad(
+                "inner_grad",
+                ids,
+                ((True, False),),
+                ((normed_mlp_t, mlp_other, grad_inner, inner_other),),
+                ((spec, spec),),
+                ((0, 0, half // 2, 0), (0, half // 2, half // 2, 1)),
+                5,
+                inner,
+            ),
+            (1, 1),
+        )
 
     def attention_back(m):
         return attention_backward(
@@ -794,77 +818,111 @@
             lses[m],
         )
 
-    rounds.begin(mlp_job, down_job)
+    gate_job = inner_job(0)
+    rounds.prepare(down_job, gate_job)
+    (grad_inner, grad_attended_t, grad_mixed_low) = rounds.end(
+        [], grad_inner, grad_attended_t, grad_mixed_low
+    )
+
+    rounds.begin(down_job, gate_job)
+    up_job = inner_job(1)
+    rounds.prepare(up_job)
+    (grad_attended_t, grad_mixed_low) = rounds.end([down_job], grad_attended_t, grad_mixed_low)
+
+    rounds.begin(up_job)
+    rounds.prepare(down_job)
     back_first = attention_back(0)
-    back_first = rounds.end([down_job], back_first)
+    (grad_attended_t, grad_mixed_low, *back_first) = rounds.end(
+        [gate_job], grad_attended_t, grad_mixed_low, *back_first
+    )
+
     rounds.begin(down_job)
+    key_first = ScatterBlocks(*back_first[1:])
+    rounds.prepare(gate_job, key_first)
+    (grad_attended_t, grad_mixed_low) = rounds.end([up_job], grad_attended_t, grad_mixed_low)
+
+    rounds.begin(gate_job, key_first)
+    rounds.prepare(up_job)
+    back_second = attention_back(1)
     mixed_other = swap_fsdp(grad_mixed_low)
-    (mixed_other,) = rounds.end([down_job], (mixed_other,))
-    while down_job.stages:
-        rounds.begin(down_job)
-        rounds.end([down_job])
-    down_spread = Spread(down_job.held)
+    (mixed_other, *back_second) = rounds.end([down_job], mixed_other, *back_second)
+
+    rounds.begin(up_job, down_job)
+    key_second = ScatterBlocks(*back_second[1:])
+    rounds.prepare(key_second)
+    grad_queries_t = jnp.concatenate([back_first[0], back_second[0]], axis=1)
+    (grad_queries_t,) = rounds.end([gate_job], grad_queries_t)
+
+    rounds.begin(key_second, gate_job)
+    queries_other = swap_fsdp(grad_queries_t)
+    (queries_other,) = rounds.end([key_first, down_job], queries_other)
+
+    rounds.begin(down_job)
+    rounds.prepare(key_first)
+    rounds.end([up_job, gate_job])
+    rounds.begin(key_first, up_job, gate_job)
+    flat = pl.BlockSpec((width, tokens), lambda i, ids: (0, 0))
+    flat_half = pl.BlockSpec((tokens, width), lambda i, ids: (0, 0))
+    query_job = Reduce(
+        weight_grad(
+            "query_grad",
+            ids,
+            ((True, True), (True, False)),
+            (
+                (normed_t, normed_other, grad_queries_t, queries_other),
+                (attended_t, attended_other, grad_mixed_low, mixed_other),
+            ),
+            ((flat, flat), (flat_half, flat_half)),
+            ((0, 0, half, 0), (1, 0, half, 1)),
+            1,
+            width,
+        ),
+        (0, 1),
+    )
+    rounds.prepare(query_job)
+    rounds.end([key_second, down_job])
+    rounds.run(down_job, 0)
+    down_spread = Spread(down_job)
+
+    rounds.begin(down_spread, query_job)
+    rounds.prepare(key_second)
+    (grad_queries_t,) = rounds.end([key_first, up_job, gate_job], grad_queries_t)
+    rounds.run(gate_job, 0)
+    gate_spread = Spread(gate_job)
+
+    rounds.begin(key_second, key_first, up_job, gate_spread)
+    grad_normed_t = dot(query_full, grad_queries_t, 1, 0)
+    (grad_normed_t,) = rounds.end([down_spread, query_job], grad_normed_t)
+    rounds.run(down_spread, 3)
+
+    rounds.begin(down_spread, query_job)
+    rounds.end([key_second, key_first, up_job, gate_spread])
+    rounds.run(up_job, 0)
+    up_spread = Spread(up_job)
+    rounds.run(gate_spread, 3)
+
+    rounds.begin(key_second, key_first, up_spread, gate_spread)
+    rounds.end([down_spread, query_job])
+
     rounds.begin(down_spread)
-    back_second = attention_back(1)
-    back_second = rounds.end([down_spread, mlp_job], back_second)
-    key_job = ScatterBlocks(*zip(back_first[1:], back_second[1:]))
-    grad_queries_t = jnp.concatenate([back_first[0], back_second[0]], axis=1)
-
-    rounds.begin(mlp_job, down_spread)
-    queries_other = swap_fsdp(grad_queries_t)
-    (queries_other,) = rounds.end([mlp_job, down_spread], (queries_other,))
-    rounds.begin(key_job, mlp_job)
-    half = rows * 2
-    flat = pl.BlockSpec((width, tokens), lambda i, ids: (0, 0))
-    tall = pl.BlockSpec((tokens, width), lambda i, ids: (0, 0))
-    query_parts = pair_grad(
-        "query_grad",
-        ids,
-        ((0, 0, True, True), (1, 0, True, False)),
-        (
-            (normed_t, normed_other, grad_queries_t, queries_other),
-            (attended_t, attended_other, grad_mixed_low, mixed_other),
-        ),
-        ((flat, flat), (tall, tall)),
-        1,
-        rows,
-        width,
-    )
-    query_parts = rounds.end([mlp_job], query_parts)
-    query_job = Reduce(query_parts[:2], query_parts[2:])
-    while mlp_job.stages:
-        rounds.begin(mlp_job)
-        rounds.end([mlp_job] if len(mlp_job.stages) > 1 else [mlp_job, key_job])
-    mlp_spread = Spread(mlp_job.held)
-    rounds.begin(key_job, mlp_spread)
-    grad_normed_t = dot(query_full, grad_queries_t, 1, 0)
-    (grad_normed_t,) = rounds.end([key_job, mlp_spread], (grad_normed_t,))
-    while len(mlp_spread.stages) > 3:
-        rounds.begin(mlp_spread)
-        rounds.end([mlp_spread])
-    while len(down_spread.stages) > 2:
-        rounds.begin(down_spread)
-        rounds.end([down_spread])
-    rounds.begin(key_job, query_job)
-    rounds.end([key_job, query_job])
-    rounds.begin(key_job, query_job, down_spread)
-    rounds.end([key_job, query_job, down_spread])
-    while key_job.stages:
-        rounds.begin(key_job)
-        rounds.end([key_job])
-    grad_keyvals = jnp.concatenate([b[0] for b in key_job.held], axis=0)
-
-    rounds.begin(mlp_spread, query_job, down_spread)
+    rounds.end([key_second, key_first, up_spread, gate_spread])
+    rounds.run(key_first, 0)
+    rounds.run(up_spread, 3)
+
+    rounds.begin(key_second, gate_spread, up_spread, query_job)
+    rounds.end([down_spread, key_second])
+    rounds.run(key_second, 0)
+    grad_keyvals = jnp.concatenate([key_first.held[0], key_second.held[0]], axis=0)
+
+    rounds.begin(down_spread)
     keyvals_other = swap_fsdp(grad_keyvals)
     grad_normed_t = grad_normed_t + dot(keyval_full, grad_keyvals, 1, 1)
+    (grad_normed_t, keyvals_other) = rounds.end(
+        [gate_spread, up_spread, query_job], grad_normed_t, keyvals_other
+    )
+
+    rounds.begin(gate_spread, query_job)
     attn_gain_grad = jnp.sum(grad_normed_t * in_t * inverse_attn, axis=1)
-    scaled = grad_normed_t * attn_gain
-    cubed = inverse_attn * inverse_attn * inverse_attn
-    input_grad_t = (
-        grad_mixed_t
-        + inverse_attn * scaled
-        - in_t * cubed * jnp.mean(scaled * in_t, axis=0, keepdims=True)
-    )
     gains = jnp.stack([attn_gain_grad, mlp_gain_grad[0]], axis=1)
     gains_theirs = theirs(gains, 0)
     normed_mine = lax.dynamic_slice_in_dim(normed_t, shard * half, half, 0)
@@ -872,29 +930,38 @@
     gains_mine = lax.dynamic_slice_in_dim(gains, shard * half, half, 0) + swap_fsdp(gains_theirs)
     pad = jnp.zeros((half, LANES - 2), bf16)
     last = jnp.concatenate([keyval_grad.astype(bf16), gains_mine.astype(bf16), pad], axis=1)
-    (last, input_grad_t) = rounds.end(
-        [mlp_spread, query_job, down_spread], (last, input_grad_t)
-    )
     last_job = Solo(last)
-    rounds.begin(last_job, mlp_spread, query_job)
+    rounds.prepare(last_job)
+    (grad_normed_t,) = rounds.end([down_spread, query_job], grad_normed_t)
+    rounds.run(query_job, 0)
+    query_spread = Spread(query_job)
+
+    rounds.begin(last_job, up_spread, query_spread)
     down_sum = jnp.concatenate(down_spread.pair, axis=0)
-    (down_sum,) = rounds.end([last_job, mlp_spread, query_job], (down_sum,))
-    while query_job.stages:
-        rounds.begin(query_job)
-        rounds.end([query_job])
-    query_spread = Spread(query_job.held)
-    rounds.begin(mlp_spread, query_spread, last_job)
-    while last_job.stages:
-        ahead = len(last_job.stages)
-        rounds.end([j for j in rounds.flying if j is not mlp_spread or ahead == 2])
-        more = [last_job]
-        if len(query_spread.stages) > 2 or ahead <= 3:
-            more.append(query_spread)
-        rounds.begin(*[j for j in more if j.stages])
-    rounds.end(list(rounds.flying))
-    while query_spread.stages:
-        rounds.begin(query_spread)
-        rounds.end([query_spread])
+    (down_sum,) = rounds.end([last_job, gate_spread, query_spread], down_sum)
+    rounds.run(query_spread, 3)
+
+    rounds.begin(last_job, query_spread)
+    scaled = grad_normed_t * attn_gain
+    cubed = inverse_attn * inverse_attn * inverse_attn
+    input_grad_t = (
+        grad_mixed_t
+        + inverse_attn * scaled
+        - in_t * cubed * jnp.mean(scaled * in_t, axis=0, keepdims=True)
+    )
+    (input_grad_t,) = rounds.end([last_job, up_spread, query_spread], input_grad_t)
+
+    rounds.begin(last_job, up_spread, query_spread)
+    gate_sum = jnp.concatenate(gate_spread.pair, axis=0)
+    (gate_sum,) = rounds.end([last_job, query_spread], gate_sum)
+    rounds.begin(last_job, query_spread)
+    rounds.end([last_job])
+    rounds.run(last_job, 2)
+    rounds.begin(last_job)
+    rounds.end([last_job, up_spread])
+    rounds.begin(last_job)
+    up_sum = jnp.concatenate(up_spread.pair, axis=0)
+    (up_sum,) = rounds.end([last_job, query_spread], up_sum)
 
     def by_token(value_t):
         parts = [value_t[:, m * BLK : (m + 1) * BLK].T[None] for m in range(micro)]
@@ -909,8 +976,8 @@
         last_job.value[:, :columns],
         query_spread.pair[1],
         last_job.value[:, columns + 1],
-        mlp_spread.pair[0],
-        mlp_spread.pair[1],
+        gate_sum,
+        up_sum,
         down_sum.T,
     )
 

time: 459 us -> 434 us (0.946); the launches traced: 452 us -> 431 us
  waiting for transfers between devices: 211 us -> 155 us
  Pallas kernels: 46.4 us -> 86.7 us
  starting transfers between devices: 97.1 us -> 105 us
  local copies, waits for them, and re-layouts: 25.9 us -> 19.8 us
  other arithmetic: 49.5 us -> 44.3 us
    ppermute x60 -> x78, waiting for transfers between devices: 203 us -> 146 us  [flip_ctx(): return lax.ppermute(value, 'ctx', [(i, i ^ 1 << bit) for i in range(size)])]
    pallas_call x2, Pallas kernels: 10 us -> 29.4 us  [attention_backward(): pl.pallas_call(functools.partial(backward_kernel, steps > WINDOW // BLK,...]
    pallas_call x3 -> x4, Pallas kernels: 12.4 us -> 23.5 us  [weight_grad(): pl.pallas_call(functools.partial(weight_grad_kernel, products, sides), gr...]
    ppermute x60 -> x78, starting transfers between devices: 91.9 us -> 102 us  [flip_ctx(): return lax.ppermute(value, 'ctx', [(i, i ^ 1 << bit) for i in range(size)])]
    unnamed x247 -> x188, local copies, waits for them, and re-layouts: 21.7 us -> 13.8 us
    pallas_call x2, Pallas kernels: 6.44 us -> 13.1 us  [attention_forward(): pl.pallas_call(functools.partial(forward_kernel, steps > WINDOW // BLK, s...]
    convert_element_type x21 -> x30, other arithmetic: 12 us -> 6.91 us  [add_low(): return (kept.astype(f32) + arrived.astype(f32)).astype(bf16)]
    concatenate x15 -> x16, other arithmetic: 12.1 us -> 7.77 us  [in_order(): return jnp.concatenate(by_bit(bit, mine, arrived), axis=dim)]
  transfers between devices with their start and end apart: 78 -> 96, of which waited for: 45 -> 49; matrix products, arithmetic and copies ran while one was open for 11% -> 12% of each run, Pallas kernels for 6% -> 14%
where the time goes in v3:
time: 434 us; the launch traced here: 431 us
  waiting for transfers between devices  155 us (36%)
  starting transfers between devices  105 us (24%)
  Pallas kernels  86.7 us (20%)
  other arithmetic  44.3 us (10%)
  local copies, waits for them, and re-layouts  19.8 us (5%)
  between operations  15.9 us (4%)
  matrix products  4.96 us (1%)
    ppermute x78, waiting for transfers between devices, flip_ctx(): return lax.ppermute(value, 'ctx', [(i, i ^ 1 << bit) for i in range(size)])  146 us
    ppermute x78, starting transfers between devices, flip_ctx(): return lax.ppermute(value, 'ctx', [(i, i ^ 1 << bit) for i in range(size)])  102 us
    pallas_call x2, Pallas kernels, attention_backward(): pl.pallas_call(functools.partial(backward_kernel, steps > WINDOW // BLK,...  29.4 us
    pallas_call x4, Pallas kernels, weight_grad(): pl.pallas_call(functools.partial(weight_grad_kernel, products, sides), gr...  23.5 us
    pallas_call x1, Pallas kernels, feed_forward(): pl.pallas_call(block_kernel, grid=(inner // tile,), in_specs=[fixed(wide)...  20.7 us
    unnamed x188, local copies, waits for them, and re-layouts  13.8 us
    pallas_call x2, Pallas kernels, attention_forward(): pl.pallas_call(functools.partial(forward_kernel, steps > WINDOW // BLK, s...  13.1 us
    select_n x30, other arithmetic, by_bit(): return (jnp.where(low, mine, arrived), jnp.where(low, arrived, mine))  9.06 us
  transfers between devices with their start and end apart: 96, of which 49 were waited for; matrix products, arithmetic and copies ran while one was open for 12% of the time, Pallas kernels for 14%

profile of v3, /device:TPU:0, one launch (start us, length us, event | category | flops | bytes accessed | tf_op | source)
XLA Modules:
  0.0 431.2 jit_solution(5061762207774643608)
XLA Ops:
  17.1 8.2 %collective-permute-done.2 = bf16[1,128,640]{2,1,0:T(8,128)(2,1)S(1)} collective-permute-done((bf16[1,128,640]{2,1,0:T(8,128)(2,1)S(1)}, bf16[1,128,640]{2,1,0:T(8,128)(2,1)S(1)}, u32[]{:S(2)}, u32[]{:S(2)}) %collective-permute-start.2) | collective-permute-done | bytes 163872 | tf_op jit(solution)/shard_map/ppermute | solution.py:36
  57.0 6.3 %collective-permute-done.15 = bf16[4,64,640]{2,1,0:T(8,128)(2,1)S(1)} collective-permute-done((bf16[4,64,640]{2,1,0:T(8,128)(2,1)S(1)}, bf16[4,64,640]{2,1,0:T(8,128)(2,1)S(1)}, u32[]{:S(2)}, u32[]{:S(2)}) %collective-permute-start.15) | collective-permute-done | bytes 327712 | tf_op jit(solution)/shard_map/ppermute | solution.py:36
  69.6 8.2 %collective-permute-done.13 = bf16[8,64,640]{2,1,0:T(8,128)(2,1)S(1)} collective-permute-done((bf16[8,64,640]{2,1,0:T(8,128)(2,1)S(1)}, bf16[8,64,640]{2,1,0:T(8,128)(2,1)S(1)}, u32[]{:S(2)}, u32[]{:S(2)}) %collective-permute-start.13) | collective-permute-done | bytes 655392 | tf_op jit(solution)/shard_map/ppermute | solution.py:36
  78.2 7.5 %attention_forward.2 = (f32[960,128]{1,0:T(8,128)S(1)}, f32[1,1920]{1,0:T(1,128)S(1)}) custom-call(s32[2]{0:T(128)S(1)} %pad_add_fusion.ids, s32[2,2,2]{2,1,0:T(2,128)S(1)} %copy-done.8, s32[2,2,16]{2,1,0:T(2,128)S(1)} %copy-done.9, bf16[16,64,640]{2,1,0:T(8,128)(2,1)S(1)} %get-tuple-element.442.first_ref, ...), custom_call_target="tpu_custom_call" | custom-call | flops 503316480 | bytes 2621440 | tf_op jit(solution)/shard_map/attention_forward/pallas_call | solution.py:438
  92.3 5.6 %attention_forward.3 = (f32[960,128]{1,0:T(8,128)S(1)}, f32[1,1920]{1,0:T(1,128)S(1)}) custom-call(s32[2]{0:T(128)S(1)} %pad_add_fusion.ids, s32[2,2,2]{2,1,0:T(2,128)S(1)} %copy-done.8, s32[2,2,16]{2,1,0:T(2,128)S(1)} %copy-done.9, bf16[16,64,640]{2,1,0:T(8,128)(2,1)S(1)} %pad_maximum_fusion.8.first_ref, ...), custom_call_target="tpu_custom_call" | custom-call | flops 503316480 | bytes 2621440 | tf_op jit(solution)/shard_map/attention_forward/pallas_call | solution.py:438
  99.5 20.7 %feed_forward.1 = (bf16[256,2560]{1,0:T(8,128)(2,1)}, bf16[2,256,2560]{2,1,0:T(8,128)(2,1)}, bf16[960,256]{1,0:T(8,128)(2,1)}, bf16[960,256]{1,0:T(8,128)(2,1)},...) custom-call(bf16[960,256]{1,0:T(8,128)(2,1)} %pad_maximum_fusion.29.x_ref, ...), custom_call_target="tpu_custom_call" | custom-call | flops 7549747200 | bytes 19660800 | tf_op jit(solution)/shard_map/feed_forward/pallas_call | solution.py:571
  127.0 5.2 %down_grad.1 = (bf16[240,1280]{1,0:T(8,128)(2,1)}, bf16[240,1280]{1,0:T(8,128)(2,1)}, bf16[240,1280]{1,0:T(8,128)(2,1)}, bf16[240,1280]{1,0:T(8,128)(2,1)}) custom-call(s32[2]{0:T(128)S(1)} %pad_add_fusion.ids, bf16[960,256]{1,0:T(8,128)(2,1)} %pad_maximum_fusion.30.cot_ref.refs_0_, bf16[960,256]{1,0:T(8,128)(2,1)} %copy-done.90, ...), custom_call_target="tpu_custom_call" | custom-call | flops 1258291200 | bytes 2457600 | tf_op jit(solution)/shard_map/down_grad/pallas_call | solution.py:653
  132.9 6.5 %inner_grad.2 = (bf16[120,2560]{1,0:T(8,128)(2,1)}, bf16[120,2560]{1,0:T(8,128)(2,1)}, bf16[120,2560]{1,0:T(8,128)(2,1)}, bf16[120,2560]{1,0:T(8,128)(2,1)}) custom-call(s32[2]{0:T(128)S(1)} %pad_add_fusion.ids, bf16[960,256]{1,0:T(8,128)(2,1)} %get-tuple-element.220.refs_0_, bf16[480,256]{1,0:T(8,128)(2,1)} %copy-done.50, ...), custom_call_target="tpu_custom_call" | custom-call | flops 1258291200 | bytes 2457600 | tf_op jit(solution)/shard_map/inner_grad/pallas_call | solution.py:653
  139.4 5.8 %collective-permute-start.21 = (bf16[240,1280]{1,0:T(8,128)(2,1)}, bf16[240,1280]{1,0:T(8,128)(2,1)}, u32[]{:S(2)}, u32[]{:S(2)}) collective-permute-start(bf16[240,1280]{1,0:T(8,128)(2,1)} %get-tuple-element.225), channel_id=1, source_target_pairs={{0,2},{2,0},{4,6},{6,4},{8,10},{10,8},{12,14},{14,12},{16,18},{18,... | collective-permute-start | bytes 1843208 | tf_op jit(solution)/shard_map/ppermute | solution.py:36
  150.4 6.5 %inner_grad.3 = (bf16[120,2560]{1,0:T(8,128)(2,1)}, bf16[120,2560]{1,0:T(8,128)(2,1)}, bf16[120,2560]{1,0:T(8,128)(2,1)}, bf16[120,2560]{1,0:T(8,128)(2,1)}) custom-call(s32[2]{0:T(128)S(1)} %pad_add_fusion.ids, bf16[960,256]{1,0:T(8,128)(2,1)} %get-tuple-element.220.refs_0_, bf16[480,256]{1,0:T(8,128)(2,1)} %copy-done.50, ...), custom_call_target="tpu_custom_call" | custom-call | flops 1258291200 | bytes 2457600 | tf_op jit(solution)/shard_map/inner_grad/pallas_call | solution.py:653
  163.7 9.8 %attention_backward.2 = (bf16[960,128]{1,0:T(8,128)(2,1)S(1)}, bf16[16,64,640]{2,1,0:T(8,128)(2,1)S(1)}, bf16[16,64,640]{2,1,0:T(8,128)(2,1)S(1)}) custom-call(s32[2]{0:T(128)S(1)} %pad_add_fusion.ids, s32[2,2,2]{2,1,0:T(2,128)S(1)} %copy-done.8, s32[2,2,16]{2,1,0:T(2,128)S(1)} %copy-done.9, bf16[16,64,640]{2,1,0:T(8,128)(2,1)S(1)} %get-tuple-element.442.first_ref, ...), custom_call_target="tpu_custom_call" | custom-call | flops 157286400 | bytes 655360 | tf_op jit(solution)/shard_map/attention_backward/pallas_call | solution.py:461
  175.3 4.5 %collective-permute-start.28 = (bf16[240,640]{1,0:T(8,128)(2,1)S(1)}, bf16[240,640]{1,0:T(8,128)(2,1)S(1)}, u32[]{:S(2)}, u32[]{:S(2)}) collective-permute-start(bf16[240,640]{1,0:T(8,128)(2,1)S(1)} %constant_dynamic-slice_fusion.17), channel_id=1, source_target_pairs={{0,4},{2,6},{4,0},{6,2},{8,12},{10,14},{12,8},{14,10},{16,20},{18,... | collective-permute-start | bytes 921608 | tf_op jit(solution)/shard_map/ppermute | solution.py:36
  180.4 6.0 %collective-permute-done.25 = bf16[120,2560]{1,0:T(8,128)(2,1)S(1)} collective-permute-done((bf16[120,2560]{1,0:T(8,128)(2,1)}, bf16[120,2560]{1,0:T(8,128)(2,1)S(1)}, u32[]{:S(2)}, u32[]{:S(2)}) %collective-permute-start.25) | collective-permute-done | bytes 614432 | tf_op jit(solution)/shard_map/ppermute | solution.py:36
  190.5 19.6 %attention_backward.3 = (bf16[960,128]{1,0:T(8,128)(2,1)S(1)}, bf16[16,64,640]{2,1,0:T(8,128)(2,1)S(1)}, bf16[16,64,640]{2,1,0:T(8,128)(2,1)S(1)}) custom-call(s32[2]{0:T(128)S(1)} %pad_add_fusion.ids, s32[2,2,2]{2,1,0:T(2,128)S(1)} %copy-done.8, s32[2,2,16]{2,1,0:T(2,128)S(1)} %copy-done.9, bf16[16,64,640]{2,1,0:T(8,128)(2,1)S(1)} %copy-done.1, ...), custom_call_target="tpu_custom_call" | custom-call | flops 157286400 | bytes 655360 | tf_op jit(solution)/shard_map/attention_backward/pallas_call | solution.py:461
  210.8 7.1 %collective-permute-start.36 = (bf16[8,64,640]{2,1,0:T(8,128)(2,1)S(1)}, bf16[8,64,640]{2,1,0:T(8,128)(2,1)S(1)}, u32[]{:S(2)}, u32[]{:S(2)}) collective-permute-start(bf16[8,64,640]{2,1,0:T(8,128)(2,1)S(1)} %slice.150), channel_id=1, source_target_pairs={{0,2},{2,0},{4,6},{6,4},{8,10},{10,8},{12,14},{14,12},{16,18},{18,... | collective-permute-start | bytes 1966088 | tf_op jit(solution)/shard_map/ppermute | solution.py:36
  219.9 13.3 %collective-permute-done.36 = bf16[8,64,640]{2,1,0:T(8,128)(2,1)S(1)} collective-permute-done((bf16[8,64,640]{2,1,0:T(8,128)(2,1)S(1)}, bf16[8,64,640]{2,1,0:T(8,128)(2,1)S(1)}, u32[]{:S(2)}, u32[]{:S(2)}) %collective-permute-start.36) | collective-permute-done | bytes 655392 | tf_op jit(solution)/shard_map/ppermute | solution.py:36
  249.4 5.2 %query_grad.1 = (bf16[240,960]{1,0:T(8,128)(2,1)}, bf16[240,960]{1,0:T(8,128)(2,1)}, bf16[240,960]{1,0:T(8,128)(2,1)}, bf16[240,960]{1,0:T(8,128)(2,1)}) custom-call(s32[2]{0:T(128)S(1)} %pad_add_fusion.ids, bf16[960,256]{1,0:T(8,128)(2,1)} %copy-done.14, bf16[480,256]{1,0:T(8,128)(2,1)} %copy-done.45, bf16[960,256]{1,0:T(8,128)(2,1)} %copy-done.31, ...), custom_call_target="tpu_custom_call" | custom-call | flops 943718400 | bytes 1843200 | tf_op jit(solution)/shard_map/query_grad/pallas_call | solution.py:653
  291.7 4.6 %collective-permute-done.59 = bf16[240,640]{1,0:T(8,128)(2,1)S(1)} collective-permute-done((bf16[240,640]{1,0:T(8,128)(2,1)S(1)}, bf16[240,640]{1,0:T(8,128)(2,1)S(1)}, u32[]{:S(2)}, u32[]{:S(2)}) %collective-permute-start.59) | collective-permute-done | bytes 307232 | tf_op jit(solution)/shard_map/ppermute | solution.py:36
  296.6 5.6 %collective-permute-start.63 = (bf16[240,640]{1,0:T(8,128)(2,1)S(1)}, bf16[240,640]{1,0:T(8,128)(2,1)S(1)}, u32[]{:S(2)}, u32[]{:S(2)}) collective-permute-start(bf16[240,640]{1,0:T(8,128)(2,1)S(1)} %get-tuple-element.406), channel_id=1, source_target_pairs={{0,2},{2,0},{4,6},{6,4},{8,10},{10,8},{12,14},{14,12},{16,18},{18,... | collective-permute-start | bytes 921608 | tf_op jit(solution)/shard_map/ppermute | solution.py:36
  304.5 8.8 %collective-permute-done.55 = bf16[2,128,640]{2,1,0:T(8,128)(2,1)S(1)} collective-permute-done((bf16[2,128,640]{2,1,0:T(8,128)(2,1)S(1)}, bf16[2,128,640]{2,1,0:T(8,128)(2,1)S(1)}, u32[]{:S(2)}, u32[]{:S(2)}) %collective-permute-start.55) | collective-permute-done | bytes 327712 | tf_op jit(solution)/shard_map/ppermute | solution.py:36
  315.8 4.9 %collective-permute-done.64 = bf16[1,128,640]{2,1,0:T(8,128)(2,1)S(1)} collective-permute-done((bf16[1,128,640]{2,1,0:T(8,128)(2,1)S(1)}, bf16[1,128,640]{2,1,0:T(8,128)(2,1)S(1)}, u32[]{:S(2)}, u32[]{:S(2)}) %collective-permute-start.64) | collective-permute-done | bytes 163872 | tf_op jit(solution)/shard_map/ppermute | solution.py:36
  362.4 7.6 %collective-permute-done.74 = bf16[240,768]{1,0:T(8,128)(2,1)S(1)} collective-permute-done((bf16[240,768]{1,0:T(8,128)(2,1)S(1)}, bf16[240,768]{1,0:T(8,128)(2,1)S(1)}, u32[]{:S(2)}, u32[]{:S(2)}) %collective-permute-start.74) | collective-permute-done | bytes 368672 | tf_op jit(solution)/shard_map/ppermute | solution.py:36
  392.3 7.5 %collective-permute-done.85 = bf16[120,768]{1,0:T(8,128)(2,1)S(1)} collective-permute-done((bf16[120,768]{1,0:T(8,128)(2,1)S(1)}, bf16[120,768]{1,0:T(8,128)(2,1)S(1)}, u32[]{:S(2)}, u32[]{:S(2)}) %collective-permute-start.85) | collective-permute-done | bytes 184352 | tf_op jit(solution)/shard_map/ppermute | solution.py:36
  402.2 6.5 %collective-permute-done.86 = bf16[120,768]{1,0:T(8,128)(2,1)S(1)} collective-permute-done((bf16[120,768]{1,0:T(8,128)(2,1)S(1)}, bf16[120,768]{1,0:T(8,128)(2,1)S(1)}, u32[]{:S(2)}, u32[]{:S(2)}) %collective-permute-start.86) | collective-permute-done | bytes 184352 | tf_op jit(solution)/shard_map/ppermute | solution.py:36
  (539 shorter events, 223.7 us)
Async XLA Ops:
  7.2 92.4 %all-gather.5.cloned.1.call-start = ((), (), s32[]{:S(2)}) async-start(), calls=%async_computation | async-start | bytes 2949120 | tf_op jit(solution)/shard_map/all_gather | solution.py:697
  7.9 91.6 %all-gather.7.cloned.1.call-start = ((), (), s32[]{:S(2)}) async-start(), calls=%async_computation.1 | async-start | bytes 7372800 | tf_op jit(solution)/shard_map/all_gather | solution.py:697
  8.7 90.9 %all-gather.9.cloned.1.call-start = ((), (), s32[]{:S(2)}) async-start(), calls=%async_computation.2 | async-start | bytes 7372800 | tf_op jit(solution)/shard_map/all_gather | solution.py:697
  9.4 90.1 %all-gather.11.cloned.1.call-start = ((), (), s32[]{:S(2)}) async-start(), calls=%async_computation.3 | async-start | bytes 7372800 | tf_op jit(solution)/shard_map/all_gather | solution.py:697
  54.7 23.0 %collective-permute-start.13 = (bf16[8,64,640]{2,1,0:T(8,128)(2,1)S(1)}, bf16[8,64,640]{2,1,0:T(8,128)(2,1)S(1)}, u32[]{:S(2)}, u32[]{:S(2)}) collective-permute-start(bf16[8,64,640]{2,1,0:T(8,128)(2,1)S(1)} %pad_maximum_fusion.18), channel_id=1, source_target_pairs={{0,4},{2,6},{4,0},{6,2},{8,12},{10,14},{12,8},{14,10},{16,20},{18,... | collective-permute-start | bytes 1966088 | tf_op jit(solution)/shard_map/ppermute | solution.py:36
  63.8 25.4 %collective-permute-start.17 = (bf16[8,64,640]{2,1,0:T(8,128)(2,1)S(1)}, bf16[8,64,640]{2,1,0:T(8,128)(2,1)S(1)}, u32[]{:S(2)}, u32[]{:S(2)}) collective-permute-start(bf16[8,64,640]{2,1,0:T(8,128)(2,1)S(1)} %pad_maximum_fusion.21), channel_id=1, source_target_pairs={{0,4},{2,6},{4,0},{6,2},{8,12},{10,14},{12,8},{14,10},{16,20},{18,... | collective-permute-start | bytes 1966088 | tf_op jit(solution)/shard_map/ppermute | solution.py:36
  65.6 23.7 %collective-permute-start.16 = (bf16[8,64,640]{2,1,0:T(8,128)(2,1)S(1)}, bf16[8,64,640]{2,1,0:T(8,128)(2,1)S(1)}, u32[]{:S(2)}, u32[]{:S(2)}) collective-permute-start(bf16[8,64,640]{2,1,0:T(8,128)(2,1)S(1)} %pad_maximum_fusion.20), channel_id=1, source_target_pairs={{0,2},{2,0},{4,6},{6,4},{8,10},{10,8},{12,14},{14,12},{16,18},{18,... | collective-permute-start | bytes 1966088 | tf_op jit(solution)/shard_map/ppermute | solution.py:36
  148.3 26.6 %collective-permute-start.23 = (bf16[120,2560]{1,0:T(8,128)(2,1)S(1)}, bf16[120,2560]{1,0:T(8,128)(2,1)S(1)}, u32[]{:S(2)}, u32[]{:S(2)}) collective-permute-start(bf16[120,2560]{1,0:T(8,128)(2,1)S(1)} %copy-done.89), channel_id=1, source_target_pairs={{0,2},{2,0},{4,6},{6,4},{8,10},{10,8},{12,14},{14,12},{16,18},{18,... | collective-permute-start | bytes 1843208 | tf_op jit(solution)/shard_map/ppermute | solution.py:36
  148.5 26.9 %collective-permute-start.24 = (bf16[120,2560]{1,0:T(8,128)(2,1)S(1)}, bf16[120,2560]{1,0:T(8,128)(2,1)S(1)}, u32[]{:S(2)}, u32[]{:S(2)}) collective-permute-start(bf16[120,2560]{1,0:T(8,128)(2,1)S(1)} %copy-done.88), channel_id=1, source_target_pairs={{0,4},{2,6},{4,0},{6,2},{8,12},{10,14},{12,8},{14,10},{16,20},{18,... | collective-permute-start | bytes 1843208 | tf_op jit(solution)/shard_map/ppermute | solution.py:36
  162.3 24.1 %collective-permute-start.25 = (bf16[120,2560]{1,0:T(8,128)(2,1)}, bf16[120,2560]{1,0:T(8,128)(2,1)S(1)}, u32[]{:S(2)}, u32[]{:S(2)}) collective-permute-start(bf16[120,2560]{1,0:T(8,128)(2,1)} %get-tuple-element.245), channel_id=1, source_target_pairs={{0,2},{2,0},{4,6},{6,4},{8,10},{10,8},{12,14},{14,12},{16,18},{18,... | collective-permute-start | bytes 1843208 | tf_op jit(solution)/shard_map/ppermute | solution.py:36
  162.4 26.1 %collective-permute-start.26 = (bf16[120,2560]{1,0:T(8,128)(2,1)}, bf16[120,2560]{1,0:T(8,128)(2,1)S(1)}, u32[]{:S(2)}, u32[]{:S(2)}) collective-permute-start(bf16[120,2560]{1,0:T(8,128)(2,1)} %get-tuple-element.246), channel_id=1, source_target_pairs={{0,4},{2,6},{4,0},{6,2},{8,12},{10,14},{12,8},{14,10},{16,20},{18,... | collective-permute-start | bytes 1843208 | tf_op jit(solution)/shard_map/ppermute | solution.py:36
  175.3 34.9 %collective-permute-start.28 = (bf16[240,640]{1,0:T(8,128)(2,1)S(1)}, bf16[240,640]{1,0:T(8,128)(2,1)S(1)}, u32[]{:S(2)}, u32[]{:S(2)}) collective-permute-start(bf16[240,640]{1,0:T(8,128)(2,1)S(1)} %constant_dynamic-slice_fusion.17), channel_id=1, source_target_pairs={{0,4},{2,6},{4,0},{6,2},{8,12},{10,14},{12,8},{14,10},{16,20},{18,... | collective-permute-start | bytes 921608 | tf_op jit(solution)/shard_map/ppermute | solution.py:36
  179.8 30.9 %collective-permute-start.29 = (bf16[240,640]{1,0:T(8,128)(2,1)S(1)}, bf16[240,640]{1,0:T(8,128)(2,1)S(1)}, u32[]{:S(2)}, u32[]{:S(2)}) collective-permute-start(bf16[240,640]{1,0:T(8,128)(2,1)S(1)} %constant_dynamic-slice_fusion.16), channel_id=1, source_target_pairs={{0,2},{2,0},{4,6},{6,4},{8,10},{10,8},{12,14},{14,12},{16,18},{18,... | collective-permute-start | bytes 921608 | tf_op jit(solution)/shard_map/ppermute | solution.py:36
  188.5 30.2 %collective-permute-start.30 = (bf16[120,1280]{1,0:T(8,128)(2,1)S(1)}, bf16[120,1280]{1,0:T(8,128)(2,1)S(1)}, u32[]{:S(2)}, u32[]{:S(2)}) collective-permute-start(bf16[120,1280]{1,0:T(8,128)(2,1)S(1)} %constant_dynamic-slice_fusion.15), channel_id=1, source_target_pairs={{0,4},{2,6},{4,0},{6,2},{8,12},{10,14},{12,8},{14,10},{16,20},{18,... | collective-permute-start | bytes 921608 | tf_op jit(solution)/shard_map/ppermute | solution.py:36
  188.5 30.2 %collective-permute-start.31 = (bf16[120,1280]{1,0:T(8,128)(2,1)S(1)}, bf16[120,1280]{1,0:T(8,128)(2,1)S(1)}, u32[]{:S(2)}, u32[]{:S(2)}) collective-permute-start(bf16[120,1280]{1,0:T(8,128)(2,1)S(1)} %constant_dynamic-slice_fusion.14), channel_id=1, source_target_pairs={{0,2},{2,0},{4,6},{6,4},{8,10},{10,8},{12,14},{14,12},{16,18},{18,... | collective-permute-start | bytes 921608 | tf_op jit(solution)/shard_map/ppermute | solution.py:36
  188.6 29.3 %collective-permute-start.27 = (bf16[256,960]{1,0:T(8,128)(2,1)S(1)}, bf16[256,960]{1,0:T(8,128)(2,1)S(1)}, u32[]{:S(2)}, u32[]{:S(2)}) collective-permute-start(bf16[256,960]{1,0:T(8,128)(2,1)S(1)} %copy-done.70), channel_id=1, source_target_pairs={{0,1},{1,0},{2,3},{3,2},{4,5},{5,4},{6,7},{7,6},{8,9},{9,8},{10,11... | collective-permute-start | bytes 1474568 | tf_op jit(solution)/shard_map/ppermute | solution.py:40
  210.2 38.5 %collective-permute-start.46 = (bf16[480,256]{1,0:T(8,128)(2,1)S(1)}, bf16[480,256]{1,0:T(8,128)(2,1)S(1)}, u32[]{:S(2)}, u32[]{:S(2)}) collective-permute-start(bf16[480,256]{1,0:T(8,128)(2,1)S(1)} %fusion.14), channel_id=1, source_target_pairs={{0,1},{1,0},{2,3},{3,2},{4,5},{5,4},{6,7},{7,6},{8,9},{9,8},{10,11... | collective-permute-start | bytes 737288 | tf_op jit(solution)/shard_map/ppermute | solution.py:40
  210.8 22.4 %collective-permute-start.36 = (bf16[8,64,640]{2,1,0:T(8,128)(2,1)S(1)}, bf16[8,64,640]{2,1,0:T(8,128)(2,1)S(1)}, u32[]{:S(2)}, u32[]{:S(2)}) collective-permute-start(bf16[8,64,640]{2,1,0:T(8,128)(2,1)S(1)} %slice.150), channel_id=1, source_target_pairs={{0,2},{2,0},{4,6},{6,4},{8,10},{10,8},{12,14},{14,12},{16,18},{18,... | collective-permute-start | bytes 1966088 | tf_op jit(solution)/shard_map/ppermute | solution.py:36
  290.7 22.6 %collective-permute-start.55 = (bf16[2,128,640]{2,1,0:T(8,128)(2,1)S(1)}, bf16[2,128,640]{2,1,0:T(8,128)(2,1)S(1)}, u32[]{:S(2)}, u32[]{:S(2)}) collective-permute-start(bf16[2,128,640]{2,1,0:T(8,128)(2,1)S(1)} %fusion.12), channel_id=1, source_target_pairs={{0,8},{2,10},{4,12},{6,14},{8,0},{10,2},{12,4},{14,6},{16,24},{18,... | collective-permute-start | bytes 983048 | tf_op jit(solution)/shard_map/ppermute | solution.py:36
  296.4 29.4 %collective-permute-start.69 = (bf16[120,960]{1,0:T(8,128)(2,1)S(1)}, bf16[120,960]{1,0:T(8,128)(2,1)S(1)}, u32[]{:S(2)}, u32[]{:S(2)}) collective-permute-start(bf16[120,960]{1,0:T(8,128)(2,1)S(1)} %broadcast_select_fusion.31), channel_id=1, source_target_pairs={{0,8},{2,10},{4,12},{6,14},{8,0},{10,2},{12,4},{14,6},{16,24},{18,... | collective-permute-start | bytes 691208 | tf_op jit(solution)/shard_map/ppermute | solution.py:36
  296.6 25.8 %collective-permute-start.63 = (bf16[240,640]{1,0:T(8,128)(2,1)S(1)}, bf16[240,640]{1,0:T(8,128)(2,1)S(1)}, u32[]{:S(2)}, u32[]{:S(2)}) collective-permute-start(bf16[240,640]{1,0:T(8,128)(2,1)S(1)} %get-tuple-element.406), channel_id=1, source_target_pairs={{0,2},{2,0},{4,6},{6,4},{8,10},{10,8},{12,14},{14,12},{16,18},{18,... | collective-permute-start | bytes 921608 | tf_op jit(solution)/shard_map/ppermute | solution.py:36
  334.6 41.8 %collective-permute-start.80 = (bf16[120,1280]{1,0:T(8,128)(2,1)}, bf16[120,1280]{1,0:T(8,128)(2,1)}, u32[]{:S(2)}, u32[]{:S(2)}) collective-permute-start(bf16[120,1280]{1,0:T(8,128)(2,1)} %get-tuple-element.394), channel_id=1, source_target_pairs={{0,2},{2,0},{4,6},{6,4},{8,10},{10,8},{12,14},{14,12},{16,18},{18,... | collective-permute-start | bytes 921608 | tf_op jit(solution)/shard_map/ppermute | solution.py:36
  385.1 23.6 %collective-permute-start.87 = (bf16[120,2560]{1,0:T(8,128)(2,1)S(1)}, bf16[120,2560]{1,0:T(8,128)(2,1)S(1)}, u32[]{:S(2)}, u32[]{:S(2)}) collective-permute-start(bf16[120,2560]{1,0:T(8,128)(2,1)S(1)} %pad_maximum_fusion.26), channel_id=1, source_target_pairs={{0,2},{2,0},{4,6},{6,4},{8,10},{10,8},{12,14},{14,12},{16,18},{18,... | collective-permute-start | bytes 1843208 | tf_op jit(solution)/shard_map/ppermute | solution.py:36
  385.5 23.2 %collective-permute-start.88 = (bf16[120,2560]{1,0:T(8,128)(2,1)S(1)}, bf16[120,2560]{1,0:T(8,128)(2,1)S(1)}, u32[]{:S(2)}, u32[]{:S(2)}) collective-permute-start(bf16[120,2560]{1,0:T(8,128)(2,1)S(1)} %pad_maximum_fusion.27), channel_id=1, source_target_pairs={{0,4},{2,6},{4,0},{6,2},{8,12},{10,14},{12,8},{14,10},{16,20},{18,... | collective-permute-start | bytes 1843208 | tf_op jit(solution)/shard_map/ppermute | solution.py:36
  (165 other events, 1503.2 us)
Sparse Core Ops, SparseCore 0:
  9.6 13.0 all-gather.4
  24.2 15.8 all-gather.6
  41.7 16.5 all-gather.8
  59.7 15.1 all-gather.10

commit v4 on v3

--- a/solution.py
+++ b/solution.py
@@ -93,27 +93,17 @@
     def __init__(self, first, second):
         self.halves = [first, second]
         self.bits = (0, 1)
-        self.stages = [None, None] + high_bits()
-        self.held = None
+        self.stages = [None, None]
 
     def operands(self):
-        if self.stages[0] is None:
-            count = self.halves[0].shape[0] // 2
-            return [half[count:] for half in self.halves], self.bits
-        if self.held is None:
-            self.held = jnp.concatenate(self.halves, axis=1)
-        count = self.held.shape[0] // 2
-        return [self.held[count:]], [self.stages[0]]
+        count = self.halves[0].shape[0] // 2
+        return [half[count:] for half in self.halves], self.bits
 
     def absorb(self, arrived):
-        def add(blocks, sums):
-            return add_low(blocks[: blocks.shape[0] // 2], sums)
-
-        if self.stages.pop(0) is None:
-            self.halves = [add(half, a) for half, a in zip(self.halves, arrived)]
-            self.bits = (1, 0)
-        else:
-            self.held = add(self.held, arrived[0])
+        self.stages.pop(0)
+        count = self.halves[0].shape[0] // 2
+        self.halves = [add_low(half[:count], a) for half, a in zip(self.halves, arrived)]
+        self.bits = (1, 0)
 
 
 def cut(value, bit, dim):
@@ -171,15 +161,58 @@
     def absorb(self, arrived):
         stage = self.stages.pop(0)
         if isinstance(stage, tuple):
-            kind, dim = (bf16, self.dims[0]) if self.stages else (f32, 0)
-            self.pair = [
-                in_order(b, v.astype(kind), a.astype(kind), dim)
-                for v, a, b in zip(self.pair, arrived, stage)
-            ]
+            parts = [by_bit(b, v, a) for v, a, b in zip(self.pair, arrived, stage)]
+            if self.stages:
+                self.pair = [jnp.concatenate(p, axis=self.dims[0]) for p in parts]
+            else:
+                self.quarters = [q for p in parts for q in p]
         elif stage == 2:
             self.pair = list(by_bit(stage, self.held, arrived[0]))
         else:
             self.held = in_order(stage, self.held, arrived[0], self.dims[1])
+
+
+class GatherHigh:
+    def __init__(self, value):
+        self.held = value[None]
+        self.stages = high_bits()[::-1]
+
+    def operands(self):
+        return [self.held], [self.stages[0]]
+
+    def absorb(self, arrived):
+        self.stages.pop(0)
+        self.held = jnp.concatenate([self.held, arrived[0]], axis=0)
+
+
+class ScatterHigh:
+    def __init__(self, held):
+        self.held = held
+        self.stages = high_bits()
+
+    def operands(self):
+        return [self.held[self.held.shape[0] // 2 :]], [self.stages[0]]
+
+    def absorb(self, arrived):
+        self.stages.pop(0)
+        self.held = add_low(self.held[: self.held.shape[0] // 2], arrived[0])
+
+
+class SumVector:
+    def __init__(self, value):
+        self.value = value
+        self.stages = list(range(lax.axis_size("ctx").bit_length() - 1))
+
+    def operands(self):
+        return [self.value], [self.stages[0]]
+
+    def absorb(self, arrived):
+        self.stages.pop(0)
+        self.value = self.value + arrived[0]
+
+
+def rows_of(quarters, columns=slice(None)):
+    return jnp.concatenate([q[:, columns] for q in quarters], axis=0).astype(f32)
 
 
 class Solo:
@@ -244,7 +277,7 @@
 
 
 def key_tile(first_ref, second_ref, places, unit):
-    lanes = pl.ds((unit // 2) * LANES, LANES)
+    lanes = pl.ds(pl.multiple_of((unit // 2) * LANES, LANES), LANES)
     parts = []
     for first, second in places:
         parts += [first_ref[first, :, lanes], second_ref[second, :, lanes]]
@@ -305,16 +338,28 @@
     return jnp.concatenate(masks, axis=0)
 
 
+def lanes_at(start, size=LANES):
+    return pl.ds(pl.multiple_of(start, LANES), size)
+
+
+def spread_heads(source_ref, pad_ref, unit, group):
+    parts = [
+        source_ref[pl.ds(pl.multiple_of((group * REP + r) * HD, HD), HD), :] for r in range(REP)
+    ]
+    row = pl.multiple_of((unit % 2) * HD, HD)
+    pad_ref[pl.ds(row, HD), lanes_at(unit * GCOLS, GCOLS)] = jnp.concatenate(parts, axis=1)
+
+
 def forward_kernel(
-    far, bits, which, ids, lengths, slots, first_ref, second_ref, query_ref, out_ref, lse_ref, pad_ref
+    far, bits, which, ids, lengths, slots, first_ref, second_ref, query_ref, out_ref, lse_ref, pad_ref, half_ref
 ):
     count, places = seen_blocks(bits, which, ids, lengths, slots)
-    queries = query_ref[...]
-    for group in range(KVH):
-        pad_ref[:, group * GCOLS : (group + 1) * GCOLS] = heads_t(queries, group, group)
-
-    for group in range(KVH):
-        columns = slice(group * GCOLS, (group + 1) * GCOLS)
+    pad_ref[...] = jnp.zeros_like(pad_ref)
+
+    @pl.loop(0, KVH)
+    def _(group):
+        spread_heads(query_ref, pad_ref, group, group)
+        columns = lanes_at(group * GCOLS, GCOLS)
         value_unit = KVH + group
 
         def step(pair, carried):
@@ -329,20 +374,20 @@
             weights = jnp.exp(scores - new_high)
             fade = jnp.exp(high - new_high)
             total = total * fade + jnp.sum(weights, axis=0, keepdims=True)
-            values_t = half_rows(values.T, value_unit)
-            acc = acc * fade + dot(values_t, weights.astype(bf16), 1, 0)
+            acc = acc * fade + dot(values.T, weights.astype(bf16), 1, 0)
             return (new_high, total, acc)
 
         start = (
             jnp.full((1, GCOLS), NEG, f32),
             jnp.zeros((1, GCOLS), f32),
-            jnp.zeros((HD, GCOLS), f32),
+            jnp.zeros((LANES, GCOLS), f32),
         )
         high, total, acc = lax.fori_loop(0, (count + 1) // 2, step, start)
-        acc = acc / total
+        half_ref[...] = acc / total
+        row = pl.multiple_of((value_unit % 2) * HD, HD)
         for r in range(REP):
-            head = group * REP + r
-            out_ref[head * HD : (head + 1) * HD, :] = acc[:, r * BLK : (r + 1) * BLK]
+            head_rows = pl.ds(pl.multiple_of((group * REP + r) * HD, HD), HD)
+            out_ref[head_rows, :] = half_ref[pl.ds(row, HD), r * BLK : (r + 1) * BLK]
         lse_ref[:, columns] = high + jnp.log(total)
 
 
@@ -445,7 +490,7 @@
         ),
         in_specs=[SMEM_SPEC] * 3 + [VMEM_SPEC] * 3,
         out_specs=(VMEM_SPEC,) * 2,
-        scratch_shapes=[pltpu.VMEM((LANES, HEADS * BLK), bf16)],
+        scratch_shapes=[pltpu.VMEM((LANES, HEADS * BLK), bf16), pltpu.VMEM((LANES, GCOLS), f32)],
         compiler_params=pltpu.CompilerParams(vmem_limit_bytes=8 << 20),
         cost_estimate=pl.CostEstimate(
             flops=4 * HEADS * HD * BLK * BLK * 8,
@@ -561,7 +606,7 @@
 def feed_forward(x_t, cot_t, attended_t, out_w, gain, gate_w, up_w, down_w_t):
     width, rows = x_t.shape
     inner = gate_w.shape[1]
-    tile = 256
+    tile = 512
 
     def fixed(shape):
         return pl.BlockSpec(shape, lambda i: (0,) * len(shape))
@@ -600,7 +645,7 @@
             pltpu.VMEM((rows, width), f32),
             pltpu.VMEM((rows, width), f32),
         ],
-        compiler_params=pltpu.CompilerParams(vmem_limit_bytes=24 << 20),
+        compiler_params=pltpu.CompilerParams(vmem_limit_bytes=32 << 20),
         cost_estimate=pl.CostEstimate(
             flops=12 * rows * width * inner,
             bytes_accessed=8 * width * inner,
@@ -669,6 +714,48 @@
     )(ids, *in_hbm([o for group in operands for o in group]))
 
 
+def keyval_grad_kernel(left, own, other, out, total):
+    step = pl.program_id(0)
+    tokens = own.shape[1]
+    value = dot(left[0, :, :tokens], own[0], 1, 0) + dot(left[0, :, tokens:], other[0], 1, 0)
+
+    @pl.when(step == 0)
+    def _():
+        total[...] = value
+
+    @pl.when(step != 0)
+    def _():
+        total[...] += value
+
+    @pl.when(step == pl.num_programs(0) - 1)
+    def _():
+        out[...] = total[...].astype(bf16)
+
+
+def keyval_grad(left, own, other):
+    count, rows, _ = left.shape
+    columns = own.shape[2]
+
+    def block(value):
+        return pl.BlockSpec((1,) + value.shape[1:], lambda i: (i, 0, 0))
+
+    return pl.pallas_call(
+        keyval_grad_kernel,
+        grid=(count,),
+        in_specs=[block(left), block(own), block(other)],
+        out_specs=pl.BlockSpec((rows, columns), lambda i: (0, 0)),
+        out_shape=jax.ShapeDtypeStruct((rows, columns), bf16),
+        scratch_shapes=[pltpu.VMEM((rows, columns), f32)],
+        compiler_params=pltpu.CompilerParams(vmem_limit_bytes=12 << 20),
+        cost_estimate=pl.CostEstimate(
+            flops=2 * left.size * columns,
+            bytes_accessed=2 * (left.size + 2 * own.size),
+            transcendentals=0,
+        ),
+        name="keyval_grad",
+    )(left, own, other)
+
+
 def per_device(
     inputs,
     gain_attn,
@@ -686,6 +773,7 @@
     micro = inputs.shape[0]
     shard = lax.axis_index("fsdp")
     is_low = shard == 0
+    ids = jnp.stack([lax.axis_index("ctx"), shard]).astype(jnp.int32)
     rounds = Rounds()
 
     def joined(part, other):
@@ -725,32 +813,36 @@
     query_other, gain_other = swap_fsdp(w_query), swap_fsdp(gain_mlp)
     cot_t = tokens_last(cotangent)
     (query_other, gain_other, cot_t) = rounds.end(gathers, query_other, gain_other, cot_t)
+    half = normed_t.shape[0] // 2
+    normed_mine = lax.dynamic_slice_in_dim(normed_t, shard * half, half, 0)
     for step in range(len(gathers[0].stages)):
         rounds.begin(*[g for g in gathers if len(g.stages) > 2 or g is gathers[0]])
         if step == 0:
+            normed_other = swap_fsdp(theirs(normed_t, 0))
             query_full = joined(w_query, query_other)
             mlp_gain = joined(gain_mlp, gain_other).astype(f32)[None]
+            (normed_other, mlp_gain) = rounds.end(list(rounds.flying), normed_other, mlp_gain)
+        elif step == 1:
+            column = GatherHigh(jnp.concatenate([normed_mine, normed_other], axis=1))
+            rounds.begin(column)
+            cot_other = swap_fsdp(cot_t)
             queries_t = dot(query_full, normed_t, 0, 0).astype(bf16)
-            normed_theirs = theirs(normed_t, 0)
-            (queries_t, mlp_gain, normed_theirs) = rounds.end(
-                list(rounds.flying), queries_t, mlp_gain, normed_theirs
+            (cot_other, queries_t) = rounds.end(
+                [j for j in rounds.flying if j is not column], cot_other, queries_t
             )
-        elif step == 1:
-            normed_other = swap_fsdp(normed_theirs)
-            cot_other = swap_fsdp(cot_t)
-            (normed_other, cot_other) = rounds.end(list(rounds.flying), normed_other, cot_other)
         else:
-            rounds.end(list(rounds.flying))
+            rounds.end([j for j in rounds.flying if j is not column])
     queries = [queries_t[:, m * BLK : (m + 1) * BLK] for m in range(micro)]
-    ids = jnp.stack([lax.axis_index("ctx"), shard]).astype(jnp.int32)
     tables = (ids, seq_blocks, block_slots)
 
     rounds.begin(gathers[1])
-    rounds.end(gathers[1:])
-    rounds.begin(gathers[1])
+    rounds.end([gathers[1], column])
+    rounds.begin(gathers[1], column)
     first = attention_forward(0, tables, *gathers[0].halves, queries[0])
     first = rounds.end(gathers[1:], *first)
     second = attention_forward(1, tables, *gathers[1].halves, queries[1])
+    second = rounds.end([column], *second)
+    rounds.run(column, 0)
     outs, lses = zip(first, second)
     attended_t = jnp.concatenate(outs, axis=1).astype(bf16)
 
@@ -773,7 +865,6 @@
 
     part = hidden_other.shape[1]
     width = cot_t.shape[0]
-    half = width // 2
     tokens, inner = hidden.shape
     near = pl.BlockSpec((tokens, part // 2), lambda i, ids: (0, ids[1] * 2 + i))
     far = pl.BlockSpec((tokens, part // 2), lambda i, ids: (0, i))
@@ -791,22 +882,6 @@
         (1, 0),
     )
 
-    def inner_job(n):
-        spec = pl.BlockSpec((1, tokens, inner // 5), lambda i, ids: (n, 0, i))
-        return Reduce(
-            weight_grad(
-                "inner_grad",
-                ids,
-                ((True, False),),
-                ((normed_mlp_t, mlp_other, grad_inner, inner_other),),
-                ((spec, spec),),
-                ((0, 0, half // 2, 0), (0, half // 2, half // 2, 1)),
-                5,
-                inner,
-            ),
-            (1, 1),
-        )
-
     def attention_back(m):
         return attention_backward(
             m,
@@ -818,49 +893,58 @@
             lses[m],
         )
 
-    gate_job = inner_job(0)
-    rounds.prepare(down_job, gate_job)
-    (grad_inner, grad_attended_t, grad_mixed_low) = rounds.end(
-        [], grad_inner, grad_attended_t, grad_mixed_low
-    )
-
-    rounds.begin(down_job, gate_job)
-    up_job = inner_job(1)
-    rounds.prepare(up_job)
+    rounds.prepare(down_job)
+    (grad_inner, inner_other, grad_attended_t, grad_mixed_low, normed_mlp_t, mlp_other) = rounds.end(
+        [], grad_inner, inner_other, grad_attended_t, grad_mixed_low, normed_mlp_t, mlp_other
+    )
+
+    rounds.begin(down_job)
+    spec = pl.BlockSpec((1, tokens, inner // 5), lambda i, ids: (i // 5, 0, i % 5))
+    inner_job = Reduce(
+        weight_grad(
+            "inner_grad",
+            ids,
+            ((True, False),),
+            ((normed_mlp_t, mlp_other, grad_inner, inner_other),),
+            ((spec, spec),),
+            ((0, 0, half // 2, 0), (0, half // 2, half // 2, 1)),
+            10,
+            2 * inner,
+        ),
+        (1, 1),
+    )
+    rounds.prepare(inner_job)
+    (grad_attended_t, grad_mixed_low) = rounds.end([], grad_attended_t, grad_mixed_low)
+
+    rounds.begin(inner_job)
     (grad_attended_t, grad_mixed_low) = rounds.end([down_job], grad_attended_t, grad_mixed_low)
 
-    rounds.begin(up_job)
-    rounds.prepare(down_job)
     back_first = attention_back(0)
+    key_first = ScatterBlocks(*back_first[1:])
+    rounds.prepare(down_job, key_first)
     (grad_attended_t, grad_mixed_low, *back_first) = rounds.end(
-        [gate_job], grad_attended_t, grad_mixed_low, *back_first
-    )
-
-    rounds.begin(down_job)
-    key_first = ScatterBlocks(*back_first[1:])
-    rounds.prepare(gate_job, key_first)
-    (grad_attended_t, grad_mixed_low) = rounds.end([up_job], grad_attended_t, grad_mixed_low)
-
-    rounds.begin(gate_job, key_first)
-    rounds.prepare(up_job)
+        [inner_job], grad_attended_t, grad_mixed_low, *back_first
+    )
+    key_first.halves = back_first[1:]
+
+    rounds.begin(down_job, key_first)
+    rounds.prepare(inner_job)
     back_second = attention_back(1)
-    mixed_other = swap_fsdp(grad_mixed_low)
-    (mixed_other, *back_second) = rounds.end([down_job], mixed_other, *back_second)
-
-    rounds.begin(up_job, down_job)
     key_second = ScatterBlocks(*back_second[1:])
     rounds.prepare(key_second)
+    mixed_other = swap_fsdp(grad_mixed_low)
+    (mixed_other, *back_second) = rounds.end([down_job, key_first], mixed_other, *back_second)
+    key_second.halves = back_second[1:]
+
+    rounds.begin(inner_job, key_second, down_job)
+    rounds.prepare(key_first)
     grad_queries_t = jnp.concatenate([back_first[0], back_second[0]], axis=1)
-    (grad_queries_t,) = rounds.end([gate_job], grad_queries_t)
-
-    rounds.begin(key_second, gate_job)
     queries_other = swap_fsdp(grad_queries_t)
-    (queries_other,) = rounds.end([key_first, down_job], queries_other)
-
-    rounds.begin(down_job)
-    rounds.prepare(key_first)
-    rounds.end([up_job, gate_job])
-    rounds.begin(key_first, up_job, gate_job)
+    (queries_other, grad_queries_t) = rounds.end(
+        [inner_job, down_job], queries_other, grad_queries_t
+    )
+
+    rounds.begin(down_job, inner_job, key_first)
     flat = pl.BlockSpec((width, tokens), lambda i, ids: (0, 0))
     flat_half = pl.BlockSpec((tokens, width), lambda i, ids: (0, 0))
     query_job = Reduce(
@@ -880,68 +964,61 @@
         (0, 1),
     )
     rounds.prepare(query_job)
-    rounds.end([key_second, down_job])
+    (grad_queries_t,) = rounds.end([key_second, down_job], grad_queries_t)
     rounds.run(down_job, 0)
     down_spread = Spread(down_job)
 
-    rounds.begin(down_spread, query_job)
+    rounds.begin(query_job, down_spread)
     rounds.prepare(key_second)
-    (grad_queries_t,) = rounds.end([key_first, up_job, gate_job], grad_queries_t)
-    rounds.run(gate_job, 0)
-    gate_spread = Spread(gate_job)
-
-    rounds.begin(key_second, key_first, up_job, gate_spread)
+    rounds.end([key_first, down_spread, inner_job])
+    rounds.run(down_spread, 3)
+
+    rounds.begin(key_second, down_spread, inner_job)
     grad_normed_t = dot(query_full, grad_queries_t, 1, 0)
-    (grad_normed_t,) = rounds.end([down_spread, query_job], grad_normed_t)
-    rounds.run(down_spread, 3)
-
-    rounds.begin(down_spread, query_job)
-    rounds.end([key_second, key_first, up_job, gate_spread])
-    rounds.run(up_job, 0)
-    up_spread = Spread(up_job)
-    rounds.run(gate_spread, 3)
-
-    rounds.begin(key_second, key_first, up_spread, gate_spread)
-    rounds.end([down_spread, query_job])
-
-    rounds.begin(down_spread)
-    rounds.end([key_second, key_first, up_spread, gate_spread])
-    rounds.run(key_first, 0)
-    rounds.run(up_spread, 3)
-
-    rounds.begin(key_second, gate_spread, up_spread, query_job)
-    rounds.end([down_spread, key_second])
-    rounds.run(key_second, 0)
-    grad_keyvals = jnp.concatenate([key_first.held[0], key_second.held[0]], axis=0)
-
-    rounds.begin(down_spread)
-    keyvals_other = swap_fsdp(grad_keyvals)
+    (grad_normed_t,) = rounds.end(
+        [key_second, query_job, down_spread, inner_job], grad_normed_t
+    )
+    rounds.run(inner_job, 0)
+    inner_spread = Spread(inner_job)
+
+    rounds.begin(down_spread, query_job, inner_spread)
+    parts = [part for job in (key_first, key_second) for part in job.halves]
+    key_column = jnp.concatenate(parts, axis=1)
+    key_other = swap_fsdp(key_column)
+    last_job = Solo(keyval_grad(column.held, key_column, key_other))
+    rounds.prepare(last_job)
+    (key_column,) = rounds.end([down_spread, query_job, inner_spread], key_column)
+    rounds.run(inner_spread, 3)
+    key_job = ScatterHigh(key_column)
+
+    rounds.begin(last_job, down_spread, inner_spread, query_job)
+    rounds.end([last_job, down_spread, inner_spread, query_job])
+
+    rounds.begin(last_job, inner_spread, key_job, query_job)
+    down_sum = rows_of(down_spread.quarters)
+    (down_sum,) = rounds.end([last_job, inner_spread, key_job, query_job], down_sum)
+    rounds.run(query_job, 0)
+    rounds.run(key_job, 1)
+    query_spread = Spread(query_job)
+
+    rounds.begin(inner_spread, last_job, key_job, query_spread)
+    rounds.end([last_job, key_job, query_spread])
+    rounds.run(last_job, 3)
+    rounds.run(query_spread, 3)
+
+    rounds.begin(last_job, query_spread)
+    grad_keyvals = key_job.held[0]
     grad_normed_t = grad_normed_t + dot(keyval_full, grad_keyvals, 1, 1)
-    (grad_normed_t, keyvals_other) = rounds.end(
-        [gate_spread, up_spread, query_job], grad_normed_t, keyvals_other
-    )
-
-    rounds.begin(gate_spread, query_job)
     attn_gain_grad = jnp.sum(grad_normed_t * in_t * inverse_attn, axis=1)
-    gains = jnp.stack([attn_gain_grad, mlp_gain_grad[0]], axis=1)
-    gains_theirs = theirs(gains, 0)
-    normed_mine = lax.dynamic_slice_in_dim(normed_t, shard * half, half, 0)
-    keyval_grad = dot(normed_mine, grad_keyvals, 1, 0) + dot(normed_other, keyvals_other, 1, 0)
-    gains_mine = lax.dynamic_slice_in_dim(gains, shard * half, half, 0) + swap_fsdp(gains_theirs)
-    pad = jnp.zeros((half, LANES - 2), bf16)
-    last = jnp.concatenate([keyval_grad.astype(bf16), gains_mine.astype(bf16), pad], axis=1)
-    last_job = Solo(last)
-    rounds.prepare(last_job)
-    (grad_normed_t,) = rounds.end([down_spread, query_job], grad_normed_t)
-    rounds.run(query_job, 0)
-    query_spread = Spread(query_job)
-
-    rounds.begin(last_job, up_spread, query_spread)
-    down_sum = jnp.concatenate(down_spread.pair, axis=0)
-    (down_sum,) = rounds.end([last_job, gate_spread, query_spread], down_sum)
-    rounds.run(query_spread, 3)
-
-    rounds.begin(last_job, query_spread)
+    gains = jnp.stack([attn_gain_grad, mlp_gain_grad[0]])
+    gains_other = swap_fsdp(theirs(gains, 1))
+    gains_mine = lax.dynamic_slice_in_dim(gains, shard * half, half, 1)
+    (grad_normed_t, gains_mine, gains_other) = rounds.end(
+        [last_job, query_spread], grad_normed_t, gains_mine, gains_other
+    )
+    gain_job = SumVector((gains_mine + gains_other).reshape(-1))
+
+    rounds.begin(last_job, query_spread, gain_job)
     scaled = grad_normed_t * attn_gain
     cubed = inverse_attn * inverse_attn * inverse_attn
     input_grad_t = (
@@ -949,33 +1026,32 @@
         + inverse_attn * scaled
         - in_t * cubed * jnp.mean(scaled * in_t, axis=0, keepdims=True)
     )
-    (input_grad_t,) = rounds.end([last_job, up_spread, query_spread], input_grad_t)
-
-    rounds.begin(last_job, up_spread, query_spread)
-    gate_sum = jnp.concatenate(gate_spread.pair, axis=0)
-    (gate_sum,) = rounds.end([last_job, query_spread], gate_sum)
-    rounds.begin(last_job, query_spread)
-    rounds.end([last_job])
-    rounds.run(last_job, 2)
-    rounds.begin(last_job)
-    rounds.end([last_job, up_spread])
-    rounds.begin(last_job)
-    up_sum = jnp.concatenate(up_spread.pair, axis=0)
-    (up_sum,) = rounds.end([last_job, query_spread], up_sum)
+    (input_grad_t,) = rounds.end(
+        [inner_spread, last_job, query_spread, gain_job], input_grad_t
+    )
+
+    rounds.begin(last_job, query_spread, gain_job)
+    gate_sum = rows_of(inner_spread.quarters, slice(0, inner))
+    (gate_sum,) = rounds.end([gain_job], gate_sum)
+    rounds.begin(gain_job)
+    up_sum = rows_of(inner_spread.quarters, slice(inner, None))
+    (up_sum,) = rounds.end([last_job, gain_job], up_sum)
+    rounds.begin(gain_job)
+    rounds.end([query_spread, gain_job])
+    rounds.run(gain_job, 0)
 
     def by_token(value_t):
         parts = [value_t[:, m * BLK : (m + 1) * BLK].T[None] for m in range(micro)]
         return jnp.stack(parts)
 
-    columns = keyval_grad.shape[1]
     return (
         by_token(layer_out_t),
         by_token(input_grad_t),
-        last_job.value[:, columns],
-        query_spread.pair[0],
-        last_job.value[:, :columns],
-        query_spread.pair[1],
-        last_job.value[:, columns + 1],
+        gain_job.value[:half],
+        rows_of(query_spread.quarters[:2]),
+        last_job.value,
+        rows_of(query_spread.quarters[2:]),
+        gain_job.value[half:],
         gate_sum,
         up_sum,
         down_sum.T,

time: 434 us -> 423 us (0.975)
  starting transfers between devices: 105 us -> 86.6 us
  waiting for transfers between devices: 155 us -> 172 us
  Pallas kernels: 86.7 us -> 77.4 us
    ppermute x78 -> x70, waiting for transfers between devices: 146 us -> 165 us  [flip_ctx(): return lax.ppermute(value, 'ctx', [(i, i ^ 1 << bit) for i in range(size)])]
    ppermute x78 -> x70, starting transfers between devices: 102 us -> 84 us  [flip_ctx(): return lax.ppermute(value, 'ctx', [(i, i ^ 1 << bit) for i in range(size)])]
    convert_element_type x1 -> x5, other arithmetic: 1.09 us -> 11.4 us  [rows_of(): jnp.concatenate([q[:, columns] for q in quarters], axis=0).astype(f32)]
    pallas_call x2, Pallas kernels: 29.4 us -> 19.8 us  [attention_backward(): pl.pallas_call(functools.partial(backward_kernel, steps > WINDOW // BLK,...]
    concatenate x16 -> x5, other arithmetic: 7.77 us -> 2.14 us  [in_order(): return jnp.concatenate(by_bit(bit, mine, arrived), axis=dim)]
    concatenate x8 -> x7, other arithmetic: 9.15 us -> 4.34 us  [the longest x6 4.23 us: absorb(): self.pair = [jnp.concatenate(p, axis=self.dims[0]) for p in parts]]
    select_n x30 -> x23, other arithmetic: 9.06 us -> 11.5 us  [by_bit(): return (jnp.where(low, mine, arrived), jnp.where(low, arrived, mine))]
    pallas_call x4 -> x3, Pallas kernels: 23.5 us -> 21.1 us  [weight_grad(): pl.pallas_call(functools.partial(weight_grad_kernel, products, sides), gr...]
  transfers between devices with their start and end apart: 96 -> 88, of which waited for: 49 -> 42; matrix products, arithmetic and copies ran while one was open for 12% -> 12% of each run, Pallas kernels for 14% -> 14%
where the time goes in v4:
time: 423 us; the launch traced here: 419 us
  waiting for transfers between devices  172 us (41%)
  starting transfers between devices  86.6 us (20%)
  Pallas kernels  77.4 us (18%)
  other arithmetic  46.3 us (11%)
  local copies, waits for them, and re-layouts  16.9 us (4%)
  between operations  15.9 us (4%)
    ppermute x70, waiting for transfers between devices, flip_ctx(): return lax.ppermute(value, 'ctx', [(i, i ^ 1 << bit) for i in range(size)])  165 us
    ppermute x70, starting transfers between devices, flip_ctx(): return lax.ppermute(value, 'ctx', [(i, i ^ 1 << bit) for i in range(size)])  84 us
    pallas_call x3, Pallas kernels, weight_grad(): pl.pallas_call(functools.partial(weight_grad_kernel, products, sides), gr...  21.1 us
    pallas_call x2, Pallas kernels, attention_backward(): pl.pallas_call(functools.partial(backward_kernel, steps > WINDOW // BLK,...  19.8 us
    pallas_call x1, Pallas kernels, feed_forward(): pl.pallas_call(block_kernel, grid=(inner // tile,), in_specs=[fixed(wide)...  17.5 us
    pallas_call x2, Pallas kernels, attention_forward(): pl.pallas_call(functools.partial(forward_kernel, steps > WINDOW // BLK, s...  15.9 us
    unnamed x153, local copies, waits for them, and re-layouts  12.6 us
    select_n x23, other arithmetic, by_bit(): return (jnp.where(low, mine, arrived), jnp.where(low, arrived, mine))  11.5 us
  transfers between devices with their start and end apart: 88, of which 42 were waited for; matrix products, arithmetic and copies ran while one was open for 12% of the time, Pallas kernels for 14%

profile of v4, /device:TPU:0, one launch (start us, length us, event | category | flops | bytes accessed | tf_op | source)
XLA Modules:
  0.0 418.9 jit_solution(16295807784322314166)
XLA Ops:
  17.1 8.2 %collective-permute-done.2 = bf16[1,128,640]{2,1,0:T(8,128)(2,1)S(1)} collective-permute-done((bf16[1,128,640]{2,1,0:T(8,128)(2,1)S(1)}, bf16[1,128,640]{2,1,0:T(8,128)(2,1)S(1)}, u32[]{:S(2)}, u32[]{:S(2)}) %collective-permute-start.2) | collective-permute-done | bytes 163872 | tf_op jit(solution)/shard_map/ppermute | solution.py:36
  26.8 3.9 collective-permute-start.5
  31.0 6.4 %collective-permute-done.6 = bf16[1,128,640]{2,1,0:T(8,128)(2,1)S(1)} collective-permute-done((bf16[1,128,640]{2,1,0:T(8,128)(2,1)S(1)}, bf16[1,128,640]{2,1,0:T(8,128)(2,1)S(1)}, u32[]{:S(2)}, u32[]{:S(2)}) %collective-permute-start.6) | collective-permute-done | bytes 163872 | tf_op jit(solution)/shard_map/ppermute | solution.py:36
  37.4 4.0 collective-permute-done.5
  45.6 5.4 %collective-permute-done.10 = bf16[2,128,640]{2,1,0:T(8,128)(2,1)S(1)} collective-permute-done((bf16[2,128,640]{2,1,0:T(8,128)(2,1)S(1)}, bf16[2,128,640]{2,1,0:T(8,128)(2,1)S(1)}, u32[]{:S(2)}, u32[]{:S(2)}) %collective-permute-start.10) | collective-permute-done | bytes 327712 | tf_op jit(solution)/shard_map/ppermute | solution.py:36
  63.8 13.8 %collective-permute-done.16 = bf16[1,480,512]{2,1,0:T(8,128)(2,1)S(1)} collective-permute-done((bf16[1,480,512]{2,1,0:T(8,128)(2,1)S(1)}, bf16[1,480,512]{2,1,0:T(8,128)(2,1)S(1)}, u32[]{:S(2)}, u32[]{:S(2)}) %collective-permute-start.16) | collective-permute-done | bytes 491552 | tf_op jit(solution)/shard_map/ppermute | solution.py:36
  81.5 10.3 %attention_forward.2 = (f32[960,128]{1,0:T(8,128)S(1)}, f32[1,1920]{1,0:T(1,128)S(1)}) custom-call(s32[2]{0:T(128)S(1)} %pad_add_fusion.ids, s32[2,2,2]{2,1,0:T(2,128)S(1)} %copy-done.8, s32[2,2,16]{2,1,0:T(2,128)S(1)} %copy-done.9, bf16[16,64,640]{2,1,0:T(8,128)(2,1)S(1)} %get-tuple-element.422.first_ref, ...), custom_call_target="tpu_custom_call" | custom-call | flops 503316480 | bytes 2621440 | tf_op jit(solution)/shard_map/attention_forward/pallas_call | solution.py:483
  95.9 5.6 %attention_forward.3 = (f32[960,128]{1,0:T(8,128)S(1)}, f32[1,1920]{1,0:T(1,128)S(1)}) custom-call(s32[2]{0:T(128)S(1)} %pad_add_fusion.ids, s32[2,2,2]{2,1,0:T(2,128)S(1)} %copy-done.8, s32[2,2,16]{2,1,0:T(2,128)S(1)} %copy-done.9, bf16[16,64,640]{2,1,0:T(8,128)(2,1)S(1)} %pad_maximum_fusion.4.first_ref, ...), custom_call_target="tpu_custom_call" | custom-call | flops 503316480 | bytes 2621440 | tf_op jit(solution)/shard_map/attention_forward/pallas_call | solution.py:483
  104.7 17.5 %feed_forward.1 = (bf16[256,2560]{1,0:T(8,128)(2,1)}, bf16[2,256,2560]{2,1,0:T(8,128)(2,1)}, bf16[960,256]{1,0:T(8,128)(2,1)}, bf16[960,256]{1,0:T(8,128)(2,1)},...) custom-call(bf16[960,256]{1,0:T(8,128)(2,1)} %pad_maximum_fusion.27.x_ref, ...), custom_call_target="tpu_custom_call" | custom-call | flops 7549747200 | bytes 19660800 | tf_op jit(solution)/shard_map/feed_forward/pallas_call | solution.py:616
  124.2 4.0 collective-permute-done.22.refs_3_
  129.0 5.2 %down_grad.1 = (bf16[240,1280]{1,0:T(8,128)(2,1)}, bf16[240,1280]{1,0:T(8,128)(2,1)}, bf16[240,1280]{1,0:T(8,128)(2,1)}, bf16[240,1280]{1,0:T(8,128)(2,1)}) custom-call(s32[2]{0:T(128)S(1)} %pad_add_fusion.ids, bf16[960,256]{1,0:T(8,128)(2,1)} %copy-done.62, bf16[960,256]{1,0:T(8,128)(2,1)} %collective-permute-done.11.refs_1_, ...), custom_call_target="tpu_custom_call" | custom-call | flops 1258291200 | bytes 2457600 | tf_op jit(solution)/shard_map/down_grad/pallas_call | solution.py:698
  143.1 10.7 %inner_grad.1 = (bf16[120,5120]{1,0:T(8,128)(2,1)}, bf16[120,5120]{1,0:T(8,128)(2,1)}, bf16[120,5120]{1,0:T(8,128)(2,1)}, bf16[120,5120]{1,0:T(8,128)(2,1)}) custom-call(s32[2]{0:T(128)S(1)} %pad_add_fusion.ids, bf16[960,256]{1,0:T(8,128)(2,1)} %get-tuple-element.216.refs_0_, bf16[480,256]{1,0:T(8,128)(2,1)} %copy-done.75, ...), custom_call_target="tpu_custom_call" | custom-call | flops 2516582400 | bytes 4915200 | tf_op jit(solution)/shard_map/inner_grad/pallas_call | solution.py:698
  155.9 12.8 %attention_backward.2 = (bf16[960,128]{1,0:T(8,128)(2,1)S(1)}, bf16[16,64,640]{2,1,0:T(8,128)(2,1)S(1)}, bf16[16,64,640]{2,1,0:T(8,128)(2,1)S(1)}) custom-call(s32[2]{0:T(128)S(1)} %pad_add_fusion.ids, s32[2,2,2]{2,1,0:T(2,128)S(1)} %copy-done.8, s32[2,2,16]{2,1,0:T(2,128)S(1)} %copy-done.9, bf16[16,64,640]{2,1,0:T(8,128)(2,1)S(1)} %get-tuple-element.422.first_ref, ...), custom_call_target="tpu_custom_call" | custom-call | flops 157286400 | bytes 655360 | tf_op jit(solution)/shard_map/attention_backward/pallas_call | solution.py:506
  172.5 10.3 %collective-permute-done.25 = bf16[120,5120]{1,0:T(8,128)(2,1)S(1)} collective-permute-done((bf16[120,5120]{1,0:T(8,128)(2,1)}, bf16[120,5120]{1,0:T(8,128)(2,1)S(1)}, u32[]{:S(2)}, u32[]{:S(2)}) %collective-permute-start.25) | collective-permute-done | bytes 1228832 | tf_op jit(solution)/shard_map/ppermute | solution.py:36
  191.4 7.0 %attention_backward.3 = (bf16[960,128]{1,0:T(8,128)(2,1)S(1)}, bf16[16,64,640]{2,1,0:T(8,128)(2,1)S(1)}, bf16[16,64,640]{2,1,0:T(8,128)(2,1)S(1)}) custom-call(s32[2]{0:T(128)S(1)} %pad_add_fusion.ids, s32[2,2,2]{2,1,0:T(2,128)S(1)} %copy-done.8, s32[2,2,16]{2,1,0:T(2,128)S(1)} %copy-done.9, bf16[16,64,640]{2,1,0:T(8,128)(2,1)S(1)} %copy-done.1, ...), custom_call_target="tpu_custom_call" | custom-call | flops 157286400 | bytes 655360 | tf_op jit(solution)/shard_map/attention_backward/pallas_call | solution.py:506
  198.8 7.4 %collective-permute-done.30 = bf16[8,64,640]{2,1,0:T(8,128)(2,1)S(1)} collective-permute-done((bf16[8,64,640]{2,1,0:T(8,128)(2,1)S(1)}, bf16[8,64,640]{2,1,0:T(8,128)(2,1)S(1)}, u32[]{:S(2)}, u32[]{:S(2)}) %collective-permute-start.30) | collective-permute-done | bytes 655392 | tf_op jit(solution)/shard_map/ppermute | solution.py:36
  215.3 7.9 %collective-permute-done.33 = bf16[120,2560]{1,0:T(8,128)(2,1)S(1)} collective-permute-done((bf16[120,2560]{1,0:T(8,128)(2,1)S(1)}, bf16[120,2560]{1,0:T(8,128)(2,1)S(1)}, u32[]{:S(2)}, u32[]{:S(2)}) %collective-permute-start.33) | collective-permute-done | bytes 614432 | tf_op jit(solution)/shard_map/ppermute | solution.py:36
  230.6 5.2 %query_grad.1 = (bf16[240,960]{1,0:T(8,128)(2,1)}, bf16[240,960]{1,0:T(8,128)(2,1)}, bf16[240,960]{1,0:T(8,128)(2,1)}, bf16[240,960]{1,0:T(8,128)(2,1)}) custom-call(s32[2]{0:T(128)S(1)} %pad_add_fusion.ids, bf16[960,256]{1,0:T(8,128)(2,1)} %copy-done.16, bf16[480,256]{1,0:T(8,128)(2,1)} %copy-done.41, bf16[960,256]{1,0:T(8,128)(2,1)} %copy-done.31, ...), custom_call_target="tpu_custom_call" | custom-call | flops 943718400 | bytes 1843200 | tf_op jit(solution)/shard_map/query_grad/pallas_call | solution.py:698
  246.4 7.3 %collective-permute-done.42 = bf16[120,640]{1,0:T(8,128)(2,1)S(1)} collective-permute-done((bf16[120,640]{1,0:T(8,128)(2,1)S(1)}, bf16[120,640]{1,0:T(8,128)(2,1)S(1)}, u32[]{:S(2)}, u32[]{:S(2)}) %collective-permute-start.42) | collective-permute-done | bytes 153632 | tf_op jit(solution)/shard_map/ppermute | solution.py:36
  265.6 5.6 %collective-permute-done.49 = bf16[120,1280]{1,0:T(8,128)(2,1)S(1)} collective-permute-done((bf16[120,1280]{1,0:T(8,128)(2,1)S(1)}, bf16[120,1280]{1,0:T(8,128)(2,1)S(1)}, u32[]{:S(2)}, u32[]{:S(2)}) %collective-permute-start.49) | collective-permute-done | bytes 307232 | tf_op jit(solution)/shard_map/ppermute | solution.py:36
  282.2 6.2 %collective-permute-done.53 = bf16[120,960]{1,0:T(8,128)(2,1)S(1)} collective-permute-done((bf16[120,960]{1,0:T(8,128)(2,1)S(1)}, bf16[120,960]{1,0:T(8,128)(2,1)S(1)}, u32[]{:S(2)}, u32[]{:S(2)}) %collective-permute-start.53) | collective-permute-done | bytes 230432 | tf_op jit(solution)/shard_map/ppermute | solution.py:36
  301.6 15.8 %collective-permute-done.60 = bf16[120,960]{1,0:T(8,128)(2,1)S(1)} collective-permute-done((bf16[120,960]{1,0:T(8,128)(2,1)S(1)}, bf16[120,960]{1,0:T(8,128)(2,1)S(1)}, u32[]{:S(2)}, u32[]{:S(2)}) %collective-permute-start.60) | collective-permute-done | bytes 230432 | tf_op jit(solution)/shard_map/ppermute | solution.py:36
  328.4 6.8 %collective-permute-done.64 = bf16[2,256,640]{2,1,0:T(8,128)(2,1)S(1)} collective-permute-done((bf16[2,256,640]{2,1,0:T(8,128)(2,1)S(1)}, bf16[2,256,640]{2,1,0:T(8,128)(2,1)S(1)}, u32[]{:S(2)}, u32[]{:S(2)}) %collective-permute-start.64) | collective-permute-done | bytes 655392 | tf_op jit(solution)/shard_map/ppermute | solution.py:36
  349.1 10.5 %collective-permute-done.67 = bf16[1,256,640]{2,1,0:T(8,128)(2,1)S(1)} collective-permute-done((bf16[1,256,640]{2,1,0:T(8,128)(2,1)S(1)}, bf16[1,256,640]{2,1,0:T(8,128)(2,1)S(1)}, u32[]{:S(2)}, u32[]{:S(2)}) %collective-permute-start.67) | collective-permute-done | bytes 327712 | tf_op jit(solution)/shard_map/ppermute | solution.py:36
  (472 shorter events, 205.0 us)
Async XLA Ops:
  7.2 97.6 %all-gather.5.cloned.1.call-start = ((), (), s32[]{:S(2)}) async-start(), calls=%async_computation | async-start | bytes 2949120 | tf_op jit(solution)/shard_map/all_gather | solution.py:785
  7.9 96.8 %all-gather.7.cloned.1.call-start = ((), (), s32[]{:S(2)}) async-start(), calls=%async_computation.1 | async-start | bytes 7372800 | tf_op jit(solution)/shard_map/all_gather | solution.py:785
  8.7 96.1 %all-gather.9.cloned.1.call-start = ((), (), s32[]{:S(2)}) async-start(), calls=%async_computation.2 | async-start | bytes 7372800 | tf_op jit(solution)/shard_map/all_gather | solution.py:785
  9.4 95.3 %all-gather.11.cloned.1.call-start = ((), (), s32[]{:S(2)}) async-start(), calls=%async_computation.3 | async-start | bytes 7372800 | tf_op jit(solution)/shard_map/all_gather | solution.py:785
  44.9 35.1 %collective-permute-start.11 = (bf16[960,256]{1,0:T(8,128)(2,1)S(1)}, bf16[960,256]{1,0:T(8,128)(2,1)}, u32[]{:S(2)}, u32[]{:S(2)}) collective-permute-start(bf16[960,256]{1,0:T(8,128)(2,1)S(1)} %pad_maximum_fusion.28.cot_ref.refs_0_), channel_id=1, source_target_pairs={{0,1},{1,0},{2,3},{3,2},{4,5},{5,4},{6,7},{7,6},{8,9},{9,8},{10,11... | collective-permute-start | bytes 1474568 | tf_op jit(solution)/shard_map/ppermute | solution.py:40
  54.8 22.8 %collective-permute-start.16 = (bf16[1,480,512]{2,1,0:T(8,128)(2,1)S(1)}, bf16[1,480,512]{2,1,0:T(8,128)(2,1)S(1)}, u32[]{:S(2)}, u32[]{:S(2)}) collective-permute-start(bf16[1,480,512]{2,1,0:T(8,128)(2,1)S(1)} %maximum_bitcast_fusion), channel_id=1, source_target_pairs={{0,16},{2,18},{4,20},{6,22},{8,24},{10,26},{12,28},{14,30},{16,0},... | collective-permute-start | bytes 1474568 | tf_op jit(solution)/shard_map/ppermute | solution.py:36
  56.9 24.0 %collective-permute-start.13 = (bf16[8,64,640]{2,1,0:T(8,128)(2,1)S(1)}, bf16[8,64,640]{2,1,0:T(8,128)(2,1)S(1)}, u32[]{:S(2)}, u32[]{:S(2)}) collective-permute-start(bf16[8,64,640]{2,1,0:T(8,128)(2,1)S(1)} %pad_maximum_fusion.19), channel_id=1, source_target_pairs={{0,4},{2,6},{4,0},{6,2},{8,12},{10,14},{12,8},{14,10},{16,20},{18,... | collective-permute-start | bytes 1966088 | tf_op jit(solution)/shard_map/ppermute | solution.py:36
  79.9 22.2 %collective-permute-start.19 = (bf16[2,480,512]{2,1,0:T(8,128)(2,1)S(1)}, bf16[2,480,512]{2,1,0:T(8,128)(2,1)S(1)}, u32[]{:S(2)}, u32[]{:S(2)}) collective-permute-start(bf16[2,480,512]{2,1,0:T(8,128)(2,1)S(1)} %pad_maximum_fusion.13), channel_id=1, source_target_pairs={{0,8},{2,10},{4,12},{6,14},{8,0},{10,2},{12,4},{14,6},{16,24},{18,... | collective-permute-start | bytes 2949128 | tf_op jit(solution)/shard_map/ppermute | solution.py:36
  135.0 20.9 %collective-permute-start.23 = (bf16[240,1280]{1,0:T(8,128)(2,1)}, bf16[240,1280]{1,0:T(8,128)(2,1)}, u32[]{:S(2)}, u32[]{:S(2)}) collective-permute-start(bf16[240,1280]{1,0:T(8,128)(2,1)} %get-tuple-element.224), channel_id=1, source_target_pairs={{0,2},{2,0},{4,6},{6,4},{8,10},{10,8},{12,14},{14,12},{16,18},{18,... | collective-permute-start | bytes 1843208 | tf_op jit(solution)/shard_map/ppermute | solution.py:36
  153.8 29.0 %collective-permute-start.25 = (bf16[120,5120]{1,0:T(8,128)(2,1)}, bf16[120,5120]{1,0:T(8,128)(2,1)S(1)}, u32[]{:S(2)}, u32[]{:S(2)}) collective-permute-start(bf16[120,5120]{1,0:T(8,128)(2,1)} %get-tuple-element.232), channel_id=1, source_target_pairs={{0,2},{2,0},{4,6},{6,4},{8,10},{10,8},{12,14},{14,12},{16,18},{18,... | collective-permute-start | bytes 3686408 | tf_op jit(solution)/shard_map/ppermute | solution.py:36
  155.8 28.4 %collective-permute-start.26 = (bf16[120,5120]{1,0:T(8,128)(2,1)}, bf16[120,5120]{1,0:T(8,128)(2,1)S(1)}, u32[]{:S(2)}, u32[]{:S(2)}) collective-permute-start(bf16[120,5120]{1,0:T(8,128)(2,1)} %get-tuple-element.233), channel_id=1, source_target_pairs={{0,4},{2,6},{4,0},{6,2},{8,12},{10,14},{12,8},{14,10},{16,20},{18,... | collective-permute-start | bytes 3686408 | tf_op jit(solution)/shard_map/ppermute | solution.py:36
  184.9 21.2 %collective-permute-start.30 = (bf16[8,64,640]{2,1,0:T(8,128)(2,1)S(1)}, bf16[8,64,640]{2,1,0:T(8,128)(2,1)S(1)}, u32[]{:S(2)}, u32[]{:S(2)}) collective-permute-start(bf16[8,64,640]{2,1,0:T(8,128)(2,1)S(1)} %slice.159), channel_id=1, source_target_pairs={{0,2},{2,0},{4,6},{6,4},{8,10},{10,8},{12,14},{14,12},{16,18},{18,... | collective-permute-start | bytes 1966088 | tf_op jit(solution)/shard_map/ppermute | solution.py:36
  198.7 30.5 %collective-permute-start.39 = (bf16[480,256]{1,0:T(8,128)(2,1)S(1)}, bf16[480,256]{1,0:T(8,128)(2,1)S(1)}, u32[]{:S(2)}, u32[]{:S(2)}) collective-permute-start(bf16[480,256]{1,0:T(8,128)(2,1)S(1)} %fusion.13), channel_id=1, source_target_pairs={{0,1},{1,0},{2,3},{3,2},{4,5},{5,4},{6,7},{7,6},{8,9},{9,8},{10,11... | collective-permute-start | bytes 737288 | tf_op jit(solution)/shard_map/ppermute | solution.py:40
  213.2 25.5 %collective-permute-start.36 = (bf16[8,64,640]{2,1,0:T(8,128)(2,1)S(1)}, bf16[8,64,640]{2,1,0:T(8,128)(2,1)S(1)}, u32[]{:S(2)}, u32[]{:S(2)}) collective-permute-start(bf16[8,64,640]{2,1,0:T(8,128)(2,1)S(1)} %slice.162), channel_id=1, source_target_pairs={{0,2},{2,0},{4,6},{6,4},{8,10},{10,8},{12,14},{14,12},{16,18},{18,... | collective-permute-start | bytes 1966088 | tf_op jit(solution)/shard_map/ppermute | solution.py:36
  214.0 26.7 %collective-permute-start.37 = (bf16[8,64,640]{2,1,0:T(8,128)(2,1)S(1)}, bf16[8,64,640]{2,1,0:T(8,128)(2,1)S(1)}, u32[]{:S(2)}, u32[]{:S(2)}) collective-permute-start(bf16[8,64,640]{2,1,0:T(8,128)(2,1)S(1)} %slice.163), channel_id=1, source_target_pairs={{0,4},{2,6},{4,0},{6,2},{8,12},{10,14},{12,8},{14,10},{16,20},{18,... | collective-permute-start | bytes 1966088 | tf_op jit(solution)/shard_map/ppermute | solution.py:36
  228.2 25.5 %collective-permute-start.40 = (bf16[4,64,640]{2,1,0:T(8,128)(2,1)S(1)}, bf16[4,64,640]{2,1,0:T(8,128)(2,1)S(1)}, u32[]{:S(2)}, u32[]{:S(2)}) collective-permute-start(bf16[4,64,640]{2,1,0:T(8,128)(2,1)S(1)} %slice.198), channel_id=1, source_target_pairs={{0,4},{2,6},{4,0},{6,2},{8,12},{10,14},{12,8},{14,10},{16,20},{18,... | collective-permute-start | bytes 983048 | tf_op jit(solution)/shard_map/ppermute | solution.py:36
  229.2 24.6 %collective-permute-start.41 = (bf16[4,64,640]{2,1,0:T(8,128)(2,1)S(1)}, bf16[4,64,640]{2,1,0:T(8,128)(2,1)S(1)}, u32[]{:S(2)}, u32[]{:S(2)}) collective-permute-start(bf16[4,64,640]{2,1,0:T(8,128)(2,1)S(1)} %slice.199), channel_id=1, source_target_pairs={{0,2},{2,0},{4,6},{6,4},{8,10},{10,8},{12,14},{14,12},{16,18},{18,... | collective-permute-start | bytes 983048 | tf_op jit(solution)/shard_map/ppermute | solution.py:36
  293.1 24.6 %collective-permute-start.57 = (bf16[240,1280]{1,0:T(8,128)(2,1)}, bf16[240,1280]{1,0:T(8,128)(2,1)}, u32[]{:S(2)}, u32[]{:S(2)}) collective-permute-start(bf16[240,1280]{1,0:T(8,128)(2,1)} %pad_maximum_fusion.23), channel_id=1, source_target_pairs={{0,2},{2,0},{4,6},{6,4},{8,10},{10,8},{12,14},{14,12},{16,18},{18,... | collective-permute-start | bytes 1843208 | tf_op jit(solution)/shard_map/ppermute | solution.py:36
  295.5 22.2 %collective-permute-start.58 = (bf16[240,1280]{1,0:T(8,128)(2,1)}, bf16[240,1280]{1,0:T(8,128)(2,1)}, u32[]{:S(2)}, u32[]{:S(2)}) collective-permute-start(bf16[240,1280]{1,0:T(8,128)(2,1)} %pad_maximum_fusion.24), channel_id=1, source_target_pairs={{0,4},{2,6},{4,0},{6,2},{8,12},{10,14},{12,8},{14,10},{16,20},{18,... | collective-permute-start | bytes 1843208 | tf_op jit(solution)/shard_map/ppermute | solution.py:36
  296.7 21.0 %collective-permute-start.59 = (bf16[120,2560]{1,0:T(8,128)(2,1)}, bf16[120,2560]{1,0:T(8,128)(2,1)}, u32[]{:S(2)}, u32[]{:S(2)}) collective-permute-start(bf16[120,2560]{1,0:T(8,128)(2,1)} %pad_maximum_fusion.25), channel_id=1, source_target_pairs={{0,8},{2,10},{4,12},{6,14},{8,0},{10,2},{12,4},{14,6},{16,24},{18,... | collective-permute-start | bytes 1843208 | tf_op jit(solution)/shard_map/ppermute | solution.py:36
  296.7 21.0 %collective-permute-start.56 = (bf16[240,640]{1,0:T(8,128)(2,1)}, bf16[240,640]{1,0:T(8,128)(2,1)S(1)}, u32[]{:S(2)}, u32[]{:S(2)}) collective-permute-start(bf16[240,640]{1,0:T(8,128)(2,1)} %constant_dynamic-slice_fusion.2), channel_id=1, source_target_pairs={{0,2},{2,0},{4,6},{6,4},{8,10},{10,8},{12,14},{14,12},{16,18},{18,... | collective-permute-start | bytes 921608 | tf_op jit(solution)/shard_map/ppermute | solution.py:36
  344.7 40.5 %collective-permute-start.72 = (bf16[120,5120]{1,0:T(8,128)(2,1)}, bf16[120,5120]{1,0:T(8,128)(2,1)}, u32[]{:S(2)}, u32[]{:S(2)}) collective-permute-start(bf16[120,5120]{1,0:T(8,128)(2,1)} %pad_maximum_fusion.10), channel_id=1, source_target_pairs={{0,2},{2,0},{4,6},{6,4},{8,10},{10,8},{12,14},{14,12},{16,18},{18,... | collective-permute-start | bytes 3686408 | tf_op jit(solution)/shard_map/ppermute | solution.py:36
  347.2 38.0 %collective-permute-start.73 = (bf16[120,5120]{1,0:T(8,128)(2,1)}, bf16[120,5120]{1,0:T(8,128)(2,1)}, u32[]{:S(2)}, u32[]{:S(2)}) collective-permute-start(bf16[120,5120]{1,0:T(8,128)(2,1)} %pad_maximum_fusion.11), channel_id=1, source_target_pairs={{0,4},{2,6},{4,0},{6,2},{8,12},{10,14},{12,8},{14,10},{16,20},{18,... | collective-permute-start | bytes 3686408 | tf_op jit(solution)/shard_map/ppermute | solution.py:36
  387.8 19.9 %collective-permute-start.81 = (bf16[240,960]{1,0:T(8,128)(2,1)S(1)}, bf16[240,960]{1,0:T(8,128)(2,1)S(1)}, u32[]{:S(2)}, u32[]{:S(2)}) collective-permute-start(bf16[240,960]{1,0:T(8,128)(2,1)S(1)} %pad_maximum_fusion.30), channel_id=1, source_target_pairs={{0,2},{2,0},{4,6},{6,4},{8,10},{10,8},{12,14},{14,12},{16,18},{18,... | collective-permute-start | bytes 1382408 | tf_op jit(solution)/shard_map/ppermute | solution.py:36
  (140 other events, 1317.0 us)
Sparse Core Ops, SparseCore 0:
  9.6 13.0 all-gather.4
  24.2 15.8 all-gather.6
  41.7 15.8 all-gather.8
  59.0 15.8 all-gather.10

commit v5 on v4

--- a/solution.py
+++ b/solution.py
@@ -198,10 +198,31 @@
         self.held = add_low(self.held[: self.held.shape[0] // 2], arrived[0])
 
 
+class Exchange:
+    def __init__(self, arrays, bits):
+        self.arrays, self.bits = arrays, bits
+        self.stages = [None]
+
+    def operands(self):
+        return self.arrays, self.bits
+
+    def absorb(self, arrived):
+        self.stages.pop()
+        self.came = arrived
+
+
+def four_rows(own, first, second, last, dim):
+    rows = []
+    for n, (low, high) in enumerate(((1, 0), (0, 1))):
+        mine = in_order(low, own[n], first[n], dim)
+        rows += by_bit(high, mine, in_order(low, second[n], last[n], dim))
+    return rows
+
+
 class SumVector:
     def __init__(self, value):
         self.value = value
-        self.stages = list(range(lax.axis_size("ctx").bit_length() - 1))
+        self.stages = high_bits() + [0, 1]
 
     def operands(self):
         return [self.value], [self.stages[0]]
@@ -964,49 +985,46 @@
         (0, 1),
     )
     rounds.prepare(query_job)
-    (grad_queries_t,) = rounds.end([key_second, down_job], grad_queries_t)
+    (grad_queries_t,) = rounds.end([key_second, down_job, inner_job], grad_queries_t)
     rounds.run(down_job, 0)
+    rounds.run(inner_job, 1)
     down_spread = Spread(down_job)
 
-    rounds.begin(query_job, down_spread)
+    rounds.begin(query_job, down_spread, inner_job)
     rounds.prepare(key_second)
     rounds.end([key_first, down_spread, inner_job])
     rounds.run(down_spread, 3)
-
-    rounds.begin(key_second, down_spread, inner_job)
+    inner_spread = Spread(inner_job)
+
+    rounds.begin(key_second, down_spread, inner_spread)
     grad_normed_t = dot(query_full, grad_queries_t, 1, 0)
     (grad_normed_t,) = rounds.end(
-        [key_second, query_job, down_spread, inner_job], grad_normed_t
-    )
-    rounds.run(inner_job, 0)
-    inner_spread = Spread(inner_job)
-
-    rounds.begin(down_spread, query_job, inner_spread)
+        [key_second, query_job, down_spread, inner_spread], grad_normed_t
+    )
+    rounds.run(inner_spread, 3)
+
     parts = [part for job in (key_first, key_second) for part in job.halves]
     key_column = jnp.concatenate(parts, axis=1)
+    rounds.begin(down_spread, query_job, inner_spread)
     key_other = swap_fsdp(key_column)
     last_job = Solo(keyval_grad(column.held, key_column, key_other))
     rounds.prepare(last_job)
     (key_column,) = rounds.end([down_spread, query_job, inner_spread], key_column)
-    rounds.run(inner_spread, 3)
     key_job = ScatterHigh(key_column)
 
-    rounds.begin(last_job, down_spread, inner_spread, query_job)
-    rounds.end([last_job, down_spread, inner_spread, query_job])
-
-    rounds.begin(last_job, inner_spread, key_job, query_job)
-    down_sum = rows_of(down_spread.quarters)
-    (down_sum,) = rounds.end([last_job, inner_spread, key_job, query_job], down_sum)
+    own = inner_spread.pair
+    first = Exchange(own, (1, 0))
+    second = Exchange(own, (0, 1))
+    rounds.begin(last_job, query_job, key_job, first, down_spread, second)
+    rounds.end([last_job, query_job, key_job])
+    rounds.run(key_job, 1)
+    rounds.begin(last_job, query_job, key_job)
+    rounds.end([first, down_spread, last_job, key_job, query_job])
     rounds.run(query_job, 0)
-    rounds.run(key_job, 1)
     query_spread = Spread(query_job)
 
-    rounds.begin(inner_spread, last_job, key_job, query_spread)
-    rounds.end([last_job, key_job, query_spread])
-    rounds.run(last_job, 3)
-    rounds.run(query_spread, 3)
-
-    rounds.begin(last_job, query_spread)
+    third = Exchange(first.came, (0, 1))
+    rounds.begin(third, last_job, query_spread)
     grad_keyvals = key_job.held[0]
     grad_normed_t = grad_normed_t + dot(keyval_full, grad_keyvals, 1, 1)
     attn_gain_grad = jnp.sum(grad_normed_t * in_t * inverse_attn, axis=1)
@@ -1014,9 +1032,16 @@
     gains_other = swap_fsdp(theirs(gains, 1))
     gains_mine = lax.dynamic_slice_in_dim(gains, shard * half, half, 1)
     (grad_normed_t, gains_mine, gains_other) = rounds.end(
-        [last_job, query_spread], grad_normed_t, gains_mine, gains_other
-    )
+        [last_job, query_spread, second], grad_normed_t, gains_mine, gains_other
+    )
+    rounds.run(query_spread, 3)
+    rounds.run(last_job, 3)
     gain_job = SumVector((gains_mine + gains_other).reshape(-1))
+
+    rounds.begin(last_job, query_spread, gain_job)
+    down_sum = rows_of(down_spread.quarters)
+    (down_sum,) = rounds.end([last_job, query_spread, gain_job, third], down_sum)
+    rounds.run(gain_job, 3)
 
     rounds.begin(last_job, query_spread, gain_job)
     scaled = grad_normed_t * attn_gain
@@ -1026,18 +1051,23 @@
         + inverse_attn * scaled
         - in_t * cubed * jnp.mean(scaled * in_t, axis=0, keepdims=True)
     )
-    (input_grad_t,) = rounds.end(
-        [inner_spread, last_job, query_spread, gain_job], input_grad_t
-    )
+    tied = rounds.end(
+        [last_job, query_spread, gain_job],
+        input_grad_t,
+        *own,
+        *first.came,
+        *second.came,
+        *third.came,
+    )
+    input_grad_t = tied[0]
+    quarters = four_rows(*[tied[i : i + 2] for i in (1, 3, 5, 7)], 1)
 
     rounds.begin(last_job, query_spread, gain_job)
-    gate_sum = rows_of(inner_spread.quarters, slice(0, inner))
-    (gate_sum,) = rounds.end([gain_job], gate_sum)
+    gate_sum = rows_of(quarters, slice(0, inner))
+    up_sum = rows_of(quarters, slice(inner, None))
+    (gate_sum, up_sum) = rounds.end([last_job, query_spread, gain_job], gate_sum, up_sum)
     rounds.begin(gain_job)
-    up_sum = rows_of(inner_spread.quarters, slice(inner, None))
-    (up_sum,) = rounds.end([last_job, gain_job], up_sum)
-    rounds.begin(gain_job)
-    rounds.end([query_spread, gain_job])
+    rounds.end([gain_job])
     rounds.run(gain_job, 0)
 
     def by_token(value_t):

time: 423 us -> 408 us (0.965)
  Pallas kernels: 77.4 us -> 57.2 us
  waiting for transfers between devices: 172 us -> 185 us
  other arithmetic: 46.3 us -> 37.9 us
    ppermute x70 -> x72, waiting for transfers between devices: 165 us -> 178 us  [flip_ctx(): return lax.ppermute(value, 'ctx', [(i, i ^ 1 << bit) for i in range(size)])]
    pallas_call x2, Pallas kernels: 19.8 us -> 8.61 us  [attention_backward(): pl.pallas_call(functools.partial(backward_kernel, steps > WINDOW // BLK,...]
    pallas_call x2, Pallas kernels: 15.9 us -> 6.94 us  [attention_forward(): pl.pallas_call(functools.partial(forward_kernel, steps > WINDOW // BLK, s...]
    ppermute x14, starting transfers between devices: 2.42 us -> 7.97 us  [swap_fsdp(): return lax.ppermute(value, 'fsdp', [(0, 1), (1, 0)])]
    ppermute x70 -> x72, starting transfers between devices: 84 us -> 80.8 us  [flip_ctx(): return lax.ppermute(value, 'ctx', [(i, i ^ 1 << bit) for i in range(size)])]
    select_n x23 -> x25, other arithmetic: 11.5 us -> 8.3 us  [by_bit(): return (jnp.where(low, mine, arrived), jnp.where(low, arrived, mine))]
    unnamed x153 -> x123, local copies, waits for them, and re-layouts: 12.6 us -> 12 us
  transfers between devices with their start and end apart: 88 -> 90, of which waited for: 42 -> 47; matrix products, arithmetic and copies ran while one was open for 12% -> 11% of each run, Pallas kernels for 14% -> 10%
where the time goes in v5:
time: 408 us; the launch traced here: 403 us
  waiting for transfers between devices  185 us (45%)
  starting transfers between devices  88.9 us (22%)
  Pallas kernels  57.2 us (14%)
  other arithmetic  37.9 us (9%)
  between operations  15.8 us (4%)
  local copies, waits for them, and re-layouts  15.7 us (4%)
    ppermute x72, waiting for transfers between devices, flip_ctx(): return lax.ppermute(value, 'ctx', [(i, i ^ 1 << bit) for i in range(size)])  178 us
    ppermute x72, starting transfers between devices, flip_ctx(): return lax.ppermute(value, 'ctx', [(i, i ^ 1 << bit) for i in range(size)])  80.8 us
    pallas_call x3, Pallas kernels, weight_grad(): pl.pallas_call(functools.partial(weight_grad_kernel, products, sides), gr...  21.1 us
    pallas_call x1, Pallas kernels, feed_forward(): pl.pallas_call(block_kernel, grid=(inner // tile,), in_specs=[fixed(wide)...  17.5 us
    unnamed x123, local copies, waits for them, and re-layouts  12 us
    convert_element_type x5, other arithmetic, rows_of(): jnp.concatenate([q[:, columns] for q in quarters], axis=0).astype(f32)  11.4 us
    pallas_call x2, Pallas kernels, attention_backward(): pl.pallas_call(functools.partial(backward_kernel, steps > WINDOW // BLK,...  8.61 us
    select_n x25, other arithmetic, by_bit(): return (jnp.where(low, mine, arrived), jnp.where(low, arrived, mine))  8.3 us
  transfers between devices with their start and end apart: 90, of which 47 were waited for; matrix products, arithmetic and copies ran while one was open for 11% of the time, Pallas kernels for 10%

profile of v5, /device:TPU:0, one launch (start us, length us, event | category | flops | bytes accessed | tf_op | source)
XLA Modules:
  0.0 402.9 jit_solution(17599076777028706860)
XLA Ops:
  17.1 8.2 %collective-permute-done.2 = bf16[1,128,640]{2,1,0:T(8,128)(2,1)S(1)} collective-permute-done((bf16[1,128,640]{2,1,0:T(8,128)(2,1)S(1)}, bf16[1,128,640]{2,1,0:T(8,128)(2,1)S(1)}, u32[]{:S(2)}, u32[]{:S(2)}) %collective-permute-start.2) | collective-permute-done | bytes 163872 | tf_op jit(solution)/shard_map/ppermute | solution.py:36
  30.9 6.4 %collective-permute-done.6 = bf16[1,128,640]{2,1,0:T(8,128)(2,1)S(1)} collective-permute-done((bf16[1,128,640]{2,1,0:T(8,128)(2,1)S(1)}, bf16[1,128,640]{2,1,0:T(8,128)(2,1)S(1)}, u32[]{:S(2)}, u32[]{:S(2)}) %collective-permute-start.6) | collective-permute-done | bytes 163872 | tf_op jit(solution)/shard_map/ppermute | solution.py:36
  45.6 5.4 %collective-permute-done.10 = bf16[2,128,640]{2,1,0:T(8,128)(2,1)S(1)} collective-permute-done((bf16[2,128,640]{2,1,0:T(8,128)(2,1)S(1)}, bf16[2,128,640]{2,1,0:T(8,128)(2,1)S(1)}, u32[]{:S(2)}, u32[]{:S(2)}) %collective-permute-start.10) | collective-permute-done | bytes 327712 | tf_op jit(solution)/shard_map/ppermute | solution.py:36
  63.8 13.8 %collective-permute-done.16 = bf16[1,480,512]{2,1,0:T(8,128)(2,1)S(1)} collective-permute-done((bf16[1,480,512]{2,1,0:T(8,128)(2,1)S(1)}, bf16[1,480,512]{2,1,0:T(8,128)(2,1)S(1)}, u32[]{:S(2)}, u32[]{:S(2)}) %collective-permute-start.16) | collective-permute-done | bytes 491552 | tf_op jit(solution)/shard_map/ppermute | solution.py:36
  85.0 8.4 %collective-permute-done.18 = bf16[8,64,640]{2,1,0:T(8,128)(2,1)S(1)} collective-permute-done((bf16[8,64,640]{2,1,0:T(8,128)(2,1)S(1)}, bf16[8,64,640]{2,1,0:T(8,128)(2,1)S(1)}, u32[]{:S(2)}, u32[]{:S(2)}) %collective-permute-start.18) | collective-permute-done | bytes 655392 | tf_op jit(solution)/shard_map/ppermute | solution.py:36
  104.6 17.5 %feed_forward.1 = (bf16[256,2560]{1,0:T(8,128)(2,1)}, bf16[2,256,2560]{2,1,0:T(8,128)(2,1)}, bf16[960,256]{1,0:T(8,128)(2,1)}, bf16[960,256]{1,0:T(8,128)(2,1)},...) custom-call(bf16[960,256]{1,0:T(8,128)(2,1)} %pad_maximum_fusion.29.x_ref, ...), custom_call_target="tpu_custom_call" | custom-call | flops 7549747200 | bytes 19660800 | tf_op jit(solution)/shard_map/feed_forward/pallas_call | solution.py:637
  128.9 5.2 %down_grad.1 = (bf16[240,1280]{1,0:T(8,128)(2,1)}, bf16[240,1280]{1,0:T(8,128)(2,1)}, bf16[240,1280]{1,0:T(8,128)(2,1)}, bf16[240,1280]{1,0:T(8,128)(2,1)}) custom-call(s32[2]{0:T(128)S(1)} %pad_add_fusion.ids, bf16[960,256]{1,0:T(8,128)(2,1)} %copy-done.48, bf16[960,256]{1,0:T(8,128)(2,1)} %collective-permute-done.11.refs_1_, ...), custom_call_target="tpu_custom_call" | custom-call | flops 1258291200 | bytes 2457600 | tf_op jit(solution)/shard_map/down_grad/pallas_call | solution.py:719
  134.8 5.3 %collective-permute-start.23 = (bf16[240,1280]{1,0:T(8,128)(2,1)}, bf16[240,1280]{1,0:T(8,128)(2,1)}, u32[]{:S(2)}, u32[]{:S(2)}) collective-permute-start(bf16[240,1280]{1,0:T(8,128)(2,1)} %get-tuple-element.233), channel_id=1, source_target_pairs={{0,2},{2,0},{4,6},{6,4},{8,10},{10,8},{12,14},{14,12},{16,18},{18,... | collective-permute-start | bytes 1843208 | tf_op jit(solution)/shard_map/ppermute | solution.py:36
  143.0 10.7 %inner_grad.1 = (bf16[120,5120]{1,0:T(8,128)(2,1)}, bf16[120,5120]{1,0:T(8,128)(2,1)}, bf16[120,5120]{1,0:T(8,128)(2,1)}, bf16[120,5120]{1,0:T(8,128)(2,1)}) custom-call(s32[2]{0:T(128)S(1)} %pad_add_fusion.ids, bf16[960,256]{1,0:T(8,128)(2,1)} %get-tuple-element.225.refs_0_, bf16[480,256]{1,0:T(8,128)(2,1)} %copy-done.60, ...), custom_call_target="tpu_custom_call" | custom-call | flops 2516582400 | bytes 4915200 | tf_op jit(solution)/shard_map/inner_grad/pallas_call | solution.py:719
  156.1 4.4 %attention_backward.2 = (bf16[960,128]{1,0:T(8,128)(2,1)S(1)}, bf16[16,64,640]{2,1,0:T(8,128)(2,1)S(1)}, bf16[16,64,640]{2,1,0:T(8,128)(2,1)S(1)}) custom-call(s32[2]{0:T(128)S(1)} %pad_add_fusion.ids, s32[2,2,2]{2,1,0:T(2,128)S(1)} %copy-done.8, s32[2,2,16]{2,1,0:T(2,128)S(1)} %copy-done.9, bf16[16,64,640]{2,1,0:T(8,128)(2,1)S(1)} %get-tuple-element.444.first_ref, ...), custom_call_target="tpu_custom_call" | custom-call | flops 157286400 | bytes 655360 | tf_op jit(solution)/shard_map/attention_backward/pallas_call | solution.py:527
  164.3 18.3 %collective-permute-done.25 = bf16[120,5120]{1,0:T(8,128)(2,1)S(1)} collective-permute-done((bf16[120,5120]{1,0:T(8,128)(2,1)}, bf16[120,5120]{1,0:T(8,128)(2,1)S(1)}, u32[]{:S(2)}, u32[]{:S(2)}) %collective-permute-start.25) | collective-permute-done | bytes 1228832 | tf_op jit(solution)/shard_map/ppermute | solution.py:36
  191.3 4.2 %attention_backward.3 = (bf16[960,128]{1,0:T(8,128)(2,1)S(1)}, bf16[16,64,640]{2,1,0:T(8,128)(2,1)S(1)}, bf16[16,64,640]{2,1,0:T(8,128)(2,1)S(1)}) custom-call(s32[2]{0:T(128)S(1)} %pad_add_fusion.ids, s32[2,2,2]{2,1,0:T(2,128)S(1)} %copy-done.8, s32[2,2,16]{2,1,0:T(2,128)S(1)} %copy-done.9, bf16[16,64,640]{2,1,0:T(8,128)(2,1)S(1)} %copy-done.1, ...), custom_call_target="tpu_custom_call" | custom-call | flops 157286400 | bytes 655360 | tf_op jit(solution)/shard_map/attention_backward/pallas_call | solution.py:527
  195.7 5.6 %collective-permute-start.40 = (bf16[480,256]{1,0:T(8,128)(2,1)S(1)}, bf16[480,256]{1,0:T(8,128)(2,1)S(1)}, u32[]{:S(2)}, u32[]{:S(2)}) collective-permute-start(bf16[480,256]{1,0:T(8,128)(2,1)S(1)} %fusion.13), channel_id=1, source_target_pairs={{0,1},{1,0},{2,3},{3,2},{4,5},{5,4},{6,7},{7,6},{8,9},{9,8},{10,11... | collective-permute-start | bytes 737288 | tf_op jit(solution)/shard_map/ppermute | solution.py:40
  201.3 4.7 %collective-permute-done.30 = bf16[8,64,640]{2,1,0:T(8,128)(2,1)S(1)} collective-permute-done((bf16[8,64,640]{2,1,0:T(8,128)(2,1)S(1)}, bf16[8,64,640]{2,1,0:T(8,128)(2,1)S(1)}, u32[]{:S(2)}, u32[]{:S(2)}) %collective-permute-start.30) | collective-permute-done | bytes 655392 | tf_op jit(solution)/shard_map/ppermute | solution.py:36
  215.2 7.9 %collective-permute-done.33 = bf16[120,2560]{1,0:T(8,128)(2,1)S(1)} collective-permute-done((bf16[120,2560]{1,0:T(8,128)(2,1)S(1)}, bf16[120,2560]{1,0:T(8,128)(2,1)S(1)}, u32[]{:S(2)}, u32[]{:S(2)}) %collective-permute-start.33) | collective-permute-done | bytes 614432 | tf_op jit(solution)/shard_map/ppermute | solution.py:36
  228.1 5.2 %query_grad.1 = (bf16[240,960]{1,0:T(8,128)(2,1)}, bf16[240,960]{1,0:T(8,128)(2,1)}, bf16[240,960]{1,0:T(8,128)(2,1)}, bf16[240,960]{1,0:T(8,128)(2,1)}) custom-call(s32[2]{0:T(128)S(1)} %pad_add_fusion.ids, bf16[960,256]{1,0:T(8,128)(2,1)} %copy-done.14, bf16[480,256]{1,0:T(8,128)(2,1)} %copy-done.24, bf16[960,256]{1,0:T(8,128)(2,1)} %copy-done.21, ...), custom_call_target="tpu_custom_call" | custom-call | flops 943718400 | bytes 1843200 | tf_op jit(solution)/shard_map/query_grad/pallas_call | solution.py:719
  247.6 4.4 %collective-permute-done.43 = bf16[120,640]{1,0:T(8,128)(2,1)S(1)} collective-permute-done((bf16[120,640]{1,0:T(8,128)(2,1)S(1)}, bf16[120,640]{1,0:T(8,128)(2,1)S(1)}, u32[]{:S(2)}, u32[]{:S(2)}) %collective-permute-start.43) | collective-permute-done | bytes 153632 | tf_op jit(solution)/shard_map/ppermute | solution.py:36
  261.7 7.3 %collective-permute-done.49 = bf16[240,640]{1,0:T(8,128)(2,1)S(1)} collective-permute-done((bf16[240,640]{1,0:T(8,128)(2,1)S(1)}, bf16[240,640]{1,0:T(8,128)(2,1)S(1)}, u32[]{:S(2)}, u32[]{:S(2)}) %collective-permute-start.49) | collective-permute-done | bytes 307232 | tf_op jit(solution)/shard_map/ppermute | solution.py:36
  280.4 8.8 %collective-permute-done.54 = bf16[120,960]{1,0:T(8,128)(2,1)S(1)} collective-permute-done((bf16[120,960]{1,0:T(8,128)(2,1)S(1)}, bf16[120,960]{1,0:T(8,128)(2,1)S(1)}, u32[]{:S(2)}, u32[]{:S(2)}) %collective-permute-start.54) | collective-permute-done | bytes 230432 | tf_op jit(solution)/shard_map/ppermute | solution.py:36
  297.6 4.0 %collective-permute-done.58 = bf16[120,960]{1,0:T(8,128)(2,1)S(1)} collective-permute-done((bf16[120,960]{1,0:T(8,128)(2,1)S(1)}, bf16[120,960]{1,0:T(8,128)(2,1)S(1)}, u32[]{:S(2)}, u32[]{:S(2)}) %collective-permute-start.58) | collective-permute-done | bytes 230432 | tf_op jit(solution)/shard_map/ppermute | solution.py:36
  303.5 10.2 %collective-permute-done.59 = bf16[2,256,640]{2,1,0:T(8,128)(2,1)S(1)} collective-permute-done((bf16[2,256,640]{2,1,0:T(8,128)(2,1)S(1)}, bf16[2,256,640]{2,1,0:T(8,128)(2,1)S(1)}, u32[]{:S(2)}, u32[]{:S(2)}) %collective-permute-start.59) | collective-permute-done | bytes 655392 | tf_op jit(solution)/shard_map/ppermute | solution.py:36
  320.4 7.2 %collective-permute-done.61 = bf16[120,2560]{1,0:T(8,128)(2,1)} collective-permute-done((bf16[120,2560]{1,0:T(8,128)(2,1)S(1)}, bf16[120,2560]{1,0:T(8,128)(2,1)}, u32[]{:S(2)}, u32[]{:S(2)}) %collective-permute-start.61) | collective-permute-done | bytes 614432 | tf_op jit(solution)/shard_map/ppermute | solution.py:36
  329.4 5.5 %collective-permute-done.66 = bf16[120,480]{1,0:T(8,128)(2,1)S(1)} collective-permute-done((bf16[120,480]{1,0:T(8,128)(2,1)S(1)}, bf16[120,480]{1,0:T(8,128)(2,1)S(1)}, u32[]{:S(2)}, u32[]{:S(2)}) %collective-permute-start.66) | collective-permute-done | bytes 115232 | tf_op jit(solution)/shard_map/ppermute | solution.py:36
  350.6 7.9 %collective-permute-done.74 = f32[960]{0:T(1024)S(1)} collective-permute-done((f32[960]{0:T(1024)S(1)}, f32[960]{0:T(1024)S(1)}, u32[]{:S(2)}, u32[]{:S(2)}) %collective-permute-start.74) | collective-permute-done | bytes 3872 | tf_op jit(solution)/shard_map/ppermute | solution.py:36
  (446 shorter events, 200.5 us)
Async XLA Ops:
  7.2 97.5 %all-gather.5.cloned.1.call-start = ((), (), s32[]{:S(2)}) async-start(), calls=%async_computation | async-start | bytes 2949120 | tf_op jit(solution)/shard_map/all_gather | solution.py:806
  7.9 96.7 %all-gather.7.cloned.1.call-start = ((), (), s32[]{:S(2)}) async-start(), calls=%async_computation.1 | async-start | bytes 7372800 | tf_op jit(solution)/shard_map/all_gather | solution.py:806
  8.7 96.0 %all-gather.9.cloned.1.call-start = ((), (), s32[]{:S(2)}) async-start(), calls=%async_computation.2 | async-start | bytes 7372800 | tf_op jit(solution)/shard_map/all_gather | solution.py:806
  9.4 95.2 %all-gather.11.cloned.1.call-start = ((), (), s32[]{:S(2)}) async-start(), calls=%async_computation.3 | async-start | bytes 7372800 | tf_op jit(solution)/shard_map/all_gather | solution.py:806
  44.8 35.1 %collective-permute-start.11 = (bf16[960,256]{1,0:T(8,128)(2,1)S(1)}, bf16[960,256]{1,0:T(8,128)(2,1)}, u32[]{:S(2)}, u32[]{:S(2)}) collective-permute-start(bf16[960,256]{1,0:T(8,128)(2,1)S(1)} %pad_maximum_fusion.30.cot_ref.refs_0_), channel_id=1, source_target_pairs={{0,1},{1,0},{2,3},{3,2},{4,5},{5,4},{6,7},{7,6},{8,9},{9,8},{10,11... | collective-permute-start | bytes 1474568 | tf_op jit(solution)/shard_map/ppermute | solution.py:40
  54.8 22.8 %collective-permute-start.16 = (bf16[1,480,512]{2,1,0:T(8,128)(2,1)S(1)}, bf16[1,480,512]{2,1,0:T(8,128)(2,1)S(1)}, u32[]{:S(2)}, u32[]{:S(2)}) collective-permute-start(bf16[1,480,512]{2,1,0:T(8,128)(2,1)S(1)} %maximum_bitcast_fusion), channel_id=1, source_target_pairs={{0,16},{2,18},{4,20},{6,22},{8,24},{10,26},{12,28},{14,30},{16,0},... | collective-permute-start | bytes 1474568 | tf_op jit(solution)/shard_map/ppermute | solution.py:36
  56.8 24.0 %collective-permute-start.13 = (bf16[8,64,640]{2,1,0:T(8,128)(2,1)S(1)}, bf16[8,64,640]{2,1,0:T(8,128)(2,1)S(1)}, u32[]{:S(2)}, u32[]{:S(2)}) collective-permute-start(bf16[8,64,640]{2,1,0:T(8,128)(2,1)S(1)} %pad_maximum_fusion.21), channel_id=1, source_target_pairs={{0,4},{2,6},{4,0},{6,2},{8,12},{10,14},{12,8},{14,10},{16,20},{18,... | collective-permute-start | bytes 1966088 | tf_op jit(solution)/shard_map/ppermute | solution.py:36
  60.9 19.9 %collective-permute-start.12 = (bf16[8,64,640]{2,1,0:T(8,128)(2,1)S(1)}, bf16[8,64,640]{2,1,0:T(8,128)(2,1)S(1)}, u32[]{:S(2)}, u32[]{:S(2)}) collective-permute-start(bf16[8,64,640]{2,1,0:T(8,128)(2,1)S(1)} %pad_maximum_fusion.20), channel_id=1, source_target_pairs={{0,2},{2,0},{4,6},{6,4},{8,10},{10,8},{12,14},{14,12},{16,18},{18,... | collective-permute-start | bytes 1966088 | tf_op jit(solution)/shard_map/ppermute | solution.py:36
  79.9 22.2 %collective-permute-start.19 = (bf16[2,480,512]{2,1,0:T(8,128)(2,1)S(1)}, bf16[2,480,512]{2,1,0:T(8,128)(2,1)S(1)}, u32[]{:S(2)}, u32[]{:S(2)}) collective-permute-start(bf16[2,480,512]{2,1,0:T(8,128)(2,1)S(1)} %pad_maximum_fusion.15), channel_id=1, source_target_pairs={{0,8},{2,10},{4,12},{6,14},{8,0},{10,2},{12,4},{14,6},{16,24},{18,... | collective-permute-start | bytes 2949128 | tf_op jit(solution)/shard_map/ppermute | solution.py:36
  134.8 20.9 %collective-permute-start.23 = (bf16[240,1280]{1,0:T(8,128)(2,1)}, bf16[240,1280]{1,0:T(8,128)(2,1)}, u32[]{:S(2)}, u32[]{:S(2)}) collective-permute-start(bf16[240,1280]{1,0:T(8,128)(2,1)} %get-tuple-element.233), channel_id=1, source_target_pairs={{0,2},{2,0},{4,6},{6,4},{8,10},{10,8},{12,14},{14,12},{16,18},{18,... | collective-permute-start | bytes 1843208 | tf_op jit(solution)/shard_map/ppermute | solution.py:36
  153.7 29.0 %collective-permute-start.25 = (bf16[120,5120]{1,0:T(8,128)(2,1)}, bf16[120,5120]{1,0:T(8,128)(2,1)S(1)}, u32[]{:S(2)}, u32[]{:S(2)}) collective-permute-start(bf16[120,5120]{1,0:T(8,128)(2,1)} %get-tuple-element.241), channel_id=1, source_target_pairs={{0,2},{2,0},{4,6},{6,4},{8,10},{10,8},{12,14},{14,12},{16,18},{18,... | collective-permute-start | bytes 3686408 | tf_op jit(solution)/shard_map/ppermute | solution.py:36
  155.7 28.4 %collective-permute-start.26 = (bf16[120,5120]{1,0:T(8,128)(2,1)}, bf16[120,5120]{1,0:T(8,128)(2,1)S(1)}, u32[]{:S(2)}, u32[]{:S(2)}) collective-permute-start(bf16[120,5120]{1,0:T(8,128)(2,1)} %get-tuple-element.242), channel_id=1, source_target_pairs={{0,4},{2,6},{4,0},{6,2},{8,12},{10,14},{12,8},{14,10},{16,20},{18,... | collective-permute-start | bytes 3686408 | tf_op jit(solution)/shard_map/ppermute | solution.py:36
  186.0 20.0 %collective-permute-start.30 = (bf16[8,64,640]{2,1,0:T(8,128)(2,1)S(1)}, bf16[8,64,640]{2,1,0:T(8,128)(2,1)S(1)}, u32[]{:S(2)}, u32[]{:S(2)}) collective-permute-start(bf16[8,64,640]{2,1,0:T(8,128)(2,1)S(1)} %slice.159), channel_id=1, source_target_pairs={{0,2},{2,0},{4,6},{6,4},{8,10},{10,8},{12,14},{14,12},{16,18},{18,... | collective-permute-start | bytes 1966088 | tf_op jit(solution)/shard_map/ppermute | solution.py:36
  186.4 19.6 %collective-permute-start.31 = (bf16[8,64,640]{2,1,0:T(8,128)(2,1)S(1)}, bf16[8,64,640]{2,1,0:T(8,128)(2,1)S(1)}, u32[]{:S(2)}, u32[]{:S(2)}) collective-permute-start(bf16[8,64,640]{2,1,0:T(8,128)(2,1)S(1)} %slice.160), channel_id=1, source_target_pairs={{0,4},{2,6},{4,0},{6,2},{8,12},{10,14},{12,8},{14,10},{16,20},{18,... | collective-permute-start | bytes 1966088 | tf_op jit(solution)/shard_map/ppermute | solution.py:36
  195.7 31.6 %collective-permute-start.40 = (bf16[480,256]{1,0:T(8,128)(2,1)S(1)}, bf16[480,256]{1,0:T(8,128)(2,1)S(1)}, u32[]{:S(2)}, u32[]{:S(2)}) collective-permute-start(bf16[480,256]{1,0:T(8,128)(2,1)S(1)} %fusion.13), channel_id=1, source_target_pairs={{0,1},{1,0},{2,3},{3,2},{4,5},{5,4},{6,7},{7,6},{8,9},{9,8},{10,11... | collective-permute-start | bytes 737288 | tf_op jit(solution)/shard_map/ppermute | solution.py:40
  213.1 22.7 %collective-permute-start.36 = (bf16[8,64,640]{2,1,0:T(8,128)(2,1)S(1)}, bf16[8,64,640]{2,1,0:T(8,128)(2,1)S(1)}, u32[]{:S(2)}, u32[]{:S(2)}) collective-permute-start(bf16[8,64,640]{2,1,0:T(8,128)(2,1)S(1)} %slice.162), channel_id=1, source_target_pairs={{0,2},{2,0},{4,6},{6,4},{8,10},{10,8},{12,14},{14,12},{16,18},{18,... | collective-permute-start | bytes 1966088 | tf_op jit(solution)/shard_map/ppermute | solution.py:36
  214.5 22.6 %collective-permute-start.37 = (bf16[8,64,640]{2,1,0:T(8,128)(2,1)S(1)}, bf16[8,64,640]{2,1,0:T(8,128)(2,1)S(1)}, u32[]{:S(2)}, u32[]{:S(2)}) collective-permute-start(bf16[8,64,640]{2,1,0:T(8,128)(2,1)S(1)} %slice.163), channel_id=1, source_target_pairs={{0,4},{2,6},{4,0},{6,2},{8,12},{10,14},{12,8},{14,10},{16,20},{18,... | collective-permute-start | bytes 1966088 | tf_op jit(solution)/shard_map/ppermute | solution.py:36
  227.4 19.4 %collective-permute-start.41 = (bf16[4,64,640]{2,1,0:T(8,128)(2,1)S(1)}, bf16[4,64,640]{2,1,0:T(8,128)(2,1)S(1)}, u32[]{:S(2)}, u32[]{:S(2)}) collective-permute-start(bf16[4,64,640]{2,1,0:T(8,128)(2,1)S(1)} %slice.198), channel_id=1, source_target_pairs={{0,4},{2,6},{4,0},{6,2},{8,12},{10,14},{12,8},{14,10},{16,20},{18,... | collective-permute-start | bytes 983048 | tf_op jit(solution)/shard_map/ppermute | solution.py:36
  293.5 20.3 %collective-permute-start.59 = (bf16[2,256,640]{2,1,0:T(8,128)(2,1)S(1)}, bf16[2,256,640]{2,1,0:T(8,128)(2,1)S(1)}, u32[]{:S(2)}, u32[]{:S(2)}) collective-permute-start(bf16[2,256,640]{2,1,0:T(8,128)(2,1)S(1)} %slice.177), channel_id=1, source_target_pairs={{0,8},{2,10},{4,12},{6,14},{8,0},{10,2},{12,4},{14,6},{16,24},{18,... | collective-permute-start | bytes 1966088 | tf_op jit(solution)/shard_map/ppermute | solution.py:36
  295.4 21.0 %collective-permute-start.62 = (bf16[240,1280]{1,0:T(8,128)(2,1)S(1)}, bf16[240,1280]{1,0:T(8,128)(2,1)S(1)}, u32[]{:S(2)}, u32[]{:S(2)}) collective-permute-start(bf16[240,1280]{1,0:T(8,128)(2,1)S(1)} %pad_maximum_fusion.26), channel_id=1, source_target_pairs={{0,2},{2,0},{4,6},{6,4},{8,10},{10,8},{12,14},{14,12},{16,18},{18,... | collective-permute-start | bytes 1843208 | tf_op jit(solution)/shard_map/ppermute | solution.py:36
  297.3 19.6 %collective-permute-start.63 = (bf16[240,1280]{1,0:T(8,128)(2,1)S(1)}, bf16[240,1280]{1,0:T(8,128)(2,1)S(1)}, u32[]{:S(2)}, u32[]{:S(2)}) collective-permute-start(bf16[240,1280]{1,0:T(8,128)(2,1)S(1)} %pad_maximum_fusion.27), channel_id=1, source_target_pairs={{0,4},{2,6},{4,0},{6,2},{8,12},{10,14},{12,8},{14,10},{16,20},{18,... | collective-permute-start | bytes 1843208 | tf_op jit(solution)/shard_map/ppermute | solution.py:36
  301.7 25.9 %collective-permute-start.61 = (bf16[120,2560]{1,0:T(8,128)(2,1)S(1)}, bf16[120,2560]{1,0:T(8,128)(2,1)}, u32[]{:S(2)}, u32[]{:S(2)}) collective-permute-start(bf16[120,2560]{1,0:T(8,128)(2,1)S(1)} %get-tuple-element.344), channel_id=1, source_target_pairs={{0,2},{2,0},{4,6},{6,4},{8,10},{10,8},{12,14},{14,12},{16,18},{18,... | collective-permute-start | bytes 1843208 | tf_op jit(solution)/shard_map/ppermute | solution.py:36
  303.3 24.8 %collective-permute-start.60 = (bf16[120,2560]{1,0:T(8,128)(2,1)S(1)}, bf16[120,2560]{1,0:T(8,128)(2,1)}, u32[]{:S(2)}, u32[]{:S(2)}) collective-permute-start(bf16[120,2560]{1,0:T(8,128)(2,1)S(1)} %get-tuple-element.340), channel_id=1, source_target_pairs={{0,4},{2,6},{4,0},{6,2},{8,12},{10,14},{12,8},{14,10},{16,20},{18,... | collective-permute-start | bytes 1843208 | tf_op jit(solution)/shard_map/ppermute | solution.py:36
  313.9 21.0 %collective-permute-start.65 = (bf16[1,256,640]{2,1,0:T(8,128)(2,1)S(1)}, bf16[1,256,640]{2,1,0:T(8,128)(2,1)S(1)}, u32[]{:S(2)}, u32[]{:S(2)}) collective-permute-start(bf16[1,256,640]{2,1,0:T(8,128)(2,1)S(1)} %slice.207), channel_id=1, source_target_pairs={{0,16},{2,18},{4,20},{6,22},{8,24},{10,26},{12,28},{14,30},{16,0},... | collective-permute-start | bytes 983048 | tf_op jit(solution)/shard_map/ppermute | solution.py:36
  (127 other events, 1244.9 us)
Sparse Core Ops, SparseCore 0:
  9.6 13.0 all-gather.4
  24.2 15.8 all-gather.6
  41.7 15.8 all-gather.8
  59.0 15.8 all-gather.10

commit v6 on v5

--- a/solution.py
+++ b/solution.py
@@ -33,7 +33,8 @@
 
 def flip_ctx(value, bit):
     size = lax.axis_size("ctx")
-    return lax.ppermute(value, "ctx", [(i, i ^ (1 << bit)) for i in range(size)])
+    mask = sum(1 << b for b in bit) if isinstance(bit, tuple) else 1 << bit
+    return lax.ppermute(value, "ctx", [(i, i ^ mask) for i in range(size)])
 
 
 def swap_fsdp(value):
@@ -68,12 +69,15 @@
 class GatherBlocks:
     def __init__(self, block):
         self.held = block[None]
-        self.stages = high_bits()[::-1] + [None, None]
+        bits = high_bits()[::-1]
+        self.stages = [tuple(bits[i : i + 2]) for i in range(0, len(bits), 2)] + [None, None]
         self.halves = None
 
     def operands(self):
-        if self.stages[0] is not None:
-            return [self.held], [self.stages[0]]
+        stage = self.stages[0]
+        if stage is not None:
+            hops = list(stage) + ([stage] if len(stage) == 2 else [])
+            return [self.held] * len(hops), hops
         if self.halves is None:
             self.halves = [self.held[:, :HALF], self.held[:, HALF:]]
             self.bits = (1, 0)
@@ -81,7 +85,7 @@
 
     def absorb(self, arrived):
         if self.stages.pop(0) is not None:
-            self.held = jnp.concatenate([self.held, arrived[0]], axis=0)
+            self.held = jnp.concatenate([self.held, *arrived], axis=0)
         else:
             self.halves = [
                 jnp.concatenate([h, a], axis=0) for h, a in zip(self.halves, arrived)
@@ -512,7 +516,7 @@
         in_specs=[SMEM_SPEC] * 3 + [VMEM_SPEC] * 3,
         out_specs=(VMEM_SPEC,) * 2,
         scratch_shapes=[pltpu.VMEM((LANES, HEADS * BLK), bf16), pltpu.VMEM((LANES, GCOLS), f32)],
-        compiler_params=pltpu.CompilerParams(vmem_limit_bytes=8 << 20),
+        compiler_params=pltpu.CompilerParams(vmem_limit_bytes=4 << 20),
         cost_estimate=pl.CostEstimate(
             flops=4 * HEADS * HD * BLK * BLK * 8,
             bytes_accessed=first.size * 4,
@@ -542,7 +546,7 @@
             pltpu.VMEM((2 * BLK, 2 * KVH * GCOLS), bf16),
             pltpu.VMEM((HD, HEADS * BLK), f32),
         ],
-        compiler_params=pltpu.CompilerParams(vmem_limit_bytes=16 << 20),
+        compiler_params=pltpu.CompilerParams(vmem_limit_bytes=8 << 20),
         cost_estimate=pl.CostEstimate(
             flops=10 * HEADS * HD * BLK * BLK,
             bytes_accessed=first.size,
@@ -666,7 +670,7 @@
             pltpu.VMEM((rows, width), f32),
             pltpu.VMEM((rows, width), f32),
         ],
-        compiler_params=pltpu.CompilerParams(vmem_limit_bytes=32 << 20),
+        compiler_params=pltpu.CompilerParams(vmem_limit_bytes=26 << 20),
         cost_estimate=pl.CostEstimate(
             flops=12 * rows * width * inner,
             bytes_accessed=8 * width * inner,
@@ -725,7 +729,7 @@
             out_specs=[pl.BlockSpec((rows, tile), lambda i, ids: (0, i)) for rows, _ in shapes],
         ),
         out_shape=[pltpu.HBM(shape, bf16) for shape in shapes],
-        compiler_params=pltpu.CompilerParams(vmem_limit_bytes=16 << 20),
+        compiler_params=pltpu.CompilerParams(vmem_limit_bytes=11 << 20),
         cost_estimate=pl.CostEstimate(
             flops=2 * sum(rows * width for rows, width in shapes) * 512,
             bytes_accessed=2 * sum(rows * width for rows, width in shapes),
@@ -767,7 +771,7 @@
         out_specs=pl.BlockSpec((rows, columns), lambda i: (0, 0)),
         out_shape=jax.ShapeDtypeStruct((rows, columns), bf16),
         scratch_shapes=[pltpu.VMEM((rows, columns), f32)],
-        compiler_params=pltpu.CompilerParams(vmem_limit_bytes=12 << 20),
+        compiler_params=pltpu.CompilerParams(vmem_limit_bytes=5 << 20),
         cost_estimate=pl.CostEstimate(
             flops=2 * left.size * columns,
             bytes_accessed=2 * (left.size + 2 * own.size),
@@ -826,38 +830,38 @@
     keyvals = dot(normed_t, keyval_full, 0, 0).astype(bf16)
     gathers = [GatherBlocks(keyvals[m * BLK : (m + 1) * BLK]) for m in range(micro)]
 
-    rounds.begin(gathers[0])
+    rounds.begin(*gathers)
     (w_query, gain_mlp, cotangent, normed_t) = rounds.end(
         gathers[:1], w_query, gain_mlp, cotangent, normed_t
     )
-    rounds.begin(*gathers)
+    while len(gathers[0].stages) > 2:
+        rounds.end(gathers[1:])
+        rounds.begin(*gathers)
+        rounds.end(gathers[:1])
+
+    half = normed_t.shape[0] // 2
+    rounds.begin(gathers[0])
     query_other, gain_other = swap_fsdp(w_query), swap_fsdp(gain_mlp)
+    normed_other = swap_fsdp(theirs(normed_t, 0))
+    (query_other, gain_other, normed_other) = rounds.end(
+        gathers[:1], query_other, gain_other, normed_other
+    )
+    rounds.begin(gathers[0])
+    normed_mine = lax.dynamic_slice_in_dim(normed_t, shard * half, half, 0)
+    column = GatherHigh(jnp.concatenate([normed_mine, normed_other], axis=1))
+    rounds.begin(column)
     cot_t = tokens_last(cotangent)
-    (query_other, gain_other, cot_t) = rounds.end(gathers, query_other, gain_other, cot_t)
-    half = normed_t.shape[0] // 2
-    normed_mine = lax.dynamic_slice_in_dim(normed_t, shard * half, half, 0)
-    for step in range(len(gathers[0].stages)):
-        rounds.begin(*[g for g in gathers if len(g.stages) > 2 or g is gathers[0]])
-        if step == 0:
-            normed_other = swap_fsdp(theirs(normed_t, 0))
-            query_full = joined(w_query, query_other)
-            mlp_gain = joined(gain_mlp, gain_other).astype(f32)[None]
-            (normed_other, mlp_gain) = rounds.end(list(rounds.flying), normed_other, mlp_gain)
-        elif step == 1:
-            column = GatherHigh(jnp.concatenate([normed_mine, normed_other], axis=1))
-            rounds.begin(column)
-            cot_other = swap_fsdp(cot_t)
-            queries_t = dot(query_full, normed_t, 0, 0).astype(bf16)
-            (cot_other, queries_t) = rounds.end(
-                [j for j in rounds.flying if j is not column], cot_other, queries_t
-            )
-        else:
-            rounds.end([j for j in rounds.flying if j is not column])
+    query_full = joined(w_query, query_other)
+    mlp_gain = joined(gain_mlp, gain_other).astype(f32)[None]
+    (cot_t, mlp_gain) = rounds.end(gathers, cot_t, mlp_gain)
+
+    rounds.begin(gathers[1])
+    cot_other = swap_fsdp(cot_t)
+    queries_t = dot(query_full, normed_t, 0, 0).astype(bf16)
+    (cot_other, queries_t) = rounds.end([gathers[1], column], cot_other, queries_t)
     queries = [queries_t[:, m * BLK : (m + 1) * BLK] for m in range(micro)]
     tables = (ids, seq_blocks, block_slots)
 
-    rounds.begin(gathers[1])
-    rounds.end([gathers[1], column])
     rounds.begin(gathers[1], column)
     first = attention_forward(0, tables, *gathers[0].halves, queries[0])
     first = rounds.end(gathers[1:], *first)

time: 408 us -> 409 us (level)
  waiting for transfers between devices: 185 us -> 159 us
  Pallas kernels: 57.2 us -> 82.3 us
    ppermute x72 -> x74, waiting for transfers between devices: 178 us -> 151 us  [flip_ctx(): return lax.ppermute(value, 'ctx', [(i, i ^ mask) for i in range(size)])]
    pallas_call x2, Pallas kernels: 8.61 us -> 22.6 us  [attention_backward(): pl.pallas_call(functools.partial(backward_kernel, steps > WINDOW // BLK,...]
    pallas_call x2, Pallas kernels: 6.94 us -> 18.2 us  [attention_forward(): pl.pallas_call(functools.partial(forward_kernel, steps > WINDOW // BLK, s...]
    ppermute x14, starting transfers between devices: 7.97 us -> 2.29 us  [swap_fsdp(): return lax.ppermute(value, 'fsdp', [(0, 1), (1, 0)])]
    ppermute x72 -> x74, starting transfers between devices: 80.8 us -> 84 us  [flip_ctx(): return lax.ppermute(value, 'ctx', [(i, i ^ mask) for i in range(size)])]
    unnamed x123 -> x139, local copies, waits for them, and re-layouts: 12 us -> 12.6 us
  transfers between devices with their start and end apart: 90 -> 92, of which waited for: 47 -> 43; matrix products, arithmetic and copies ran while one was open for 11% -> 11% of each run, Pallas kernels for 10% -> 16%
where the time goes in v6:
time: 409 us; the launch traced here: 403 us
  waiting for transfers between devices  159 us (39%)
  starting transfers between devices  86.4 us (21%)
  Pallas kernels  82.3 us (20%)
  other arithmetic  39.8 us (10%)
  local copies, waits for them, and re-layouts  16.3 us (4%)
  between operations  15.9 us (4%)
    ppermute x74, waiting for transfers between devices, flip_ctx(): return lax.ppermute(value, 'ctx', [(i, i ^ mask) for i in range(size)])  151 us
    ppermute x74, starting transfers between devices, flip_ctx(): return lax.ppermute(value, 'ctx', [(i, i ^ mask) for i in range(size)])  84 us
    pallas_call x2, Pallas kernels, attention_backward(): pl.pallas_call(functools.partial(backward_kernel, steps > WINDOW // BLK,...  22.6 us
    pallas_call x3, Pallas kernels, weight_grad(): pl.pallas_call(functools.partial(weight_grad_kernel, products, sides), gr...  21 us
    pallas_call x2, Pallas kernels, attention_forward(): pl.pallas_call(functools.partial(forward_kernel, steps > WINDOW // BLK, s...  18.2 us
    pallas_call x1, Pallas kernels, feed_forward(): pl.pallas_call(block_kernel, grid=(inner // tile,), in_specs=[fixed(wide)...  17.5 us
    unnamed x139, local copies, waits for them, and re-layouts  12.6 us
    convert_element_type x5, other arithmetic, rows_of(): jnp.concatenate([q[:, columns] for q in quarters], axis=0).astype(f32)  11.4 us
  transfers between devices with their start and end apart: 92, of which 43 were waited for; matrix products, arithmetic and copies ran while one was open for 11% of the time, Pallas kernels for 16%

profile of v6, /device:TPU:0, one launch (start us, length us, event | category | flops | bytes accessed | tf_op | source)
XLA Modules:
  0.0 402.6 jit_solution(6728515760239803936)
XLA Ops:
  13.3 4.9 %collective-permute-start.4 = (bf16[1,128,640]{2,1,0:T(8,128)(2,1)S(1)}, bf16[1,128,640]{2,1,0:T(8,128)(2,1)S(1)}, u32[]{:S(2)}, u32[]{:S(2)}) collective-permute-start(bf16[1,128,640]{2,1,0:T(8,128)(2,1)S(1)} %get-tuple-element.431), channel_id=1, source_target_pairs={{0,24},{2,26},{4,28},{6,30},{8,16},{10,18},{12,20},{14,22},{16,8},... | collective-permute-start | bytes 491528 | tf_op jit(solution)/shard_map/ppermute | solution.py:37
  18.8 4.4 %collective-permute-done.4 = bf16[1,128,640]{2,1,0:T(8,128)(2,1)S(1)} collective-permute-done((bf16[1,128,640]{2,1,0:T(8,128)(2,1)S(1)}, bf16[1,128,640]{2,1,0:T(8,128)(2,1)S(1)}, u32[]{:S(2)}, u32[]{:S(2)}) %collective-permute-start.4) | collective-permute-done | bytes 163872 | tf_op jit(solution)/shard_map/ppermute | solution.py:37
  23.2 4.3 %collective-permute-done.3 = bf16[1,128,640]{2,1,0:T(8,128)(2,1)S(1)} collective-permute-done((bf16[1,128,640]{2,1,0:T(8,128)(2,1)S(1)}, bf16[1,128,640]{2,1,0:T(8,128)(2,1)S(1)}, u32[]{:S(2)}, u32[]{:S(2)}) %collective-permute-start.3) | collective-permute-done | bytes 163872 | tf_op jit(solution)/shard_map/ppermute | solution.py:37
  27.4 5.1 %collective-permute-done.2 = bf16[1,128,640]{2,1,0:T(8,128)(2,1)S(1)} collective-permute-done((bf16[1,128,640]{2,1,0:T(8,128)(2,1)S(1)}, bf16[1,128,640]{2,1,0:T(8,128)(2,1)S(1)}, u32[]{:S(2)}, u32[]{:S(2)}) %collective-permute-start.2) | collective-permute-done | bytes 163872 | tf_op jit(solution)/shard_map/ppermute | solution.py:37
  52.5 12.1 %collective-permute-done.12 = bf16[1,128,640]{2,1,0:T(8,128)(2,1)S(1)} collective-permute-done((bf16[1,128,640]{2,1,0:T(8,128)(2,1)S(1)}, bf16[1,128,640]{2,1,0:T(8,128)(2,1)S(1)}, u32[]{:S(2)}, u32[]{:S(2)}) %collective-permute-start.12) | collective-permute-done | bytes 163872 | tf_op jit(solution)/shard_map/ppermute | solution.py:37
  79.4 8.1 %attention_forward.2 = (f32[960,128]{1,0:T(8,128)S(1)}, f32[1,1920]{1,0:T(1,128)S(1)}) custom-call(s32[2]{0:T(128)S(1)} %pad_add_fusion.ids, s32[2,2,2]{2,1,0:T(2,128)S(1)} %copy-done.8, s32[2,2,16]{2,1,0:T(2,128)S(1)} %copy-done.9, bf16[16,64,640]{2,1,0:T(8,128)(2,1)S(1)} %get-tuple-element.448.first_ref, ...), custom_call_target="tpu_custom_call" | custom-call | flops 503316480 | bytes 2621440 | tf_op jit(solution)/shard_map/attention_forward/pallas_call | solution.py:508
  93.7 10.1 %attention_forward.3 = (f32[960,128]{1,0:T(8,128)S(1)}, f32[1,1920]{1,0:T(1,128)S(1)}) custom-call(s32[2]{0:T(128)S(1)} %pad_add_fusion.ids, s32[2,2,2]{2,1,0:T(2,128)S(1)} %copy-done.8, s32[2,2,16]{2,1,0:T(2,128)S(1)} %copy-done.9, bf16[16,64,640]{2,1,0:T(8,128)(2,1)S(1)} %pad_maximum_fusion.4.first_ref, ...), custom_call_target="tpu_custom_call" | custom-call | flops 503316480 | bytes 2621440 | tf_op jit(solution)/shard_map/attention_forward/pallas_call | solution.py:508
  106.4 17.5 %feed_forward.1 = (bf16[256,2560]{1,0:T(8,128)(2,1)}, bf16[2,256,2560]{2,1,0:T(8,128)(2,1)}, bf16[960,256]{1,0:T(8,128)(2,1)}, bf16[960,256]{1,0:T(8,128)(2,1)},...) custom-call(bf16[960,256]{1,0:T(8,128)(2,1)} %pad_maximum_fusion.29.x_ref, ...), custom_call_target="tpu_custom_call" | custom-call | flops 7549747200 | bytes 19660800 | tf_op jit(solution)/shard_map/feed_forward/pallas_call | solution.py:641
  130.7 5.2 %down_grad.1 = (bf16[240,1280]{1,0:T(8,128)(2,1)}, bf16[240,1280]{1,0:T(8,128)(2,1)}, bf16[240,1280]{1,0:T(8,128)(2,1)}, bf16[240,1280]{1,0:T(8,128)(2,1)}) custom-call(s32[2]{0:T(128)S(1)} %pad_add_fusion.ids, bf16[960,256]{1,0:T(8,128)(2,1)} %copy-done.55, bf16[960,256]{1,0:T(8,128)(2,1)} %copy-done.65, bf16[256,2560]{1,0:T(8,128)(2,1)} %get-tuple-element.224.refs_2_, ...), custom_call_target="tpu_custom_call" | custom-call | flops 1258291200 | bytes 2457600 | tf_op jit(solution)/shard_map/down_grad/pallas_call | solution.py:723
  140.4 10.6 %inner_grad.1 = (bf16[120,5120]{1,0:T(8,128)(2,1)}, bf16[120,5120]{1,0:T(8,128)(2,1)}, bf16[120,5120]{1,0:T(8,128)(2,1)}, bf16[120,5120]{1,0:T(8,128)(2,1)}) custom-call(s32[2]{0:T(128)S(1)} %pad_add_fusion.ids, bf16[960,256]{1,0:T(8,128)(2,1)} %get-tuple-element.229.refs_0_, bf16[480,256]{1,0:T(8,128)(2,1)} %copy-done.68, ...), custom_call_target="tpu_custom_call" | custom-call | flops 2516582400 | bytes 4915200 | tf_op jit(solution)/shard_map/inner_grad/pallas_call | solution.py:723
  154.0 10.0 %attention_backward.2 = (bf16[960,128]{1,0:T(8,128)(2,1)S(1)}, bf16[16,64,640]{2,1,0:T(8,128)(2,1)S(1)}, bf16[16,64,640]{2,1,0:T(8,128)(2,1)S(1)}) custom-call(s32[2]{0:T(128)S(1)} %pad_add_fusion.ids, s32[2,2,2]{2,1,0:T(2,128)S(1)} %copy-done.8, s32[2,2,16]{2,1,0:T(2,128)S(1)} %copy-done.9, bf16[16,64,640]{2,1,0:T(8,128)(2,1)S(1)} %get-tuple-element.448.first_ref, ...), custom_call_target="tpu_custom_call" | custom-call | flops 157286400 | bytes 655360 | tf_op jit(solution)/shard_map/attention_backward/pallas_call | solution.py:531
  167.8 12.2 %collective-permute-done.27 = bf16[120,5120]{1,0:T(8,128)(2,1)S(1)} collective-permute-done((bf16[120,5120]{1,0:T(8,128)(2,1)}, bf16[120,5120]{1,0:T(8,128)(2,1)S(1)}, u32[]{:S(2)}, u32[]{:S(2)}) %collective-permute-start.27) | collective-permute-done | bytes 1228832 | tf_op jit(solution)/shard_map/ppermute | solution.py:37
  188.7 12.6 %attention_backward.3 = (bf16[960,128]{1,0:T(8,128)(2,1)S(1)}, bf16[16,64,640]{2,1,0:T(8,128)(2,1)S(1)}, bf16[16,64,640]{2,1,0:T(8,128)(2,1)S(1)}) custom-call(s32[2]{0:T(128)S(1)} %pad_add_fusion.ids, s32[2,2,2]{2,1,0:T(2,128)S(1)} %copy-done.8, s32[2,2,16]{2,1,0:T(2,128)S(1)} %copy-done.9, bf16[16,64,640]{2,1,0:T(8,128)(2,1)S(1)} %copy-done.1, ...), custom_call_target="tpu_custom_call" | custom-call | flops 157286400 | bytes 655360 | tf_op jit(solution)/shard_map/attention_backward/pallas_call | solution.py:531
  206.7 4.8 %collective-permute-done.37 = bf16[240,640]{1,0:T(8,128)(2,1)S(1)} collective-permute-done((bf16[240,640]{1,0:T(8,128)(2,1)S(1)}, bf16[240,640]{1,0:T(8,128)(2,1)S(1)}, u32[]{:S(2)}, u32[]{:S(2)}) %collective-permute-start.37) | collective-permute-done | bytes 307232 | tf_op jit(solution)/shard_map/ppermute | solution.py:37
  212.6 8.2 %collective-permute-done.35 = bf16[120,2560]{1,0:T(8,128)(2,1)S(1)} collective-permute-done((bf16[120,2560]{1,0:T(8,128)(2,1)S(1)}, bf16[120,2560]{1,0:T(8,128)(2,1)S(1)}, u32[]{:S(2)}, u32[]{:S(2)}) %collective-permute-start.35) | collective-permute-done | bytes 614432 | tf_op jit(solution)/shard_map/ppermute | solution.py:37
  226.8 5.2 %query_grad.1 = (bf16[240,960]{1,0:T(8,128)(2,1)}, bf16[240,960]{1,0:T(8,128)(2,1)}, bf16[240,960]{1,0:T(8,128)(2,1)}, bf16[240,960]{1,0:T(8,128)(2,1)}) custom-call(s32[2]{0:T(128)S(1)} %pad_add_fusion.ids, bf16[960,256]{1,0:T(8,128)(2,1)} %copy-done.14, bf16[480,256]{1,0:T(8,128)(2,1)} %copy-done.32, bf16[960,256]{1,0:T(8,128)(2,1)} %copy-done.29, ...), custom_call_target="tpu_custom_call" | custom-call | flops 943718400 | bytes 1843200 | tf_op jit(solution)/shard_map/query_grad/pallas_call | solution.py:723
  244.8 5.2 %collective-permute-done.45 = bf16[120,640]{1,0:T(8,128)(2,1)S(1)} collective-permute-done((bf16[120,640]{1,0:T(8,128)(2,1)S(1)}, bf16[120,640]{1,0:T(8,128)(2,1)S(1)}, u32[]{:S(2)}, u32[]{:S(2)}) %collective-permute-start.45) | collective-permute-done | bytes 153632 | tf_op jit(solution)/shard_map/ppermute | solution.py:37
  250.1 5.3 %collective-permute-done.46 = bf16[120,1280]{1,0:T(8,128)(2,1)S(1)} collective-permute-done((bf16[120,1280]{1,0:T(8,128)(2,1)S(1)}, bf16[120,1280]{1,0:T(8,128)(2,1)S(1)}, u32[]{:S(2)}, u32[]{:S(2)}) %collective-permute-start.46) | collective-permute-done | bytes 307232 | tf_op jit(solution)/shard_map/ppermute | solution.py:37
  260.5 8.3 %collective-permute-done.51 = bf16[240,640]{1,0:T(8,128)(2,1)S(1)} collective-permute-done((bf16[240,640]{1,0:T(8,128)(2,1)S(1)}, bf16[240,640]{1,0:T(8,128)(2,1)S(1)}, u32[]{:S(2)}, u32[]{:S(2)}) %collective-permute-start.51) | collective-permute-done | bytes 307232 | tf_op jit(solution)/shard_map/ppermute | solution.py:37
  281.7 7.3 %collective-permute-done.56 = bf16[120,960]{1,0:T(8,128)(2,1)S(1)} collective-permute-done((bf16[120,960]{1,0:T(8,128)(2,1)S(1)}, bf16[120,960]{1,0:T(8,128)(2,1)S(1)}, u32[]{:S(2)}, u32[]{:S(2)}) %collective-permute-start.56) | collective-permute-done | bytes 230432 | tf_op jit(solution)/shard_map/ppermute | solution.py:37
  304.7 9.1 %collective-permute-done.61 = bf16[2,256,640]{2,1,0:T(8,128)(2,1)S(1)} collective-permute-done((bf16[2,256,640]{2,1,0:T(8,128)(2,1)S(1)}, bf16[2,256,640]{2,1,0:T(8,128)(2,1)S(1)}, u32[]{:S(2)}, u32[]{:S(2)}) %collective-permute-start.61) | collective-permute-done | bytes 655392 | tf_op jit(solution)/shard_map/ppermute | solution.py:37
  320.7 7.1 %collective-permute-done.63 = bf16[120,2560]{1,0:T(8,128)(2,1)} collective-permute-done((bf16[120,2560]{1,0:T(8,128)(2,1)S(1)}, bf16[120,2560]{1,0:T(8,128)(2,1)}, u32[]{:S(2)}, u32[]{:S(2)}) %collective-permute-start.63) | collective-permute-done | bytes 614432 | tf_op jit(solution)/shard_map/ppermute | solution.py:37
  329.9 5.1 %collective-permute-done.68 = bf16[120,480]{1,0:T(8,128)(2,1)S(1)} collective-permute-done((bf16[120,480]{1,0:T(8,128)(2,1)S(1)}, bf16[120,480]{1,0:T(8,128)(2,1)S(1)}, u32[]{:S(2)}, u32[]{:S(2)}) %collective-permute-start.68) | collective-permute-done | bytes 115232 | tf_op jit(solution)/shard_map/ppermute | solution.py:37
  350.4 7.9 %collective-permute-done.76 = f32[960]{0:T(1024)S(1)} collective-permute-done((f32[960]{0:T(1024)S(1)}, f32[960]{0:T(1024)S(1)}, u32[]{:S(2)}, u32[]{:S(2)}) %collective-permute-start.76) | collective-permute-done | bytes 3872 | tf_op jit(solution)/shard_map/ppermute | solution.py:37
  (464 shorter events, 196.2 us)
Async XLA Ops:
  7.2 99.2 %all-gather.5.cloned.1.call-start = ((), (), s32[]{:S(2)}) async-start(), calls=%async_computation | async-start | bytes 2949120 | tf_op jit(solution)/shard_map/all_gather | solution.py:810
  7.9 98.5 %all-gather.7.cloned.1.call-start = ((), (), s32[]{:S(2)}) async-start(), calls=%async_computation.1 | async-start | bytes 7372800 | tf_op jit(solution)/shard_map/all_gather | solution.py:810
  8.7 97.7 %all-gather.9.cloned.1.call-start = ((), (), s32[]{:S(2)}) async-start(), calls=%async_computation.2 | async-start | bytes 7372800 | tf_op jit(solution)/shard_map/all_gather | solution.py:810
  9.4 97.0 %all-gather.11.cloned.1.call-start = ((), (), s32[]{:S(2)}) async-start(), calls=%async_computation.3 | async-start | bytes 7372800 | tf_op jit(solution)/shard_map/all_gather | solution.py:810
  42.9 21.6 %collective-permute-start.12 = (bf16[1,128,640]{2,1,0:T(8,128)(2,1)S(1)}, bf16[1,128,640]{2,1,0:T(8,128)(2,1)S(1)}, u32[]{:S(2)}, u32[]{:S(2)}) collective-permute-start(bf16[1,128,640]{2,1,0:T(8,128)(2,1)S(1)} %get-tuple-element.430), channel_id=1, source_target_pairs={{0,16},{2,18},{4,20},{6,22},{8,24},{10,26},{12,28},{14,30},{16,0},... | collective-permute-start | bytes 491528 | tf_op jit(solution)/shard_map/ppermute | solution.py:37
  44.2 20.3 %collective-permute-start.11 = (bf16[8,64,640]{2,1,0:T(8,128)(2,1)S(1)}, bf16[8,64,640]{2,1,0:T(8,128)(2,1)S(1)}, u32[]{:S(2)}, u32[]{:S(2)}) collective-permute-start(bf16[8,64,640]{2,1,0:T(8,128)(2,1)S(1)} %pad_maximum_fusion.21), channel_id=1, source_target_pairs={{0,4},{2,6},{4,0},{6,2},{8,12},{10,14},{12,8},{14,10},{16,20},{18,... | collective-permute-start | bytes 1966088 | tf_op jit(solution)/shard_map/ppermute | solution.py:37
  47.4 27.1 %collective-permute-start.18 = (bf16[1,480,512]{2,1,0:T(8,128)(2,1)S(1)}, bf16[1,480,512]{2,1,0:T(8,128)(2,1)S(1)}, u32[]{:S(2)}, u32[]{:S(2)}) collective-permute-start(bf16[1,480,512]{2,1,0:T(8,128)(2,1)S(1)} %maximum_bitcast_fusion), channel_id=1, source_target_pairs={{0,16},{2,18},{4,20},{6,22},{8,24},{10,26},{12,28},{14,30},{16,0},... | collective-permute-start | bytes 1474568 | tf_op jit(solution)/shard_map/ppermute | solution.py:37
  77.7 26.1 %collective-permute-start.21 = (bf16[2,480,512]{2,1,0:T(8,128)(2,1)S(1)}, bf16[2,480,512]{2,1,0:T(8,128)(2,1)S(1)}, u32[]{:S(2)}, u32[]{:S(2)}) collective-permute-start(bf16[2,480,512]{2,1,0:T(8,128)(2,1)S(1)} %pad_maximum_fusion.15), channel_id=1, source_target_pairs={{0,8},{2,10},{4,12},{6,14},{8,0},{10,2},{12,4},{14,6},{16,24},{18,... | collective-permute-start | bytes 2949128 | tf_op jit(solution)/shard_map/ppermute | solution.py:37
  151.1 29.0 %collective-permute-start.27 = (bf16[120,5120]{1,0:T(8,128)(2,1)}, bf16[120,5120]{1,0:T(8,128)(2,1)S(1)}, u32[]{:S(2)}, u32[]{:S(2)}) collective-permute-start(bf16[120,5120]{1,0:T(8,128)(2,1)} %get-tuple-element.245), channel_id=1, source_target_pairs={{0,2},{2,0},{4,6},{6,4},{8,10},{10,8},{12,14},{14,12},{16,18},{18,... | collective-permute-start | bytes 3686408 | tf_op jit(solution)/shard_map/ppermute | solution.py:37
  153.1 28.4 %collective-permute-start.28 = (bf16[120,5120]{1,0:T(8,128)(2,1)}, bf16[120,5120]{1,0:T(8,128)(2,1)S(1)}, u32[]{:S(2)}, u32[]{:S(2)}) collective-permute-start(bf16[120,5120]{1,0:T(8,128)(2,1)} %get-tuple-element.246), channel_id=1, source_target_pairs={{0,4},{2,6},{4,0},{6,2},{8,12},{10,14},{12,8},{14,10},{16,20},{18,... | collective-permute-start | bytes 3686408 | tf_op jit(solution)/shard_map/ppermute | solution.py:37
  181.5 20.0 %collective-permute-start.30 = (bf16[240,640]{1,0:T(8,128)(2,1)S(1)}, bf16[240,640]{1,0:T(8,128)(2,1)S(1)}, u32[]{:S(2)}, u32[]{:S(2)}) collective-permute-start(bf16[240,640]{1,0:T(8,128)(2,1)S(1)} %constant_dynamic-slice_fusion.10), channel_id=1, source_target_pairs={{0,4},{2,6},{4,0},{6,2},{8,12},{10,14},{12,8},{14,10},{16,20},{18,... | collective-permute-start | bytes 921608 | tf_op jit(solution)/shard_map/ppermute | solution.py:37
  182.4 19.2 %collective-permute-start.31 = (bf16[240,640]{1,0:T(8,128)(2,1)S(1)}, bf16[240,640]{1,0:T(8,128)(2,1)S(1)}, u32[]{:S(2)}, u32[]{:S(2)}) collective-permute-start(bf16[240,640]{1,0:T(8,128)(2,1)S(1)} %constant_dynamic-slice_fusion.9), channel_id=1, source_target_pairs={{0,2},{2,0},{4,6},{6,4},{8,10},{10,8},{12,14},{14,12},{16,18},{18,... | collective-permute-start | bytes 921608 | tf_op jit(solution)/shard_map/ppermute | solution.py:37
  182.8 18.8 %collective-permute-start.29 = (bf16[256,960]{1,0:T(8,128)(2,1)S(1)}, bf16[256,960]{1,0:T(8,128)(2,1)S(1)}, u32[]{:S(2)}, u32[]{:S(2)}) collective-permute-start(bf16[256,960]{1,0:T(8,128)(2,1)S(1)} %copy-done.49), channel_id=1, source_target_pairs={{0,1},{1,0},{2,3},{3,2},{4,5},{5,4},{6,7},{7,6},{8,9},{9,8},{10,11... | collective-permute-start | bytes 1474568 | tf_op jit(solution)/shard_map/ppermute | solution.py:41
  182.8 21.0 %collective-permute-start.32 = (bf16[8,64,640]{2,1,0:T(8,128)(2,1)S(1)}, bf16[8,64,640]{2,1,0:T(8,128)(2,1)S(1)}, u32[]{:S(2)}, u32[]{:S(2)}) collective-permute-start(bf16[8,64,640]{2,1,0:T(8,128)(2,1)S(1)} %slice.159), channel_id=1, source_target_pairs={{0,2},{2,0},{4,6},{6,4},{8,10},{10,8},{12,14},{14,12},{16,18},{18,... | collective-permute-start | bytes 1966088 | tf_op jit(solution)/shard_map/ppermute | solution.py:37
  184.5 19.3 %collective-permute-start.33 = (bf16[8,64,640]{2,1,0:T(8,128)(2,1)S(1)}, bf16[8,64,640]{2,1,0:T(8,128)(2,1)S(1)}, u32[]{:S(2)}, u32[]{:S(2)}) collective-permute-start(bf16[8,64,640]{2,1,0:T(8,128)(2,1)S(1)} %slice.160), channel_id=1, source_target_pairs={{0,4},{2,6},{4,0},{6,2},{8,12},{10,14},{12,8},{14,10},{16,20},{18,... | collective-permute-start | bytes 1966088 | tf_op jit(solution)/shard_map/ppermute | solution.py:37
  201.5 23.8 %collective-permute-start.42 = (bf16[480,256]{1,0:T(8,128)(2,1)S(1)}, bf16[480,256]{1,0:T(8,128)(2,1)S(1)}, u32[]{:S(2)}, u32[]{:S(2)}) collective-permute-start(bf16[480,256]{1,0:T(8,128)(2,1)S(1)} %fusion.13), channel_id=1, source_target_pairs={{0,1},{1,0},{2,3},{3,2},{4,5},{5,4},{6,7},{7,6},{8,9},{9,8},{10,11... | collective-permute-start | bytes 737288 | tf_op jit(solution)/shard_map/ppermute | solution.py:41
  211.5 21.7 %collective-permute-start.38 = (bf16[8,64,640]{2,1,0:T(8,128)(2,1)S(1)}, bf16[8,64,640]{2,1,0:T(8,128)(2,1)S(1)}, u32[]{:S(2)}, u32[]{:S(2)}) collective-permute-start(bf16[8,64,640]{2,1,0:T(8,128)(2,1)S(1)} %slice.162), channel_id=1, source_target_pairs={{0,2},{2,0},{4,6},{6,4},{8,10},{10,8},{12,14},{14,12},{16,18},{18,... | collective-permute-start | bytes 1966088 | tf_op jit(solution)/shard_map/ppermute | solution.py:37
  211.6 23.4 %collective-permute-start.39 = (bf16[8,64,640]{2,1,0:T(8,128)(2,1)S(1)}, bf16[8,64,640]{2,1,0:T(8,128)(2,1)S(1)}, u32[]{:S(2)}, u32[]{:S(2)}) collective-permute-start(bf16[8,64,640]{2,1,0:T(8,128)(2,1)S(1)} %slice.163), channel_id=1, source_target_pairs={{0,4},{2,6},{4,0},{6,2},{8,12},{10,14},{12,8},{14,10},{16,20},{18,... | collective-permute-start | bytes 1966088 | tf_op jit(solution)/shard_map/ppermute | solution.py:37
  293.5 20.3 %collective-permute-start.61 = (bf16[2,256,640]{2,1,0:T(8,128)(2,1)S(1)}, bf16[2,256,640]{2,1,0:T(8,128)(2,1)S(1)}, u32[]{:S(2)}, u32[]{:S(2)}) collective-permute-start(bf16[2,256,640]{2,1,0:T(8,128)(2,1)S(1)} %slice.177), channel_id=1, source_target_pairs={{0,8},{2,10},{4,12},{6,14},{8,0},{10,2},{12,4},{14,6},{16,24},{18,... | collective-permute-start | bytes 1966088 | tf_op jit(solution)/shard_map/ppermute | solution.py:37
  295.4 21.0 %collective-permute-start.64 = (bf16[240,1280]{1,0:T(8,128)(2,1)S(1)}, bf16[240,1280]{1,0:T(8,128)(2,1)S(1)}, u32[]{:S(2)}, u32[]{:S(2)}) collective-permute-start(bf16[240,1280]{1,0:T(8,128)(2,1)S(1)} %pad_maximum_fusion.26), channel_id=1, source_target_pairs={{0,2},{2,0},{4,6},{6,4},{8,10},{10,8},{12,14},{14,12},{16,18},{18,... | collective-permute-start | bytes 1843208 | tf_op jit(solution)/shard_map/ppermute | solution.py:37
  297.3 20.7 %collective-permute-start.65 = (bf16[240,1280]{1,0:T(8,128)(2,1)S(1)}, bf16[240,1280]{1,0:T(8,128)(2,1)S(1)}, u32[]{:S(2)}, u32[]{:S(2)}) collective-permute-start(bf16[240,1280]{1,0:T(8,128)(2,1)S(1)} %pad_maximum_fusion.27), channel_id=1, source_target_pairs={{0,4},{2,6},{4,0},{6,2},{8,12},{10,14},{12,8},{14,10},{16,20},{18,... | collective-permute-start | bytes 1843208 | tf_op jit(solution)/shard_map/ppermute | solution.py:37
  301.7 26.1 %collective-permute-start.63 = (bf16[120,2560]{1,0:T(8,128)(2,1)S(1)}, bf16[120,2560]{1,0:T(8,128)(2,1)}, u32[]{:S(2)}, u32[]{:S(2)}) collective-permute-start(bf16[120,2560]{1,0:T(8,128)(2,1)S(1)} %get-tuple-element.348), channel_id=1, source_target_pairs={{0,2},{2,0},{4,6},{6,4},{8,10},{10,8},{12,14},{14,12},{16,18},{18,... | collective-permute-start | bytes 1843208 | tf_op jit(solution)/shard_map/ppermute | solution.py:37
  303.3 25.9 %collective-permute-start.62 = (bf16[120,2560]{1,0:T(8,128)(2,1)S(1)}, bf16[120,2560]{1,0:T(8,128)(2,1)}, u32[]{:S(2)}, u32[]{:S(2)}) collective-permute-start(bf16[120,2560]{1,0:T(8,128)(2,1)S(1)} %get-tuple-element.344), channel_id=1, source_target_pairs={{0,4},{2,6},{4,0},{6,2},{8,12},{10,14},{12,8},{14,10},{16,20},{18,... | collective-permute-start | bytes 1843208 | tf_op jit(solution)/shard_map/ppermute | solution.py:37
  314.0 21.0 %collective-permute-start.67 = (bf16[1,256,640]{2,1,0:T(8,128)(2,1)S(1)}, bf16[1,256,640]{2,1,0:T(8,128)(2,1)S(1)}, u32[]{:S(2)}, u32[]{:S(2)}) collective-permute-start(bf16[1,256,640]{2,1,0:T(8,128)(2,1)S(1)} %slice.207), channel_id=1, source_target_pairs={{0,16},{2,18},{4,20},{6,22},{8,24},{10,26},{12,28},{14,30},{16,0},... | collective-permute-start | bytes 983048 | tf_op jit(solution)/shard_map/ppermute | solution.py:37
  (137 other events, 1348.3 us)
Sparse Core Ops, SparseCore 0:
  9.6 13.0 all-gather.4
  24.2 16.2 all-gather.6
  42.0 15.5 all-gather.8
  59.0 15.8 all-gather.10

commit v7 on v6

--- a/solution.py
+++ b/solution.py
@@ -518,7 +518,7 @@
         scratch_shapes=[pltpu.VMEM((LANES, HEADS * BLK), bf16), pltpu.VMEM((LANES, GCOLS), f32)],
         compiler_params=pltpu.CompilerParams(vmem_limit_bytes=4 << 20),
         cost_estimate=pl.CostEstimate(
-            flops=4 * HEADS * HD * BLK * BLK * 8,
+            flops=256 * HEADS * HD * BLK * BLK,
             bytes_accessed=first.size * 4,
             transcendentals=HEADS * BLK * BLK * 8,
         ),
@@ -548,7 +548,7 @@
         ],
         compiler_params=pltpu.CompilerParams(vmem_limit_bytes=8 << 20),
         cost_estimate=pl.CostEstimate(
-            flops=10 * HEADS * HD * BLK * BLK,
+            flops=640 * HEADS * HD * BLK * BLK,
             bytes_accessed=first.size,
             transcendentals=HEADS * BLK * BLK,
         ),
@@ -731,7 +731,7 @@
         out_shape=[pltpu.HBM(shape, bf16) for shape in shapes],
         compiler_params=pltpu.CompilerParams(vmem_limit_bytes=11 << 20),
         cost_estimate=pl.CostEstimate(
-            flops=2 * sum(rows * width for rows, width in shapes) * 512,
+            flops=16 * sum(rows * width for rows, width in shapes) * 512,
             bytes_accessed=2 * sum(rows * width for rows, width in shapes),
             transcendentals=0,
         ),

time: 409 us -> 405 us (level)
  waiting for transfers between devices: 159 us -> 175 us
  Pallas kernels: 82.3 us -> 67.3 us
    ppermute x74, waiting for transfers between devices: 151 us -> 171 us  [flip_ctx(): return lax.ppermute(value, 'ctx', [(i, i ^ mask) for i in range(size)])]
    pallas_call x2, Pallas kernels: 22.6 us -> 14.2 us  [attention_backward(): pl.pallas_call(functools.partial(backward_kernel, steps > WINDOW // BLK,...]
    pallas_call x2, Pallas kernels: 18.2 us -> 11.4 us  [attention_forward(): pl.pallas_call(functools.partial(forward_kernel, steps > WINDOW // BLK, s...]
    ppermute x14, waiting for transfers between devices: 6.32 us -> 1.8 us  [swap_fsdp(): return lax.ppermute(value, 'fsdp', [(0, 1), (1, 0)])]
    unnamed x139 -> x125, local copies, waits for them, and re-layouts: 12.6 us -> 11 us
  transfers between devices with their start and end apart: 92 -> 92, of which waited for: 43 -> 47; matrix products, arithmetic and copies ran while one was open for 11% -> 11% of each run, Pallas kernels for 16% -> 12%
where the time goes in v7:
time: 405 us; the launch traced here: 400 us
  waiting for transfers between devices  175 us (43%)
  starting transfers between devices  87.5 us (22%)
  Pallas kernels  67.3 us (17%)
  other arithmetic  36.8 us (9%)
  between operations  15.8 us (4%)
  local copies, waits for them, and re-layouts  15.4 us (4%)
    ppermute x74, waiting for transfers between devices, flip_ctx(): return lax.ppermute(value, 'ctx', [(i, i ^ mask) for i in range(size)])  171 us
    ppermute x74, starting transfers between devices, flip_ctx(): return lax.ppermute(value, 'ctx', [(i, i ^ mask) for i in range(size)])  85.1 us
    pallas_call x3, Pallas kernels, weight_grad(): pl.pallas_call(functools.partial(weight_grad_kernel, products, sides), gr...  21.1 us
    pallas_call x1, Pallas kernels, feed_forward(): pl.pallas_call(block_kernel, grid=(inner // tile,), in_specs=[fixed(wide)...  17.5 us
    pallas_call x2, Pallas kernels, attention_backward(): pl.pallas_call(functools.partial(backward_kernel, steps > WINDOW // BLK,...  14.2 us
    pallas_call x2, Pallas kernels, attention_forward(): pl.pallas_call(functools.partial(forward_kernel, steps > WINDOW // BLK, s...  11.4 us
    convert_element_type x5, other arithmetic, rows_of(): jnp.concatenate([q[:, columns] for q in quarters], axis=0).astype(f32)  11.4 us
    unnamed x125, local copies, waits for them, and re-layouts  11 us
  transfers between devices with their start and end apart: 92, of which 47 were waited for; matrix products, arithmetic and copies ran while one was open for 11% of the time, Pallas kernels for 12%

profile of v7, /device:TPU:0, one launch (start us, length us, event | category | flops | bytes accessed | tf_op | source)
XLA Modules:
  0.0 400.0 jit_solution(2218876813792499973)
XLA Ops:
  13.3 4.9 %collective-permute-start.4 = (bf16[1,128,640]{2,1,0:T(8,128)(2,1)S(1)}, bf16[1,128,640]{2,1,0:T(8,128)(2,1)S(1)}, u32[]{:S(2)}, u32[]{:S(2)}) collective-permute-start(bf16[1,128,640]{2,1,0:T(8,128)(2,1)S(1)} %get-tuple-element.431), channel_id=1, source_target_pairs={{0,24},{2,26},{4,28},{6,30},{8,16},{10,18},{12,20},{14,22},{16,8},... | collective-permute-start | bytes 491528 | tf_op jit(solution)/shard_map/ppermute | solution.py:37
  23.1 4.3 %collective-permute-done.3 = bf16[1,128,640]{2,1,0:T(8,128)(2,1)S(1)} collective-permute-done((bf16[1,128,640]{2,1,0:T(8,128)(2,1)S(1)}, bf16[1,128,640]{2,1,0:T(8,128)(2,1)S(1)}, u32[]{:S(2)}, u32[]{:S(2)}) %collective-permute-start.3) | collective-permute-done | bytes 163872 | tf_op jit(solution)/shard_map/ppermute | solution.py:37
  28.1 4.5 %collective-permute-done.2 = bf16[1,128,640]{2,1,0:T(8,128)(2,1)} collective-permute-done((bf16[1,128,640]{2,1,0:T(8,128)(2,1)S(1)}, bf16[1,128,640]{2,1,0:T(8,128)(2,1)}, u32[]{:S(2)}, u32[]{:S(2)}) %collective-permute-start.2) | collective-permute-done | bytes 163872 | tf_op jit(solution)/shard_map/ppermute | solution.py:37
  52.8 12.1 %collective-permute-done.12 = bf16[1,128,640]{2,1,0:T(8,128)(2,1)S(1)} collective-permute-done((bf16[1,128,640]{2,1,0:T(8,128)(2,1)S(1)}, bf16[1,128,640]{2,1,0:T(8,128)(2,1)S(1)}, u32[]{:S(2)}, u32[]{:S(2)}) %collective-permute-start.12) | collective-permute-done | bytes 163872 | tf_op jit(solution)/shard_map/ppermute | solution.py:37
  70.0 5.0 %collective-permute-done.18 = bf16[1,480,512]{2,1,0:T(8,128)(2,1)S(1)} collective-permute-done((bf16[1,480,512]{2,1,0:T(8,128)(2,1)S(1)}, bf16[1,480,512]{2,1,0:T(8,128)(2,1)S(1)}, u32[]{:S(2)}, u32[]{:S(2)}) %collective-permute-start.18) | collective-permute-done | bytes 491552 | tf_op jit(solution)/shard_map/ppermute | solution.py:37
  83.7 9.8 %collective-permute-done.20 = bf16[8,64,640]{2,1,0:T(8,128)(2,1)S(1)} collective-permute-done((bf16[8,64,640]{2,1,0:T(8,128)(2,1)S(1)}, bf16[8,64,640]{2,1,0:T(8,128)(2,1)S(1)}, u32[]{:S(2)}, u32[]{:S(2)}) %collective-permute-start.20) | collective-permute-done | bytes 655392 | tf_op jit(solution)/shard_map/ppermute | solution.py:37
  96.9 7.9 %attention_forward.3 = (f32[960,128]{1,0:T(8,128)S(1)}, f32[1,1920]{1,0:T(1,128)S(1)}) custom-call(s32[2]{0:T(128)S(1)} %pad_add_fusion.ids, s32[2,2,2]{2,1,0:T(2,128)S(1)} %copy-done.8, s32[2,2,16]{2,1,0:T(2,128)S(1)} %copy-done.9, bf16[16,64,640]{2,1,0:T(8,128)(2,1)S(1)} %pad_maximum_fusion.4.first_ref, ...), custom_call_target="tpu_custom_call" | custom-call | flops 4026531840 | bytes 2621440 | tf_op jit(solution)/shard_map/attention_forward/pallas_call | solution.py:508
  107.4 17.5 %feed_forward.1 = (bf16[256,2560]{1,0:T(8,128)(2,1)}, bf16[2,256,2560]{2,1,0:T(8,128)(2,1)}, bf16[960,256]{1,0:T(8,128)(2,1)}, bf16[960,256]{1,0:T(8,128)(2,1)},...) custom-call(bf16[960,256]{1,0:T(8,128)(2,1)} %pad_maximum_fusion.29.x_ref, ...), custom_call_target="tpu_custom_call" | custom-call | flops 7549747200 | bytes 19660800 | tf_op jit(solution)/shard_map/feed_forward/pallas_call | solution.py:641
  131.1 5.2 %down_grad.1 = (bf16[240,1280]{1,0:T(8,128)(2,1)}, bf16[240,1280]{1,0:T(8,128)(2,1)}, bf16[240,1280]{1,0:T(8,128)(2,1)}, bf16[240,1280]{1,0:T(8,128)(2,1)}) custom-call(s32[2]{0:T(128)S(1)} %pad_add_fusion.ids, bf16[960,256]{1,0:T(8,128)(2,1)} %copy-done.41, bf16[960,256]{1,0:T(8,128)(2,1)} %copy-done.56, bf16[256,2560]{1,0:T(8,128)(2,1)} %get-tuple-element.224.refs_2_, ...), custom_call_target="tpu_custom_call" | custom-call | flops 10066329600 | bytes 2457600 | tf_op jit(solution)/shard_map/down_grad/pallas_call | solution.py:723
  138.1 10.7 %inner_grad.1 = (bf16[120,5120]{1,0:T(8,128)(2,1)}, bf16[120,5120]{1,0:T(8,128)(2,1)}, bf16[120,5120]{1,0:T(8,128)(2,1)}, bf16[120,5120]{1,0:T(8,128)(2,1)}) custom-call(s32[2]{0:T(128)S(1)} %pad_add_fusion.ids, bf16[960,256]{1,0:T(8,128)(2,1)} %get-tuple-element.229.refs_0_, bf16[480,256]{1,0:T(8,128)(2,1)} %copy-done.61, ...), custom_call_target="tpu_custom_call" | custom-call | flops 20132659200 | bytes 4915200 | tf_op jit(solution)/shard_map/inner_grad/pallas_call | solution.py:723
  153.4 4.4 %attention_backward.2 = (bf16[960,128]{1,0:T(8,128)(2,1)S(1)}, bf16[16,64,640]{2,1,0:T(8,128)(2,1)S(1)}, bf16[16,64,640]{2,1,0:T(8,128)(2,1)S(1)}) custom-call(s32[2]{0:T(128)S(1)} %pad_add_fusion.ids, s32[2,2,2]{2,1,0:T(2,128)S(1)} %copy-done.8, s32[2,2,16]{2,1,0:T(2,128)S(1)} %copy-done.9, bf16[16,64,640]{2,1,0:T(8,128)(2,1)S(1)} %get-tuple-element.448.first_ref, ...), custom_call_target="tpu_custom_call" | custom-call | flops 10066329600 | bytes 655360 | tf_op jit(solution)/shard_map/attention_backward/pallas_call | solution.py:531
  159.4 19.5 %collective-permute-done.27 = bf16[120,5120]{1,0:T(8,128)(2,1)S(1)} collective-permute-done((bf16[120,5120]{1,0:T(8,128)(2,1)}, bf16[120,5120]{1,0:T(8,128)(2,1)S(1)}, u32[]{:S(2)}, u32[]{:S(2)}) %collective-permute-start.27) | collective-permute-done | bytes 1228832 | tf_op jit(solution)/shard_map/ppermute | solution.py:37
  186.2 9.8 %attention_backward.3 = (bf16[960,128]{1,0:T(8,128)(2,1)S(1)}, bf16[16,64,640]{2,1,0:T(8,128)(2,1)S(1)}, bf16[16,64,640]{2,1,0:T(8,128)(2,1)S(1)}) custom-call(s32[2]{0:T(128)S(1)} %pad_add_fusion.ids, s32[2,2,2]{2,1,0:T(2,128)S(1)} %copy-done.8, s32[2,2,16]{2,1,0:T(2,128)S(1)} %copy-done.9, bf16[16,64,640]{2,1,0:T(8,128)(2,1)S(1)} %copy-done.1, ...), custom_call_target="tpu_custom_call" | custom-call | flops 10066329600 | bytes 655360 | tf_op jit(solution)/shard_map/attention_backward/pallas_call | solution.py:531
  196.4 6.4 %collective-permute-done.32 = bf16[8,64,640]{2,1,0:T(8,128)(2,1)S(1)} collective-permute-done((bf16[8,64,640]{2,1,0:T(8,128)(2,1)S(1)}, bf16[8,64,640]{2,1,0:T(8,128)(2,1)S(1)}, u32[]{:S(2)}, u32[]{:S(2)}) %collective-permute-start.32) | collective-permute-done | bytes 655392 | tf_op jit(solution)/shard_map/ppermute | solution.py:37
  212.3 8.8 %collective-permute-done.35 = bf16[120,2560]{1,0:T(8,128)(2,1)S(1)} collective-permute-done((bf16[120,2560]{1,0:T(8,128)(2,1)S(1)}, bf16[120,2560]{1,0:T(8,128)(2,1)S(1)}, u32[]{:S(2)}, u32[]{:S(2)}) %collective-permute-start.35) | collective-permute-done | bytes 614432 | tf_op jit(solution)/shard_map/ppermute | solution.py:37
  227.4 5.2 %query_grad.1 = (bf16[240,960]{1,0:T(8,128)(2,1)}, bf16[240,960]{1,0:T(8,128)(2,1)}, bf16[240,960]{1,0:T(8,128)(2,1)}, bf16[240,960]{1,0:T(8,128)(2,1)}) custom-call(s32[2]{0:T(128)S(1)} %pad_add_fusion.ids, bf16[960,256]{1,0:T(8,128)(2,1)} %copy-done.17, bf16[480,256]{1,0:T(8,128)(2,1)} %copy-done.46, bf16[960,256]{1,0:T(8,128)(2,1)} %copy-done.49, ...), custom_call_target="tpu_custom_call" | custom-call | flops 7549747200 | bytes 1843200 | tf_op jit(solution)/shard_map/query_grad/pallas_call | solution.py:723
  247.9 4.5 %collective-permute-done.45 = bf16[120,640]{1,0:T(8,128)(2,1)S(1)} collective-permute-done((bf16[120,640]{1,0:T(8,128)(2,1)S(1)}, bf16[120,640]{1,0:T(8,128)(2,1)S(1)}, u32[]{:S(2)}, u32[]{:S(2)}) %collective-permute-start.45) | collective-permute-done | bytes 153632 | tf_op jit(solution)/shard_map/ppermute | solution.py:37
  260.6 7.1 %collective-permute-done.51 = bf16[240,640]{1,0:T(8,128)(2,1)S(1)} collective-permute-done((bf16[240,640]{1,0:T(8,128)(2,1)S(1)}, bf16[240,640]{1,0:T(8,128)(2,1)S(1)}, u32[]{:S(2)}, u32[]{:S(2)}) %collective-permute-start.51) | collective-permute-done | bytes 307232 | tf_op jit(solution)/shard_map/ppermute | solution.py:37
  278.6 6.9 %collective-permute-done.56 = bf16[120,960]{1,0:T(8,128)(2,1)S(1)} collective-permute-done((bf16[120,960]{1,0:T(8,128)(2,1)S(1)}, bf16[120,960]{1,0:T(8,128)(2,1)S(1)}, u32[]{:S(2)}, u32[]{:S(2)}) %collective-permute-start.56) | collective-permute-done | bytes 230432 | tf_op jit(solution)/shard_map/ppermute | solution.py:37
  294.2 4.0 %collective-permute-done.60 = bf16[120,960]{1,0:T(8,128)(2,1)S(1)} collective-permute-done((bf16[120,960]{1,0:T(8,128)(2,1)S(1)}, bf16[120,960]{1,0:T(8,128)(2,1)S(1)}, u32[]{:S(2)}, u32[]{:S(2)}) %collective-permute-start.60) | collective-permute-done | bytes 230432 | tf_op jit(solution)/shard_map/ppermute | solution.py:37
  300.2 10.2 %collective-permute-done.61 = bf16[2,256,640]{2,1,0:T(8,128)(2,1)S(1)} collective-permute-done((bf16[2,256,640]{2,1,0:T(8,128)(2,1)S(1)}, bf16[2,256,640]{2,1,0:T(8,128)(2,1)S(1)}, u32[]{:S(2)}, u32[]{:S(2)}) %collective-permute-start.61) | collective-permute-done | bytes 655392 | tf_op jit(solution)/shard_map/ppermute | solution.py:37
  317.0 7.2 %collective-permute-done.63 = bf16[120,2560]{1,0:T(8,128)(2,1)} collective-permute-done((bf16[120,2560]{1,0:T(8,128)(2,1)S(1)}, bf16[120,2560]{1,0:T(8,128)(2,1)}, u32[]{:S(2)}, u32[]{:S(2)}) %collective-permute-start.63) | collective-permute-done | bytes 614432 | tf_op jit(solution)/shard_map/ppermute | solution.py:37
  326.2 5.3 %collective-permute-done.68 = bf16[120,480]{1,0:T(8,128)(2,1)S(1)} collective-permute-done((bf16[120,480]{1,0:T(8,128)(2,1)S(1)}, bf16[120,480]{1,0:T(8,128)(2,1)S(1)}, u32[]{:S(2)}, u32[]{:S(2)}) %collective-permute-start.68) | collective-permute-done | bytes 115232 | tf_op jit(solution)/shard_map/ppermute | solution.py:37
  347.3 7.9 %collective-permute-done.76 = f32[960]{0:T(1024)S(1)} collective-permute-done((f32[960]{0:T(1024)S(1)}, f32[960]{0:T(1024)S(1)}, u32[]{:S(2)}, u32[]{:S(2)}) %collective-permute-start.76) | collective-permute-done | bytes 3872 | tf_op jit(solution)/shard_map/ppermute | solution.py:37
  (450 shorter events, 194.9 us)
Async XLA Ops:
  7.2 100.2 %all-gather.5.cloned.1.call-start = ((), (), s32[]{:S(2)}) async-start(), calls=%async_computation | async-start | bytes 2949120 | tf_op jit(solution)/shard_map/all_gather | solution.py:810
  7.9 99.4 %all-gather.7.cloned.1.call-start = ((), (), s32[]{:S(2)}) async-start(), calls=%async_computation.1 | async-start | bytes 7372800 | tf_op jit(solution)/shard_map/all_gather | solution.py:810
  8.7 98.7 %all-gather.9.cloned.1.call-start = ((), (), s32[]{:S(2)}) async-start(), calls=%async_computation.2 | async-start | bytes 7372800 | tf_op jit(solution)/shard_map/all_gather | solution.py:810
  9.4 97.9 %all-gather.11.cloned.1.call-start = ((), (), s32[]{:S(2)}) async-start(), calls=%async_computation.3 | async-start | bytes 7372800 | tf_op jit(solution)/shard_map/all_gather | solution.py:810
  44.1 20.8 %collective-permute-start.12 = (bf16[1,128,640]{2,1,0:T(8,128)(2,1)S(1)}, bf16[1,128,640]{2,1,0:T(8,128)(2,1)S(1)}, u32[]{:S(2)}, u32[]{:S(2)}) collective-permute-start(bf16[1,128,640]{2,1,0:T(8,128)(2,1)S(1)} %get-tuple-element.430), channel_id=1, source_target_pairs={{0,16},{2,18},{4,20},{6,22},{8,24},{10,26},{12,28},{14,30},{16,0},... | collective-permute-start | bytes 491528 | tf_op jit(solution)/shard_map/ppermute | solution.py:37
  45.4 19.5 %collective-permute-start.11 = (bf16[8,64,640]{2,1,0:T(8,128)(2,1)S(1)}, bf16[8,64,640]{2,1,0:T(8,128)(2,1)S(1)}, u32[]{:S(2)}, u32[]{:S(2)}) collective-permute-start(bf16[8,64,640]{2,1,0:T(8,128)(2,1)S(1)} %pad_maximum_fusion.21), channel_id=1, source_target_pairs={{0,4},{2,6},{4,0},{6,2},{8,12},{10,14},{12,8},{14,10},{16,20},{18,... | collective-permute-start | bytes 1966088 | tf_op jit(solution)/shard_map/ppermute | solution.py:37
  48.7 26.3 %collective-permute-start.18 = (bf16[1,480,512]{2,1,0:T(8,128)(2,1)S(1)}, bf16[1,480,512]{2,1,0:T(8,128)(2,1)S(1)}, u32[]{:S(2)}, u32[]{:S(2)}) collective-permute-start(bf16[1,480,512]{2,1,0:T(8,128)(2,1)S(1)} %maximum_bitcast_fusion), channel_id=1, source_target_pairs={{0,16},{2,18},{4,20},{6,22},{8,24},{10,26},{12,28},{14,30},{16,0},... | collective-permute-start | bytes 1474568 | tf_op jit(solution)/shard_map/ppermute | solution.py:37
  80.0 24.8 %collective-permute-start.21 = (bf16[2,480,512]{2,1,0:T(8,128)(2,1)S(1)}, bf16[2,480,512]{2,1,0:T(8,128)(2,1)S(1)}, u32[]{:S(2)}, u32[]{:S(2)}) collective-permute-start(bf16[2,480,512]{2,1,0:T(8,128)(2,1)S(1)} %pad_maximum_fusion.15), channel_id=1, source_target_pairs={{0,8},{2,10},{4,12},{6,14},{8,0},{10,2},{12,4},{14,6},{16,24},{18,... | collective-permute-start | bytes 2949128 | tf_op jit(solution)/shard_map/ppermute | solution.py:37
  148.8 30.2 %collective-permute-start.27 = (bf16[120,5120]{1,0:T(8,128)(2,1)}, bf16[120,5120]{1,0:T(8,128)(2,1)S(1)}, u32[]{:S(2)}, u32[]{:S(2)}) collective-permute-start(bf16[120,5120]{1,0:T(8,128)(2,1)} %get-tuple-element.245), channel_id=1, source_target_pairs={{0,2},{2,0},{4,6},{6,4},{8,10},{10,8},{12,14},{14,12},{16,18},{18,... | collective-permute-start | bytes 3686408 | tf_op jit(solution)/shard_map/ppermute | solution.py:37
  150.2 28.8 %collective-permute-start.28 = (bf16[120,5120]{1,0:T(8,128)(2,1)}, bf16[120,5120]{1,0:T(8,128)(2,1)S(1)}, u32[]{:S(2)}, u32[]{:S(2)}) collective-permute-start(bf16[120,5120]{1,0:T(8,128)(2,1)} %get-tuple-element.246), channel_id=1, source_target_pairs={{0,4},{2,6},{4,0},{6,2},{8,12},{10,14},{12,8},{14,10},{16,20},{18,... | collective-permute-start | bytes 3686408 | tf_op jit(solution)/shard_map/ppermute | solution.py:37
  182.0 20.8 %collective-permute-start.32 = (bf16[8,64,640]{2,1,0:T(8,128)(2,1)S(1)}, bf16[8,64,640]{2,1,0:T(8,128)(2,1)S(1)}, u32[]{:S(2)}, u32[]{:S(2)}) collective-permute-start(bf16[8,64,640]{2,1,0:T(8,128)(2,1)S(1)} %slice.159), channel_id=1, source_target_pairs={{0,2},{2,0},{4,6},{6,4},{8,10},{10,8},{12,14},{14,12},{16,18},{18,... | collective-permute-start | bytes 1966088 | tf_op jit(solution)/shard_map/ppermute | solution.py:37
  182.4 20.4 %collective-permute-start.33 = (bf16[8,64,640]{2,1,0:T(8,128)(2,1)S(1)}, bf16[8,64,640]{2,1,0:T(8,128)(2,1)S(1)}, u32[]{:S(2)}, u32[]{:S(2)}) collective-permute-start(bf16[8,64,640]{2,1,0:T(8,128)(2,1)S(1)} %slice.160), channel_id=1, source_target_pairs={{0,4},{2,6},{4,0},{6,2},{8,12},{10,14},{12,8},{14,10},{16,20},{18,... | collective-permute-start | bytes 1966088 | tf_op jit(solution)/shard_map/ppermute | solution.py:37
  196.3 30.4 %collective-permute-start.42 = (bf16[480,256]{1,0:T(8,128)(2,1)S(1)}, bf16[480,256]{1,0:T(8,128)(2,1)S(1)}, u32[]{:S(2)}, u32[]{:S(2)}) collective-permute-start(bf16[480,256]{1,0:T(8,128)(2,1)S(1)} %fusion.13), channel_id=1, source_target_pairs={{0,1},{1,0},{2,3},{3,2},{4,5},{5,4},{6,7},{7,6},{8,9},{9,8},{10,11... | collective-permute-start | bytes 737288 | tf_op jit(solution)/shard_map/ppermute | solution.py:41
  210.5 23.3 %collective-permute-start.38 = (bf16[8,64,640]{2,1,0:T(8,128)(2,1)S(1)}, bf16[8,64,640]{2,1,0:T(8,128)(2,1)S(1)}, u32[]{:S(2)}, u32[]{:S(2)}) collective-permute-start(bf16[8,64,640]{2,1,0:T(8,128)(2,1)S(1)} %slice.162), channel_id=1, source_target_pairs={{0,2},{2,0},{4,6},{6,4},{8,10},{10,8},{12,14},{14,12},{16,18},{18,... | collective-permute-start | bytes 1966088 | tf_op jit(solution)/shard_map/ppermute | solution.py:37
  211.7 23.4 %collective-permute-start.39 = (bf16[8,64,640]{2,1,0:T(8,128)(2,1)S(1)}, bf16[8,64,640]{2,1,0:T(8,128)(2,1)S(1)}, u32[]{:S(2)}, u32[]{:S(2)}) collective-permute-start(bf16[8,64,640]{2,1,0:T(8,128)(2,1)S(1)} %slice.163), channel_id=1, source_target_pairs={{0,4},{2,6},{4,0},{6,2},{8,12},{10,14},{12,8},{14,10},{16,20},{18,... | collective-permute-start | bytes 1966088 | tf_op jit(solution)/shard_map/ppermute | solution.py:37
  226.0 20.2 %collective-permute-start.43 = (bf16[4,64,640]{2,1,0:T(8,128)(2,1)S(1)}, bf16[4,64,640]{2,1,0:T(8,128)(2,1)S(1)}, u32[]{:S(2)}, u32[]{:S(2)}) collective-permute-start(bf16[4,64,640]{2,1,0:T(8,128)(2,1)S(1)} %slice.198), channel_id=1, source_target_pairs={{0,4},{2,6},{4,0},{6,2},{8,12},{10,14},{12,8},{14,10},{16,20},{18,... | collective-permute-start | bytes 983048 | tf_op jit(solution)/shard_map/ppermute | solution.py:37
  291.2 19.1 %collective-permute-start.61 = (bf16[2,256,640]{2,1,0:T(8,128)(2,1)S(1)}, bf16[2,256,640]{2,1,0:T(8,128)(2,1)S(1)}, u32[]{:S(2)}, u32[]{:S(2)}) collective-permute-start(bf16[2,256,640]{2,1,0:T(8,128)(2,1)S(1)} %slice.177), channel_id=1, source_target_pairs={{0,8},{2,10},{4,12},{6,14},{8,0},{10,2},{12,4},{14,6},{16,24},{18,... | collective-permute-start | bytes 1966088 | tf_op jit(solution)/shard_map/ppermute | solution.py:37
  293.2 19.9 %collective-permute-start.64 = (bf16[240,1280]{1,0:T(8,128)(2,1)S(1)}, bf16[240,1280]{1,0:T(8,128)(2,1)S(1)}, u32[]{:S(2)}, u32[]{:S(2)}) collective-permute-start(bf16[240,1280]{1,0:T(8,128)(2,1)S(1)} %pad_maximum_fusion.26), channel_id=1, source_target_pairs={{0,2},{2,0},{4,6},{6,4},{8,10},{10,8},{12,14},{14,12},{16,18},{18,... | collective-permute-start | bytes 1843208 | tf_op jit(solution)/shard_map/ppermute | solution.py:37
  293.9 19.6 %collective-permute-start.65 = (bf16[240,1280]{1,0:T(8,128)(2,1)S(1)}, bf16[240,1280]{1,0:T(8,128)(2,1)S(1)}, u32[]{:S(2)}, u32[]{:S(2)}) collective-permute-start(bf16[240,1280]{1,0:T(8,128)(2,1)S(1)} %pad_maximum_fusion.27), channel_id=1, source_target_pairs={{0,4},{2,6},{4,0},{6,2},{8,12},{10,14},{12,8},{14,10},{16,20},{18,... | collective-permute-start | bytes 1843208 | tf_op jit(solution)/shard_map/ppermute | solution.py:37
  298.3 25.9 %collective-permute-start.63 = (bf16[120,2560]{1,0:T(8,128)(2,1)S(1)}, bf16[120,2560]{1,0:T(8,128)(2,1)}, u32[]{:S(2)}, u32[]{:S(2)}) collective-permute-start(bf16[120,2560]{1,0:T(8,128)(2,1)S(1)} %get-tuple-element.348), channel_id=1, source_target_pairs={{0,2},{2,0},{4,6},{6,4},{8,10},{10,8},{12,14},{14,12},{16,18},{18,... | collective-permute-start | bytes 1843208 | tf_op jit(solution)/shard_map/ppermute | solution.py:37
  299.9 24.9 %collective-permute-start.62 = (bf16[120,2560]{1,0:T(8,128)(2,1)S(1)}, bf16[120,2560]{1,0:T(8,128)(2,1)}, u32[]{:S(2)}, u32[]{:S(2)}) collective-permute-start(bf16[120,2560]{1,0:T(8,128)(2,1)S(1)} %get-tuple-element.344), channel_id=1, source_target_pairs={{0,4},{2,6},{4,0},{6,2},{8,12},{10,14},{12,8},{14,10},{16,20},{18,... | collective-permute-start | bytes 1843208 | tf_op jit(solution)/shard_map/ppermute | solution.py:37
  310.6 21.0 %collective-permute-start.67 = (bf16[1,256,640]{2,1,0:T(8,128)(2,1)S(1)}, bf16[1,256,640]{2,1,0:T(8,128)(2,1)S(1)}, u32[]{:S(2)}, u32[]{:S(2)}) collective-permute-start(bf16[1,256,640]{2,1,0:T(8,128)(2,1)S(1)} %slice.207), channel_id=1, source_target_pairs={{0,16},{2,18},{4,20},{6,22},{8,24},{10,26},{12,28},{14,30},{16,0},... | collective-permute-start | bytes 983048 | tf_op jit(solution)/shard_map/ppermute | solution.py:37
  313.0 18.5 %collective-permute-start.66 = (bf16[120,640]{1,0:T(8,128)(2,1)S(1)}, bf16[120,640]{1,0:T(8,128)(2,1)S(1)}, u32[]{:S(2)}, u32[]{:S(2)}) collective-permute-start(bf16[120,640]{1,0:T(8,128)(2,1)S(1)} %constant_dynamic-slice_fusion.1), channel_id=1, source_target_pairs={{0,4},{2,6},{4,0},{6,2},{8,12},{10,14},{12,8},{14,10},{16,20},{18,... | collective-permute-start | bytes 460808 | tf_op jit(solution)/shard_map/ppermute | solution.py:37
  313.4 18.1 %collective-permute-start.68 = (bf16[120,480]{1,0:T(8,128)(2,1)S(1)}, bf16[120,480]{1,0:T(8,128)(2,1)S(1)}, u32[]{:S(2)}, u32[]{:S(2)}) collective-permute-start(bf16[120,480]{1,0:T(8,128)(2,1)S(1)} %constant_dynamic-slice_fusion), channel_id=1, source_target_pairs={{0,16},{2,18},{4,20},{6,22},{8,24},{10,26},{12,28},{14,30},{16,0},... | collective-permute-start | bytes 345608 | tf_op jit(solution)/shard_map/ppermute | solution.py:37
  (130 other events, 1280.9 us)
Sparse Core Ops, SparseCore 0:
  9.6 13.0 all-gather.4
  24.2 16.2 all-gather.6
  42.0 15.5 all-gather.8
  59.0 15.8 all-gather.10

commit v8 on v7

--- a/solution.py
+++ b/solution.py
@@ -226,7 +226,7 @@
 class SumVector:
     def __init__(self, value):
         self.value = value
-        self.stages = high_bits() + [0, 1]
+        self.stages = [0, 1] + high_bits()
 
     def operands(self):
         return [self.value], [self.stages[0]]
@@ -1045,7 +1045,6 @@
     rounds.begin(last_job, query_spread, gain_job)
     down_sum = rows_of(down_spread.quarters)
     (down_sum,) = rounds.end([last_job, query_spread, gain_job, third], down_sum)
-    rounds.run(gain_job, 3)
 
     rounds.begin(last_job, query_spread, gain_job)
     scaled = grad_normed_t * attn_gain
@@ -1068,11 +1067,11 @@
 
     rounds.begin(last_job, query_spread, gain_job)
     gate_sum = rows_of(quarters, slice(0, inner))
+    (gate_sum,) = rounds.end([gain_job], gate_sum)
+    rounds.run(gain_job, 1)
+    rounds.begin(gain_job)
     up_sum = rows_of(quarters, slice(inner, None))
-    (gate_sum, up_sum) = rounds.end([last_job, query_spread, gain_job], gate_sum, up_sum)
-    rounds.begin(gain_job)
-    rounds.end([gain_job])
-    rounds.run(gain_job, 0)
+    (up_sum,) = rounds.end([last_job, query_spread, gain_job], up_sum)
 
     def by_token(value_t):
         parts = [value_t[:, m * BLK : (m + 1) * BLK].T[None] for m in range(micro)]

time: 405 us -> 406 us (level)
  Pallas kernels: 67.3 us -> 57.2 us
  waiting for transfers between devices: 175 us -> 180 us
  starting transfers between devices: 87.5 us -> 92.2 us
    pallas_call x2, Pallas kernels: 14.2 us -> 8.62 us  [attention_backward(): pl.pallas_call(functools.partial(backward_kernel, steps > WINDOW // BLK,...]
    ppermute x74, waiting for transfers between devices: 171 us -> 176 us  [flip_ctx(): return lax.ppermute(value, 'ctx', [(i, i ^ mask) for i in range(size)])]
    pallas_call x2, Pallas kernels: 11.4 us -> 6.94 us  [attention_forward(): pl.pallas_call(functools.partial(forward_kernel, steps > WINDOW // BLK, s...]
  transfers between devices with their start and end apart: 92 -> 92, of which waited for: 47 -> 45; matrix products, arithmetic and copies ran while one was open for 11% -> 9% of each run, Pallas kernels for 12% -> 10%
where the time goes in v8:
time: 406 us; the launch traced here: 400 us
  waiting for transfers between devices  180 us (44%)
  starting transfers between devices  92.2 us (23%)
  Pallas kernels  57.2 us (14%)
  other arithmetic  36.8 us (9%)
  between operations  15.8 us (4%)
  local copies, waits for them, and re-layouts  15.5 us (4%)
    ppermute x74, waiting for transfers between devices, flip_ctx(): return lax.ppermute(value, 'ctx', [(i, i ^ mask) for i in range(size)])  176 us
    ppermute x74, starting transfers between devices, flip_ctx(): return lax.ppermute(value, 'ctx', [(i, i ^ mask) for i in range(size)])  87 us
    pallas_call x3, Pallas kernels, weight_grad(): pl.pallas_call(functools.partial(weight_grad_kernel, products, sides), gr...  21.1 us
    pallas_call x1, Pallas kernels, feed_forward(): pl.pallas_call(block_kernel, grid=(inner // tile,), in_specs=[fixed(wide)...  17.5 us
    convert_element_type x5, other arithmetic, rows_of(): jnp.concatenate([q[:, columns] for q in quarters], axis=0).astype(f32)  11.4 us
    unnamed x125, local copies, waits for them, and re-layouts  11 us
    pallas_call x2, Pallas kernels, attention_backward(): pl.pallas_call(functools.partial(backward_kernel, steps > WINDOW // BLK,...  8.62 us
    select_n x25, other arithmetic, by_bit(): return (jnp.where(low, mine, arrived), jnp.where(low, arrived, mine))  8.27 us
  transfers between devices with their start and end apart: 92, of which 45 were waited for; matrix products, arithmetic and copies ran while one was open for 9% of the time, Pallas kernels for 10%

profile of v8, /device:TPU:0, one launch (start us, length us, event | category | flops | bytes accessed | tf_op | source)
XLA Modules:
  0.0 400.2 jit_solution(3204520546960885907)
XLA Ops:
  13.3 4.9 %collective-permute-start.4 = (bf16[1,128,640]{2,1,0:T(8,128)(2,1)S(1)}, bf16[1,128,640]{2,1,0:T(8,128)(2,1)S(1)}, u32[]{:S(2)}, u32[]{:S(2)}) collective-permute-start(bf16[1,128,640]{2,1,0:T(8,128)(2,1)S(1)} %get-tuple-element.433), channel_id=1, source_target_pairs={{0,24},{2,26},{4,28},{6,30},{8,16},{10,18},{12,20},{14,22},{16,8},... | collective-permute-start | bytes 491528 | tf_op jit(solution)/shard_map/ppermute | solution.py:37
  23.1 4.3 %collective-permute-done.3 = bf16[1,128,640]{2,1,0:T(8,128)(2,1)S(1)} collective-permute-done((bf16[1,128,640]{2,1,0:T(8,128)(2,1)S(1)}, bf16[1,128,640]{2,1,0:T(8,128)(2,1)S(1)}, u32[]{:S(2)}, u32[]{:S(2)}) %collective-permute-start.3) | collective-permute-done | bytes 163872 | tf_op jit(solution)/shard_map/ppermute | solution.py:37
  28.1 4.5 %collective-permute-done.2 = bf16[1,128,640]{2,1,0:T(8,128)(2,1)} collective-permute-done((bf16[1,128,640]{2,1,0:T(8,128)(2,1)S(1)}, bf16[1,128,640]{2,1,0:T(8,128)(2,1)}, u32[]{:S(2)}, u32[]{:S(2)}) %collective-permute-start.2) | collective-permute-done | bytes 163872 | tf_op jit(solution)/shard_map/ppermute | solution.py:37
  52.8 12.1 %collective-permute-done.12 = bf16[1,128,640]{2,1,0:T(8,128)(2,1)S(1)} collective-permute-done((bf16[1,128,640]{2,1,0:T(8,128)(2,1)S(1)}, bf16[1,128,640]{2,1,0:T(8,128)(2,1)S(1)}, u32[]{:S(2)}, u32[]{:S(2)}) %collective-permute-start.12) | collective-permute-done | bytes 163872 | tf_op jit(solution)/shard_map/ppermute | solution.py:37
  70.0 5.0 %collective-permute-done.18 = bf16[1,480,512]{2,1,0:T(8,128)(2,1)S(1)} collective-permute-done((bf16[1,480,512]{2,1,0:T(8,128)(2,1)S(1)}, bf16[1,480,512]{2,1,0:T(8,128)(2,1)S(1)}, u32[]{:S(2)}, u32[]{:S(2)}) %collective-permute-start.18) | collective-permute-done | bytes 491552 | tf_op jit(solution)/shard_map/ppermute | solution.py:37
  83.7 9.8 %collective-permute-done.20 = bf16[8,64,640]{2,1,0:T(8,128)(2,1)S(1)} collective-permute-done((bf16[8,64,640]{2,1,0:T(8,128)(2,1)S(1)}, bf16[8,64,640]{2,1,0:T(8,128)(2,1)S(1)}, u32[]{:S(2)}, u32[]{:S(2)}) %collective-permute-start.20) | collective-permute-done | bytes 655392 | tf_op jit(solution)/shard_map/ppermute | solution.py:37
  105.1 17.5 %feed_forward.1 = (bf16[256,2560]{1,0:T(8,128)(2,1)}, bf16[2,256,2560]{2,1,0:T(8,128)(2,1)}, bf16[960,256]{1,0:T(8,128)(2,1)}, bf16[960,256]{1,0:T(8,128)(2,1)},...) custom-call(bf16[960,256]{1,0:T(8,128)(2,1)} %pad_maximum_fusion.29.x_ref, ...), custom_call_target="tpu_custom_call" | custom-call | flops 7549747200 | bytes 19660800 | tf_op jit(solution)/shard_map/feed_forward/pallas_call | solution.py:641
  128.9 5.3 %down_grad.1 = (bf16[240,1280]{1,0:T(8,128)(2,1)}, bf16[240,1280]{1,0:T(8,128)(2,1)}, bf16[240,1280]{1,0:T(8,128)(2,1)}, bf16[240,1280]{1,0:T(8,128)(2,1)}) custom-call(s32[2]{0:T(128)S(1)} %pad_add_fusion.ids, bf16[960,256]{1,0:T(8,128)(2,1)} %copy-done.41, bf16[960,256]{1,0:T(8,128)(2,1)} %copy-done.56, bf16[256,2560]{1,0:T(8,128)(2,1)} %get-tuple-element.225.refs_2_, ...), custom_call_target="tpu_custom_call" | custom-call | flops 10066329600 | bytes 2457600 | tf_op jit(solution)/shard_map/down_grad/pallas_call | solution.py:723
  139.7 10.7 %inner_grad.1 = (bf16[120,5120]{1,0:T(8,128)(2,1)}, bf16[120,5120]{1,0:T(8,128)(2,1)}, bf16[120,5120]{1,0:T(8,128)(2,1)}, bf16[120,5120]{1,0:T(8,128)(2,1)}) custom-call(s32[2]{0:T(128)S(1)} %pad_add_fusion.ids, bf16[960,256]{1,0:T(8,128)(2,1)} %get-tuple-element.230.refs_0_, bf16[480,256]{1,0:T(8,128)(2,1)} %copy-done.61, ...), custom_call_target="tpu_custom_call" | custom-call | flops 20132659200 | bytes 4915200 | tf_op jit(solution)/shard_map/inner_grad/pallas_call | solution.py:723
  154.2 4.4 %attention_backward.2 = (bf16[960,128]{1,0:T(8,128)(2,1)S(1)}, bf16[16,64,640]{2,1,0:T(8,128)(2,1)S(1)}, bf16[16,64,640]{2,1,0:T(8,128)(2,1)S(1)}) custom-call(s32[2]{0:T(128)S(1)} %pad_add_fusion.ids, s32[2,2,2]{2,1,0:T(2,128)S(1)} %copy-done.8, s32[2,2,16]{2,1,0:T(2,128)S(1)} %copy-done.9, bf16[16,64,640]{2,1,0:T(8,128)(2,1)S(1)} %get-tuple-element.450.first_ref, ...), custom_call_target="tpu_custom_call" | custom-call | flops 10066329600 | bytes 655360 | tf_op jit(solution)/shard_map/attention_backward/pallas_call | solution.py:531
  160.2 19.1 %collective-permute-done.27 = bf16[120,5120]{1,0:T(8,128)(2,1)S(1)} collective-permute-done((bf16[120,5120]{1,0:T(8,128)(2,1)}, bf16[120,5120]{1,0:T(8,128)(2,1)S(1)}, u32[]{:S(2)}, u32[]{:S(2)}) %collective-permute-start.27) | collective-permute-done | bytes 1228832 | tf_op jit(solution)/shard_map/ppermute | solution.py:37
  187.8 4.2 %attention_backward.3 = (bf16[960,128]{1,0:T(8,128)(2,1)S(1)}, bf16[16,64,640]{2,1,0:T(8,128)(2,1)S(1)}, bf16[16,64,640]{2,1,0:T(8,128)(2,1)S(1)}) custom-call(s32[2]{0:T(128)S(1)} %pad_add_fusion.ids, s32[2,2,2]{2,1,0:T(2,128)S(1)} %copy-done.8, s32[2,2,16]{2,1,0:T(2,128)S(1)} %copy-done.9, bf16[16,64,640]{2,1,0:T(8,128)(2,1)S(1)} %copy-done.1, ...), custom_call_target="tpu_custom_call" | custom-call | flops 10066329600 | bytes 655360 | tf_op jit(solution)/shard_map/attention_backward/pallas_call | solution.py:531
  195.2 9.2 %collective-permute-done.32 = bf16[8,64,640]{2,1,0:T(8,128)(2,1)S(1)} collective-permute-done((bf16[8,64,640]{2,1,0:T(8,128)(2,1)S(1)}, bf16[8,64,640]{2,1,0:T(8,128)(2,1)S(1)}, u32[]{:S(2)}, u32[]{:S(2)}) %collective-permute-start.32) | collective-permute-done | bytes 655392 | tf_op jit(solution)/shard_map/ppermute | solution.py:37
  207.7 4.2 %collective-permute-done.37 = bf16[240,640]{1,0:T(8,128)(2,1)S(1)} collective-permute-done((bf16[240,640]{1,0:T(8,128)(2,1)S(1)}, bf16[240,640]{1,0:T(8,128)(2,1)S(1)}, u32[]{:S(2)}, u32[]{:S(2)}) %collective-permute-start.37) | collective-permute-done | bytes 307232 | tf_op jit(solution)/shard_map/ppermute | solution.py:37
  213.9 7.7 %collective-permute-done.35 = bf16[120,2560]{1,0:T(8,128)(2,1)S(1)} collective-permute-done((bf16[120,2560]{1,0:T(8,128)(2,1)S(1)}, bf16[120,2560]{1,0:T(8,128)(2,1)S(1)}, u32[]{:S(2)}, u32[]{:S(2)}) %collective-permute-start.35) | collective-permute-done | bytes 614432 | tf_op jit(solution)/shard_map/ppermute | solution.py:37
  228.1 5.2 %query_grad.1 = (bf16[240,960]{1,0:T(8,128)(2,1)}, bf16[240,960]{1,0:T(8,128)(2,1)}, bf16[240,960]{1,0:T(8,128)(2,1)}, bf16[240,960]{1,0:T(8,128)(2,1)}) custom-call(s32[2]{0:T(128)S(1)} %pad_add_fusion.ids, bf16[960,256]{1,0:T(8,128)(2,1)} %copy-done.17, bf16[480,256]{1,0:T(8,128)(2,1)} %copy-done.46, bf16[960,256]{1,0:T(8,128)(2,1)} %copy-done.49, ...), custom_call_target="tpu_custom_call" | custom-call | flops 7549747200 | bytes 1843200 | tf_op jit(solution)/shard_map/query_grad/pallas_call | solution.py:723
  235.6 4.2 %collective-permute-done.41 = bf16[120,2560]{1,0:T(8,128)(2,1)S(1)} collective-permute-done((bf16[120,2560]{1,0:T(8,128)(2,1)S(1)}, bf16[120,2560]{1,0:T(8,128)(2,1)S(1)}, u32[]{:S(2)}, u32[]{:S(2)}) %collective-permute-start.41) | collective-permute-done | bytes 614432 | tf_op jit(solution)/shard_map/ppermute | solution.py:37
  246.8 4.7 %collective-permute-done.45 = bf16[120,640]{1,0:T(8,128)(2,1)S(1)} collective-permute-done((bf16[120,640]{1,0:T(8,128)(2,1)S(1)}, bf16[120,640]{1,0:T(8,128)(2,1)S(1)}, u32[]{:S(2)}, u32[]{:S(2)}) %collective-permute-start.45) | collective-permute-done | bytes 153632 | tf_op jit(solution)/shard_map/ppermute | solution.py:37
  260.1 7.5 %collective-permute-done.51 = bf16[240,640]{1,0:T(8,128)(2,1)S(1)} collective-permute-done((bf16[240,640]{1,0:T(8,128)(2,1)S(1)}, bf16[240,640]{1,0:T(8,128)(2,1)S(1)}, u32[]{:S(2)}, u32[]{:S(2)}) %collective-permute-start.51) | collective-permute-done | bytes 307232 | tf_op jit(solution)/shard_map/ppermute | solution.py:37
  278.0 8.2 %collective-permute-done.56 = bf16[120,960]{1,0:T(8,128)(2,1)S(1)} collective-permute-done((bf16[120,960]{1,0:T(8,128)(2,1)S(1)}, bf16[120,960]{1,0:T(8,128)(2,1)S(1)}, u32[]{:S(2)}, u32[]{:S(2)}) %collective-permute-start.56) | collective-permute-done | bytes 230432 | tf_op jit(solution)/shard_map/ppermute | solution.py:37
  300.9 10.0 %collective-permute-done.61 = bf16[2,256,640]{2,1,0:T(8,128)(2,1)S(1)} collective-permute-done((bf16[2,256,640]{2,1,0:T(8,128)(2,1)S(1)}, bf16[2,256,640]{2,1,0:T(8,128)(2,1)S(1)}, u32[]{:S(2)}, u32[]{:S(2)}) %collective-permute-start.61) | collective-permute-done | bytes 655392 | tf_op jit(solution)/shard_map/ppermute | solution.py:37
  316.8 8.2 %collective-permute-done.63 = bf16[120,2560]{1,0:T(8,128)(2,1)} collective-permute-done((bf16[120,2560]{1,0:T(8,128)(2,1)S(1)}, bf16[120,2560]{1,0:T(8,128)(2,1)}, u32[]{:S(2)}, u32[]{:S(2)}) %collective-permute-start.63) | collective-permute-done | bytes 614432 | tf_op jit(solution)/shard_map/ppermute | solution.py:37
  326.7 5.5 %collective-permute-done.68 = bf16[120,480]{1,0:T(8,128)(2,1)S(1)} collective-permute-done((bf16[120,480]{1,0:T(8,128)(2,1)S(1)}, bf16[120,480]{1,0:T(8,128)(2,1)S(1)}, u32[]{:S(2)}, u32[]{:S(2)}) %collective-permute-start.68) | collective-permute-done | bytes 115232 | tf_op jit(solution)/shard_map/ppermute | solution.py:37
  348.0 7.4 %collective-permute-done.76 = f32[960]{0:T(1024)S(1)} collective-permute-done((f32[960]{0:T(1024)S(1)}, f32[960]{0:T(1024)S(1)}, u32[]{:S(2)}, u32[]{:S(2)}) %collective-permute-start.76) | collective-permute-done | bytes 3872 | tf_op jit(solution)/shard_map/ppermute | solution.py:37
  (450 shorter events, 200.7 us)
Async XLA Ops:
  7.2 97.9 %all-gather.5.cloned.1.call-start = ((), (), s32[]{:S(2)}) async-start(), calls=%async_computation | async-start | bytes 2949120 | tf_op jit(solution)/shard_map/all_gather | solution.py:810
  7.9 97.2 %all-gather.7.cloned.1.call-start = ((), (), s32[]{:S(2)}) async-start(), calls=%async_computation.1 | async-start | bytes 7372800 | tf_op jit(solution)/shard_map/all_gather | solution.py:810
  8.7 96.4 %all-gather.9.cloned.1.call-start = ((), (), s32[]{:S(2)}) async-start(), calls=%async_computation.2 | async-start | bytes 7372800 | tf_op jit(solution)/shard_map/all_gather | solution.py:810
  9.4 95.7 %all-gather.11.cloned.1.call-start = ((), (), s32[]{:S(2)}) async-start(), calls=%async_computation.3 | async-start | bytes 7372800 | tf_op jit(solution)/shard_map/all_gather | solution.py:810
  44.1 20.8 %collective-permute-start.12 = (bf16[1,128,640]{2,1,0:T(8,128)(2,1)S(1)}, bf16[1,128,640]{2,1,0:T(8,128)(2,1)S(1)}, u32[]{:S(2)}, u32[]{:S(2)}) collective-permute-start(bf16[1,128,640]{2,1,0:T(8,128)(2,1)S(1)} %get-tuple-element.432), channel_id=1, source_target_pairs={{0,16},{2,18},{4,20},{6,22},{8,24},{10,26},{12,28},{14,30},{16,0},... | collective-permute-start | bytes 491528 | tf_op jit(solution)/shard_map/ppermute | solution.py:37
  45.4 19.5 %collective-permute-start.11 = (bf16[8,64,640]{2,1,0:T(8,128)(2,1)S(1)}, bf16[8,64,640]{2,1,0:T(8,128)(2,1)S(1)}, u32[]{:S(2)}, u32[]{:S(2)}) collective-permute-start(bf16[8,64,640]{2,1,0:T(8,128)(2,1)S(1)} %pad_maximum_fusion.21), channel_id=1, source_target_pairs={{0,4},{2,6},{4,0},{6,2},{8,12},{10,14},{12,8},{14,10},{16,20},{18,... | collective-permute-start | bytes 1966088 | tf_op jit(solution)/shard_map/ppermute | solution.py:37
  48.7 26.3 %collective-permute-start.18 = (bf16[1,480,512]{2,1,0:T(8,128)(2,1)S(1)}, bf16[1,480,512]{2,1,0:T(8,128)(2,1)S(1)}, u32[]{:S(2)}, u32[]{:S(2)}) collective-permute-start(bf16[1,480,512]{2,1,0:T(8,128)(2,1)S(1)} %maximum_bitcast_fusion), channel_id=1, source_target_pairs={{0,16},{2,18},{4,20},{6,22},{8,24},{10,26},{12,28},{14,30},{16,0},... | collective-permute-start | bytes 1474568 | tf_op jit(solution)/shard_map/ppermute | solution.py:37
  80.0 22.6 %collective-permute-start.21 = (bf16[2,480,512]{2,1,0:T(8,128)(2,1)S(1)}, bf16[2,480,512]{2,1,0:T(8,128)(2,1)S(1)}, u32[]{:S(2)}, u32[]{:S(2)}) collective-permute-start(bf16[2,480,512]{2,1,0:T(8,128)(2,1)S(1)} %pad_maximum_fusion.15), channel_id=1, source_target_pairs={{0,8},{2,10},{4,12},{6,14},{8,0},{10,2},{12,4},{14,6},{16,24},{18,... | collective-permute-start | bytes 2949128 | tf_op jit(solution)/shard_map/ppermute | solution.py:37
  150.3 29.0 %collective-permute-start.27 = (bf16[120,5120]{1,0:T(8,128)(2,1)}, bf16[120,5120]{1,0:T(8,128)(2,1)S(1)}, u32[]{:S(2)}, u32[]{:S(2)}) collective-permute-start(bf16[120,5120]{1,0:T(8,128)(2,1)} %get-tuple-element.246), channel_id=1, source_target_pairs={{0,2},{2,0},{4,6},{6,4},{8,10},{10,8},{12,14},{14,12},{16,18},{18,... | collective-permute-start | bytes 3686408 | tf_op jit(solution)/shard_map/ppermute | solution.py:37
  152.3 28.4 %collective-permute-start.28 = (bf16[120,5120]{1,0:T(8,128)(2,1)}, bf16[120,5120]{1,0:T(8,128)(2,1)S(1)}, u32[]{:S(2)}, u32[]{:S(2)}) collective-permute-start(bf16[120,5120]{1,0:T(8,128)(2,1)} %get-tuple-element.247), channel_id=1, source_target_pairs={{0,4},{2,6},{4,0},{6,2},{8,12},{10,14},{12,8},{14,10},{16,20},{18,... | collective-permute-start | bytes 3686408 | tf_op jit(solution)/shard_map/ppermute | solution.py:37
  183.8 20.6 %collective-permute-start.32 = (bf16[8,64,640]{2,1,0:T(8,128)(2,1)S(1)}, bf16[8,64,640]{2,1,0:T(8,128)(2,1)S(1)}, u32[]{:S(2)}, u32[]{:S(2)}) collective-permute-start(bf16[8,64,640]{2,1,0:T(8,128)(2,1)S(1)} %slice.159), channel_id=1, source_target_pairs={{0,2},{2,0},{4,6},{6,4},{8,10},{10,8},{12,14},{14,12},{16,18},{18,... | collective-permute-start | bytes 1966088 | tf_op jit(solution)/shard_map/ppermute | solution.py:37
  184.2 20.2 %collective-permute-start.33 = (bf16[8,64,640]{2,1,0:T(8,128)(2,1)S(1)}, bf16[8,64,640]{2,1,0:T(8,128)(2,1)S(1)}, u32[]{:S(2)}, u32[]{:S(2)}) collective-permute-start(bf16[8,64,640]{2,1,0:T(8,128)(2,1)S(1)} %slice.160), channel_id=1, source_target_pairs={{0,4},{2,6},{4,0},{6,2},{8,12},{10,14},{12,8},{14,10},{16,20},{18,... | collective-permute-start | bytes 1966088 | tf_op jit(solution)/shard_map/ppermute | solution.py:37
  192.4 35.0 %collective-permute-start.42 = (bf16[480,256]{1,0:T(8,128)(2,1)S(1)}, bf16[480,256]{1,0:T(8,128)(2,1)S(1)}, u32[]{:S(2)}, u32[]{:S(2)}) collective-permute-start(bf16[480,256]{1,0:T(8,128)(2,1)S(1)} %fusion.13), channel_id=1, source_target_pairs={{0,1},{1,0},{2,3},{3,2},{4,5},{5,4},{6,7},{7,6},{8,9},{9,8},{10,11... | collective-permute-start | bytes 737288 | tf_op jit(solution)/shard_map/ppermute | solution.py:41
  211.9 21.4 %collective-permute-start.38 = (bf16[8,64,640]{2,1,0:T(8,128)(2,1)S(1)}, bf16[8,64,640]{2,1,0:T(8,128)(2,1)S(1)}, u32[]{:S(2)}, u32[]{:S(2)}) collective-permute-start(bf16[8,64,640]{2,1,0:T(8,128)(2,1)S(1)} %slice.162), channel_id=1, source_target_pairs={{0,2},{2,0},{4,6},{6,4},{8,10},{10,8},{12,14},{14,12},{16,18},{18,... | collective-permute-start | bytes 1966088 | tf_op jit(solution)/shard_map/ppermute | solution.py:37
  212.9 22.6 %collective-permute-start.39 = (bf16[8,64,640]{2,1,0:T(8,128)(2,1)S(1)}, bf16[8,64,640]{2,1,0:T(8,128)(2,1)S(1)}, u32[]{:S(2)}, u32[]{:S(2)}) collective-permute-start(bf16[8,64,640]{2,1,0:T(8,128)(2,1)S(1)} %slice.163), channel_id=1, source_target_pairs={{0,4},{2,6},{4,0},{6,2},{8,12},{10,14},{12,8},{14,10},{16,20},{18,... | collective-permute-start | bytes 1966088 | tf_op jit(solution)/shard_map/ppermute | solution.py:37
  225.6 20.4 %collective-permute-start.43 = (bf16[4,64,640]{2,1,0:T(8,128)(2,1)S(1)}, bf16[4,64,640]{2,1,0:T(8,128)(2,1)S(1)}, u32[]{:S(2)}, u32[]{:S(2)}) collective-permute-start(bf16[4,64,640]{2,1,0:T(8,128)(2,1)S(1)} %slice.198), channel_id=1, source_target_pairs={{0,4},{2,6},{4,0},{6,2},{8,12},{10,14},{12,8},{14,10},{16,20},{18,... | collective-permute-start | bytes 983048 | tf_op jit(solution)/shard_map/ppermute | solution.py:37
  290.6 20.3 %collective-permute-start.61 = (bf16[2,256,640]{2,1,0:T(8,128)(2,1)S(1)}, bf16[2,256,640]{2,1,0:T(8,128)(2,1)S(1)}, u32[]{:S(2)}, u32[]{:S(2)}) collective-permute-start(bf16[2,256,640]{2,1,0:T(8,128)(2,1)S(1)} %slice.177), channel_id=1, source_target_pairs={{0,8},{2,10},{4,12},{6,14},{8,0},{10,2},{12,4},{14,6},{16,24},{18,... | collective-permute-start | bytes 1966088 | tf_op jit(solution)/shard_map/ppermute | solution.py:37
  292.6 21.0 %collective-permute-start.64 = (bf16[240,1280]{1,0:T(8,128)(2,1)S(1)}, bf16[240,1280]{1,0:T(8,128)(2,1)S(1)}, u32[]{:S(2)}, u32[]{:S(2)}) collective-permute-start(bf16[240,1280]{1,0:T(8,128)(2,1)S(1)} %pad_maximum_fusion.26), channel_id=1, source_target_pairs={{0,2},{2,0},{4,6},{6,4},{8,10},{10,8},{12,14},{14,12},{16,18},{18,... | collective-permute-start | bytes 1843208 | tf_op jit(solution)/shard_map/ppermute | solution.py:37
  294.4 19.8 %collective-permute-start.65 = (bf16[240,1280]{1,0:T(8,128)(2,1)S(1)}, bf16[240,1280]{1,0:T(8,128)(2,1)S(1)}, u32[]{:S(2)}, u32[]{:S(2)}) collective-permute-start(bf16[240,1280]{1,0:T(8,128)(2,1)S(1)} %pad_maximum_fusion.27), channel_id=1, source_target_pairs={{0,4},{2,6},{4,0},{6,2},{8,12},{10,14},{12,8},{14,10},{16,20},{18,... | collective-permute-start | bytes 1843208 | tf_op jit(solution)/shard_map/ppermute | solution.py:37
  298.8 26.1 %collective-permute-start.63 = (bf16[120,2560]{1,0:T(8,128)(2,1)S(1)}, bf16[120,2560]{1,0:T(8,128)(2,1)}, u32[]{:S(2)}, u32[]{:S(2)}) collective-permute-start(bf16[120,2560]{1,0:T(8,128)(2,1)S(1)} %get-tuple-element.349), channel_id=1, source_target_pairs={{0,2},{2,0},{4,6},{6,4},{8,10},{10,8},{12,14},{14,12},{16,18},{18,... | collective-permute-start | bytes 1843208 | tf_op jit(solution)/shard_map/ppermute | solution.py:37
  300.4 25.0 %collective-permute-start.62 = (bf16[120,2560]{1,0:T(8,128)(2,1)S(1)}, bf16[120,2560]{1,0:T(8,128)(2,1)}, u32[]{:S(2)}, u32[]{:S(2)}) collective-permute-start(bf16[120,2560]{1,0:T(8,128)(2,1)S(1)} %get-tuple-element.345), channel_id=1, source_target_pairs={{0,4},{2,6},{4,0},{6,2},{8,12},{10,14},{12,8},{14,10},{16,20},{18,... | collective-permute-start | bytes 1843208 | tf_op jit(solution)/shard_map/ppermute | solution.py:37
  311.1 21.0 %collective-permute-start.67 = (bf16[1,256,640]{2,1,0:T(8,128)(2,1)S(1)}, bf16[1,256,640]{2,1,0:T(8,128)(2,1)S(1)}, u32[]{:S(2)}, u32[]{:S(2)}) collective-permute-start(bf16[1,256,640]{2,1,0:T(8,128)(2,1)S(1)} %slice.207), channel_id=1, source_target_pairs={{0,16},{2,18},{4,20},{6,22},{8,24},{10,26},{12,28},{14,30},{16,0},... | collective-permute-start | bytes 983048 | tf_op jit(solution)/shard_map/ppermute | solution.py:37
  367.4 20.4 %collective-permute-start.84 = (bf16[240,640]{1,0:T(8,128)(2,1)S(1)}, bf16[240,640]{1,0:T(8,128)(2,1)S(1)}, u32[]{:S(2)}, u32[]{:S(2)}) collective-permute-start(bf16[240,640]{1,0:T(8,128)(2,1)S(1)} %pad_maximum_fusion.35), channel_id=1, source_target_pairs={{0,2},{2,0},{4,6},{6,4},{8,10},{10,8},{12,14},{14,12},{16,18},{18,... | collective-permute-start | bytes 921608 | tf_op jit(solution)/shard_map/ppermute | solution.py:37
  369.0 18.8 %collective-permute-start.85 = (bf16[240,960]{1,0:T(8,128)(2,1)S(1)}, bf16[240,960]{1,0:T(8,128)(2,1)S(1)}, u32[]{:S(2)}, u32[]{:S(2)}) collective-permute-start(bf16[240,960]{1,0:T(8,128)(2,1)S(1)} %pad_maximum_fusion.32), channel_id=1, source_target_pairs={{0,2},{2,0},{4,6},{6,4},{8,10},{10,8},{12,14},{14,12},{16,18},{18,... | collective-permute-start | bytes 1382408 | tf_op jit(solution)/shard_map/ppermute | solution.py:37
  (130 other events, 1269.2 us)
Sparse Core Ops, SparseCore 0:
  9.6 13.0 all-gather.4
  24.2 16.2 all-gather.6
  42.0 15.5 all-gather.8
  59.0 15.8 all-gather.10
